TPU v7x, 32 devices: a whole 2x2x4 slice. The times are simulated.
32 devices in a mesh: dp: 8 (over y, x, core), blk: 4 (over z).
Axes of the slice: x: 2, y: 2, z: 4, core: 2. Of those that a mesh axis runs over, the one named last changes fastest.
Arguments:
- raw_input: float32 [8, 1024, 768], P('dp', 'blk'), may hold values from -72 to 72
- cotangent: bfloat16 [8, 1024, 768], P('dp', 'blk'), may hold values from -36 to 36
- segment_ids: int32 [8, 1024], P('dp', 'blk'), may hold values from 0 to 3, never falling along the last dimension, each value on 1 to 512 neighbouring positions
- step_count: int32 [1], replicated, may hold values from 10 to 20
- inlet_copy: bfloat16 [768, 2304], replicated, may hold values from -0.3125 to 0.3125
- inlet_master: float32 [768, 2304], P('dp'), may hold values from -0.3125 to 0.3125
- inlet_moment: float32 [768, 2304], P('dp'), may hold values from -512 to 512
- inlet_square: float32 [768, 2304], P('dp'), may hold values from 2703.36 to 22118.4
- outlet_copy: bfloat16 [768, 768], replicated, may hold values from -0.875 to 0.875
- outlet_master: float32 [768, 768], P('dp'), may hold values from -0.875 to 0.875
- outlet_moment: float32 [768, 768], P('dp'), may hold values from -256 to 256
- outlet_square: float32 [768, 768], P('dp'), may hold values from 548.864 to 4423.68
- expand_copy: bfloat16 [768, 3072], replicated, may hold values from -0.21875 to 0.21875
- expand_master: float32 [768, 3072], P('dp'), may hold values from -0.21875 to 0.21875
- expand_moment: float32 [768, 3072], P('dp'), may hold values from -256 to 256
- expand_square: float32 [768, 3072], P('dp'), may hold values from 548.864 to 4423.68
- shrink_copy: bfloat16 [3072, 768], replicated, may hold values from -0.109375 to 0.109375
- shrink_master: float32 [3072, 768], P('dp'), may hold values from -0.109375 to 0.109375
- shrink_moment: float32 [3072, 768], P('dp'), may hold values from -512 to 512
- shrink_square: float32 [3072, 768], P('dp'), may hold values from 2211.84 to 18022.4
- vector_copy: bfloat16 [12, 768], replicated, may hold values from -2 to 2
- vector_master: float32 [12, 768], P(None, 'dp'), may hold values from -2 to 2
- vector_moment: float32 [12, 768], P(None, 'dp'), may hold values from -512 to 512
- vector_square: float32 [12, 768], P(None, 'dp'), may hold values from 2703.36 to 22118.4
Outputs:
- layer_output: bfloat16 [8, 1024, 768], P('dp', 'blk')
- input_gradient: float32 [8, 1024, 768], P('dp', 'blk')
- band_mean: float32 [768], replicated
- band_variance: float32 [768], replicated
- inlet_weight: float32 [768, 2304], P('dp')
- inlet_drift: float32 [768, 2304], P('dp')
- inlet_spread: float32 [768, 2304], P('dp')
- inlet_shadow: bfloat16 [768, 2304], P('dp')
- outlet_weight: float32 [768, 768], P('dp')
- outlet_drift: float32 [768, 768], P('dp')
- outlet_spread: float32 [768, 768], P('dp')
- outlet_shadow: bfloat16 [768, 768], P('dp')
- expand_weight: float32 [768, 3072], P('dp')
- expand_drift: float32 [768, 3072], P('dp')
- expand_spread: float32 [768, 3072], P('dp')
- expand_shadow: bfloat16 [768, 3072], P('dp')
- shrink_weight: float32 [3072, 768], P('dp')
- shrink_drift: float32 [3072, 768], P('dp')
- shrink_spread: float32 [3072, 768], P('dp')
- shrink_shadow: bfloat16 [3072, 768], P('dp')
- vector_weight: float32 [12, 768], P(None, 'dp')
- vector_drift: float32 [12, 768], P(None, 'dp')
- vector_spread: float32 [12, 768], P(None, 'dp')
- vector_shadow: bfloat16 [12, 768], P(None, 'dp')
Inputs may be any that keep to these rules, and one draw needn't show every extreme that they name: `segment_ids`: within each sequence the ids never fall; each segment holds 1 to 512 positions, one of them exactly that many.
All inputs are finite; a program needn't handle non-finite values.
Results may differ from a plain program's by a relative error of at most 0.014.
Values may be sent and summed in bfloat16 or wider, within the bound.
No kernel may reach another device: no remote copies, remote signals or barrier semaphores. Data moves between devices by JAX's collectives and lax.ppermute only.
A program may use at most 256 MiB of HBM per device.

v0:
```python
import jax
import jax.numpy as jnp
from jax import lax
from jax.sharding import PartitionSpec as P

HEADS = 12


ln_epsilon = 1e-05
stat_epsilon = 1e-06
beta_one = 0.5
beta_two = 0.6
rate_matrix = 0.04
rate_vector = 0.8
warmup_length = 20.0
decay_matrix = 0.05
adam_epsilon = 1e-08
score_scale = 0.125
masked_score = -1e30


def shifted(block, axis, distance):
    devices = range(lax.axis_size(axis))
    route = [((i - distance) % len(devices), i) for i in devices]
    return lax.ppermute(block, axis, route)


def layer_norm(inputs, scaling, offset):
    centred = inputs - jnp.mean(inputs, axis=-1, keepdims=True)
    spread = jnp.mean(centred * centred, axis=-1, keepdims=True)
    return centred * lax.rsqrt(spread + ln_epsilon) * scaling + offset


def exact_gelu(inputs):
    return jax.nn.gelu(inputs, approximate=False)


def outer_rows(left, right):
    return lax.dot_general(
        left, right, (((0,), (0,)), ((), ())), preferred_element_type=jnp.float32
    )


def against_rows(left, right):
    return lax.dot_general(
        left, right, (((1,), (1,)), ((), ())), preferred_element_type=jnp.float32
    )


def adam_rule(master, moment, square, gradient, step_value, step_rate, weight_decay):
    moment_new = beta_one * moment + (1.0 - beta_one) * gradient
    square_new = beta_two * square + (1.0 - beta_two) * gradient * gradient
    fix_first = 1.0 - jnp.power(beta_one, step_value)
    fix_second = 1.0 - jnp.power(beta_two, step_value)
    planned = step_rate * jnp.minimum(1.0, step_value / warmup_length)
    direction = moment_new / fix_first / (jnp.sqrt(square_new / fix_second) + adam_epsilon)
    weight_new = master - planned * (direction + weight_decay * master)
    return (weight_new, moment_new, square_new, weight_new.astype(jnp.bfloat16))


def per_device(
    raw_input,
    cotangent,
    segment_ids,
    step_count,
    inlet_copy,
    inlet_master,
    inlet_moment,
    inlet_square,
    outlet_copy,
    outlet_master,
    outlet_moment,
    outlet_square,
    expand_copy,
    expand_master,
    expand_moment,
    expand_square,
    shrink_copy,
    shrink_master,
    shrink_moment,
    shrink_square,
    vector_copy,
    vector_master,
    vector_moment,
    vector_square,
):
    sequences, block_length, features = raw_input.shape
    group_size = lax.axis_size("blk")
    group_index = lax.axis_index("blk")
    total_tokens = lax.axis_size("dp") * group_size * sequences * block_length
    local_tokens = sequences * block_length
    head_width = features // HEADS
    shape_heads = (sequences, block_length, HEADS, head_width)
    vectors = vector_copy.astype(jnp.float32)
    flat_raw = raw_input.reshape(local_tokens, features)
    band_totals = lax.psum(
        (jnp.sum(flat_raw, axis=0), jnp.sum(flat_raw * flat_raw, axis=0)), ("dp", "blk")
    )
    band_mean = band_totals[0] / total_tokens
    band_variance = band_totals[1] / total_tokens - band_mean * band_mean
    inverse_std = lax.rsqrt(band_variance + stat_epsilon)
    normed = (flat_raw - band_mean) * inverse_std
    first_norm, first_back = jax.vjp(layer_norm, normed, vectors[0], vectors[1])
    first_in = first_norm.astype(jnp.bfloat16)
    mixed = jnp.dot(first_in, inlet_copy, preferred_element_type=jnp.float32)
    queries = (
        ((mixed[:, :features] + vectors[4]) * score_scale).astype(jnp.bfloat16).reshape(shape_heads)
    )
    own_keys = mixed[:, features : 2 * features].astype(jnp.bfloat16).reshape(shape_heads)
    own_values = (mixed[:, 2 * features :] + vectors[5]).astype(jnp.bfloat16).reshape(shape_heads)
    all_ids = lax.all_gather(segment_ids, "blk", axis=1, tiled=True)

    def allowed_pairs(offset):
        source = (group_index - offset) % group_size
        source_ids = lax.dynamic_slice_in_dim(all_ids, source * block_length, block_length, 1)
        return (segment_ids[:, :, None] == source_ids[:, None, :])[:, None]

    def score_block(key_block):
        return jnp.einsum("sqhd,skhd->shqk", queries, key_block, preferred_element_type=jnp.float32)

    running_top = jnp.full((sequences, HEADS, block_length), masked_score, jnp.float32)
    running_total = jnp.zeros((sequences, HEADS, block_length), jnp.float32)
    moving_keys = own_keys
    for offset in range(group_size):
        allowed = allowed_pairs(offset)
        masked = jnp.where(allowed, score_block(moving_keys), masked_score)
        newest_top = jnp.maximum(running_top, jnp.max(masked, axis=-1))
        fresh = jnp.sum(jnp.where(allowed, jnp.exp(masked - newest_top[..., None]), 0.0), axis=-1)
        running_total = running_total * jnp.exp(running_top - newest_top) + fresh
        running_top = newest_top
        if offset + 1 < group_size:
            moving_keys = shifted(moving_keys, "blk", 1)
    log_total = running_top + jnp.log(running_total)

    def block_probs(key_block, allowed):
        return jnp.where(allowed, jnp.exp(score_block(key_block) - log_total[..., None]), 0.0)

    attended_heads = jnp.zeros(shape_heads, jnp.float32)
    moving_pair = jnp.stack((own_keys, own_values))
    for offset in range(group_size):
        weights_low = block_probs(moving_pair[0], allowed_pairs(offset)).astype(jnp.bfloat16)
        attended_heads = attended_heads + jnp.einsum(
            "shqk,skhd->sqhd", weights_low, moving_pair[1], preferred_element_type=jnp.float32
        )
        if offset + 1 < group_size:
            moving_pair = shifted(moving_pair, "blk", 1)
    attended_low = attended_heads.reshape(local_tokens, features).astype(jnp.bfloat16)
    middle = (
        normed + jnp.dot(attended_low, outlet_copy, preferred_element_type=jnp.float32) + vectors[6]
    )
    second_norm, second_back = jax.vjp(layer_norm, middle, vectors[2], vectors[3])
    second_in = second_norm.astype(jnp.bfloat16)
    hidden_pre = jnp.dot(second_in, expand_copy, preferred_element_type=jnp.float32) + vectors[
        8:12
    ].reshape(-1)
    hidden_full, gelu_back = jax.vjp(exact_gelu, hidden_pre)
    hidden = hidden_full.astype(jnp.bfloat16)
    result = middle + jnp.dot(hidden, shrink_copy, preferred_element_type=jnp.float32) + vectors[7]
    layer_output = result.astype(jnp.bfloat16).reshape(sequences, block_length, features)
    grad_down = cotangent.reshape(local_tokens, features)
    shrink_grad = outer_rows(hidden, grad_down)
    down_grad = jnp.sum(grad_down.astype(jnp.float32), axis=0)
    grad_pre = gelu_back(against_rows(grad_down, shrink_copy))[0].astype(jnp.bfloat16)
    expand_grad = outer_rows(second_in, grad_pre)
    up_grad = jnp.sum(grad_pre.astype(jnp.float32), axis=0)
    grad_second, gain_two, shift_two = second_back(against_rows(grad_pre, expand_copy))
    grad_middle = grad_down.astype(jnp.float32) + grad_second
    grad_branch = grad_middle.astype(jnp.bfloat16)
    outlet_grad = outer_rows(attended_low, grad_branch)
    out_grad = jnp.sum(grad_branch.astype(jnp.float32), axis=0)
    grad_attended = against_rows(grad_branch, outlet_copy).astype(jnp.bfloat16).reshape(shape_heads)
    delta_rows = jnp.einsum("sqhd,sqhd->shq", grad_attended.astype(jnp.float32), attended_heads)
    grad_queries = jnp.zeros(shape_heads, jnp.float32)
    moving_pair = jnp.stack((own_keys, own_values))
    moving_grads = jnp.zeros((2,) + shape_heads, jnp.float32)
    for offset in range(group_size):
        allowed = allowed_pairs(offset)
        probs = block_probs(moving_pair[0], allowed)
        grad_probs = jnp.einsum(
            "sqhd,skhd->shqk", grad_attended, moving_pair[1], preferred_element_type=jnp.float32
        )
        grad_scores = jnp.where(allowed, probs * (grad_probs - delta_rows[..., None]), 0.0).astype(
            jnp.bfloat16
        )
        grad_queries = grad_queries + jnp.einsum(
            "shqk,skhd->sqhd", grad_scores, moving_pair[0], preferred_element_type=jnp.float32
        )
        key_part = jnp.einsum(
            "shqk,sqhd->skhd", grad_scores, queries, preferred_element_type=jnp.float32
        )
        value_part = jnp.einsum(
            "shqk,sqhd->skhd",
            probs.astype(jnp.bfloat16),
            grad_attended,
            preferred_element_type=jnp.float32,
        )
        moving_grads = moving_grads + jnp.stack((key_part, value_part))
        if offset + 1 < group_size:
            moving_pair = shifted(moving_pair, "blk", 1)
        moving_grads = shifted(moving_grads.astype(jnp.bfloat16), "blk", 1).astype(
            moving_grads.dtype
        )
    query_low = (grad_queries.astype(jnp.bfloat16) * score_scale).reshape(local_tokens, features)
    key_low = moving_grads[0].astype(jnp.bfloat16).reshape(local_tokens, features)
    value_low = moving_grads[1].astype(jnp.bfloat16).reshape(local_tokens, features)
    grad_mixed = jnp.concatenate([query_low, key_low, value_low], axis=1)
    inlet_grad = outer_rows(first_in, grad_mixed)
    query_grad = jnp.sum(query_low.astype(jnp.float32), axis=0)
    value_grad = jnp.sum(value_low.astype(jnp.float32), axis=0)
    grad_first, gain_one, shift_one = first_back(against_rows(grad_mixed, inlet_copy))
    grad_normed = grad_middle + grad_first
    centred = flat_raw - band_mean
    back_totals = lax.psum(
        (jnp.sum(grad_normed, axis=0), jnp.sum(grad_normed * centred, axis=0)), ("dp", "blk")
    )
    grad_variance = -0.5 * back_totals[1] * inverse_std * inverse_std * inverse_std
    grad_centre = -inverse_std * back_totals[0] - 2.0 * band_mean * grad_variance
    input_gradient = (
        grad_normed * inverse_std
        + grad_centre / total_tokens
        + 2.0 * grad_variance * flat_raw / total_tokens
    )
    input_gradient = input_gradient.reshape(sequences, block_length, features)
    small_rows = jnp.stack(
        [gain_one, shift_one, gain_two, shift_two, query_grad, value_grad, out_grad, down_grad]
    )
    vector_grad = jnp.concatenate([small_rows, up_grad.reshape(4, features)], axis=0)
    gradients = (inlet_grad, outlet_grad, expand_grad, shrink_grad, vector_grad)
    summed = lax.psum(
        (gradients[0], gradients[1], gradients[2], gradients[3], gradients[4]), ("dp", "blk")
    )
    owner = lax.axis_index("dp")
    shares = (
        lax.dynamic_slice_in_dim(
            summed[0], owner * inlet_master.shape[0], inlet_master.shape[0], 0
        ),
        lax.dynamic_slice_in_dim(
            summed[1], owner * outlet_master.shape[0], outlet_master.shape[0], 0
        ),
        lax.dynamic_slice_in_dim(
            summed[2], owner * expand_master.shape[0], expand_master.shape[0], 0
        ),
        lax.dynamic_slice_in_dim(
            summed[3], owner * shrink_master.shape[0], shrink_master.shape[0], 0
        ),
        lax.dynamic_slice_in_dim(
            summed[4], owner * vector_master.shape[1], vector_master.shape[1], 1
        ),
    )
    step_value = step_count[0].astype(jnp.float32)
    inlet_weight, inlet_drift, inlet_spread, inlet_shadow = adam_rule(
        inlet_master, inlet_moment, inlet_square, shares[0], step_value, rate_matrix, decay_matrix
    )
    outlet_weight, outlet_drift, outlet_spread, outlet_shadow = adam_rule(
        outlet_master,
        outlet_moment,
        outlet_square,
        shares[1],
        step_value,
        rate_matrix,
        decay_matrix,
    )
    expand_weight, expand_drift, expand_spread, expand_shadow = adam_rule(
        expand_master,
        expand_moment,
        expand_square,
        shares[2],
        step_value,
        rate_matrix,
        decay_matrix,
    )
    shrink_weight, shrink_drift, shrink_spread, shrink_shadow = adam_rule(
        shrink_master,
        shrink_moment,
        shrink_square,
        shares[3],
        step_value,
        rate_matrix,
        decay_matrix,
    )
    vector_weight, vector_drift, vector_spread, vector_shadow = adam_rule(
        vector_master, vector_moment, vector_square, shares[4], step_value, rate_vector, 0.0
    )
    return (
        layer_output,
        input_gradient,
        band_mean,
        band_variance,
        inlet_weight,
        inlet_drift,
        inlet_spread,
        inlet_shadow,
        outlet_weight,
        outlet_drift,
        outlet_spread,
        outlet_shadow,
        expand_weight,
        expand_drift,
        expand_spread,
        expand_shadow,
        shrink_weight,
        shrink_drift,
        shrink_spread,
        shrink_shadow,
        vector_weight,
        vector_drift,
        vector_spread,
        vector_shadow,
    )


def solution(mesh):
    placed = (
        P("dp", "blk", None),
        P("dp", "blk", None),
        P("dp", "blk"),
        P(),
        P(),
        P("dp", None),
        P("dp", None),
        P("dp", None),
        P(),
        P("dp", None),
        P("dp", None),
        P("dp", None),
        P(),
        P("dp", None),
        P("dp", None),
        P("dp", None),
        P(),
        P("dp", None),
        P("dp", None),
        P("dp", None),
        P(),
        P(None, "dp"),
        P(None, "dp"),
        P(None, "dp"),
    )
    return jax.shard_map(
        per_device,
        mesh=mesh,
        in_specs=placed,
        out_specs=(
            P("dp", "blk", None),
            P("dp", "blk", None),
            P(),
            P(),
            P("dp", None),
            P("dp", None),
            P("dp", None),
            P("dp", None),
            P("dp", None),
            P("dp", None),
            P("dp", None),
            P("dp", None),
            P("dp", None),
            P("dp", None),
            P("dp", None),
            P("dp", None),
            P("dp", None),
            P("dp", None),
            P("dp", None),
            P("dp", None),
            P(None, "dp"),
            P(None, "dp"),
            P(None, "dp"),
            P(None, "dp"),
        ),
        check_vma=False,
    )
```

profile of v0, /device:TPU:0, one launch (start us, length us, event | category | flops | bytes accessed | tf_op | source)
XLA Modules:
  0.0 713.9 jit_solution(8610555048467626515)
XLA Ops:
  9.8 42.1 %all-reduce.1 = (f32[768]{0:T(1024)S(1)}, f32[768]{0:T(1024)S(1)}) all-reduce(f32[768]{0:T(1024)S(1)} %reduce_sum.218, f32[768]{0:T(1024)S(1)} %fusion.28), channel_id=1, replica_groups=mesh['dp'=8,'blk'=4] {'dp','blk'}, use_global_device_ids=true, to_apply=%region_1.0 | all-reduce | flops 1536 | bytes 12288 | tf_op jit(solution)/shard_map/psum | solution.py:96
  57.2 2.3 fusion.77
  65.2 2.4 fusion.25
  69.5 2.1 pad_maximum_fusion.1
  74.9 20.8 %all_gather.3 = s32[1,1024]{1,0:T(1,128)S(1)} all-gather(s32[1,256]{1,0:T(1,128)S(1)} %copy-done.94), channel_id=1, replica_groups=mesh['dp'=8,'blk'=4] {'blk'}, dimensions={1}, use_global_device_ids=true | all-gather | bytes 5120 | tf_op jit(solution)/shard_map/all_gather | solution.py:111
  97.2 3.4 select_reduce_fusion.7
  104.4 3.0 collective-permute-done.1
  111.0 10.4 %collective-permute-done.2 = bf16[1,256,12,64]{1,3,2,0:T(8,128)(2,1)S(1)} collective-permute-done((bf16[1,256,12,64]{1,3,2,0:T(8,128)(2,1)}, bf16[1,256,12,64]{1,3,2,0:T(8,128)(2,1)S(1)}, u32[]{:S(2)}, u32[]{:S(2)}) %collective-permute-start.2) | collective-permute-done | bytes 393248 | tf_op jit(solution)/shard_map/ppermute | solution.py:25
  126.0 7.9 %collective-permute-done.4 = bf16[2,1,256,12,64]{2,4,3,1,0:T(8,128)(2,1)S(1)} collective-permute-done((bf16[2,1,256,12,64]{2,4,3,1,0:T(8,128)(2,1)}, bf16[2,1,256,12,64]{2,4,3,1,0:T(8,128)(2,1)S(1)}, u32[]{:S(2)}, u32[]{:S(2)}) %collective-permute-start.4) | collective-permute-done | bytes 786464 | tf_op jit(solution)/shard_map/ppermute | solution.py:25
  137.2 14.0 %collective-permute-done.5 = bf16[2,1,256,12,64]{2,4,3,1,0:T(8,128)(2,1)S(1)} collective-permute-done((bf16[2,1,256,12,64]{2,4,3,1,0:T(8,128)(2,1)S(1)}, bf16[2,1,256,12,64]{2,4,3,1,0:T(8,128)(2,1)S(1)}, u32[]{:S(2)}, u32[]{:S(2)}) %collective-permute-start.5) | collective-permute-done | bytes 786464 | tf_op jit(solution)/shard_map/ppermute | solution.py:25
  156.2 9.5 %multiply_convert_fusion = (bf16[256,3072]{1,0:T(8,128)(2,1)}, f32[256,3072]{1,0:T(8,128)S(1)}, f32[256,3072]{1,0:T(8,128)S(1)}) fusion(f32[3072]{0:T(1024)S(1)} %copy-done.89, bf16[768,3072]{1,0:T(8,128)(2,1)S(1)} %bitcast.276, f32[256,768]{1,0:T(8,128)S(1)} %get-tuple-element.110, f32[768]{0:T(1024)S(1)} %copy-done.75, f32[768]{0:T(1024)S(1)} %copy-done.69, ...), kind=kOutput, calls=%fused_computation.9 | convolution fusion | flops 1260847104 | bytes 13389824 | tf_op jit(solution)/shard_map/dot_general | solution.py:153
  165.8 2.8 convert_reduce_fusion
  168.5 2.2 multiply_reduce_fusion
  176.7 2.7 fusion.18
  188.4 2.1 select_convert_fusion.2
  194.2 11.6 %collective-permute-done.6 = bf16[2,1,256,12,64]{2,4,3,1,0:T(8,128)(2,1)S(1)} collective-permute-done((bf16[2,1,256,12,64]{2,4,3,1,0:T(8,128)(2,1)S(1)}, bf16[2,1,256,12,64]{2,4,3,1,0:T(8,128)(2,1)S(1)}, u32[]{:S(2)}, u32[]{:S(2)}) %collective-permute-start.6) | collective-permute-done | bytes 786464 | tf_op jit(solution)/shard_map/ppermute | solution.py:25
  208.5 15.0 %collective-permute-done.7 = bf16[2,1,256,12,64]{2,4,3,1,0:T(8,128)(2,1)S(1)} collective-permute-done((bf16[2,1,256,12,64]{2,4,3,1,0:T(8,128)(2,1)S(1)}, bf16[2,1,256,12,64]{2,4,3,1,0:T(8,128)(2,1)S(1)}, u32[]{:S(2)}, u32[]{:S(2)}) %collective-permute-start.7) | collective-permute-done | bytes 786464 | tf_op jit(solution)/shard_map/ppermute | solution.py:25
  224.5 5.1 fusion.38
  229.6 11.4 %collective-permute-done.8 = bf16[2,1,256,12,64]{2,4,3,1,0:T(8,128)(2,1)S(1)} collective-permute-done((bf16[2,1,256,12,64]{2,4,3,1,0:T(8,128)(2,1)S(1)}, bf16[2,1,256,12,64]{2,4,3,1,0:T(8,128)(2,1)S(1)}, u32[]{:S(2)}, u32[]{:S(2)}) %collective-permute-start.8) | collective-permute-done | bytes 786464 | tf_op jit(solution)/shard_map/ppermute | solution.py:25
  242.7 5.2 fusion.79
  247.9 7.3 %collective-permute-done.9 = bf16[2,1,256,12,64]{2,4,3,1,0:T(8,128)(2,1)S(1)} collective-permute-done((bf16[2,1,256,12,64]{2,4,3,1,0:T(8,128)(2,1)S(1)}, bf16[2,1,256,12,64]{2,4,3,1,0:T(8,128)(2,1)S(1)}, u32[]{:S(2)}, u32[]{:S(2)}) %collective-permute-start.9) | collective-permute-done | bytes 786464 | tf_op jit(solution)/shard_map/ppermute | solution.py:25
  257.2 4.2 fusion.36
  268.6 5.3 fusion.19
  276.1 2.9 fusion.82
  282.7 2.8 concatenate.16
  285.5 40.2 %all-reduce = (f32[768]{0:T(1024)S(1)}, f32[768]{0:T(1024)S(1)}, f32[12,768]{1,0:T(8,128)}) all-reduce(f32[768]{0:T(1024)} %get-tuple-element.32, f32[768]{0:T(1024)} %get-tuple-element.31, f32[12,768]{1,0:T(8,128)} %concatenate.16), channel_id=1, replica_groups=mesh['dp'=8,'blk'=4] {'dp','blk'}, use_global_device_ids=true, to_apply=%region_23.24 | all-reduce | flops 10752 | bytes 86016 | tf_op jit(solution)/shard_map/psum | solution.py:213
  327.8 2.4 fusion.31
  330.3 362.6 %all-reduce.5.cloned.1.call-done = (f32[768,2304]{1,0:T(8,128)}, f32[768,768]{1,0:T(8,128)}, f32[768,3072]{1,0:T(8,128)}, f32[3072,768]{1,0:T(8,128)}) async-done(((f32[768,2304]{1,0:T(8,128)}, f32[768,768]{1,0:T(8,128)}, f32[768,3072]{1,0:T(8,128)}, f32[3072,768]{1,0:T(8,128)}), (f32[768,2304]{1,0:T(8,128)}, f32[768,768]{1,0:T(8,128)}, f32[768,3072]{1,0:T(8,128)}, ...) | async-done | bytes 28311568 | tf_op jit(solution)/shard_map/psum | solution.py:229
  692.9 4.1 fusion.92
  697.0 2.0 fusion.90
  699.1 4.0 fusion.88
  703.1 3.8 fusion.86
  (292 shorter events, 80.1 us)
Async XLA Ops:
  7.2 50.0 %copy-start = (bf16[768,2304]{1,0:T(8,128)(2,1)S(1)}, bf16[768,2304]{1,0:T(8,128)(2,1)}, u32[]{:S(2)}) copy-start(bf16[768,2304]{1,0:T(8,128)(2,1)} %param.28) | copy-start | bytes 10616836
  7.2 685.6 %all-reduce.5.cloned.1.call-start = ((), (), s32[]{:S(2)}) async-start(), calls=%async_computation | async-start | bytes 56623104 | tf_op jit(solution)/shard_map/psum | solution.py:229
  61.8 13.1 %copy-start.94 = (s32[1,256]{1,0:T(1,128)S(1)}, s32[1,256]{1,0:T(1,128)}, u32[]{:S(2)}) copy-start(s32[1,256]{1,0:T(1,128)} %param.26) | copy-start | bytes 3076
  63.7 32.9 %collective-permute-start = (bf16[1,256,12,64]{1,3,2,0:T(8,128)(2,1)}, bf16[1,256,12,64]{1,3,2,0:T(8,128)(2,1)}, u32[]{:S(2)}, u32[]{:S(2)}) collective-permute-start(bf16[1,256,12,64]{1,3,2,0:T(8,128)(2,1)} %bitcast.255), channel_id=1, source_target_pairs={{3,0},{0,1},{1,2},{2,3},{7,4},{4,5},{5,6},{6,7},{11,8},{8,9},{9,10... | collective-permute-start | bytes 1179656 | tf_op jit(solution)/shard_map/ppermute | solution.py:25
  71.6 35.8 %collective-permute-start.3 = (bf16[2,1,256,12,64]{2,4,3,1,0:T(8,128)(2,1)}, bf16[2,1,256,12,64]{2,4,3,1,0:T(8,128)(2,1)}, u32[]{:S(2)}, u32[]{:S(2)}) collective-permute-start(bf16[2,1,256,12,64]{2,4,3,1,0:T(8,128)(2,1)} %pad_maximum_fusion.1), channel_id=1, source_target_pairs={{3,0},{0,1},{1,2},{2,3},{7,4},{4,5},{5,6},{6,7},{11,8},{8,9},{9,10... | collective-permute-start | bytes 2359304 | tf_op jit(solution)/shard_map/ppermute | solution.py:25
  74.9 25.7 %copy-start.77 = (bf16[12,768]{1,0:T(8,128)(2,1)S(1)}, bf16[12,768]{1,0:T(8,128)(2,1)}, u32[]{:S(2)}) copy-start(bf16[12,768]{1,0:T(8,128)(2,1)} %param.44) | copy-start | bytes 55300
  96.6 10.8 %collective-permute-start.1 = (bf16[1,256,12,64]{1,3,2,0:T(8,128)(2,1)}, bf16[1,256,12,64]{1,3,2,0:T(8,128)(2,1)}, u32[]{:S(2)}, u32[]{:S(2)}) collective-permute-start(bf16[1,256,12,64]{1,3,2,0:T(8,128)(2,1)} %collective-permute-done), channel_id=1, source_target_pairs={{3,0},{0,1},{1,2},{2,3},{7,4},{4,5},{5,6},{6,7},{11,8},{8,9},{9,10... | collective-permute-start | bytes 1179656 | tf_op jit(solution)/shard_map/ppermute | solution.py:25
  100.6 21.5 %copy-start.71 = (f32[12,256]{1,0:T(8,128)}, f32[12,256]{1,0:T(8,128)S(1)}, u32[]{:S(2)}) copy-start(f32[12,256]{1,0:T(8,128)S(1)} %get-tuple-element.105) | copy-start | bytes 36868
  104.3 17.1 %copy-start.37 = (pred[256,256]{0,1:T(8,128)(4,1)S(1)}, pred[256,256]{0,1:T(8,128)(4,1)}, u32[]{:S(2)}) copy-start(pred[256,256]{0,1:T(8,128)(4,1)} %get-tuple-element.98) | copy-start | bytes 196612
  107.4 14.1 %collective-permute-start.2 = (bf16[1,256,12,64]{1,3,2,0:T(8,128)(2,1)}, bf16[1,256,12,64]{1,3,2,0:T(8,128)(2,1)S(1)}, u32[]{:S(2)}, u32[]{:S(2)}) collective-permute-start(bf16[1,256,12,64]{1,3,2,0:T(8,128)(2,1)} %collective-permute-done.1), channel_id=1, source_target_pairs={{3,0},{0,1},{1,2},{2,3},{7,4},{4,5},{5,6},{6,7},{11,8},{8,9},{9,10... | collective-permute-start | bytes 1179656 | tf_op jit(solution)/shard_map/ppermute | solution.py:25
  107.4 26.6 %collective-permute-start.4 = (bf16[2,1,256,12,64]{2,4,3,1,0:T(8,128)(2,1)}, bf16[2,1,256,12,64]{2,4,3,1,0:T(8,128)(2,1)S(1)}, u32[]{:S(2)}, u32[]{:S(2)}) collective-permute-start(bf16[2,1,256,12,64]{2,4,3,1,0:T(8,128)(2,1)} %collective-permute-done.3), channel_id=1, source_target_pairs={{3,0},{0,1},{1,2},{2,3},{7,4},{4,5},{5,6},{6,7},{11,8},{8,9},{9,10... | collective-permute-start | bytes 2359304 | tf_op jit(solution)/shard_map/ppermute | solution.py:25
  109.0 25.1 %copy-start.8 = (f32[12,256,256]{1,2,0:T(8,128)}, f32[12,256,256]{1,2,0:T(8,128)S(1)}, u32[]{:S(2)}) copy-start(f32[12,256,256]{1,2,0:T(8,128)S(1)} %fusion.50) | copy-start | bytes 9437188
  134.0 17.2 %collective-permute-start.5 = (bf16[2,1,256,12,64]{2,4,3,1,0:T(8,128)(2,1)S(1)}, bf16[2,1,256,12,64]{2,4,3,1,0:T(8,128)(2,1)S(1)}, u32[]{:S(2)}, u32[]{:S(2)}) collective-permute-start(bf16[2,1,256,12,64]{2,4,3,1,0:T(8,128)(2,1)S(1)} %collective-permute-done.4), channel_id=1, source_target_pairs={{3,0},{0,1},{1,2},{2,3},{7,4},{4,5},{5,6},{6,7},{11,8},{8,9},{9,10... | collective-permute-start | bytes 2359304 | tf_op jit(solution)/shard_map/ppermute | solution.py:25
  136.5 14.7 %copy-start.10 = (f32[12,256,256]{1,2,0:T(8,128)}, f32[12,256,256]{1,2,0:T(8,128)S(1)}, u32[]{:S(2)}) copy-start(f32[12,256,256]{1,2,0:T(8,128)S(1)} %fusion.51) | copy-start | bytes 9437188
  136.5 19.2 %slice-start = ((s8[4718592]{0:T(1024)(128)(4,1)}), s8[524288]{0:T(1024)(128)(4,1)S(1)}, s32[]{:S(2)}) async-start(s8[4718592]{0:T(1024)(128)(4,1)} %bitcast.275), calls=%async_computation.1 | async-start | bytes 1048576
  155.4 15.3 %copy-start.15 = (f32[256,768]{1,0:T(8,128)}, f32[256,768]{1,0:T(8,128)S(1)}, u32[]{:S(2)}) copy-start(f32[256,768]{1,0:T(8,128)S(1)} %get-tuple-element.110) | copy-start | bytes 2359300
  155.4 15.3 %copy-start.83 = (f32[256]{0:T(256)}, f32[256]{0:T(256)S(1)}, u32[]{:S(2)}) copy-start(f32[256]{0:T(256)S(1)} %broadcast_multiply_fusion.2) | copy-start | bytes 3076
  155.7 15.1 %copy-start.87 = (f32[256]{0:T(256)}, f32[256]{0:T(256)S(1)}, u32[]{:S(2)}) copy-start(f32[256]{0:T(256)S(1)} %fusion.65) | copy-start | bytes 3076
  187.9 17.9 %collective-permute-start.6 = (bf16[2,1,256,12,64]{2,4,3,1,0:T(8,128)(2,1)S(1)}, bf16[2,1,256,12,64]{2,4,3,1,0:T(8,128)(2,1)S(1)}, u32[]{:S(2)}, u32[]{:S(2)}) collective-permute-start(bf16[2,1,256,12,64]{2,4,3,1,0:T(8,128)(2,1)S(1)} %pad_maximum_fusion.2), channel_id=1, source_target_pairs={{3,0},{0,1},{1,2},{2,3},{7,4},{4,5},{5,6},{6,7},{11,8},{8,9},{9,10... | collective-permute-start | bytes 2359304 | tf_op jit(solution)/shard_map/ppermute | solution.py:25
  206.0 17.4 %collective-permute-start.7 = (bf16[2,1,256,12,64]{2,4,3,1,0:T(8,128)(2,1)S(1)}, bf16[2,1,256,12,64]{2,4,3,1,0:T(8,128)(2,1)S(1)}, u32[]{:S(2)}, u32[]{:S(2)}) collective-permute-start(bf16[2,1,256,12,64]{2,4,3,1,0:T(8,128)(2,1)S(1)} %fusion.10), channel_id=1, source_target_pairs={{3,0},{0,1},{1,2},{2,3},{7,4},{4,5},{5,6},{6,7},{11,8},{8,9},{9,10... | collective-permute-start | bytes 2359304 | tf_op jit(solution)/shard_map/ppermute | solution.py:25
  208.5 15.9 %copy-start.22 = (bf16[1,256,768]{2,1,0:T(8,128)(2,1)S(1)}, bf16[1,256,768]{2,1,0:T(8,128)(2,1)}, u32[]{:S(2)}) copy-start(bf16[1,256,768]{2,1,0:T(8,128)(2,1)} %param.25) | copy-start | bytes 1179652
  208.5 15.9 %copy-start.30 = (bf16[256,3072]{1,0:T(8,128)(2,1)S(1)}, bf16[256,3072]{1,0:T(8,128)(2,1)}, u32[]{:S(2)}) copy-start(bf16[256,3072]{1,0:T(8,128)(2,1)} %get-tuple-element.75) | copy-start | bytes 4718596
  223.7 17.3 %collective-permute-start.8 = (bf16[2,1,256,12,64]{2,4,3,1,0:T(8,128)(2,1)S(1)}, bf16[2,1,256,12,64]{2,4,3,1,0:T(8,128)(2,1)S(1)}, u32[]{:S(2)}, u32[]{:S(2)}) collective-permute-start(bf16[2,1,256,12,64]{2,4,3,1,0:T(8,128)(2,1)S(1)} %fusion.11), channel_id=1, source_target_pairs={{3,0},{0,1},{1,2},{2,3},{7,4},{4,5},{5,6},{6,7},{11,8},{8,9},{9,10... | collective-permute-start | bytes 2359304 | tf_op jit(solution)/shard_map/ppermute | solution.py:25
  241.3 14.0 %collective-permute-start.9 = (bf16[2,1,256,12,64]{2,4,3,1,0:T(8,128)(2,1)S(1)}, bf16[2,1,256,12,64]{2,4,3,1,0:T(8,128)(2,1)S(1)}, u32[]{:S(2)}, u32[]{:S(2)}) collective-permute-start(bf16[2,1,256,12,64]{2,4,3,1,0:T(8,128)(2,1)S(1)} %fusion.12), channel_id=1, source_target_pairs={{3,0},{0,1},{1,2},{2,3},{7,4},{4,5},{5,6},{6,7},{11,8},{8,9},{9,10... | collective-permute-start | bytes 2359304 | tf_op jit(solution)/shard_map/ppermute | solution.py:25
  242.6 13.6 %copy-start.47 = (bf16[12,64,256]{2,1,0:T(8,128)(2,1)}, bf16[12,64,256]{2,1,0:T(8,128)(2,1)S(1)}, u32[]{:S(2)}) copy-start(bf16[12,64,256]{2,1,0:T(8,128)(2,1)S(1)} %get-tuple-element.115) | copy-start | bytes 1179652
  242.7 14.5 %copy-start.2 = (f32[1,256,768]{2,1,0:T(8,128)S(1)}, f32[1,256,768]{2,1,0:T(8,128)}, u32[]{:S(2)}) copy-start(f32[1,256,768]{2,1,0:T(8,128)} %param.24) | copy-start | bytes 2359300
  242.7 14.5 %copy-start.60 = (f32[768]{0:T(1024)S(1)}, f32[768]{0:T(1024)}, u32[]{:S(2)}) copy-start(f32[768]{0:T(1024)} %copy-done.58) | copy-start | bytes 9220
  242.7 14.5 %copy-start.63 = (f32[768]{0:T(1024)S(1)}, f32[768]{0:T(1024)}, u32[]{:S(2)}) copy-start(f32[768]{0:T(1024)} %copy-done.61) | copy-start | bytes 9220
  242.7 14.4 %copy-start.68 = (f32[768]{0:T(1024)S(1)}, f32[768]{0:T(1024)}, u32[]{:S(2)}) copy-start(f32[768]{0:T(1024)} %copy-done.67) | copy-start | bytes 9220
  242.7 14.4 %copy-start.74 = (f32[768]{0:T(1024)S(1)}, f32[768]{0:T(1024)}, u32[]{:S(2)}) copy-start(f32[768]{0:T(1024)} %copy-done.73) | copy-start | bytes 9220
  242.7 14.4 %copy-start.79 = (f32[256]{0:T(256)S(1)}, f32[256]{0:T(256)}, u32[]{:S(2)}) copy-start(f32[256]{0:T(256)} %copy-done.78) | copy-start | bytes 3076
  242.7 14.4 %copy-start.81 = (f32[256]{0:T(256)S(1)}, f32[256]{0:T(256)}, u32[]{:S(2)}) copy-start(f32[256]{0:T(256)} %copy-done.80) | copy-start | bytes 3076
  (78 other events, 326.0 us)
Sparse Core Ops, SparseCore 0:
  261.6 431.2 all-reduce.4
where the time goes:
time: 723 us; the launch traced here: 714 us
  waiting for transfers between devices  443 us (61%)
  blocking collectives  103 us (14%)
  matrix products  74.2 us (10%)
  other arithmetic  39.8 us (6%)
  local copies, waits for them, and re-layouts  32.8 us (5%)
  between operations  16.1 us (2%)
    psum x1, waiting for transfers between devices, per_device(): lax.psum((gradients[0], gradients[1], gradients[2], gradients[3], gradien...  363 us
    ppermute x10, waiting for transfers between devices, shifted(): return lax.ppermute(block, axis, route)  80.6 us
    psum x1, blocking collectives, per_device(): lax.psum((jnp.sum(flat_raw, axis=0), jnp.sum(flat_raw * flat_raw, axis=0)...  42.1 us
    psum x1, blocking collectives, per_device(): lax.psum((jnp.sum(grad_normed, axis=0), jnp.sum(grad_normed * centred, ax...  40.2 us
    all_gather x1, blocking collectives, per_device(): all_ids = lax.all_gather(segment_ids, 'blk', axis=1, tiled=True)  20.8 us
    dot_general x4, matrix products, outer_rows(): lax.dot_general(left, right, (((0,), (0,)), ((), ())), preferred_element_...  16.5 us
    convert_element_type x5, other arithmetic, adam_rule(): return (weight_new, moment_new, square_new, weight_new.astype(jnp.bfloat16))  15.4 us
  transfers between devices with their start and end apart: 11, of which 9 were waited for; matrix products, arithmetic and copies ran while one was open for 10% of the time, Pallas kernels for 0%

commit v1 on v0

v1 whole, which is shorter than its diff:
```python
import functools

import jax
import jax.numpy as jnp
from jax import lax
from jax.experimental import pallas as pl
from jax.experimental.pallas import tpu as pltpu
from jax.sharding import PartitionSpec as P

HEADS = 12
HEAD_WIDTH = 64
GROUP = 4

ln_epsilon = 1e-05
stat_epsilon = 1e-06
beta_one = 0.5
beta_two = 0.6
rate_matrix = 0.04
rate_vector = 0.8
warmup_length = 20.0
decay_matrix = 0.05
adam_epsilon = 1e-08
score_scale = 0.125
masked_score = -1e30

f32 = jnp.float32
bf16 = jnp.bfloat16


def nn(a, b):
    return lax.dot_general(a, b, (((1,), (0,)), ((), ())), preferred_element_type=f32)


def nt(a, b):
    return lax.dot_general(a, b, (((1,), (1,)), ((), ())), preferred_element_type=f32)


def tn(a, b):
    return lax.dot_general(a, b, (((0,), (0,)), ((), ())), preferred_element_type=f32)


def flipped(block, axis, bit):
    size = lax.axis_size(axis)
    return lax.ppermute(block, axis, [(i, i ^ bit) for i in range(size)])


def moved(block, axis, distance):
    size = lax.axis_size(axis)
    route = [(i, i + distance) for i in range(size) if 0 <= i + distance < size]
    return lax.ppermute(block, axis, route)


def bits_of(axis):
    size = lax.axis_size(axis)
    return [1 << i for i in range(size.bit_length() - 1)]


def everywhere_sum(block):
    for axis in ("dp", "blk"):
        for bit in bits_of(axis):
            block = block + flipped(block, axis, bit)
    return block


def halves(block, axis, way, position):
    own = (lax.axis_index(axis) // way) % 2
    keep = lax.dynamic_index_in_dim(block, own, position, keepdims=False)
    send = lax.dynamic_index_in_dim(block, 1 - own, position, keepdims=False)
    return keep, send


def owned_sum(gradient, order):
    dp_bits = bits_of("dp")
    count = len(dp_bits)
    rows, columns = gradient.shape
    owners = lax.axis_size("dp")
    block = gradient.reshape((2,) * count + (rows // owners, columns))
    left = list(reversed(dp_bits))
    for bit in order:
        where = left.index(bit)
        keep, send = halves(block, "dp", bit, where)
        block = (keep.astype(f32) + flipped(send, "dp", bit).astype(f32)).astype(bf16)
        left.pop(where)
    share = block
    blk_bits = bits_of("blk")
    trail = []
    for bit in blk_bits[:-1]:
        keep, send = halves(share.reshape(2, share.shape[0] // 2, columns), "blk", bit, 0)
        share = (keep.astype(f32) + flipped(send, "blk", bit).astype(f32)).astype(bf16)
        trail.append(bit)
    if blk_bits:
        share = (share.astype(f32) + flipped(share, "blk", blk_bits[-1]).astype(f32)).astype(bf16)
    for bit in reversed(trail):
        other = flipped(share, "blk", bit)
        own = (lax.axis_index("blk") // bit) % 2
        share = jnp.where(
            own == 0, jnp.concatenate([share, other], 0), jnp.concatenate([other, share], 0)
        )
    return share


def lane_half(rows, which):
    lanes = lax.broadcasted_iota(jnp.int32, (rows, 128), 1)
    return (lanes >= 64) if which else (lanes < 64)


def attend_kernel(bounds, q_ref, k_ref, v_ref, qid_ref, kid_ref, o_ref, lse_ref, acc, top, total):
    width = q_ref.shape[0]
    top[...] = jnp.full_like(top, masked_score)
    total[...] = jnp.zeros_like(total)
    acc[...] = jnp.zeros_like(acc)
    own = qid_ref[...]
    masked_q = []
    for h in range(GROUP):
        pair = q_ref[:, 128 * (h // 2) : 128 * (h // 2) + 128]
        masked_q.append(jnp.where(lane_half(width, h % 2), pair, jnp.zeros_like(pair)))

    def step(s, carry):
        keys = k_ref[s]
        values_t = v_ref[s].T
        allowed = kid_ref[s] == own
        for h in range(GROUP):
            lanes = slice(128 * (h // 2), 128 * (h // 2) + 128)
            score = jnp.where(allowed, nt(keys[:, lanes], masked_q[h]), masked_score)
            old = top[h : h + 1, :]
            new = jnp.maximum(old, jnp.max(score, axis=0, keepdims=True))
            fade = jnp.exp(old - new)
            weight = jnp.exp(score - new)
            total[h : h + 1, :] = total[h : h + 1, :] * fade + jnp.sum(
                weight, axis=0, keepdims=True
            )
            top[h : h + 1, :] = new
            rows = slice(64 * h, 64 * h + 64)
            acc[rows, :] = acc[rows, :] * fade + nn(values_t[rows, :], weight.astype(bf16))
        return carry

    lax.fori_loop(bounds[0], bounds[1], step, 0)
    for h in range(GROUP):
        rows = slice(64 * h, 64 * h + 64)
        acc[rows, :] = acc[rows, :] / total[h : h + 1, :]
    o_ref[...] = acc[...].T
    lse_ref[0] = top[0:GROUP, :] + jnp.log(total[0:GROUP, :])


def attend(bounds, queries, pairs, own_ids, slot_ids):
    slots, width, _ = pairs.shape
    features = queries.shape[1]
    lanes = GROUP * HEAD_WIDTH
    steps = features // lanes
    return pl.pallas_call(
        attend_kernel,
        grid_spec=pltpu.PrefetchScalarGridSpec(
            num_scalar_prefetch=1,
            grid=(steps,),
            in_specs=[
                pl.BlockSpec((width, lanes), lambda i, b: (0, i)),
                pl.BlockSpec((slots, width, lanes), lambda i, b: (0, 0, i)),
                pl.BlockSpec((slots, width, lanes), lambda i, b: (0, 0, i + steps)),
                pl.BlockSpec((1, width), lambda i, b: (0, 0)),
                pl.BlockSpec((slots, width, 1), lambda i, b: (0, 0, 0)),
            ],
            out_specs=[
                pl.BlockSpec((width, lanes), lambda i, b: (0, i)),
                pl.BlockSpec((1, GROUP, width), lambda i, b: (i, 0, 0)),
            ],
            scratch_shapes=[
                pltpu.VMEM((lanes, width), f32),
                pltpu.VMEM((8, width), f32),
                pltpu.VMEM((8, width), f32),
            ],
        ),
        out_shape=[
            jax.ShapeDtypeStruct((width, features), f32),
            jax.ShapeDtypeStruct((steps, GROUP, width), f32),
        ],
        name="attend",
    )(bounds, queries, pairs, pairs, own_ids, slot_ids)


def attend_back_kernel(
    bounds, q_ref, k_ref, v_ref, o_ref, g_ref, lse_ref, qid_ref, kid_ref, dq_ref, dk_ref, dv_ref, acc
):
    width = q_ref.shape[0]
    slots = k_ref.shape[0]
    acc[...] = jnp.zeros_like(acc)
    own = qid_ref[...]
    product = (g_ref[...].astype(f32) * o_ref[...]).T
    masked_q, masked_g, deltas, lses = [], [], [], []
    for h in range(GROUP):
        lanes = slice(128 * (h // 2), 128 * (h // 2) + 128)
        half = lane_half(width, h % 2)
        pair = q_ref[:, lanes]
        masked_q.append(jnp.where(half, pair, jnp.zeros_like(pair)))
        pair = g_ref[:, lanes]
        masked_g.append(jnp.where(half, pair, jnp.zeros_like(pair)))
        deltas.append(jnp.sum(product[64 * h : 64 * h + 64, :], axis=0, keepdims=True))
        lses.append(lse_ref[0, h : h + 1, :])

    def blank(s, carry):
        dk_ref[s] = jnp.zeros(dk_ref.shape[1:], dk_ref.dtype)
        dv_ref[s] = jnp.zeros(dv_ref.shape[1:], dv_ref.dtype)
        return carry

    lax.fori_loop(0, bounds[0], blank, 0)
    lax.fori_loop(bounds[1], slots, blank, 0)

    def step(s, carry):
        keys = k_ref[s]
        values = v_ref[s]
        keys_t = keys.T
        allowed = kid_ref[s] == own
        for j in range(GROUP // 2):
            lanes = slice(128 * j, 128 * j + 128)
            key_part, value_part = None, None
            for h in (2 * j, 2 * j + 1):
                score = jnp.where(allowed, nt(keys[:, lanes], masked_q[h]), masked_score)
                prob = jnp.exp(score - lses[h])
                grad = (prob * (nt(values[:, lanes], masked_g[h]) - deltas[h])).astype(bf16)
                rows = slice(64 * h, 64 * h + 64)
                acc[rows, :] += nn(keys_t[rows, :], grad)
                k_now = nn(grad, masked_q[h])
                v_now = nn(prob.astype(bf16), masked_g[h])
                key_part = k_now if key_part is None else key_part + k_now
                value_part = v_now if value_part is None else value_part + v_now
            dk_ref[s, :, lanes] = key_part.astype(bf16)
            dv_ref[s, :, lanes] = value_part.astype(bf16)
        return carry

    lax.fori_loop(bounds[0], bounds[1], step, 0)
    dq_ref[...] = (acc[...].T.astype(bf16).astype(f32) * score_scale).astype(bf16)


def attend_back(bounds, queries, pairs, outputs, grads, lse, own_ids, slot_ids):
    slots, width, _ = pairs.shape
    features = queries.shape[1]
    lanes = GROUP * HEAD_WIDTH
    steps = features // lanes
    flat = pl.BlockSpec((width, lanes), lambda i, b: (0, i))
    return pl.pallas_call(
        attend_back_kernel,
        grid_spec=pltpu.PrefetchScalarGridSpec(
            num_scalar_prefetch=1,
            grid=(steps,),
            in_specs=[
                flat,
                pl.BlockSpec((slots, width, lanes), lambda i, b: (0, 0, i)),
                pl.BlockSpec((slots, width, lanes), lambda i, b: (0, 0, i + steps)),
                flat,
                flat,
                pl.BlockSpec((1, GROUP, width), lambda i, b: (i, 0, 0)),
                pl.BlockSpec((1, width), lambda i, b: (0, 0)),
                pl.BlockSpec((slots, width, 1), lambda i, b: (0, 0, 0)),
            ],
            out_specs=[
                flat,
                pl.BlockSpec((slots, width, lanes), lambda i, b: (0, 0, i)),
                pl.BlockSpec((slots, width, lanes), lambda i, b: (0, 0, i)),
            ],
            scratch_shapes=[pltpu.VMEM((lanes, width), f32)],
        ),
        out_shape=[
            jax.ShapeDtypeStruct((width, features), bf16),
            jax.ShapeDtypeStruct((slots, width, features), bf16),
            jax.ShapeDtypeStruct((slots, width, features), bf16),
        ],
        name="attend_back",
    )(bounds, queries, pairs, pairs, outputs, grads, lse, own_ids, slot_ids)


def norm_parts(inputs):
    centred = inputs - jnp.mean(inputs, axis=-1, keepdims=True)
    scale = lax.rsqrt(jnp.mean(centred * centred, axis=-1, keepdims=True) + ln_epsilon)
    return centred * scale, scale


def norm_back(grad, unit, scale, gain):
    inner = grad * gain
    return scale * (
        inner
        - jnp.mean(inner, axis=-1, keepdims=True)
        - unit * jnp.mean(inner * unit, axis=-1, keepdims=True)
    )


def adam_rule(master, moment, square, gradient, step_value, step_rate, weight_decay):
    moment_new = beta_one * moment + (1.0 - beta_one) * gradient
    square_new = beta_two * square + (1.0 - beta_two) * gradient * gradient
    fix_first = 1.0 - jnp.power(beta_one, step_value)
    fix_second = 1.0 - jnp.power(beta_two, step_value)
    planned = step_rate * jnp.minimum(1.0, step_value / warmup_length)
    direction = moment_new / fix_first / (jnp.sqrt(square_new / fix_second) + adam_epsilon)
    weight_new = master - planned * (direction + weight_decay * master)
    return (weight_new, moment_new, square_new, weight_new.astype(bf16))


def per_device(
    raw_input,
    cotangent,
    segment_ids,
    step_count,
    inlet_copy,
    inlet_master,
    inlet_moment,
    inlet_square,
    outlet_copy,
    outlet_master,
    outlet_moment,
    outlet_square,
    expand_copy,
    expand_master,
    expand_moment,
    expand_square,
    shrink_copy,
    shrink_master,
    shrink_moment,
    shrink_square,
    vector_copy,
    vector_master,
    vector_moment,
    vector_square,
):
    sequences, block_length, features = raw_input.shape
    assert sequences == 1
    group_size = lax.axis_size("blk")
    group_index = lax.axis_index("blk")
    owners = lax.axis_size("dp")
    total_tokens = owners * group_size * block_length
    reach = group_size // 2
    slots = 2 * reach + 1
    vectors = vector_copy.astype(f32)
    raw = raw_input.reshape(block_length, features)
    grad_down = cotangent.reshape(block_length, features)

    own_ids = segment_ids.astype(jnp.int32)
    slot_ids = [None] * slots
    slot_ids[reach] = own_ids
    ahead, behind = own_ids + 1, own_ids + 1
    for d in range(1, reach + 1):
        ahead, behind = moved(ahead, "blk", 1), moved(behind, "blk", -1)
        slot_ids[reach - d], slot_ids[reach + d] = ahead - 1, behind - 1
    slot_ids = jnp.concatenate(slot_ids, axis=0)
    active = (slot_ids[:, -1] >= own_ids[0, 0]) & (slot_ids[:, 0] <= own_ids[0, -1])
    places = jnp.arange(slots, dtype=jnp.int32)
    bounds = jnp.stack(
        [
            jnp.min(jnp.where(active, places, slots)),
            jnp.max(jnp.where(active, places + 1, 0)),
        ]
    ).astype(jnp.int32)
    slot_columns = slot_ids[:, :, None]

    band_totals = everywhere_sum(jnp.stack([jnp.sum(raw, axis=0), jnp.sum(raw * raw, axis=0)]))
    band_mean = band_totals[0] / total_tokens
    band_variance = band_totals[1] / total_tokens - band_mean * band_mean
    inverse_std = lax.rsqrt(band_variance + stat_epsilon)
    normed = (raw - band_mean) * inverse_std
    unit_one, scale_one = norm_parts(normed)
    first_in = (unit_one * vectors[0] + vectors[1]).astype(bf16)

    blocks = [None] * slots
    blocks[reach] = first_in
    ahead, behind = first_in, first_in
    for d in range(1, reach + 1):
        ahead, behind = moved(ahead, "blk", 1), moved(behind, "blk", -1)
        blocks[reach - d], blocks[reach + d] = ahead, behind
    stacked = jnp.concatenate(blocks, axis=0)

    queries = (
        (nn(first_in, inlet_copy[:, :features]) + vectors[4]) * score_scale
    ).astype(bf16)
    pair_bias = jnp.concatenate([jnp.zeros((features,), f32), vectors[5]])
    pairs = (nn(stacked, inlet_copy[:, features:]) + pair_bias).astype(bf16)
    pairs = pairs.reshape(slots, block_length, 2 * features)
    attended, lse = attend(bounds, queries, pairs, own_ids, slot_columns)
    attended_low = attended.astype(bf16)

    middle = normed + nn(attended_low, outlet_copy) + vectors[6]
    unit_two, scale_two = norm_parts(middle)
    second_in = (unit_two * vectors[2] + vectors[3]).astype(bf16)
    hidden_pre = nn(second_in, expand_copy) + vectors[8:12].reshape(-1)
    half_erf = 0.5 * (1.0 + lax.erf(hidden_pre * (0.5**0.5)))
    hidden = (hidden_pre * half_erf).astype(bf16)
    bell = jnp.exp(-0.5 * hidden_pre * hidden_pre) * (1.0 / (2.0 * jnp.pi) ** 0.5)
    slope = half_erf + hidden_pre * bell
    result = middle + nn(hidden, shrink_copy) + vectors[7]
    layer_output = result.astype(bf16).reshape(sequences, block_length, features)

    bits = bits_of("dp")
    order_one = bits
    order_two = bits[:1] + bits[:0:-1]

    shrink_grad = tn(hidden, grad_down).astype(bf16)
    shrink_share = owned_sum(shrink_grad, order_one)
    down_grad = jnp.sum(grad_down.astype(f32), axis=0)
    grad_pre = (slope * nt(grad_down, shrink_copy)).astype(bf16)
    expand_grad = tn(second_in, grad_pre).astype(bf16)
    expand_share = owned_sum(expand_grad, order_two)
    up_grad = jnp.sum(grad_pre.astype(f32), axis=0)
    grad_second = nt(grad_pre, expand_copy)
    gain_two = jnp.sum(grad_second * unit_two, axis=0)
    shift_two = jnp.sum(grad_second, axis=0)
    grad_middle = grad_down.astype(f32) + norm_back(grad_second, unit_two, scale_two, vectors[2])
    grad_branch = grad_middle.astype(bf16)
    outlet_grad = tn(attended_low, grad_branch).astype(bf16)
    outlet_share = owned_sum(outlet_grad, order_two)
    out_grad = jnp.sum(grad_branch.astype(f32), axis=0)
    grad_attended = nt(grad_branch, outlet_copy).astype(bf16)

    query_low, key_low, value_low = attend_back(
        bounds, queries, pairs, attended, grad_attended, lse, own_ids, slot_columns
    )
    tokens = slots * block_length
    key_low = key_low.reshape(tokens, features)
    value_low = value_low.reshape(tokens, features)
    inlet_grad = jnp.concatenate(
        [tn(first_in, query_low), tn(stacked, key_low), tn(stacked, value_low)], axis=1
    ).astype(bf16)
    middle_column = inlet_grad.shape[1] // 2
    inlet_share = jnp.concatenate(
        [
            owned_sum(inlet_grad[:, :middle_column], order_one),
            owned_sum(inlet_grad[:, middle_column:], order_two),
        ],
        axis=1,
    )
    query_grad = jnp.sum(query_low.astype(f32), axis=0)
    value_grad = jnp.sum(value_low.astype(f32), axis=0)

    parts = nt(key_low, inlet_copy[:, features : 2 * features]) + nt(
        value_low, inlet_copy[:, 2 * features :]
    )
    parts = parts.reshape(slots, block_length, features)
    to_left = parts[0].astype(bf16)
    to_right = parts[slots - 1].astype(bf16)
    for d in range(reach - 1, 0, -1):
        to_left = (parts[reach - d] + moved(to_left, "blk", -1).astype(f32)).astype(bf16)
        to_right = (parts[reach + d] + moved(to_right, "blk", 1).astype(f32)).astype(bf16)
    grad_first = (
        parts[reach]
        + nt(query_low, inlet_copy[:, :features])
        + moved(to_left, "blk", -1).astype(f32)
        + moved(to_right, "blk", 1).astype(f32)
    )
    gain_one = jnp.sum(grad_first * unit_one, axis=0)
    shift_one = jnp.sum(grad_first, axis=0)
    grad_normed = grad_middle + norm_back(grad_first, unit_one, scale_one, vectors[0])
    small = jnp.stack(
        [
            gain_one,
            shift_one,
            gain_two,
            shift_two,
            query_grad,
            value_grad,
            out_grad,
            down_grad,
        ]
        + [up_grad[i * features : (i + 1) * features] for i in range(4)]
        + [jnp.sum(grad_normed, axis=0), jnp.sum(grad_normed * (raw - band_mean), axis=0)]
    )
    small = everywhere_sum(small)
    back_totals = small[12:14]
    grad_variance = -0.5 * back_totals[1] * inverse_std * inverse_std * inverse_std
    grad_centre = -inverse_std * back_totals[0] - 2.0 * band_mean * grad_variance
    input_gradient = (
        grad_normed * inverse_std
        + grad_centre / total_tokens
        + 2.0 * grad_variance * raw / total_tokens
    ).reshape(sequences, block_length, features)
    owner = lax.axis_index("dp")
    columns = vector_master.shape[1]
    vector_share = lax.dynamic_slice_in_dim(small[:12], owner * columns, columns, 1)

    step_value = step_count[0].astype(f32)
    updates = []
    for master, moment, square, share in (
        (inlet_master, inlet_moment, inlet_square, inlet_share),
        (outlet_master, outlet_moment, outlet_square, outlet_share),
        (expand_master, expand_moment, expand_square, expand_share),
        (shrink_master, shrink_moment, shrink_square, shrink_share),
    ):
        updates.extend(
            adam_rule(
                master, moment, square, share.astype(f32), step_value, rate_matrix, decay_matrix
            )
        )
    updates.extend(
        adam_rule(
            vector_master, vector_moment, vector_square, vector_share, step_value, rate_vector, 0.0
        )
    )
    return (layer_output, input_gradient, band_mean, band_variance, *updates)


def solution(mesh):
    tokens = P("dp", "blk", None)
    rows = P("dp", None)
    columns = P(None, "dp")
    matrix = (P(), rows, rows, rows)
    return jax.shard_map(
        per_device,
        mesh=mesh,
        in_specs=(tokens, tokens, P("dp", "blk"), P())
        + matrix * 4
        + (P(), columns, columns, columns),
        out_specs=(tokens, tokens, P(), P()) + (rows,) * 16 + (columns,) * 4,
        check_vma=False,
    )
```

time: 723 us -> 335 us (0.46); the launches traced: 714 us -> 335 us
  waiting for transfers between devices: 443 us -> 72.1 us
  starting transfers between devices: 4.63 us -> 117 us
  blocking collectives: 103 us -> 0 us
  Pallas kernels: 0 us -> 24.7 us
  matrix products: 74.2 us -> 52.6 us
  between operations: 16.1 us -> 3.07 us
    psum x1 -> x0, waiting for transfers between devices: 363 us -> none  [per_device(): lax.psum((gradients[0], gradients[1], gradients[2], gradients[3], gradien...]
    ppermute x10 -> x52, starting transfers between devices: 4.59 us -> 117 us  [the longest x40 78 us: flipped(): return lax.ppermute(block, axis, [(i, i ^ bit) for i in range(size)])]
    psum x2 -> x0, blocking collectives: 82.3 us -> none  [the longest x1 42.1 us: per_device(): lax.psum((jnp.sum(flat_raw, axis=0), jnp.sum(flat_raw * flat_raw, axis=0)...]
    pallas_call x0 -> x2, Pallas kernels: none -> 24.7 us  [the longest x1 13.2 us: attend_back(): pl.pallas_call(attend_back_kernel, grid_spec=pltpu.PrefetchScalarGridSpec...]
    dot_general x39 -> x17, matrix products: 74.2 us -> 52.6 us  [the longest x6 20.1 us: nt(): lax.dot_general(a, b, (((1,), (1,)), ((), ())), preferred_element_type=f32)]
    all_gather x1 -> x0, blocking collectives: 20.8 us -> none  [per_device(): all_ids = lax.all_gather(segment_ids, 'blk', axis=1, tiled=True)]
    ppermute x10 -> x52, waiting for transfers between devices: 80.6 us -> 72.1 us  [the longest x40 57.6 us: flipped(): return lax.ppermute(block, axis, [(i, i ^ bit) for i in range(size)])]
    squeeze x0 -> x20, local copies, waits for them, and re-layouts: none -> 7.94 us  [halves(): send = lax.dynamic_index_in_dim(block, 1 - own, position, keepdims=False)]
  transfers between devices with their start and end apart: 11 -> 52, of which waited for: 9 -> 26; matrix products, arithmetic and copies ran while one was open for 10% -> 18% of each run, Pallas kernels for 0% -> 0%
where the time goes in v1:
time: 335 us
  starting transfers between devices  117 us (35%)
  waiting for transfers between devices  72.1 us (22%)
  matrix products  52.6 us (16%)
  other arithmetic  36.1 us (11%)
  local copies, waits for them, and re-layouts  29.5 us (9%)
  Pallas kernels  24.7 us (7%)
    ppermute x40, starting transfers between devices, flipped(): return lax.ppermute(block, axis, [(i, i ^ bit) for i in range(size)])  78 us
    ppermute x40, waiting for transfers between devices, flipped(): return lax.ppermute(block, axis, [(i, i ^ bit) for i in range(size)])  57.6 us
    ppermute x12, starting transfers between devices, moved(): return lax.ppermute(block, axis, route)  39 us
    dot_general x6, matrix products, nt(): lax.dot_general(a, b, (((1,), (1,)), ((), ())), preferred_element_type=f32)  20.1 us
    dot_general x5, matrix products, nn(): lax.dot_general(a, b, (((1,), (0,)), ((), ())), preferred_element_type=f32)  16.7 us
    dot_general x6, matrix products, tn(): lax.dot_general(a, b, (((0,), (0,)), ((), ())), preferred_element_type=f32)  15.8 us
    ppermute x12, waiting for transfers between devices, moved(): return lax.ppermute(block, axis, route)  14.4 us
    pallas_call x1, Pallas kernels, attend_back(): pl.pallas_call(attend_back_kernel, grid_spec=pltpu.PrefetchScalarGridSpec...  13.2 us
  transfers between devices with their start and end apart: 52, of which 26 were waited for; matrix products, arithmetic and copies ran while one was open for 18% of the time, Pallas kernels for 0%

profile of v1, /device:TPU:0, one launch (start us, length us, event | category | flops | bytes accessed | tf_op | source)
XLA Modules:
  0.0 335.0 jit_solution(446398143095397461)
XLA Ops:
  5.8 5.1 %collective-permute-start.5 = (s32[1,256]{1,0:T(1,128)S(1)}, s32[1,256]{1,0:T(1,128)S(1)}, u32[]{:S(2)}, u32[]{:S(2)}) collective-permute-start(s32[1,256]{1,0:T(1,128)S(1)} %broadcast_add_fusion.4), channel_id=1, source_target_pairs={{0,1},{1,2},{2,3},{4,5},{5,6},{6,7},{8,9},{9,10},{10,11},{12,13},{... | collective-permute-start | bytes 3080 | tf_op jit(solution)/shard_map/ppermute | solution.py:50
  22.0 3.0 collective-permute-start.4
  29.8 3.5 %collective-permute-start.9 = (bf16[256,768]{1,0:T(8,128)(2,1)S(1)}, bf16[256,768]{1,0:T(8,128)(2,1)S(1)}, u32[]{:S(2)}, u32[]{:S(2)}) collective-permute-start(bf16[256,768]{1,0:T(8,128)(2,1)S(1)} %add_convert_fusion.1), channel_id=1, source_target_pairs={{0,1},{1,2},{2,3},{4,5},{5,6},{6,7},{8,9},{9,10},{10,11},{12,13},{... | collective-permute-start | bytes 1179656 | tf_op jit(solution)/shard_map/ppermute | solution.py:50
  39.0 4.4 %collective-permute-start.10 = (bf16[256,768]{1,0:T(8,128)(2,1)S(1)}, bf16[256,768]{1,0:T(8,128)(2,1)S(1)}, u32[]{:S(2)}, u32[]{:S(2)}) collective-permute-start(bf16[256,768]{1,0:T(8,128)(2,1)S(1)} %collective-permute-done.9), channel_id=1, source_target_pairs={{0,1},{1,2},{2,3},{4,5},{5,6},{6,7},{8,9},{9,10},{10,11},{12,13},{... | collective-permute-start | bytes 1179656 | tf_op jit(solution)/shard_map/ppermute | solution.py:50
  52.8 7.8 %collective-permute-done.12 = bf16[256,768]{1,0:T(8,128)(2,1)S(1)} collective-permute-done((bf16[256,768]{1,0:T(8,128)(2,1)S(1)}, bf16[256,768]{1,0:T(8,128)(2,1)S(1)}, u32[]{:S(2)}, u32[]{:S(2)}) %collective-permute-start.12) | collective-permute-done | bytes 393248 | tf_op jit(solution)/shard_map/ppermute | solution.py:50
  60.7 4.8 %fusion = bf16[1280,1536]{1,0:T(8,128)(2,1)} fusion(bf16[1280,768]{1,0:T(8,128)(2,1)S(1)} %constant_dynamic-update-slice_fusion, f32[1536]{0:T(1024)S(1)} %concatenate.52, bf16[768,2304]{1,0:T(8,128)(2,1)S(1)} %copy-done.18), kind=kOutput, calls=%fused_computation.1 | convolution fusion | flops 3023831040 | bytes 8265728 | tf_op jit(solution)/shard_map/dot_general | solution.py:31
  65.5 11.4 %attend.1 = (f32[256,768]{1,0:T(8,128)}, f32[3,4,256]{2,1,0:T(4,128)}) custom-call(s32[2]{0:T(128)} %pad_add_fusion.bounds, bf16[256,768]{1,0:T(8,128)(2,1)} %fusion.17.q_ref, bf16[5,256,1536]{2,1,0:T(8,128)(2,1)} %bitcast.191, bf16[5,256,1536]{2,1,0:T(8,128)(2,1)} %bitcast.192, s32[1,256]{1,0:T(1,128)} %qid_ref.3, s32[5,256,1]{2,1,0:T(8,128)} %copy.50.kid_ref), custom_call_target="tpu_custom_call" | custom-call | tf_op jit(solution)/shard_map/attend/pallas_call | solution.py:150
  79.0 5.5 %multiply_convert_fusion = (bf16[256,3072]{1,0:T(8,128)(2,1)}, f32[256,3072]{1,0:T(8,128)S(1)}) fusion(f32[3072]{0:T(1024)S(1)} %copy-done.72, bf16[768,3072]{1,0:T(8,128)(2,1)} %param.36, f32[256,768]{1,0:T(8,128)S(1)} %get-tuple-element.98, f32[768]{0:T(1024)S(1)} %copy-done.36, f32[768]{0:T(1024)S(1)} %get-tuple-element.48, f32[256]{0:T(256)S(1)} %add_rsqrt_fusion.1, ...), kind=kOutput, calls=%fused_computation.19 | convolution fusion | flops 1213661184 | bytes 10244096 | tf_op jit(solution)/shard_map/dot_general | solution.py:31
  84.5 4.9 %convert_reduce_fusion.1 = (f32[3072]{0:T(1024)}, bf16[256,3072]{1,0:T(8,128)(2,1)S(1)}) fusion(bf16[3072,768]{1,0:T(8,128)(2,1)} %param.40, bf16[1,256,768]{2,1,0:T(8,128)(2,1)S(1)} %copy-done.16, f32[256,3072]{1,0:T(8,128)S(1)} %get-tuple-element.100), kind=kOutput, calls=%fused_computation.18 | convolution fusion | flops 1217393664 | bytes 9842688 | tf_op jit(solution)/shard_map/dot_general | solution.py:35
  95.3 13.2 %attend_back.1 = (bf16[256,768]{1,0:T(8,128)(2,1)}, bf16[5,256,768]{2,1,0:T(8,128)(2,1)}, bf16[5,256,768]{2,1,0:T(8,128)(2,1)}) custom-call(s32[2]{0:T(128)} %pad_add_fusion.bounds, bf16[256,768]{1,0:T(8,128)(2,1)} %fusion.17.q_ref, bf16[5,256,1536]{2,1,0:T(8,128)(2,1)} %bitcast.193, bf16[5,256,1536]{2,1,0:T(8,128)(2,1)} %bitcast.194, ...), custom_call_target="tpu_custom_call" | custom-call | tf_op jit(solution)/shard_map/attend_back/pallas_call | solution.py:239
  111.5 3.4 %convolution_convert_fusion.4 = bf16[768,768]{0,1:T(8,128)(2,1)S(1)} fusion(bf16[1280,768]{1,0:T(8,128)(2,1)S(1)} %copy-done.39, bf16[1280,768]{1,0:T(8,128)(2,1)} %bitcast.227), kind=kOutput, calls=%fused_computation.38 | convolution fusion | flops 1510539264 | bytes 5111808 | tf_op jit(solution)/shard_map/dot_general | solution.py:39
  114.9 5.1 %fusion.27 = f32[1280,768]{1,0:T(8,128)} fusion(bf16[1280,768]{1,0:T(8,128)(2,1)S(1)} %bitcast.228, bf16[768,2304]{1,0:T(8,128)(2,1)} %param.28), kind=kOutput, calls=%fused_computation.69 | convolution fusion | flops 1509949440 | bytes 7077888 | tf_op jit(solution)/shard_map/dot_general | solution.py:35
  120.1 3.8 %convolution_convert_fusion.1 = bf16[768,3072]{1,0:T(8,128)(2,1)} fusion(bf16[256,3072]{1,0:T(8,128)(2,1)S(1)} %copy-done.21, f32[256,768]{1,0:T(8,128)S(1)} %get-tuple-element.98, f32[768]{0:T(1024)S(1)} %copy-done.37, f32[768]{0:T(1024)S(1)} %get-tuple-element.48, f32[256]{0:T(256)S(1)} %copy-done.60, f32[256]{0:T(256)S(1)} %copy-done.54), kind=kOutput, calls=%fused_computation.3 | convolution fusion | flops 1211301888 | bytes 7086080 | tf_op jit(solution)/shard_map/dot_general | solution.py:39
  126.2 3.6 %convolution_convert_fusion = bf16[3072,768]{1,0:T(8,128)(2,1)} fusion(bf16[256,3072]{1,0:T(8,128)(2,1)S(1)} %copy-done.13, bf16[1,256,768]{2,1,0:T(8,128)(2,1)S(1)} %copy-done.17), kind=kOutput, calls=%fused_computation.2 | convolution fusion | flops 1210318848 | bytes 6684672 | tf_op jit(solution)/shard_map/dot_general | solution.py:39
  141.4 3.9 %copy.52 = bf16[768,1152]{1,0:T(8,128)(2,1)} copy(bf16[768,1152]{0,1:T(8,128)(2,1)} %get-tuple-element.87) | data formatting | bytes 3538944 | tf_op jit(solution)/shard_map/slice | solution.py:421
  145.3 5.0 %fusion.86 = (bf16[1280,768]{1,0:T(8,128)(2,1)S(1)}, f32[1280,768]{1,0:T(8,128)S(1)}) fusion(f32[1280,768]{1,0:T(8,128)} %fusion.27, bf16[1280,768]{1,0:T(8,128)(2,1)} %bitcast.203, bf16[768,2304]{1,0:T(8,128)(2,1)} %param.28), kind=kOutput, calls=%fused_computation.231 | convolution fusion | flops 1511915520 | bytes 12976128 | tf_op jit(solution)/shard_map/dot_general | solution.py:35
  152.5 5.3 %collective-permute-start.15 = (bf16[256,768]{1,0:T(8,128)(2,1)}, bf16[256,768]{1,0:T(8,128)(2,1)}, u32[]{:S(2)}, u32[]{:S(2)}) collective-permute-start(bf16[256,768]{1,0:T(8,128)(2,1)} %get-tuple-element.86), channel_id=1, source_target_pairs={{0,1},{1,2},{2,3},{4,5},{5,6},{6,7},{8,9},{9,10},{10,11},{12,13},{... | collective-permute-start | bytes 1179656 | tf_op jit(solution)/shard_map/ppermute | solution.py:50
  160.6 3.9 %copy.53 = bf16[768,1152]{1,0:T(8,128)(2,1)} copy(bf16[768,1152]{0,1:T(8,128)(2,1)} %get-tuple-element.88) | data formatting | bytes 3538944 | tf_op jit(solution)/shard_map/slice | solution.py:422
  168.6 10.5 %collective-permute-start.16 = (bf16[256,768]{1,0:T(8,128)(2,1)S(1)}, bf16[256,768]{1,0:T(8,128)(2,1)S(1)}, u32[]{:S(2)}, u32[]{:S(2)}) collective-permute-start(bf16[256,768]{1,0:T(8,128)(2,1)S(1)} %get-tuple-element.84), channel_id=1, source_target_pairs={{0,1},{1,2},{2,3},{4,5},{5,6},{6,7},{8,9},{9,10},{10,11},{12,13},{... | collective-permute-start | bytes 1179656 | tf_op jit(solution)/shard_map/ppermute | solution.py:50
  190.7 10.9 %collective-permute-start.18 = (f32[14,768]{1,0:T(8,128)S(1)}, f32[14,768]{1,0:T(8,128)S(1)}, u32[]{:S(2)}, u32[]{:S(2)}) collective-permute-start(f32[14,768]{1,0:T(8,128)S(1)} %add.505), channel_id=1, source_target_pairs={{0,8},{4,12},{8,0},{12,4},{16,24},{20,28},{24,16},{28,20},{1,9},{5... | collective-permute-start | bytes 129032 | tf_op jit(solution)/shard_map/ppermute | solution.py:44
  215.2 3.2 collective-permute-start.21
  225.8 3.7 %collective-permute-start.38 = (bf16[48,768]{1,0:T(8,128)(2,1)S(1)}, bf16[48,768]{1,0:T(8,128)(2,1)S(1)}, u32[]{:S(2)}, u32[]{:S(2)}) collective-permute-start(bf16[48,768]{1,0:T(8,128)(2,1)S(1)} %fusion.57), channel_id=1, source_target_pairs={{0,2},{1,3},{2,0},{3,1},{4,6},{5,7},{6,4},{7,5},{8,10},{9,11},{10,... | collective-permute-start | bytes 221192 | tf_op jit(solution)/shard_map/ppermute | solution.py:44
  239.8 3.8 %collective-permute-done.24 = bf16[96,1152]{1,0:T(8,128)(2,1)S(1)} collective-permute-done((bf16[96,1152]{1,0:T(8,128)(2,1)S(1)}, bf16[96,1152]{1,0:T(8,128)(2,1)S(1)}, u32[]{:S(2)}, u32[]{:S(2)}) %collective-permute-start.24) | collective-permute-done | bytes 221216 | tf_op jit(solution)/shard_map/ppermute | solution.py:44
  255.2 3.1 collective-permute-start.27
  264.1 18.4 %collective-permute-done.41 = bf16[2,96,3072]{2,1,0:T(8,128)(2,1)S(1)} collective-permute-done((bf16[2,96,3072]{2,1,0:T(8,128)(2,1)S(1)}, bf16[2,96,3072]{2,1,0:T(8,128)(2,1)S(1)}, u32[]{:S(2)}, u32[]{:S(2)}) %collective-permute-start.41) | collective-permute-done | bytes 1179680 | tf_op jit(solution)/shard_map/ppermute | solution.py:44
  288.3 4.8 %collective-permute-done.42 = bf16[96,3072]{1,0:T(8,128)(2,1)S(1)} collective-permute-done((bf16[96,3072]{1,0:T(8,128)(2,1)S(1)}, bf16[96,3072]{1,0:T(8,128)(2,1)S(1)}, u32[]{:S(2)}, u32[]{:S(2)}) %collective-permute-start.42) | collective-permute-done | bytes 589856 | tf_op jit(solution)/shard_map/ppermute | solution.py:44
  298.4 3.5 %collective-permute-done.43 = bf16[48,3072]{1,0:T(8,128)(2,1)S(1)} collective-permute-done((bf16[48,3072]{1,0:T(8,128)(2,1)S(1)}, bf16[48,3072]{1,0:T(8,128)(2,1)S(1)}, u32[]{:S(2)}, u32[]{:S(2)}) %collective-permute-start.43) | collective-permute-done | bytes 294944 | tf_op jit(solution)/shard_map/ppermute | solution.py:44
  302.0 6.5 %collective-permute-start.44 = (bf16[48,3072]{1,0:T(8,128)(2,1)S(1)}, bf16[48,3072]{1,0:T(8,128)(2,1)S(1)}, u32[]{:S(2)}, u32[]{:S(2)}) collective-permute-start(bf16[48,3072]{1,0:T(8,128)(2,1)S(1)} %fusion.43), channel_id=1, source_target_pairs={{0,2},{1,3},{2,0},{3,1},{4,6},{5,7},{6,4},{7,5},{8,10},{9,11},{10,... | collective-permute-start | bytes 884744 | tf_op jit(solution)/shard_map/ppermute | solution.py:44
  308.5 4.2 %collective-permute-start.50 = (bf16[192,768]{1,0:T(8,128)(2,1)S(1)}, bf16[192,768]{1,0:T(8,128)(2,1)S(1)}, u32[]{:S(2)}, u32[]{:S(2)}) collective-permute-start(bf16[192,768]{1,0:T(8,128)(2,1)S(1)} %fusion.42), channel_id=1, source_target_pairs={{0,2},{1,3},{2,0},{3,1},{4,6},{5,7},{6,4},{7,5},{8,10},{9,11},{10,... | collective-permute-start | bytes 884744 | tf_op jit(solution)/shard_map/ppermute | solution.py:44
  314.8 6.0 %collective-permute-done.50 = bf16[192,768]{1,0:T(8,128)(2,1)S(1)} collective-permute-done((bf16[192,768]{1,0:T(8,128)(2,1)S(1)}, bf16[192,768]{1,0:T(8,128)(2,1)S(1)}, u32[]{:S(2)}, u32[]{:S(2)}) %collective-permute-start.50) | collective-permute-done | bytes 294944 | tf_op jit(solution)/shard_map/ppermute | solution.py:44
  320.8 3.5 %collective-permute-start.51 = (bf16[192,768]{1,0:T(8,128)(2,1)S(1)}, bf16[192,768]{1,0:T(8,128)(2,1)S(1)}, u32[]{:S(2)}, u32[]{:S(2)}) collective-permute-start(bf16[192,768]{1,0:T(8,128)(2,1)S(1)} %add_convert_fusion.2), channel_id=1, source_target_pairs={{0,1},{1,0},{2,3},{3,2},{4,5},{5,4},{6,7},{7,6},{8,9},{9,8},{10,11... | collective-permute-start | bytes 884744 | tf_op jit(solution)/shard_map/ppermute | solution.py:44
  324.5 4.5 %collective-permute-done.51 = bf16[192,768]{1,0:T(8,128)(2,1)S(1)} collective-permute-done((bf16[192,768]{1,0:T(8,128)(2,1)S(1)}, bf16[192,768]{1,0:T(8,128)(2,1)S(1)}, u32[]{:S(2)}, u32[]{:S(2)}) %collective-permute-start.51) | collective-permute-done | bytes 294944 | tf_op jit(solution)/shard_map/ppermute | solution.py:44
  (400 shorter events, 147.7 us)
Async XLA Ops:
  4.5 15.9 %collective-permute-start.7 = (s32[1,256]{1,0:T(1,128)S(1)}, s32[1,256]{1,0:T(1,128)S(1)}, u32[]{:S(2)}, u32[]{:S(2)}) collective-permute-start(s32[1,256]{1,0:T(1,128)S(1)} %broadcast_add_fusion.4), channel_id=1, source_target_pairs={{1,0},{2,1},{3,2},{5,4},{6,5},{7,6},{9,8},{10,9},{11,10},{13,12},{... | collective-permute-start | bytes 3080 | tf_op jit(solution)/shard_map/ppermute | solution.py:50
  5.8 19.2 %collective-permute-start.5 = (s32[1,256]{1,0:T(1,128)S(1)}, s32[1,256]{1,0:T(1,128)S(1)}, u32[]{:S(2)}, u32[]{:S(2)}) collective-permute-start(s32[1,256]{1,0:T(1,128)S(1)} %broadcast_add_fusion.4), channel_id=1, source_target_pairs={{0,1},{1,2},{2,3},{4,5},{5,6},{6,7},{8,9},{9,10},{10,11},{12,13},{... | collective-permute-start | bytes 3080 | tf_op jit(solution)/shard_map/ppermute | solution.py:50
  20.4 12.9 %collective-permute-start.8 = (s32[1,256]{1,0:T(1,128)S(1)}, s32[1,256]{1,0:T(1,128)S(1)}, u32[]{:S(2)}, u32[]{:S(2)}) collective-permute-start(s32[1,256]{1,0:T(1,128)S(1)} %collective-permute-done.7), channel_id=1, source_target_pairs={{1,0},{2,1},{3,2},{5,4},{6,5},{7,6},{9,8},{10,9},{11,10},{13,12},{... | collective-permute-start | bytes 3080 | tf_op jit(solution)/shard_map/ppermute | solution.py:50
  25.0 8.3 %collective-permute-start.6 = (s32[1,256]{1,0:T(1,128)S(1)}, s32[1,256]{1,0:T(1,128)S(1)}, u32[]{:S(2)}, u32[]{:S(2)}) collective-permute-start(s32[1,256]{1,0:T(1,128)S(1)} %collective-permute-done.5), channel_id=1, source_target_pairs={{0,1},{1,2},{2,3},{4,5},{5,6},{6,7},{8,9},{9,10},{10,11},{12,13},{... | collective-permute-start | bytes 3080 | tf_op jit(solution)/shard_map/ppermute | solution.py:50
  29.8 9.2 %collective-permute-start.9 = (bf16[256,768]{1,0:T(8,128)(2,1)S(1)}, bf16[256,768]{1,0:T(8,128)(2,1)S(1)}, u32[]{:S(2)}, u32[]{:S(2)}) collective-permute-start(bf16[256,768]{1,0:T(8,128)(2,1)S(1)} %add_convert_fusion.1), channel_id=1, source_target_pairs={{0,1},{1,2},{2,3},{4,5},{5,6},{6,7},{8,9},{9,10},{10,11},{12,13},{... | collective-permute-start | bytes 1179656 | tf_op jit(solution)/shard_map/ppermute | solution.py:50
  35.5 15.5 %collective-permute-start.11 = (bf16[256,768]{1,0:T(8,128)(2,1)S(1)}, bf16[256,768]{1,0:T(8,128)(2,1)S(1)}, u32[]{:S(2)}, u32[]{:S(2)}) collective-permute-start(bf16[256,768]{1,0:T(8,128)(2,1)S(1)} %add_convert_fusion.1), channel_id=1, source_target_pairs={{1,0},{2,1},{3,2},{5,4},{6,5},{7,6},{9,8},{10,9},{11,10},{13,12},{... | collective-permute-start | bytes 1179656 | tf_op jit(solution)/shard_map/ppermute | solution.py:50
  39.0 13.4 %collective-permute-start.10 = (bf16[256,768]{1,0:T(8,128)(2,1)S(1)}, bf16[256,768]{1,0:T(8,128)(2,1)S(1)}, u32[]{:S(2)}, u32[]{:S(2)}) collective-permute-start(bf16[256,768]{1,0:T(8,128)(2,1)S(1)} %collective-permute-done.9), channel_id=1, source_target_pairs={{0,1},{1,2},{2,3},{4,5},{5,6},{6,7},{8,9},{9,10},{10,11},{12,13},{... | collective-permute-start | bytes 1179656 | tf_op jit(solution)/shard_map/ppermute | solution.py:50
  51.0 9.7 %collective-permute-start.12 = (bf16[256,768]{1,0:T(8,128)(2,1)S(1)}, bf16[256,768]{1,0:T(8,128)(2,1)S(1)}, u32[]{:S(2)}, u32[]{:S(2)}) collective-permute-start(bf16[256,768]{1,0:T(8,128)(2,1)S(1)} %collective-permute-done.11), channel_id=1, source_target_pairs={{1,0},{2,1},{3,2},{5,4},{6,5},{7,6},{9,8},{10,9},{11,10},{13,12},{... | collective-permute-start | bytes 1179656 | tf_op jit(solution)/shard_map/ppermute | solution.py:50
  136.8 43.4 %collective-permute-start.34 = (bf16[2,2,96,768]{3,2,1,0:T(8,128)(2,1)}, bf16[2,2,96,768]{3,2,1,0:T(8,128)(2,1)}, u32[]{:S(2)}, u32[]{:S(2)}) collective-permute-start(bf16[2,2,96,768]{3,2,1,0:T(8,128)(2,1)} %dynamic-slice_bitcast_fusion.8), channel_id=1, source_target_pairs={{0,4},{4,0},{8,12},{12,8},{16,20},{20,16},{24,28},{28,24},{1,5},{5... | collective-permute-start | bytes 1769480 | tf_op jit(solution)/shard_map/ppermute | solution.py:44
  151.2 13.3 %collective-permute-start.13 = (bf16[256,768]{1,0:T(8,128)(2,1)}, bf16[256,768]{1,0:T(8,128)(2,1)}, u32[]{:S(2)}, u32[]{:S(2)}) collective-permute-start(bf16[256,768]{1,0:T(8,128)(2,1)} %get-tuple-element.85), channel_id=1, source_target_pairs={{1,0},{2,1},{3,2},{5,4},{6,5},{7,6},{9,8},{10,9},{11,10},{13,12},{... | collective-permute-start | bytes 1179656 | tf_op jit(solution)/shard_map/ppermute | solution.py:50
  152.5 13.1 %collective-permute-start.15 = (bf16[256,768]{1,0:T(8,128)(2,1)}, bf16[256,768]{1,0:T(8,128)(2,1)}, u32[]{:S(2)}, u32[]{:S(2)}) collective-permute-start(bf16[256,768]{1,0:T(8,128)(2,1)} %get-tuple-element.86), channel_id=1, source_target_pairs={{0,1},{1,2},{2,3},{4,5},{5,6},{6,7},{8,9},{9,10},{10,11},{12,13},{... | collective-permute-start | bytes 1179656 | tf_op jit(solution)/shard_map/ppermute | solution.py:50
  158.8 46.7 %collective-permute-start.22 = (bf16[2,2,96,1152]{3,2,1,0:T(8,128)(2,1)}, bf16[2,2,96,1152]{3,2,1,0:T(8,128)(2,1)}, u32[]{:S(2)}, u32[]{:S(2)}) collective-permute-start(bf16[2,2,96,1152]{3,2,1,0:T(8,128)(2,1)} %dynamic-slice_bitcast_fusion.5), channel_id=1, source_target_pairs={{0,4},{4,0},{8,12},{12,8},{16,20},{20,16},{24,28},{28,24},{1,5},{5... | collective-permute-start | bytes 2654216 | tf_op jit(solution)/shard_map/ppermute | solution.py:44
  167.3 18.2 %collective-permute-start.14 = (bf16[256,768]{1,0:T(8,128)(2,1)S(1)}, bf16[256,768]{1,0:T(8,128)(2,1)S(1)}, u32[]{:S(2)}, u32[]{:S(2)}) collective-permute-start(bf16[256,768]{1,0:T(8,128)(2,1)S(1)} %get-tuple-element.83), channel_id=1, source_target_pairs={{1,0},{2,1},{3,2},{5,4},{6,5},{7,6},{9,8},{10,9},{11,10},{13,12},{... | collective-permute-start | bytes 1179656 | tf_op jit(solution)/shard_map/ppermute | solution.py:50
  168.6 18.1 %collective-permute-start.16 = (bf16[256,768]{1,0:T(8,128)(2,1)S(1)}, bf16[256,768]{1,0:T(8,128)(2,1)S(1)}, u32[]{:S(2)}, u32[]{:S(2)}) collective-permute-start(bf16[256,768]{1,0:T(8,128)(2,1)S(1)} %get-tuple-element.84), channel_id=1, source_target_pairs={{0,1},{1,2},{2,3},{4,5},{5,6},{6,7},{8,9},{9,10},{10,11},{12,13},{... | collective-permute-start | bytes 1179656 | tf_op jit(solution)/shard_map/ppermute | solution.py:50
  180.2 30.4 %collective-permute-start.28 = (bf16[2,2,96,1152]{3,2,1,0:T(8,128)(2,1)}, bf16[2,2,96,1152]{3,2,1,0:T(8,128)(2,1)}, u32[]{:S(2)}, u32[]{:S(2)}) collective-permute-start(bf16[2,2,96,1152]{3,2,1,0:T(8,128)(2,1)} %dynamic-slice_bitcast_fusion.4), channel_id=1, source_target_pairs={{0,4},{4,0},{8,12},{12,8},{16,20},{20,16},{24,28},{28,24},{1,5},{5... | collective-permute-start | bytes 2654216 | tf_op jit(solution)/shard_map/ppermute | solution.py:44
  182.2 21.5 %collective-permute-start.35 = (bf16[2,96,768]{2,1,0:T(8,128)(2,1)}, bf16[2,96,768]{2,1,0:T(8,128)(2,1)S(1)}, u32[]{:S(2)}, u32[]{:S(2)}) collective-permute-start(bf16[2,96,768]{2,1,0:T(8,128)(2,1)} %dynamic-slice_bitcast_fusion.13), channel_id=1, source_target_pairs={{0,16},{4,20},{8,24},{12,28},{16,0},{20,4},{24,8},{28,12},{1,17},{... | collective-permute-start | bytes 884744 | tf_op jit(solution)/shard_map/ppermute | solution.py:44
  190.1 68.2 %collective-permute-start.40 = (bf16[2,2,96,3072]{3,2,1,0:T(8,128)(2,1)S(1)}, bf16[2,2,96,3072]{3,2,1,0:T(8,128)(2,1)S(1)}, u32[]{:S(2)}, u32[]{:S(2)}) collective-permute-start(bf16[2,2,96,3072]{3,2,1,0:T(8,128)(2,1)S(1)} %dynamic-slice_bitcast_fusion.1), channel_id=1, source_target_pairs={{0,4},{4,0},{8,12},{12,8},{16,20},{20,16},{24,28},{28,24},{1,5},{5... | collective-permute-start | bytes 7077896 | tf_op jit(solution)/shard_map/ppermute | solution.py:44
  190.7 13.0 %collective-permute-start.18 = (f32[14,768]{1,0:T(8,128)S(1)}, f32[14,768]{1,0:T(8,128)S(1)}, u32[]{:S(2)}, u32[]{:S(2)}) collective-permute-start(f32[14,768]{1,0:T(8,128)S(1)} %add.505), channel_id=1, source_target_pairs={{0,8},{4,12},{8,0},{12,4},{16,24},{20,28},{24,16},{28,20},{1,9},{5... | collective-permute-start | bytes 129032 | tf_op jit(solution)/shard_map/ppermute | solution.py:44
  203.6 57.6 %collective-permute-start.46 = (bf16[2,2,384,768]{3,2,1,0:T(8,128)(2,1)S(1)}, bf16[2,2,384,768]{3,2,1,0:T(8,128)(2,1)S(1)}, u32[]{:S(2)}, u32[]{:S(2)}) collective-permute-start(bf16[2,2,384,768]{3,2,1,0:T(8,128)(2,1)S(1)} %dynamic-slice_bitcast_fusion), channel_id=1, source_target_pairs={{0,4},{4,0},{8,12},{12,8},{16,20},{20,16},{24,28},{28,24},{1,5},{5... | collective-permute-start | bytes 7077896 | tf_op jit(solution)/shard_map/ppermute | solution.py:44
  205.5 15.8 %collective-permute-start.36 = (bf16[96,768]{1,0:T(8,128)(2,1)S(1)}, bf16[96,768]{1,0:T(8,128)(2,1)S(1)}, u32[]{:S(2)}, u32[]{:S(2)}) collective-permute-start(bf16[96,768]{1,0:T(8,128)(2,1)S(1)} %dynamic-slice_bitcast_fusion.16), channel_id=1, source_target_pairs={{0,8},{4,12},{8,0},{12,4},{16,24},{20,28},{24,16},{28,20},{1,9},{5... | collective-permute-start | bytes 442376 | tf_op jit(solution)/shard_map/ppermute | solution.py:44
  209.0 28.4 %collective-permute-start.23 = (bf16[2,96,1152]{2,1,0:T(8,128)(2,1)S(1)}, bf16[2,96,1152]{2,1,0:T(8,128)(2,1)S(1)}, u32[]{:S(2)}, u32[]{:S(2)}) collective-permute-start(bf16[2,96,1152]{2,1,0:T(8,128)(2,1)S(1)} %dynamic-slice_bitcast_fusion.10), channel_id=1, source_target_pairs={{0,8},{4,12},{8,0},{12,4},{16,24},{20,28},{24,16},{28,20},{1,9},{5... | collective-permute-start | bytes 1327112 | tf_op jit(solution)/shard_map/ppermute | solution.py:44
  220.5 19.0 %collective-permute-start.29 = (bf16[2,96,1152]{2,1,0:T(8,128)(2,1)S(1)}, bf16[2,96,1152]{2,1,0:T(8,128)(2,1)S(1)}, u32[]{:S(2)}, u32[]{:S(2)}) collective-permute-start(bf16[2,96,1152]{2,1,0:T(8,128)(2,1)S(1)} %dynamic-slice_bitcast_fusion.9), channel_id=1, source_target_pairs={{0,16},{4,20},{8,24},{12,28},{16,0},{20,4},{24,8},{28,12},{1,17},{... | collective-permute-start | bytes 1327112 | tf_op jit(solution)/shard_map/ppermute | solution.py:44
  252.3 8.8 %collective-permute-start.32 = (bf16[48,1152]{1,0:T(8,128)(2,1)S(1)}, bf16[48,1152]{1,0:T(8,128)(2,1)S(1)}, u32[]{:S(2)}, u32[]{:S(2)}) collective-permute-start(bf16[48,1152]{1,0:T(8,128)(2,1)S(1)} %fusion.52), channel_id=1, source_target_pairs={{0,2},{1,3},{2,0},{3,1},{4,6},{5,7},{6,4},{7,5},{8,10},{9,11},{10,... | collective-permute-start | bytes 331784 | tf_op jit(solution)/shard_map/ppermute | solution.py:44
  259.3 23.1 %collective-permute-start.41 = (bf16[2,96,3072]{2,1,0:T(8,128)(2,1)S(1)}, bf16[2,96,3072]{2,1,0:T(8,128)(2,1)S(1)}, u32[]{:S(2)}, u32[]{:S(2)}) collective-permute-start(bf16[2,96,3072]{2,1,0:T(8,128)(2,1)S(1)} %dynamic-slice_bitcast_fusion.3), channel_id=1, source_target_pairs={{0,16},{4,20},{8,24},{12,28},{16,0},{20,4},{24,8},{28,12},{1,17},{... | collective-permute-start | bytes 3538952 | tf_op jit(solution)/shard_map/ppermute | solution.py:44
  261.1 24.2 %collective-permute-start.33 = (bf16[48,1152]{1,0:T(8,128)(2,1)S(1)}, bf16[48,1152]{1,0:T(8,128)(2,1)S(1)}, u32[]{:S(2)}, u32[]{:S(2)}) collective-permute-start(bf16[48,1152]{1,0:T(8,128)(2,1)S(1)} %add_convert_fusion.4), channel_id=1, source_target_pairs={{0,1},{1,0},{2,3},{3,2},{4,5},{5,4},{6,7},{7,6},{8,9},{9,8},{10,11... | collective-permute-start | bytes 331784 | tf_op jit(solution)/shard_map/ppermute | solution.py:44
  262.0 24.8 %collective-permute-start.47 = (bf16[2,384,768]{2,1,0:T(8,128)(2,1)S(1)}, bf16[2,384,768]{2,1,0:T(8,128)(2,1)S(1)}, u32[]{:S(2)}, u32[]{:S(2)}) collective-permute-start(bf16[2,384,768]{2,1,0:T(8,128)(2,1)S(1)} %dynamic-slice_bitcast_fusion.2), channel_id=1, source_target_pairs={{0,8},{4,12},{8,0},{12,4},{16,24},{20,28},{24,16},{28,20},{1,9},{5... | collective-permute-start | bytes 3538952 | tf_op jit(solution)/shard_map/ppermute | solution.py:44
  282.9 10.3 %collective-permute-start.42 = (bf16[96,3072]{1,0:T(8,128)(2,1)S(1)}, bf16[96,3072]{1,0:T(8,128)(2,1)S(1)}, u32[]{:S(2)}, u32[]{:S(2)}) collective-permute-start(bf16[96,3072]{1,0:T(8,128)(2,1)S(1)} %dynamic-slice_bitcast_fusion.7), channel_id=1, source_target_pairs={{0,8},{4,12},{8,0},{12,4},{16,24},{20,28},{24,16},{28,20},{1,9},{5... | collective-permute-start | bytes 1769480 | tf_op jit(solution)/shard_map/ppermute | solution.py:44
  287.1 9.9 %collective-permute-start.48 = (bf16[384,768]{1,0:T(8,128)(2,1)S(1)}, bf16[384,768]{1,0:T(8,128)(2,1)S(1)}, u32[]{:S(2)}, u32[]{:S(2)}) collective-permute-start(bf16[384,768]{1,0:T(8,128)(2,1)S(1)} %dynamic-slice_bitcast_fusion.6), channel_id=1, source_target_pairs={{0,16},{4,20},{8,24},{12,28},{16,0},{20,4},{24,8},{28,12},{1,17},{... | collective-permute-start | bytes 1769480 | tf_op jit(solution)/shard_map/ppermute | solution.py:44
  293.4 8.5 %collective-permute-start.43 = (bf16[48,3072]{1,0:T(8,128)(2,1)S(1)}, bf16[48,3072]{1,0:T(8,128)(2,1)S(1)}, u32[]{:S(2)}, u32[]{:S(2)}) collective-permute-start(bf16[48,3072]{1,0:T(8,128)(2,1)S(1)} %dynamic-slice_bitcast_fusion.12), channel_id=1, source_target_pairs={{0,1},{1,0},{2,3},{3,2},{4,5},{5,4},{6,7},{7,6},{8,9},{9,8},{10,11... | collective-permute-start | bytes 884744 | tf_op jit(solution)/shard_map/ppermute | solution.py:44
  297.2 11.2 %collective-permute-start.49 = (bf16[192,768]{1,0:T(8,128)(2,1)S(1)}, bf16[192,768]{1,0:T(8,128)(2,1)S(1)}, u32[]{:S(2)}, u32[]{:S(2)}) collective-permute-start(bf16[192,768]{1,0:T(8,128)(2,1)S(1)} %dynamic-slice_bitcast_fusion.11), channel_id=1, source_target_pairs={{0,1},{1,0},{2,3},{3,2},{4,5},{5,4},{6,7},{7,6},{8,9},{9,8},{10,11... | collective-permute-start | bytes 884744 | tf_op jit(solution)/shard_map/ppermute | solution.py:44
  302.0 22.3 %collective-permute-start.44 = (bf16[48,3072]{1,0:T(8,128)(2,1)S(1)}, bf16[48,3072]{1,0:T(8,128)(2,1)S(1)}, u32[]{:S(2)}, u32[]{:S(2)}) collective-permute-start(bf16[48,3072]{1,0:T(8,128)(2,1)S(1)} %fusion.43), channel_id=1, source_target_pairs={{0,2},{1,3},{2,0},{3,1},{4,6},{5,7},{6,4},{7,5},{8,10},{9,11},{10,... | collective-permute-start | bytes 884744 | tf_op jit(solution)/shard_map/ppermute | solution.py:44
  308.5 12.2 %collective-permute-start.50 = (bf16[192,768]{1,0:T(8,128)(2,1)S(1)}, bf16[192,768]{1,0:T(8,128)(2,1)S(1)}, u32[]{:S(2)}, u32[]{:S(2)}) collective-permute-start(bf16[192,768]{1,0:T(8,128)(2,1)S(1)} %fusion.42), channel_id=1, source_target_pairs={{0,2},{1,3},{2,0},{3,1},{4,6},{5,7},{6,4},{7,5},{8,10},{9,11},{10,... | collective-permute-start | bytes 884744 | tf_op jit(solution)/shard_map/ppermute | solution.py:44
  (108 other events, 1087.0 us)

commit v2 on v1

v2 whole, which is shorter than its diff:
```python
import functools

import jax
import jax.numpy as jnp
from jax import lax
from jax.experimental import pallas as pl
from jax.experimental.pallas import tpu as pltpu
from jax.sharding import PartitionSpec as P

HEADS = 12
HEAD_WIDTH = 64
GROUP = 4

ln_epsilon = 1e-05
stat_epsilon = 1e-06
beta_one = 0.5
beta_two = 0.6
rate_matrix = 0.04
rate_vector = 0.8
warmup_length = 20.0
decay_matrix = 0.05
adam_epsilon = 1e-08
score_scale = 0.125
masked_score = -1e30

f32 = jnp.float32
bf16 = jnp.bfloat16


def nn(a, b):
    return lax.dot_general(a, b, (((1,), (0,)), ((), ())), preferred_element_type=f32)


def nt(a, b):
    return lax.dot_general(a, b, (((1,), (1,)), ((), ())), preferred_element_type=f32)


def tn(a, b):
    return lax.dot_general(a, b, (((0,), (0,)), ((), ())), preferred_element_type=f32)


def flipped(block, axis, bit):
    size = lax.axis_size(axis)
    return lax.ppermute(block, axis, [(i, i ^ bit) for i in range(size)])


def moved(block, axis, distance):
    size = lax.axis_size(axis)
    route = [(i, i + distance) for i in range(size) if 0 <= i + distance < size]
    return lax.ppermute(block, axis, route)


def bits_of(axis):
    size = lax.axis_size(axis)
    return [1 << i for i in range(size.bit_length() - 1)]


def everywhere_sum(block):
    for axis in ("dp", "blk"):
        bits = bits_of(axis)
        rounds = [bits[:1]] if len(bits) % 2 else []
        rounds += [bits[i : i + 2] for i in range(len(bits) % 2, len(bits), 2)]
        for part in rounds:
            if len(part) == 1:
                block = block + flipped(block, axis, part[0])
            else:
                low, high = part
                others = [flipped(block, axis, bit) for bit in (low, high, low | high)]
                block = (block + others[0]) + (others[1] + others[2])
    return block


def added(kept, arrived):
    return (kept.astype(f32) + arrived.astype(f32)).astype(bf16)


class Scatter:
    def __init__(self, block, order):
        self.block, self.order = block, list(order)
        self.left = list(bits_of("dp")[1:])

    def send(self):
        where = self.left.index(self.order.pop(0))
        bit = self.left.pop(where)
        self.keep = lax.index_in_dim(self.block, 0, where, keepdims=False)
        self.arrived = flipped(lax.index_in_dim(self.block, 1, where, keepdims=False), "dp", bit)

    def add(self):
        self.block = added(self.keep, self.arrived)


class Line:
    def __init__(self, first, second):
        self.bits = bits_of("blk")
        own = lax.axis_index("blk") % 2
        self.trail = []
        self.keep = jnp.where(own == 0, first, second)
        self.sent = jnp.where(own == 0, second, first)

    def scatter(self):
        self.arrived = flipped(self.sent, "blk", 1)

    def exchange(self):
        share = added(self.keep, self.arrived)
        for bit in self.bits[1:-1]:
            own = (lax.axis_index("blk") // bit) % 2
            parts = share.reshape(2, share.shape[0] // 2, share.shape[1])
            keep = lax.dynamic_index_in_dim(parts, own, 0, keepdims=False)
            sent = lax.dynamic_index_in_dim(parts, 1 - own, 0, keepdims=False)
            share = added(keep, flipped(sent, "blk", bit))
            self.trail.append((bit, own))
        self.keep = share
        self.arrived = flipped(share, "blk", self.bits[-1])

    def gather(self):
        share = added(self.keep, self.arrived)
        for bit, own in reversed(self.trail):
            other = flipped(share, "blk", bit)
            share = jnp.concatenate(
                [jnp.where(own == 0, share, other), jnp.where(own == 0, other, share)], axis=0
            )
        self.keep = share
        self.arrived = flipped(share, "blk", 1)

    def result(self):
        own = lax.axis_index("blk") % 2
        mine, other = self.keep, self.arrived
        return jnp.concatenate(
            [jnp.where(own == 0, mine, other), jnp.where(own == 0, other, mine)], axis=0
        )


def together(*values):
    return lax.optimization_barrier(values)


def whole(shape):
    return pl.BlockSpec(shape, lambda *a: (0,) * len(shape))


def call(kernel, name, grid, ins, outs, scratch, operands, table, aliases=None, flops=0, moved_bytes=0, mib=16):
    return pl.pallas_call(
        kernel,
        grid_spec=pltpu.PrefetchScalarGridSpec(
            num_scalar_prefetch=1,
            grid=grid,
            in_specs=[spec for spec, _ in ins],
            out_specs=[spec for spec, _ in outs],
            scratch_shapes=scratch,
        ),
        out_shape=[shape for _, shape in outs],
        input_output_aliases=aliases or {},
        cost_estimate=pl.CostEstimate(
            flops=flops, bytes_accessed=moved_bytes, transcendentals=0
        ),
        compiler_params=pltpu.CompilerParams(vmem_limit_bytes=mib << 20),
        name=name,
    )(table, *[operand for _, operand in ins])


def struct(shape, dtype):
    return jax.ShapeDtypeStruct(shape, dtype)


def unit_rows(rows):
    centred = rows - jnp.mean(rows, axis=-1, keepdims=True)
    scale = lax.rsqrt(jnp.mean(centred * centred, axis=-1, keepdims=True) + ln_epsilon)
    return centred * scale, scale


def norm_back(grad, unit, scale, gain):
    inner = grad * gain
    return scale * (
        inner
        - jnp.mean(inner, axis=-1, keepdims=True)
        - unit * jnp.mean(inner * unit, axis=-1, keepdims=True)
    )


def column_sum(rows):
    return jnp.sum(rows, axis=0, keepdims=True)


def totals_kernel(table, raw_ref, out_ref):
    raw = raw_ref[...]
    out_ref[0:1, :] = column_sum(raw)
    out_ref[1:2, :] = column_sum(raw * raw)


def enter_kernel(total_tokens, table, raw_ref, sum_ref, vec_ref, id_ref, x_ref, mean_ref, var_ref, std_ref):
    width = raw_ref.shape[0]
    mean = sum_ref[0:1, :] / total_tokens
    variance = sum_ref[1:2, :] / total_tokens - mean * mean
    inverse = lax.rsqrt(variance + stat_epsilon)
    mean_ref[...] = mean
    var_ref[...] = variance
    std_ref[...] = inverse
    unit, _ = unit_rows((raw_ref[...] - mean) * inverse)
    x_ref[0:width, :] = (unit * vec_ref[0:1, :] + vec_ref[1:2, :]).astype(bf16)
    x_ref[width:, :] = jnp.zeros((x_ref.shape[0] - width, x_ref.shape[1]), bf16)
    ids = jnp.broadcast_to(id_ref[...], (16, width)).astype(f32).astype(bf16)
    x_ref[width:, 0:width] = ids


def project_own_kernel(table, x_ref, w_ref, vec_ref, q_ref, kv_ref, id_ref):
    width = q_ref.shape[0]
    features = q_ref.shape[1]
    x = x_ref[0:width, :]
    q_ref[...] = (
        (nn(x, w_ref[:, :features]) + vec_ref[4:5, :]) * score_scale
    ).astype(bf16)
    kv_ref[0, :, :features] = nn(x, w_ref[:, features : 2 * features]).astype(bf16)
    kv_ref[0, :, features:] = (nn(x, w_ref[:, 2 * features :]) + vec_ref[5:6, :]).astype(bf16)
    id_ref[0] = id_columns(x_ref, width)


def id_columns(x_ref, width):
    rows = jnp.broadcast_to(x_ref[width : width + 8, 0:width].astype(f32)[0:1], (128, width))
    return rows.T


def project_pair_kernel(table, xa_ref, xb_ref, w_ref, vec_ref, kv_in, id_in, kv_ref, id_ref):
    width = kv_ref.shape[1]
    features = kv_ref.shape[2] // 2
    step = pl.program_id(0)

    def fill(x_ref, inside):
        x = x_ref[0:width, :]
        kv_ref[0, :, :features] = nn(x, w_ref[:, features : 2 * features]).astype(bf16)
        kv_ref[0, :, features:] = (nn(x, w_ref[:, 2 * features :]) + vec_ref[5:6, :]).astype(bf16)
        ids = id_columns(x_ref, width)
        id_ref[0] = jnp.where(inside > 0, ids, -1.0 - jnp.zeros_like(ids))

    @pl.when(step == 0)
    def _():
        fill(xa_ref, table[0])

    @pl.when(step == 1)
    def _():
        fill(xb_ref, table[1])


def lane_half(rows, which):
    lanes = lax.broadcasted_iota(jnp.int32, (rows, 128), 1)
    return (lanes >= 64) if which else (lanes < 64)


def attend_kernel(
    reach, table, q_ref, k_ref, v_ref, qid_ref, kid_ref, o_ref, lse_ref, bound_ref, acc, top, total
):
    width = q_ref.shape[0]
    slots = k_ref.shape[0]

    @pl.when(pl.program_id(0) == 0)
    def _():
        low = kid_ref[reach, 0:1, :]
        high = kid_ref[reach, width - 1 : width, :]
        start = jnp.full_like(low, float(reach))
        end = jnp.full_like(low, float(reach))
        for s in range(slots):
            active = (kid_ref[s, width - 1 : width, :] >= low) & (kid_ref[s, 0:1, :] <= high)
            start = jnp.where(active, jnp.minimum(start, float(s)), start)
            end = jnp.where(active, jnp.maximum(end, float(s)), end)
        bound_ref[0] = jnp.min(start).astype(jnp.int32)
        bound_ref[1] = jnp.max(end).astype(jnp.int32) + 1

    top[...] = jnp.full_like(top, masked_score)
    total[...] = jnp.zeros_like(total)
    acc[...] = jnp.zeros_like(acc)
    own = qid_ref[...].astype(f32)
    masked_q = []
    for h in range(GROUP):
        pair = q_ref[:, 128 * (h // 2) : 128 * (h // 2) + 128]
        masked_q.append(jnp.where(lane_half(width, h % 2), pair, jnp.zeros_like(pair)))

    def step(s, carry):
        keys = k_ref[s]
        values_t = v_ref[s].T
        column = kid_ref[s]
        allowed = jnp.concatenate([column] * (width // 128), axis=1) == own
        for h in range(GROUP):
            lanes = slice(128 * (h // 2), 128 * (h // 2) + 128)
            score = jnp.where(allowed, nt(keys[:, lanes], masked_q[h]), masked_score)
            old = top[h : h + 1, :]
            new = jnp.maximum(old, jnp.max(score, axis=0, keepdims=True))
            fade = jnp.exp(old - new)
            weight = jnp.exp(score - new)
            total[h : h + 1, :] = total[h : h + 1, :] * fade + column_sum(weight)
            top[h : h + 1, :] = new
            rows = slice(64 * h, 64 * h + 64)
            acc[rows, :] = acc[rows, :] * fade + nn(values_t[rows, :], weight.astype(bf16))
        return carry

    lax.fori_loop(bound_ref[0], bound_ref[1], step, 0)
    for h in range(GROUP):
        rows = slice(64 * h, 64 * h + 64)
        acc[rows, :] = acc[rows, :] / total[h : h + 1, :]
    o_ref[...] = acc[...].T.astype(bf16)
    lse_ref[0] = top[0:GROUP, :] + jnp.log(total[0:GROUP, :])


def ffn_kernel(
    half,
    table,
    o_ref,
    wo_ref,
    raw_ref,
    mean_ref,
    std_ref,
    vec_ref,
    cot_ref,
    w1_ref,
    w2_ref,
    ub_ref,
    middle_ref,
    out_ref,
    gsec_ref,
    sk_ref,
    ss_ref,
    ek_ref,
    es_ref,
    ug_ref,
    s2,
    s2t,
    plain_t,
    rows_s,
    acc,
):
    step = pl.program_id(0)
    features = middle_ref.shape[1]
    owners = 2 * half
    owned = features // owners

    @pl.when(step == 0)
    def _():
        normed = (raw_ref[...] - mean_ref[...]) * std_ref[...]
        middle = normed + nn(o_ref[...], wo_ref[...]) + vec_ref[6:7, :]
        middle_ref[...] = middle
        unit, _ = unit_rows(middle)
        second = unit * vec_ref[2:3, :] + vec_ref[3:4, :]
        s2[...] = second.astype(bf16)
        plain_t[...] = second.T.astype(bf16)
        for p in range(owners):
            place = pl.multiple_of(table[half + p] * owned, 16)
            s2t[owned * p : owned * p + owned, :] = plain_t[pl.ds(place, owned), :]
        acc[...] = jnp.zeros_like(acc)
        gsec_ref[...] = jnp.zeros_like(gsec_ref)

    pre = nn(s2[...], w1_ref[...]) + ub_ref[...]
    area = 0.5 * (1.0 + lax.erf(pre * (0.5**0.5)))
    bell = jnp.exp(-0.5 * pre * pre) * (1.0 / (2.0 * jnp.pi) ** 0.5)
    hidden = (pre * area).astype(bf16)
    grad = ((area + pre * bell) * nt(cot_ref[...], w2_ref[...])).astype(bf16)
    acc[...] += nn(hidden, w2_ref[...])
    gsec_ref[...] += nt(grad, w1_ref[...])
    ug_ref[...] = column_sum(grad.astype(f32))
    wide = rows_s.shape[0] // 2
    rows_s[...] = nn(hidden.T, cot_ref[...]).astype(bf16)
    own = table[half] % 2
    sk_ref[0] = rows_s[pl.ds(pl.multiple_of(own * wide, 16), wide), :]
    ss_ref[0] = rows_s[pl.ds(pl.multiple_of((1 - own) * wide, 16), wide), :]
    ek_ref[...] = nn(s2t[: features // 2, :], grad).astype(bf16)
    es_ref[...] = nn(s2t[features // 2 :, :], grad).astype(bf16)

    @pl.when(step == half - 1)
    def _():
        out_ref[...] = (middle_ref[...] + acc[...] + vec_ref[7:8, :]).astype(bf16)


def branch_kernel(table, gsec_ref, middle_ref, cot_ref, vec_ref, wo_ref, gm_ref, gb_ref, ga_ref, row_ref):
    unit, scale = unit_rows(middle_ref[...])
    grad = gsec_ref[...]
    cot = cot_ref[...].astype(f32)
    row_ref[0:1, :] = column_sum(grad * unit)
    row_ref[1:2, :] = column_sum(grad)
    grad_middle = cot + norm_back(grad, unit, scale, vec_ref[2:3, :])
    gm_ref[...] = grad_middle
    branch = grad_middle.astype(bf16)
    gb_ref[...] = branch
    row_ref[2:3, :] = column_sum(branch.astype(f32))
    row_ref[3:4, :] = column_sum(cot)
    ga_ref[...] = nt(branch, wo_ref[...]).astype(bf16)


def attend_back_kernel(
    bounds,
    q_ref,
    k_ref,
    v_ref,
    o_ref,
    g_ref,
    lse_ref,
    qid_ref,
    kid_ref,
    dq_ref,
    dk_ref,
    dv_ref,
    row_ref,
    acc,
):
    width = q_ref.shape[0]
    slots = k_ref.shape[0]
    acc[...] = jnp.zeros_like(acc)
    own = qid_ref[...].astype(f32)
    product = (g_ref[...].astype(f32) * o_ref[...].astype(f32)).T
    masked_q, masked_g, deltas, lses = [], [], [], []
    for h in range(GROUP):
        lanes = slice(128 * (h // 2), 128 * (h // 2) + 128)
        half = lane_half(width, h % 2)
        pair = q_ref[:, lanes]
        masked_q.append(jnp.where(half, pair, jnp.zeros_like(pair)))
        pair = g_ref[:, lanes]
        masked_g.append(jnp.where(half, pair, jnp.zeros_like(pair)))
        deltas.append(column_sum(product[64 * h : 64 * h + 64, :]))
        lses.append(lse_ref[0, h : h + 1, :])
    row_ref[...] = jnp.zeros_like(row_ref)

    def blank(s, carry):
        dk_ref[s] = jnp.zeros(dk_ref.shape[1:], dk_ref.dtype)
        dv_ref[s] = jnp.zeros(dv_ref.shape[1:], dv_ref.dtype)
        return carry

    lax.fori_loop(0, bounds[0], blank, 0)
    lax.fori_loop(bounds[1], slots, blank, 0)

    def step(s, carry):
        keys = k_ref[s]
        values = v_ref[s]
        keys_t = keys.T
        column = kid_ref[s]
        allowed = jnp.concatenate([column] * (width // 128), axis=1) == own
        for j in range(GROUP // 2):
            lanes = slice(128 * j, 128 * j + 128)
            key_part, value_part = None, None
            for h in (2 * j, 2 * j + 1):
                score = jnp.where(allowed, nt(keys[:, lanes], masked_q[h]), masked_score)
                prob = jnp.exp(score - lses[h])
                grad = (prob * (nt(values[:, lanes], masked_g[h]) - deltas[h])).astype(bf16)
                rows = slice(64 * h, 64 * h + 64)
                acc[rows, :] += nn(keys_t[rows, :], grad)
                k_now = nn(grad, masked_q[h])
                v_now = nn(prob.astype(bf16), masked_g[h])
                key_part = k_now if key_part is None else key_part + k_now
                value_part = v_now if value_part is None else value_part + v_now
            dk_ref[s, :, lanes] = key_part.astype(bf16)
            dv_ref[s, :, lanes] = value_part.astype(bf16)
            row_ref[1:2, lanes] += column_sum(value_part)
        return carry

    lax.fori_loop(bounds[0], bounds[1], step, 0)
    dq = (acc[...].T.astype(bf16).astype(f32) * score_scale).astype(bf16)
    dq_ref[...] = dq
    row_ref[0:1, :] = column_sum(dq.astype(f32))


def parts_kernel(reach, bounds, dq_ref, dk_ref, dv_ref, w_ref, p_ref, own_ref):
    step = pl.program_id(0)
    features = dq_ref.shape[1]
    slot = jnp.where(step % 2 == 0, step // 2, 2 * reach - step // 2)
    active = (slot >= bounds[0]) & (slot < bounds[1])

    @pl.when(jnp.logical_not(active))
    def _():
        p_ref[0] = jnp.zeros(p_ref.shape[1:], p_ref.dtype)

    @pl.when(active)
    def _():
        part = nt(dk_ref[0], w_ref[:, features : 2 * features]) + nt(
            dv_ref[0], w_ref[:, 2 * features :]
        )
        p_ref[0] = part.astype(bf16)

        @pl.when(step == 2 * reach)
        def _():
            own_ref[...] = part + nt(dq_ref[...], w_ref[:, :features])


def weight_kernel(reach, owners, table, *refs):
    slots = 2 * reach + 1
    xs = refs[:slots]
    dq_ref, dk_ref, dv_ref, o_ref, gb_ref, keep_ref, send_ref, xt, ot, plain = refs[slots:]
    width, features = dq_ref.shape
    owned = features // owners
    step = pl.program_id(0)

    def turn(rows, ref, lanes):
        plain[...] = rows.T
        for p in range(owners):
            place = pl.multiple_of(table[2 + p] * owned, 16)
            ref[owned * p : owned * p + owned, lanes] = plain[pl.ds(place, owned), :]

    @pl.when(step == 0)
    def _():
        for s in range(slots):
            turn(xs[s][0:width, :], xt, slice(width * s, width * s + width))
        turn(o_ref[...], ot, slice(0, width))
        own = slice(width * reach, width * reach + width)
        keep_ref[...] = nn(xt[: features // 2, own], dq_ref[...]).astype(bf16)
        send_ref[...] = nn(xt[features // 2 :, own], dq_ref[...]).astype(bf16)

    def summed(d_ref):
        few = min(3, slots)
        small = table[1] - table[0] <= few

        def over(start, size):
            lanes = pl.ds(pl.multiple_of(start * width, 128), size * width)
            rows = d_ref[pl.ds(start, size)].reshape(size * width, features)
            keep_ref[...] = nn(xt[: features // 2, lanes], rows).astype(bf16)
            send_ref[...] = nn(xt[features // 2 :, lanes], rows).astype(bf16)

        @pl.when(small)
        def _():
            over(jnp.minimum(table[0], slots - few), few)

        @pl.when(jnp.logical_not(small))
        def _():
            over(0, slots)

    @pl.when(step == 1)
    def _():
        summed(dk_ref)

    @pl.when(step == 2)
    def _():
        summed(dv_ref)

    @pl.when(step == 3)
    def _():
        keep_ref[...] = nn(ot[: features // 2, :], gb_ref[...]).astype(bf16)
        send_ref[...] = nn(ot[features // 2 :, :], gb_ref[...]).astype(bf16)


def leave_kernel(
    table,
    raw_ref,
    mean_ref,
    std_ref,
    vec_ref,
    gm_ref,
    own_ref,
    left_ref,
    right_ref,
    branch_rows,
    attend_rows,
    up_ref,
    gn_ref,
    row_ref,
):
    features = raw_ref.shape[1]
    centred = raw_ref[...] - mean_ref[...]
    unit, scale = unit_rows(centred * std_ref[...])
    grad = own_ref[...] + left_ref[...].astype(f32) + right_ref[...].astype(f32)
    row_ref[0:1, :] = column_sum(grad * unit)
    row_ref[1:2, :] = column_sum(grad)
    row_ref[2:4, :] = branch_rows[0:2, :]
    row_ref[4:6, :] = attend_rows[0:2, :]
    row_ref[6:8, :] = branch_rows[2:4, :]
    for r in range(4):
        row_ref[8 + r : 9 + r, :] = up_ref[0:1, r * features : (r + 1) * features]
    whole_grad = gm_ref[...] + norm_back(grad, unit, scale, vec_ref[0:1, :])
    gn_ref[...] = whole_grad
    row_ref[12:13, :] = column_sum(whole_grad)
    row_ref[13:14, :] = column_sum(whole_grad * centred)
    row_ref[14:16, :] = jnp.zeros((2, features), f32)


def adam_rule(master, moment, square, gradient, step_value, step_rate, weight_decay):
    moment_new = beta_one * moment + (1.0 - beta_one) * gradient
    square_new = beta_two * square + (1.0 - beta_two) * gradient * gradient
    fix_first = 1.0 - jnp.power(beta_one, step_value)
    fix_second = 1.0 - jnp.power(beta_two, step_value)
    planned = step_rate * jnp.minimum(1.0, step_value / warmup_length)
    direction = moment_new / fix_first / (jnp.sqrt(square_new / fix_second) + adam_epsilon)
    weight_new = master - planned * (direction + weight_decay * master)
    return (weight_new, moment_new, square_new, weight_new.astype(bf16))


def per_device(
    raw_input,
    cotangent,
    segment_ids,
    step_count,
    inlet_copy,
    inlet_master,
    inlet_moment,
    inlet_square,
    outlet_copy,
    outlet_master,
    outlet_moment,
    outlet_square,
    expand_copy,
    expand_master,
    expand_moment,
    expand_square,
    shrink_copy,
    shrink_master,
    shrink_moment,
    shrink_square,
    vector_copy,
    vector_master,
    vector_moment,
    vector_square,
):
    sequences, block_length, features = raw_input.shape
    assert sequences == 1
    width = block_length
    group_size = lax.axis_size("blk")
    group_index = lax.axis_index("blk")
    owners = lax.axis_size("dp")
    owner = lax.axis_index("dp")
    half = owners // 2
    total_tokens = owners * group_size * block_length
    reach = group_size // 2
    slots = 2 * reach + 1
    inner = expand_copy.shape[1]
    chunk = inner // half
    vectors = vector_copy.astype(f32)
    up_bias = vectors[8:12].reshape(1, inner)
    raw = raw_input.reshape(width, features)
    cot = cotangent.reshape(width, features)
    own_ids = segment_ids
    no_table = jnp.zeros((1,), jnp.int32)

    count = owners.bit_length() - 1

    def reversed_bits(value, size):
        return int(format(value, f"0{size}b")[::-1], 2) if size else 0

    pair_order = (owner // 2) ^ jnp.array(
        [reversed_bits(i, count - 1) for i in range(half)], jnp.int32
    )
    owner_order = owner ^ jnp.array([reversed_bits(i, count) for i in range(owners)], jnp.int32)
    table = jnp.concatenate([pair_order, owner_order])

    tokens = (width, features)
    row = (1, features)

    (totals,) = call(
        totals_kernel,
        "totals",
        (1,),
        [(whole(tokens), raw)],
        [(whole((2, features)), struct((2, features), f32))],
        [],
        None,
        no_table,
        mib=4,
    )
    totals = everywhere_sum(totals)
    packed = width + 16
    x, band_mean, band_variance, inverse_std = call(
        functools.partial(enter_kernel, total_tokens),
        "enter",
        (1,),
        [(whole(tokens), raw), (whole((2, features)), totals), (whole((12, features)), vectors), (whole((1, width)), own_ids)],
        [(whole((packed, features)), struct((packed, features), bf16))]
        + [(whole(row), struct(row, f32))] * 3,
        [],
        None,
        no_table,
        mib=8,
    )

    xs = [None] * slots
    xs[reach] = x
    wkv = 3 * features
    queries, pairs, columns = call(
        project_own_kernel,
        "project_own",
        (1,),
        [(whole((packed, features)), x), (whole((features, wkv)), inlet_copy), (whole((12, features)), vectors)],
        [
            (whole(tokens), struct(tokens, bf16)),
            (pl.BlockSpec((1, width, 2 * features), lambda i, t: (reach, 0, 0)), struct((slots, width, 2 * features), bf16)),
            (pl.BlockSpec((1, width, 128), lambda i, t: (reach, 0, 0)), struct((slots, width, 128), f32)),
        ],
        [],
        None,
        no_table,
        flops=2 * width * features * wkv,
        mib=12,
    )
    ahead, behind = x, x
    for d in range(1, reach + 1):
        ahead, behind = moved(ahead, "blk", 1), moved(behind, "blk", -1)
        xs[reach - d], xs[reach + d] = ahead, behind
        inside = jnp.stack([group_index >= d, group_index + d < group_size]).astype(jnp.int32)
        place = lambda i, t, d=d: (reach - d + 2 * d * i, 0, 0)
        pairs, columns = call(
            project_pair_kernel,
            "project_pair",
            (2,),
            [
                (whole((packed, features)), ahead),
                (whole((packed, features)), behind),
                (whole((features, wkv)), inlet_copy),
                (whole((12, features)), vectors),
                (pl.BlockSpec(memory_space=pl.ANY), pairs),
                (pl.BlockSpec(memory_space=pl.ANY), columns),
            ],
            [
                (pl.BlockSpec((1, width, 2 * features), place), struct(pairs.shape, bf16)),
                (pl.BlockSpec((1, width, 128), place), struct(columns.shape, f32)),
            ],
            [],
            None,
            inside,
            aliases={5: 0, 6: 1},
            flops=8 * width * features * features,
        mib=14,
    )

    lanes = GROUP * HEAD_WIDTH
    steps = features // lanes
    flat = pl.BlockSpec((width, lanes), lambda i, t: (0, i))
    first_part = pl.BlockSpec((slots, width, lanes), lambda i, t: (0, 0, i))
    second_part = pl.BlockSpec((slots, width, lanes), lambda i, t: (0, 0, i + steps))
    lse_spec = pl.BlockSpec((1, GROUP, width), lambda i, t: (i, 0, 0))
    attended, lse, bounds = call(
        functools.partial(attend_kernel, reach),
        "attend",
        (steps,),
        [
            (flat, queries),
            (first_part, pairs),
            (second_part, pairs),
            (whole((1, width)), own_ids),
            (whole(columns.shape), columns),
        ],
        [
            (flat, struct(tokens, bf16)),
            (lse_spec, struct((steps, GROUP, width), f32)),
            (pl.BlockSpec(memory_space=pltpu.SMEM), struct((2,), jnp.int32)),
        ],
        [pltpu.VMEM((lanes, width), f32), pltpu.VMEM((8, width), f32), pltpu.VMEM((8, width), f32)],
        None,
        no_table,
        flops=4 * slots * width * width * features,
        mib=10,
    )

    owned_wide = inner // owners
    middle, layer_output, grad_second, shrink_keep, shrink_send, expand_keep, expand_send, up_grad = call(
        functools.partial(ffn_kernel, half),
        "ffn",
        (half,),
        [
            (whole(tokens), attended),
            (whole((features, features)), outlet_copy),
            (whole(tokens), raw),
            (whole(row), band_mean),
            (whole(row), inverse_std),
            (whole((12, features)), vectors),
            (whole(tokens), cot),
            (pl.BlockSpec((features, chunk), lambda i, t: (0, t[i])), expand_copy),
            (pl.BlockSpec((chunk, features), lambda i, t: (t[i], 0)), shrink_copy),
            (pl.BlockSpec((1, chunk), lambda i, t: (0, t[i])), up_bias),
        ],
        [
            (whole(tokens), struct(tokens, f32)),
            (whole(tokens), struct(tokens, bf16)),
            (whole(tokens), struct(tokens, f32)),
            (pl.BlockSpec((1, owned_wide, features), lambda i, t: (i, 0, 0)), struct((half, owned_wide, features), bf16)),
            (pl.BlockSpec((1, owned_wide, features), lambda i, t: (i, 0, 0)), struct((half, owned_wide, features), bf16)),
            (pl.BlockSpec((features // 2, chunk), lambda i, t: (0, t[i])), struct((features // 2, inner), bf16)),
            (pl.BlockSpec((features // 2, chunk), lambda i, t: (0, t[i])), struct((features // 2, inner), bf16)),
            (pl.BlockSpec((1, chunk), lambda i, t: (0, t[i])), struct((1, inner), f32)),
        ],
        [
            pltpu.VMEM(tokens, bf16),
            pltpu.VMEM((features, width), bf16),
            pltpu.VMEM((features, width), bf16),
            pltpu.VMEM((chunk, features), bf16),
            pltpu.VMEM(tokens, f32),
        ],
        None,
        table,
        flops=12 * width * features * inner,
        mib=30,
    )
    bits = bits_of("dp")
    order_one, order_two = bits[1:], bits[:0:-1]
    relative = (2,) * (count - 1)
    owned = features // owners
    shrink_in = flipped(shrink_send, "dp", 1)
    expand_in = flipped(expand_send, "dp", 1)

    def scatters(block, rows):
        block = block.reshape(relative + (2, rows // 2, block.shape[-1]))
        return [
            Scatter(lax.index_in_dim(block, h, count - 1, keepdims=False), order)
            for h, order in ((0, order_one), (1, order_two))
        ]

    grad_middle, grad_branch, grad_attended, branch_rows = call(
        branch_kernel,
        "branch",
        (1,),
        [
            (whole(tokens), grad_second),
            (whole(tokens), middle),
            (whole(tokens), cot),
            (whole((12, features)), vectors),
            (whole((features, features)), outlet_copy),
        ],
        [
            (whole(tokens), struct(tokens, f32)),
            (whole(tokens), struct(tokens, bf16)),
            (whole(tokens), struct(tokens, bf16)),
            (whole((4, features)), struct((4, features), f32)),
        ],
        [],
        None,
        no_table,
        flops=2 * width * features * features,
        mib=10,
    )
    shrink_sum, expand_sum = added(shrink_keep, shrink_in), added(expand_keep, expand_in)
    shrink_sum, expand_sum, grad_attended = together(shrink_sum, expand_sum, grad_attended)
    first = scatters(shrink_sum, owned_wide)
    second = scatters(expand_sum, owned)
    for one in first + second:
        one.send()
    spread = (slots, width, features)
    query_low, key_low, value_low, attend_rows = call(
        attend_back_kernel,
        "attend_back",
        (steps,),
        [
            (flat, queries),
            (first_part, pairs),
            (second_part, pairs),
            (flat, attended),
            (flat, grad_attended),
            (lse_spec, lse),
            (whole((1, width)), own_ids),
            (whole(columns.shape), columns),
        ],
        [
            (flat, struct(tokens, bf16)),
            (first_part, struct(spread, bf16)),
            (first_part, struct(spread, bf16)),
            (pl.BlockSpec((2, lanes), lambda i, t: (0, i)), struct((2, features), f32)),
        ],
        [pltpu.VMEM((lanes, width), f32)],
        None,
        bounds,
        flops=10 * slots * width * width * features,
        mib=12,
    )

    query_low, key_low, value_low, first[0].arrived, first[1].arrived = together(
        query_low, key_low, value_low, first[0].arrived, first[1].arrived
    )
    for one in first:
        one.add()
        if one.order:
            one.send()

    def slot_at(i, t):
        return (jnp.where(i % 2 == 0, i // 2, 2 * reach - i // 2), 0, 0)

    one_slot = pl.BlockSpec((1, width, features), slot_at)
    parts, own_part = call(
        functools.partial(parts_kernel, reach),
        "parts",
        (slots,),
        [
            (whole(tokens), query_low),
            (one_slot, key_low),
            (one_slot, value_low),
            (whole((features, wkv)), inlet_copy),
        ],
        [(one_slot, struct(spread, bf16)), (whole(tokens), struct(tokens, f32))],
        [],
        None,
        bounds,
        flops=4 * slots * width * features * features,
        mib=14,
    )
    to_left, to_right = parts[0], parts[slots - 1]
    for d in range(reach - 1, 0, -1):
        to_left = added(parts[reach - d], moved(to_left, "blk", -1))
        to_right = added(parts[reach + d], moved(to_right, "blk", 1))
    from_right, from_left = moved(to_left, "blk", -1), moved(to_right, "blk", 1)

    from_right, from_left, query_low, key_low, value_low, second[0].arrived, second[1].arrived = (
        together(from_right, from_left, query_low, key_low, value_low, second[0].arrived, second[1].arrived)
    ) if False else (from_right, from_left, query_low, key_low, value_low, second[0].arrived, second[1].arrived)
    column_block = pl.BlockSpec((features // 2, features), lambda i, t: (0, i))
    inlet_keep, inlet_send = call(
        functools.partial(weight_kernel, reach, owners),
        "weights",
        (4,),
        [(whole((packed, features)), block) for block in xs]
        + [
            (whole(tokens), query_low),
            (whole(spread), key_low),
            (whole(spread), value_low),
            (whole(tokens), attended),
            (whole(tokens), grad_branch),
        ],
        [
            (column_block, struct((features // 2, 4 * features), bf16)),
            (column_block, struct((features // 2, 4 * features), bf16)),
        ],
        [
            pltpu.VMEM((features, slots * width), bf16),
            pltpu.VMEM((features, width), bf16),
            pltpu.VMEM((features, width), bf16),
        ],
        None,
        jnp.concatenate([bounds, owner_order]),
        flops=4 * (slots + 1) * width * features * features,
        mib=24,
    )
    inlet_in = flipped(inlet_send, "dp", 1)
    for one in second:
        one.add()
        if one.order:
            one.send()
    third = scatters(added(inlet_keep, inlet_in), owned)
    for one in first + second:
        while one.order:
            one.add()
            one.send()
        one.add()
    for one in third:
        one.send()
        while one.order:
            one.add()
            one.send()
        one.add()
    lines = [Line(a.block, b.block) for a, b in (first, second, third)]
    for line in lines:
        line.scatter()
        line.exchange()
        line.gather()
    shrink_share, expand_share, last_share = [line.result() for line in lines]

    grad_normed, small = call(
        leave_kernel,
        "leave",
        (1,),
        [
            (whole(tokens), raw),
            (whole(row), band_mean),
            (whole(row), inverse_std),
            (whole((12, features)), vectors),
            (whole(tokens), grad_middle),
            (whole(tokens), own_part),
            (whole(tokens), from_left),
            (whole(tokens), from_right),
            (whole((4, features)), branch_rows),
            (whole((2, features)), attend_rows),
            (whole((1, inner)), up_grad),
        ],
        [(whole(tokens), struct(tokens, f32)), (whole((16, features)), struct((16, features), f32))],
        [],
        None,
        no_table,
        mib=12,
    )
    small = everywhere_sum(small)
    back_totals = small[12:14]
    mean, inverse = band_mean[0], inverse_std[0]
    grad_variance = -0.5 * back_totals[1] * inverse * inverse * inverse
    grad_centre = -inverse * back_totals[0] - 2.0 * mean * grad_variance
    input_gradient = (
        grad_normed * inverse
        + grad_centre / total_tokens
        + 2.0 * grad_variance * raw / total_tokens
    ).reshape(sequences, block_length, features)
    column_count = vector_master.shape[1]
    vector_share = lax.dynamic_slice_in_dim(small[:12], owner * column_count, column_count, 1)

    step_value = step_count[0].astype(f32)
    updates = []
    for master, moment, square, share in (
        (inlet_master, inlet_moment, inlet_square, last_share[:, :wkv]),
        (outlet_master, outlet_moment, outlet_square, last_share[:, wkv:]),
        (expand_master, expand_moment, expand_square, expand_share),
        (shrink_master, shrink_moment, shrink_square, shrink_share),
    ):
        updates.extend(
            adam_rule(
                master, moment, square, share.astype(f32), step_value, rate_matrix, decay_matrix
            )
        )
    updates.extend(
        adam_rule(
            vector_master, vector_moment, vector_square, vector_share, step_value, rate_vector, 0.0
        )
    )
    layer_output = layer_output.reshape(sequences, block_length, features)
    return (layer_output, input_gradient, band_mean[0], band_variance[0], *updates)


def solution(mesh):
    tokens = P("dp", "blk", None)
    rows = P("dp", None)
    columns = P(None, "dp")
    matrix = (P(), rows, rows, rows)
    return jax.shard_map(
        per_device,
        mesh=mesh,
        in_specs=(tokens, tokens, P("dp", "blk"), P())
        + matrix * 4
        + (P(), columns, columns, columns),
        out_specs=(tokens, tokens, P(), P()) + (rows,) * 16 + (columns,) * 4,
        check_vma=False,
    )
```

time: 335 us -> 249 us (0.74)
  matrix products: 52.6 us -> 0 us
  starting transfers between devices: 117 us -> 77 us
  Pallas kernels: 24.7 us -> 50.8 us
  other arithmetic: 36.1 us -> 21.1 us
  local copies, waits for them, and re-layouts: 29.5 us -> 21.6 us
    dot_general x17 -> x0, matrix products: 52.6 us -> none  [the longest x6 20.1 us: nt(): lax.dot_general(a, b, (((1,), (1,)), ((), ())), preferred_element_type=f32)]
    ppermute x40 -> x38, starting transfers between devices: 78 us -> 43.5 us  [flipped(): return lax.ppermute(block, axis, [(i, i ^ bit) for i in range(size)])]
    pallas_call x2 -> x12, Pallas kernels: 24.7 us -> 50.8 us  [call(): pl.pallas_call(kernel, grid_spec=pltpu.PrefetchScalarGridSpec(num_scalar_...]
    unnamed x179 -> x148, local copies, waits for them, and re-layouts: 2.57 us -> 20.9 us
    ppermute x40 -> x38, waiting for transfers between devices: 57.6 us -> 71.9 us  [flipped(): return lax.ppermute(block, axis, [(i, i ^ bit) for i in range(size)])]
    ppermute x12 -> x8, waiting for transfers between devices: 14.4 us -> 3.04 us  [moved(): return lax.ppermute(block, axis, route)]
    slice x6 -> x0, local copies, waits for them, and re-layouts: 9.93 us -> none  [the longest x1 3.89 us: per_device(): inlet_grad[:, middle_column:]]
    squeeze x20 -> x16, local copies, waits for them, and re-layouts: 7.94 us -> 0.65 us  [the longest x12 0.36 us: send(): lax.index_in_dim(self.block, 1, where, keepdims=False)]
  transfers between devices with their start and end apart: 52 -> 46, of which waited for: 26 -> 22; matrix products, arithmetic and copies ran while one was open for 18% -> 7% of each run, Pallas kernels for 0% -> 11%
where the time goes in v2:
time: 249 us; the launch traced here: 248 us
  starting transfers between devices  77 us (31%)
  waiting for transfers between devices  75 us (30%)
  Pallas kernels  50.8 us (20%)
  local copies, waits for them, and re-layouts  21.6 us (9%)
  other arithmetic  21.1 us (8%)
  between operations  2.59 us (1%)
    ppermute x38, waiting for transfers between devices, flipped(): return lax.ppermute(block, axis, [(i, i ^ bit) for i in range(size)])  71.9 us
    pallas_call x12, Pallas kernels, call(): pl.pallas_call(kernel, grid_spec=pltpu.PrefetchScalarGridSpec(num_scalar_...  50.8 us
    ppermute x38, starting transfers between devices, flipped(): return lax.ppermute(block, axis, [(i, i ^ bit) for i in range(size)])  43.5 us
    ppermute x8, starting transfers between devices, moved(): return lax.ppermute(block, axis, route)  33.5 us
    unnamed x148, local copies, waits for them, and re-layouts  20.9 us
    convert_element_type x5, other arithmetic, adam_rule(): return (weight_new, moment_new, square_new, weight_new.astype(bf16))  8.98 us
    convert_element_type x16, other arithmetic, added(): return (kept.astype(f32) + arrived.astype(f32)).astype(bf16)  7.46 us
  transfers between devices with their start and end apart: 46, of which 22 were waited for; matrix products, arithmetic and copies ran while one was open for 7% of the time, Pallas kernels for 11%

profile of v2, /device:TPU:0, one launch (start us, length us, event | category | flops | bytes accessed | tf_op | source)
XLA Modules:
  0.0 248.0 jit_solution(18303261835389325858)
XLA Ops:
  3.3 2.9 %collective-permute-start.2 = (f32[2,768]{1,0:T(2,128)S(1)}, f32[2,768]{1,0:T(2,128)S(1)}, u32[]{:S(2)}, u32[]{:S(2)}) collective-permute-start(f32[2,768]{1,0:T(2,128)S(1)} %add.223), channel_id=1, source_target_pairs={{0,16},{4,20},{8,24},{12,28},{16,0},{20,4},{24,8},{28,12},{1,17},{... | collective-permute-start | bytes 18440 | tf_op jit(solution)/shard_map/ppermute | solution.py:44
  8.4 2.2 collective-permute-done.3
  11.2 2.7 %collective-permute-start.5 = (f32[2,768]{1,0:T(2,128)S(1)}, f32[2,768]{1,0:T(2,128)S(1)}, u32[]{:S(2)}, u32[]{:S(2)}) collective-permute-start(f32[2,768]{1,0:T(2,128)S(1)} %add_add_fusion.3), channel_id=1, source_target_pairs={{0,2},{1,3},{2,0},{3,1},{4,6},{5,7},{6,4},{7,5},{8,10},{9,11},{10,... | collective-permute-start | bytes 18440 | tf_op jit(solution)/shard_map/ppermute | solution.py:44
  15.9 3.4 %collective-permute-done.6 = f32[2,768]{1,0:T(2,128)S(1)} collective-permute-done((f32[2,768]{1,0:T(2,128)S(1)}, f32[2,768]{1,0:T(2,128)S(1)}, u32[]{:S(2)}, u32[]{:S(2)}) %collective-permute-start.6) | collective-permute-done | bytes 6176 | tf_op jit(solution)/shard_map/ppermute | solution.py:44
  21.5 2.5 collective-permute-start.7
  26.7 2.5 %collective-permute-done.7.xa_ref.refs_1_ = bf16[272,768]{1,0:T(8,128)(2,1)} collective-permute-done((bf16[272,768]{1,0:T(8,128)(2,1)S(1)}, bf16[272,768]{1,0:T(8,128)(2,1)}, u32[]{:S(2)}, u32[]{:S(2)}) %collective-permute-start.7) | collective-permute-done | bytes 417824 | tf_op jit(solution)/shard_map/ppermute | solution.py:50
  29.3 4.5 %collective-permute-start.8 = (bf16[272,768]{1,0:T(8,128)(2,1)}, bf16[272,768]{1,0:T(8,128)(2,1)S(1)}, u32[]{:S(2)}, u32[]{:S(2)}) collective-permute-start(bf16[272,768]{1,0:T(8,128)(2,1)} %collective-permute-done.7.xa_ref.refs_1_), channel_id=1, source_target_pairs={{0,1},{1,2},{2,3},{4,5},{5,6},{6,7},{8,9},{9,10},{10,11},{12,13},{... | collective-permute-start | bytes 1253384 | tf_op jit(solution)/shard_map/ppermute | solution.py:50
  41.5 3.8 %project_pair.2 = (bf16[5,256,1536]{2,1,0:T(8,128)(2,1)S(1)}, f32[5,256,128]{2,1,0:T(8,128)S(1)}) custom-call(s32[2]{0:T(128)S(1)} %add_convert_fusion.10.table, bf16[272,768]{1,0:T(8,128)(2,1)} %collective-permute-done.7.xa_ref.refs_1_, bf16[272,768]{1,0:T(8,128)(2,1)} %collective-permute-done.9.xb_ref.refs_3_, ...), custom_call_target="tpu_custom_call", output_to_operand_aliasing={{0}: (5, {}), {1}: (6, {})} | custom-call | flops 1207959552 | tf_op jit(solution)/shard_map/project_pair/pallas_call | solution.py:142
  45.4 2.2 project_pair.3
  47.7 9.2 %attend.1 = (bf16[256,768]{1,0:T(8,128)(2,1)S(1)}, f32[3,4,256]{2,1,0:T(4,128)S(1)}, s32[2]{0:T(128)S(1)}) custom-call(s32[1]{0:T(128)} %constant.46.clone.1.table, bf16[256,768]{1,0:T(8,128)(2,1)S(1)} %get-tuple-element.69.q_ref, bf16[5,256,1536]{2,1,0:T(8,128)(2,1)S(1)} %get-tuple-element.74.k_ref.v_ref, ...), custom_call_target="tpu_custom_call" | custom-call | flops 1006632960 | tf_op jit(solution)/shard_map/attend/pallas_call | solution.py:142
  58.1 12.8 %ffn.1 = (f32[256,768]{1,0:T(8,128)S(1)}, bf16[256,768]{1,0:T(8,128)(2,1)}, f32[256,768]{1,0:T(8,128)S(1)}, bf16[4,384,768]{2,1,0:T(8,128)(2,1)S(1)}, bf16[4,384...) custom-call(s32[12]{0:T(128)S(1)} %pad_add_fusion.table, ...), custom_call_target="tpu_custom_call" | custom-call | flops 7247757312 | tf_op jit(solution)/shard_map/ffn/pallas_call | solution.py:142
  85.1 2.4 add_convert_fusion.2
  87.5 2.3 add_convert_fusion.1
  94.6 10.3 %attend_back.1 = (bf16[256,768]{1,0:T(8,128)(2,1)S(1)}, bf16[5,256,768]{2,1,0:T(8,128)(2,1)S(1)}, bf16[5,256,768]{2,1,0:T(8,128)(2,1)S(1)}, f32[2,768]{1,0:T(2,128)S(1)}) custom-call(s32[2]{0:T(128)S(1)} %copy-done.49, bf16[256,768]{1,0:T(8,128)(2,1)S(1)} %copy-done.20, bf16[5,256,1536]{2,1,0:T(8,128)(2,1)S(1)} %copy-done.1, ...), custom_call_target="tpu_custom_call" | custom-call | flops 2516582400 | tf_op jit(solution)/shard_map/attend_back/pallas_call | solution.py:142
  107.8 3.1 %parts.1 = (bf16[5,256,768]{2,1,0:T(8,128)(2,1)S(1)}, f32[256,768]{1,0:T(8,128)S(1)}) custom-call(s32[2]{0:T(128)S(1)} %copy-done.49, bf16[256,768]{1,0:T(8,128)(2,1)S(1)} %get-tuple-element.95.dq_ref.refs_5_, bf16[5,256,768]{2,1,0:T(8,128)(2,1)S(1)} %get-tuple-element.96.dk_ref.refs_6_, bf16[5,256,768]{2,1,0:T(8,128)(2,1)S(1)} %get-tuple-element.97.dv_ref.refs_7_, ...), custom_call_target="tpu_custom_call" | custom-call | flops 3019898880 | tf_op jit(solution)/shard_map/parts/pallas_call | solution.py:142
  112.2 19.3 %collective-permute-start.15 = (bf16[256,768]{1,0:T(8,128)(2,1)S(1)}, bf16[256,768]{1,0:T(8,128)(2,1)S(1)}, u32[]{:S(2)}, u32[]{:S(2)}) collective-permute-start(bf16[256,768]{1,0:T(8,128)(2,1)S(1)} %get-tuple-element.139), channel_id=1, source_target_pairs={{0,1},{1,2},{2,3},{4,5},{5,6},{6,7},{8,9},{9,10},{10,11},{12,13},{... | collective-permute-start | bytes 1179656 | tf_op jit(solution)/shard_map/ppermute | solution.py:50
  135.7 6.0 %collective-permute-done.35 = bf16[48,3072]{1,0:T(8,128)(2,1)S(1)} collective-permute-done((bf16[48,3072]{1,0:T(8,128)(2,1)S(1)}, bf16[48,3072]{1,0:T(8,128)(2,1)S(1)}, u32[]{:S(2)}, u32[]{:S(2)}) %collective-permute-start.35) | collective-permute-done | bytes 294944 | tf_op jit(solution)/shard_map/ppermute | solution.py:44
  142.0 2.1 collective-permute-start.38
  147.7 6.0 %weights.1 = (bf16[384,3072]{1,0:T(8,128)(2,1)S(1)}, bf16[384,3072]{1,0:T(8,128)(2,1)S(1)}) custom-call(s32[10]{0:T(128)S(1)} %pad_add_fusion.1.table, bf16[272,768]{1,0:T(8,128)(2,1)S(1)} %copy-done.31, bf16[272,768]{1,0:T(8,128)(2,1)} %collective-permute-done.7.xa_ref.refs_1_, bf16[272,768]{1,0:T(8,128)(2,1)S(1)} %copy-done.29, ...), custom_call_target="tpu_custom_call" | custom-call | flops 3623878656 | tf_op jit(solution)/shard_map/weights/pallas_call | solution.py:142
  154.0 3.9 %collective-permute-start.43 = (bf16[192,768]{1,0:T(8,128)(2,1)S(1)}, bf16[192,768]{1,0:T(8,128)(2,1)S(1)}, u32[]{:S(2)}, u32[]{:S(2)}) collective-permute-start(bf16[192,768]{1,0:T(8,128)(2,1)S(1)} %broadcast_select_fusion.2), channel_id=1, source_target_pairs={{0,1},{1,0},{2,3},{3,2},{4,5},{5,4},{6,7},{7,6},{8,9},{9,8},{10,11... | collective-permute-start | bytes 884744 | tf_op jit(solution)/shard_map/ppermute | solution.py:44
  163.6 4.0 %collective-permute-done.43 = bf16[192,768]{1,0:T(8,128)(2,1)S(1)} collective-permute-done((bf16[192,768]{1,0:T(8,128)(2,1)S(1)}, bf16[192,768]{1,0:T(8,128)(2,1)S(1)}, u32[]{:S(2)}, u32[]{:S(2)}) %collective-permute-start.43) | collective-permute-done | bytes 294944 | tf_op jit(solution)/shard_map/ppermute | solution.py:44
  169.9 3.0 %collective-permute-start.44 = (bf16[192,768]{1,0:T(8,128)(2,1)S(1)}, bf16[192,768]{1,0:T(8,128)(2,1)S(1)}, u32[]{:S(2)}, u32[]{:S(2)}) collective-permute-start(bf16[192,768]{1,0:T(8,128)(2,1)S(1)} %add_convert_fusion.4), channel_id=1, source_target_pairs={{0,2},{1,3},{2,0},{3,1},{4,6},{5,7},{6,4},{7,5},{8,10},{9,11},{10,... | collective-permute-start | bytes 884744 | tf_op jit(solution)/shard_map/ppermute | solution.py:44
  174.7 3.1 %collective-permute-start.25 = (f32[16,768]{1,0:T(8,128)S(1)}, f32[16,768]{1,0:T(8,128)S(1)}, u32[]{:S(2)}, u32[]{:S(2)}) collective-permute-start(f32[16,768]{1,0:T(8,128)S(1)} %add_add_fusion.1), channel_id=1, source_target_pairs={{0,3},{1,2},{2,1},{3,0},{4,7},{5,6},{6,5},{7,4},{8,11},{9,10},{10,... | collective-permute-start | bytes 147464 | tf_op jit(solution)/shard_map/ppermute | solution.py:44
  177.8 7.1 %collective-permute-done.39 = bf16[48,3072]{1,0:T(8,128)(2,1)S(1)} collective-permute-done((bf16[48,3072]{1,0:T(8,128)(2,1)S(1)}, bf16[48,3072]{1,0:T(8,128)(2,1)S(1)}, u32[]{:S(2)}, u32[]{:S(2)}) %collective-permute-start.39) | collective-permute-done | bytes 294944 | tf_op jit(solution)/shard_map/ppermute | solution.py:44
  184.9 6.3 %collective-permute-done.44 = bf16[192,768]{1,0:T(8,128)(2,1)S(1)} collective-permute-done((bf16[192,768]{1,0:T(8,128)(2,1)S(1)}, bf16[192,768]{1,0:T(8,128)(2,1)S(1)}, u32[]{:S(2)}, u32[]{:S(2)}) %collective-permute-start.44) | collective-permute-done | bytes 294944 | tf_op jit(solution)/shard_map/ppermute | solution.py:44
  197.3 12.6 %collective-permute-done.27 = bf16[2,48,3072]{2,1,0:T(8,128)(2,1)S(1)} collective-permute-done((bf16[2,48,3072]{2,1,0:T(8,128)(2,1)S(1)}, bf16[2,48,3072]{2,1,0:T(8,128)(2,1)S(1)}, u32[]{:S(2)}, u32[]{:S(2)}) %collective-permute-start.27) | collective-permute-done | bytes 589856 | tf_op jit(solution)/shard_map/ppermute | solution.py:44
  213.9 4.0 %collective-permute-done.28 = bf16[48,3072]{1,0:T(8,128)(2,1)S(1)} collective-permute-done((bf16[48,3072]{1,0:T(8,128)(2,1)S(1)}, bf16[48,3072]{1,0:T(8,128)(2,1)S(1)}, u32[]{:S(2)}, u32[]{:S(2)}) %collective-permute-start.28) | collective-permute-done | bytes 294944 | tf_op jit(solution)/shard_map/ppermute | solution.py:44
  219.7 6.1 %collective-permute-done.31 = bf16[48,3072]{1,0:T(8,128)(2,1)S(1)} collective-permute-done((bf16[48,3072]{1,0:T(8,128)(2,1)S(1)}, bf16[48,3072]{1,0:T(8,128)(2,1)S(1)}, u32[]{:S(2)}, u32[]{:S(2)}) %collective-permute-start.31) | collective-permute-done | bytes 294944 | tf_op jit(solution)/shard_map/ppermute | solution.py:44
  226.1 2.6 %fusion.30 = (bf16[96,3072]{1,0:T(8,128)(2,1)}, f32[96,3072]{1,0:T(8,128)}, f32[96,3072]{1,0:T(8,128)}, f32[96,3072]{1,0:T(8,128)}) fusion(f32[96,3072]{1,0:T(8,128)S(1)} %copy-done.50, f32[]{:T(128)} %bitcast.28, f32[]{:T(128)} %bitcast.27, f32[]{:T(128)} %bitcast.16, bf16[48,3072]{1,0:T(8,128)(2,1)S(1)} %get-tuple-element.143, ...), kind=kLoop, calls=%fused_computation.125 | loop fusion | flops 5603328 | bytes 8257548 | tf_op jit(solution)/shard_map/convert_element_type | solution.py:575
  228.7 9.1 %collective-permute-done.32 = bf16[48,3072]{1,0:T(8,128)(2,1)S(1)} collective-permute-done((bf16[48,3072]{1,0:T(8,128)(2,1)S(1)}, bf16[48,3072]{1,0:T(8,128)(2,1)S(1)}, u32[]{:S(2)}, u32[]{:S(2)}) %collective-permute-start.32) | collective-permute-done | bytes 294944 | tf_op jit(solution)/shard_map/ppermute | solution.py:44
  238.0 2.5 %fusion.27 = (bf16[384,768]{1,0:T(8,128)(2,1)}, f32[384,768]{1,0:T(8,128)}, f32[384,768]{1,0:T(8,128)}, f32[384,768]{1,0:T(8,128)}) fusion(f32[384,768]{1,0:T(8,128)S(1)} %copy-done.53, f32[]{:T(128)} %bitcast.28, f32[]{:T(128)} %bitcast.27, f32[]{:T(128)} %bitcast.16, bf16[192,768]{1,0:T(8,128)(2,1)S(1)} %get-tuple-element.141, ...), kind=kLoop, calls=%fused_computation.124 | loop fusion | flops 5603328 | bytes 8257548 | tf_op jit(solution)/shard_map/convert_element_type | solution.py:575
  240.6 4.2 %collective-permute-done.33 = bf16[48,3072]{1,0:T(8,128)(2,1)S(1)} collective-permute-done((bf16[48,3072]{1,0:T(8,128)(2,1)S(1)}, bf16[48,3072]{1,0:T(8,128)(2,1)S(1)}, u32[]{:S(2)}, u32[]{:S(2)}) %collective-permute-start.33) | collective-permute-done | bytes 294944 | tf_op jit(solution)/shard_map/ppermute | solution.py:44
  (281 shorter events, 76.8 us)
Async XLA Ops:
  24.0 10.3 %collective-permute-start.9 = (bf16[272,768]{1,0:T(8,128)(2,1)S(1)}, bf16[272,768]{1,0:T(8,128)(2,1)}, u32[]{:S(2)}, u32[]{:S(2)}) collective-permute-start(bf16[272,768]{1,0:T(8,128)(2,1)S(1)} %get-tuple-element.68.x_ref.refs_2_), channel_id=1, source_target_pairs={{1,0},{2,1},{3,2},{5,4},{6,5},{7,6},{9,8},{10,9},{11,10},{13,12},{... | collective-permute-start | bytes 1253384 | tf_op jit(solution)/shard_map/ppermute | solution.py:50
  29.3 16.1 %collective-permute-start.8 = (bf16[272,768]{1,0:T(8,128)(2,1)}, bf16[272,768]{1,0:T(8,128)(2,1)S(1)}, u32[]{:S(2)}, u32[]{:S(2)}) collective-permute-start(bf16[272,768]{1,0:T(8,128)(2,1)} %collective-permute-done.7.xa_ref.refs_1_), channel_id=1, source_target_pairs={{0,1},{1,2},{2,3},{4,5},{5,6},{6,7},{8,9},{9,10},{10,11},{12,13},{... | collective-permute-start | bytes 1253384 | tf_op jit(solution)/shard_map/ppermute | solution.py:50
  34.2 11.1 %collective-permute-start.10 = (bf16[272,768]{1,0:T(8,128)(2,1)}, bf16[272,768]{1,0:T(8,128)(2,1)S(1)}, u32[]{:S(2)}, u32[]{:S(2)}) collective-permute-start(bf16[272,768]{1,0:T(8,128)(2,1)} %collective-permute-done.9.xb_ref.refs_3_), channel_id=1, source_target_pairs={{1,0},{2,1},{3,2},{5,4},{6,5},{7,6},{9,8},{10,9},{11,10},{13,12},{... | collective-permute-start | bytes 1253384 | tf_op jit(solution)/shard_map/ppermute | solution.py:50
  75.6 9.0 %collective-permute-start.11 = (bf16[4,384,768]{2,1,0:T(8,128)(2,1)}, bf16[4,384,768]{2,1,0:T(8,128)(2,1)}, u32[]{:S(2)}, u32[]{:S(2)}) collective-permute-start(bf16[4,384,768]{2,1,0:T(8,128)(2,1)} %get-tuple-element.85), channel_id=1, source_target_pairs={{0,4},{4,0},{8,12},{12,8},{16,20},{20,16},{24,28},{28,24},{1,5},{5... | collective-permute-start | bytes 7077896 | tf_op jit(solution)/shard_map/ppermute | solution.py:44
  75.6 11.9 %collective-permute-start.12 = (bf16[384,3072]{1,0:T(8,128)(2,1)}, bf16[384,3072]{1,0:T(8,128)(2,1)}, u32[]{:S(2)}, u32[]{:S(2)}) collective-permute-start(bf16[384,3072]{1,0:T(8,128)(2,1)} %get-tuple-element.87), channel_id=1, source_target_pairs={{0,4},{4,0},{8,12},{12,8},{16,20},{20,16},{24,28},{28,24},{1,5},{5... | collective-permute-start | bytes 7077896 | tf_op jit(solution)/shard_map/ppermute | solution.py:44
  90.2 16.3 %collective-permute-start.13 = (bf16[2,192,768]{2,1,0:T(8,128)(2,1)S(1)}, bf16[2,192,768]{2,1,0:T(8,128)(2,1)S(1)}, u32[]{:S(2)}, u32[]{:S(2)}) collective-permute-start(bf16[2,192,768]{2,1,0:T(8,128)(2,1)S(1)} %slice_bitcast_fusion.11), channel_id=1, source_target_pairs={{0,8},{4,12},{8,0},{12,4},{16,24},{20,28},{24,16},{28,20},{1,9},{5... | collective-permute-start | bytes 1769480 | tf_op jit(solution)/shard_map/ppermute | solution.py:44
  91.5 16.3 %collective-permute-start.14 = (bf16[2,192,768]{2,1,0:T(8,128)(2,1)S(1)}, bf16[2,192,768]{2,1,0:T(8,128)(2,1)S(1)}, u32[]{:S(2)}, u32[]{:S(2)}) collective-permute-start(bf16[2,192,768]{2,1,0:T(8,128)(2,1)S(1)} %slice_bitcast_fusion.10), channel_id=1, source_target_pairs={{0,16},{4,20},{8,24},{12,28},{16,0},{20,4},{24,8},{28,12},{1,17},{... | collective-permute-start | bytes 1769480 | tf_op jit(solution)/shard_map/ppermute | solution.py:44
  92.4 39.2 %collective-permute-start.34 = (bf16[2,48,3072]{2,1,0:T(8,128)(2,1)S(1)}, bf16[2,48,3072]{2,1,0:T(8,128)(2,1)S(1)}, u32[]{:S(2)}, u32[]{:S(2)}) collective-permute-start(bf16[2,48,3072]{2,1,0:T(8,128)(2,1)S(1)} %slice_bitcast_fusion.4), channel_id=1, source_target_pairs={{0,8},{4,12},{8,0},{12,4},{16,24},{20,28},{24,16},{28,20},{1,9},{5... | collective-permute-start | bytes 1769480 | tf_op jit(solution)/shard_map/ppermute | solution.py:44
  94.1 39.4 %collective-permute-start.36 = (bf16[2,48,3072]{2,1,0:T(8,128)(2,1)S(1)}, bf16[2,48,3072]{2,1,0:T(8,128)(2,1)S(1)}, u32[]{:S(2)}, u32[]{:S(2)}) collective-permute-start(bf16[2,48,3072]{2,1,0:T(8,128)(2,1)S(1)} %slice_bitcast_fusion.2), channel_id=1, source_target_pairs={{0,16},{4,20},{8,24},{12,28},{16,0},{20,4},{24,8},{28,12},{1,17},{... | collective-permute-start | bytes 1769480 | tf_op jit(solution)/shard_map/ppermute | solution.py:44
  110.9 33.1 %collective-permute-start.17 = (bf16[256,768]{1,0:T(8,128)(2,1)S(1)}, bf16[256,768]{1,0:T(8,128)(2,1)S(1)}, u32[]{:S(2)}, u32[]{:S(2)}) collective-permute-start(bf16[256,768]{1,0:T(8,128)(2,1)S(1)} %get-tuple-element.138), channel_id=1, source_target_pairs={{1,0},{2,1},{3,2},{5,4},{6,5},{7,6},{9,8},{10,9},{11,10},{13,12},{... | collective-permute-start | bytes 1179656 | tf_op jit(solution)/shard_map/ppermute | solution.py:50
  112.2 31.8 %collective-permute-start.15 = (bf16[256,768]{1,0:T(8,128)(2,1)S(1)}, bf16[256,768]{1,0:T(8,128)(2,1)S(1)}, u32[]{:S(2)}, u32[]{:S(2)}) collective-permute-start(bf16[256,768]{1,0:T(8,128)(2,1)S(1)} %get-tuple-element.139), channel_id=1, source_target_pairs={{0,1},{1,2},{2,3},{4,5},{5,6},{6,7},{8,9},{9,10},{10,11},{12,13},{... | collective-permute-start | bytes 1179656 | tf_op jit(solution)/shard_map/ppermute | solution.py:50
  131.8 10.0 %collective-permute-start.35 = (bf16[48,3072]{1,0:T(8,128)(2,1)S(1)}, bf16[48,3072]{1,0:T(8,128)(2,1)S(1)}, u32[]{:S(2)}, u32[]{:S(2)}) collective-permute-start(bf16[48,3072]{1,0:T(8,128)(2,1)S(1)} %slice_bitcast_fusion.20), channel_id=1, source_target_pairs={{0,16},{4,20},{8,24},{12,28},{16,0},{20,4},{24,8},{28,12},{1,17},{... | collective-permute-start | bytes 884744 | tf_op jit(solution)/shard_map/ppermute | solution.py:44
  133.7 8.0 %collective-permute-start.37 = (bf16[48,3072]{1,0:T(8,128)(2,1)S(1)}, bf16[48,3072]{1,0:T(8,128)(2,1)S(1)}, u32[]{:S(2)}, u32[]{:S(2)}) collective-permute-start(bf16[48,3072]{1,0:T(8,128)(2,1)S(1)} %slice_bitcast_fusion.18), channel_id=1, source_target_pairs={{0,8},{4,12},{8,0},{12,4},{16,24},{20,28},{24,16},{28,20},{1,9},{5... | collective-permute-start | bytes 884744 | tf_op jit(solution)/shard_map/ppermute | solution.py:44
  134.0 19.8 %collective-permute-start.41 = (bf16[192,768]{1,0:T(8,128)(2,1)S(1)}, bf16[192,768]{1,0:T(8,128)(2,1)S(1)}, u32[]{:S(2)}, u32[]{:S(2)}) collective-permute-start(bf16[192,768]{1,0:T(8,128)(2,1)S(1)} %slice_bitcast_fusion.16), channel_id=1, source_target_pairs={{0,16},{4,20},{8,24},{12,28},{16,0},{20,4},{24,8},{28,12},{1,17},{... | collective-permute-start | bytes 884744 | tf_op jit(solution)/shard_map/ppermute | solution.py:44
  141.8 12.1 %collective-permute-start.42 = (bf16[192,768]{1,0:T(8,128)(2,1)S(1)}, bf16[192,768]{1,0:T(8,128)(2,1)S(1)}, u32[]{:S(2)}, u32[]{:S(2)}) collective-permute-start(bf16[192,768]{1,0:T(8,128)(2,1)S(1)} %slice_bitcast_fusion.14), channel_id=1, source_target_pairs={{0,8},{4,12},{8,0},{12,4},{16,24},{20,28},{24,16},{28,20},{1,9},{5... | collective-permute-start | bytes 884744 | tf_op jit(solution)/shard_map/ppermute | solution.py:44
  142.0 17.1 %collective-permute-start.38 = (bf16[48,3072]{1,0:T(8,128)(2,1)S(1)}, bf16[48,3072]{1,0:T(8,128)(2,1)S(1)}, u32[]{:S(2)}, u32[]{:S(2)}) collective-permute-start(bf16[48,3072]{1,0:T(8,128)(2,1)S(1)} %broadcast_select_fusion.5), channel_id=1, source_target_pairs={{0,1},{1,0},{2,3},{3,2},{4,5},{5,4},{6,7},{7,6},{8,9},{9,8},{10,11... | collective-permute-start | bytes 884744 | tf_op jit(solution)/shard_map/ppermute | solution.py:44
  144.3 13.6 %collective-permute-start.16 = (bf16[256,768]{1,0:T(8,128)(2,1)S(1)}, bf16[256,768]{1,0:T(8,128)(2,1)S(1)}, u32[]{:S(2)}, u32[]{:S(2)}) collective-permute-start(bf16[256,768]{1,0:T(8,128)(2,1)S(1)} %get-tuple-element.137), channel_id=1, source_target_pairs={{0,1},{1,2},{2,3},{4,5},{5,6},{6,7},{8,9},{9,10},{10,11},{12,13},{... | collective-permute-start | bytes 1179656 | tf_op jit(solution)/shard_map/ppermute | solution.py:50
  146.4 11.5 %collective-permute-start.18 = (bf16[256,768]{1,0:T(8,128)(2,1)S(1)}, bf16[256,768]{1,0:T(8,128)(2,1)S(1)}, u32[]{:S(2)}, u32[]{:S(2)}) collective-permute-start(bf16[256,768]{1,0:T(8,128)(2,1)S(1)} %get-tuple-element.136), channel_id=1, source_target_pairs={{1,0},{2,1},{3,2},{5,4},{6,5},{7,6},{9,8},{10,9},{11,10},{13,12},{... | collective-permute-start | bytes 1179656 | tf_op jit(solution)/shard_map/ppermute | solution.py:50
  153.8 40.4 %collective-permute-start.26 = (bf16[384,3072]{1,0:T(8,128)(2,1)S(1)}, bf16[384,3072]{1,0:T(8,128)(2,1)S(1)}, u32[]{:S(2)}, u32[]{:S(2)}) collective-permute-start(bf16[384,3072]{1,0:T(8,128)(2,1)S(1)} %get-tuple-element.108), channel_id=1, source_target_pairs={{0,4},{4,0},{8,12},{12,8},{16,20},{20,16},{24,28},{28,24},{1,5},{5... | collective-permute-start | bytes 7077896 | tf_op jit(solution)/shard_map/ppermute | solution.py:44
  154.0 13.6 %collective-permute-start.43 = (bf16[192,768]{1,0:T(8,128)(2,1)S(1)}, bf16[192,768]{1,0:T(8,128)(2,1)S(1)}, u32[]{:S(2)}, u32[]{:S(2)}) collective-permute-start(bf16[192,768]{1,0:T(8,128)(2,1)S(1)} %broadcast_select_fusion.2), channel_id=1, source_target_pairs={{0,1},{1,0},{2,3},{3,2},{4,5},{5,4},{6,7},{7,6},{8,9},{9,8},{10,11... | collective-permute-start | bytes 884744 | tf_op jit(solution)/shard_map/ppermute | solution.py:44
  159.2 25.6 %collective-permute-start.39 = (bf16[48,3072]{1,0:T(8,128)(2,1)S(1)}, bf16[48,3072]{1,0:T(8,128)(2,1)S(1)}, u32[]{:S(2)}, u32[]{:S(2)}) collective-permute-start(bf16[48,3072]{1,0:T(8,128)(2,1)S(1)} %add_convert_fusion.6), channel_id=1, source_target_pairs={{0,2},{1,3},{2,0},{3,1},{4,6},{5,7},{6,4},{7,5},{8,10},{9,11},{10,... | collective-permute-start | bytes 884744 | tf_op jit(solution)/shard_map/ppermute | solution.py:44
  160.1 9.8 %collective-permute-start.21 = (f32[16,768]{1,0:T(8,128)S(1)}, f32[16,768]{1,0:T(8,128)S(1)}, u32[]{:S(2)}, u32[]{:S(2)}) collective-permute-start(f32[16,768]{1,0:T(8,128)S(1)} %add.236), channel_id=1, source_target_pairs={{0,16},{4,20},{8,24},{12,28},{16,0},{20,4},{24,8},{28,12},{1,17},{... | collective-permute-start | bytes 147464 | tf_op jit(solution)/shard_map/ppermute | solution.py:44
  161.6 11.2 %collective-permute-start.22 = (f32[16,768]{1,0:T(8,128)S(1)}, f32[16,768]{1,0:T(8,128)S(1)}, u32[]{:S(2)}, u32[]{:S(2)}) collective-permute-start(f32[16,768]{1,0:T(8,128)S(1)} %add.236), channel_id=1, source_target_pairs={{0,24},{4,28},{8,16},{12,20},{16,8},{20,12},{24,0},{28,4},{1,25},{... | collective-permute-start | bytes 147464 | tf_op jit(solution)/shard_map/ppermute | solution.py:44
  169.9 21.3 %collective-permute-start.44 = (bf16[192,768]{1,0:T(8,128)(2,1)S(1)}, bf16[192,768]{1,0:T(8,128)(2,1)S(1)}, u32[]{:S(2)}, u32[]{:S(2)}) collective-permute-start(bf16[192,768]{1,0:T(8,128)(2,1)S(1)} %add_convert_fusion.4), channel_id=1, source_target_pairs={{0,2},{1,3},{2,0},{3,1},{4,6},{5,7},{6,4},{7,5},{8,10},{9,11},{10,... | collective-permute-start | bytes 884744 | tf_op jit(solution)/shard_map/ppermute | solution.py:44
  172.9 19.3 %collective-permute-start.24 = (f32[16,768]{1,0:T(8,128)S(1)}, f32[16,768]{1,0:T(8,128)S(1)}, u32[]{:S(2)}, u32[]{:S(2)}) collective-permute-start(f32[16,768]{1,0:T(8,128)S(1)} %add_add_fusion.1), channel_id=1, source_target_pairs={{0,2},{1,3},{2,0},{3,1},{4,6},{5,7},{6,4},{7,5},{8,10},{9,11},{10,... | collective-permute-start | bytes 147464 | tf_op jit(solution)/shard_map/ppermute | solution.py:44
  174.7 18.7 %collective-permute-start.25 = (f32[16,768]{1,0:T(8,128)S(1)}, f32[16,768]{1,0:T(8,128)S(1)}, u32[]{:S(2)}, u32[]{:S(2)}) collective-permute-start(f32[16,768]{1,0:T(8,128)S(1)} %add_add_fusion.1), channel_id=1, source_target_pairs={{0,3},{1,2},{2,1},{3,0},{4,7},{5,6},{6,5},{7,4},{8,11},{9,10},{10,... | collective-permute-start | bytes 147464 | tf_op jit(solution)/shard_map/ppermute | solution.py:44
  184.8 8.5 %collective-permute-start.23 = (f32[16,768]{1,0:T(8,128)S(1)}, f32[16,768]{1,0:T(8,128)S(1)}, u32[]{:S(2)}, u32[]{:S(2)}) collective-permute-start(f32[16,768]{1,0:T(8,128)S(1)} %add_add_fusion.1), channel_id=1, source_target_pairs={{0,1},{1,0},{2,3},{3,2},{4,5},{5,4},{6,7},{7,6},{8,9},{9,8},{10,11... | collective-permute-start | bytes 147464 | tf_op jit(solution)/shard_map/ppermute | solution.py:44
  191.2 28.4 %collective-permute-start.40 = (bf16[48,3072]{1,0:T(8,128)(2,1)S(1)}, bf16[48,3072]{1,0:T(8,128)(2,1)S(1)}, u32[]{:S(2)}, u32[]{:S(2)}) collective-permute-start(bf16[48,3072]{1,0:T(8,128)(2,1)S(1)} %add_convert_fusion.5), channel_id=1, source_target_pairs={{0,1},{1,0},{2,3},{3,2},{4,5},{5,4},{6,7},{7,6},{8,9},{9,8},{10,11... | collective-permute-start | bytes 884744 | tf_op jit(solution)/shard_map/ppermute | solution.py:44
  192.2 36.5 %collective-permute-start.45 = (bf16[192,768]{1,0:T(8,128)(2,1)S(1)}, bf16[192,768]{1,0:T(8,128)(2,1)S(1)}, u32[]{:S(2)}, u32[]{:S(2)}) collective-permute-start(bf16[192,768]{1,0:T(8,128)(2,1)S(1)} %add_convert_fusion.3), channel_id=1, source_target_pairs={{0,1},{1,0},{2,3},{3,2},{4,5},{5,4},{6,7},{7,6},{8,9},{9,8},{10,11... | collective-permute-start | bytes 884744 | tf_op jit(solution)/shard_map/ppermute | solution.py:44
  195.2 14.8 %collective-permute-start.27 = (bf16[2,48,3072]{2,1,0:T(8,128)(2,1)S(1)}, bf16[2,48,3072]{2,1,0:T(8,128)(2,1)S(1)}, u32[]{:S(2)}, u32[]{:S(2)}) collective-permute-start(bf16[2,48,3072]{2,1,0:T(8,128)(2,1)S(1)} %slice_bitcast_fusion.8), channel_id=1, source_target_pairs={{0,8},{4,12},{8,0},{12,4},{16,24},{20,28},{24,16},{28,20},{1,9},{5... | collective-permute-start | bytes 1769480 | tf_op jit(solution)/shard_map/ppermute | solution.py:44
  197.3 14.4 %collective-permute-start.29 = (bf16[2,48,3072]{2,1,0:T(8,128)(2,1)S(1)}, bf16[2,48,3072]{2,1,0:T(8,128)(2,1)S(1)}, u32[]{:S(2)}, u32[]{:S(2)}) collective-permute-start(bf16[2,48,3072]{2,1,0:T(8,128)(2,1)S(1)} %slice_bitcast_fusion.6), channel_id=1, source_target_pairs={{0,16},{4,20},{8,24},{12,28},{16,0},{20,4},{24,8},{28,12},{1,17},{... | collective-permute-start | bytes 1769480 | tf_op jit(solution)/shard_map/ppermute | solution.py:44
  226.0 11.8 %collective-permute-start.32 = (bf16[48,3072]{1,0:T(8,128)(2,1)S(1)}, bf16[48,3072]{1,0:T(8,128)(2,1)S(1)}, u32[]{:S(2)}, u32[]{:S(2)}) collective-permute-start(bf16[48,3072]{1,0:T(8,128)(2,1)S(1)} %add_convert_fusion.8), channel_id=1, source_target_pairs={{0,2},{1,3},{2,0},{3,1},{4,6},{5,7},{6,4},{7,5},{8,10},{9,11},{10,... | collective-permute-start | bytes 884744 | tf_op jit(solution)/shard_map/ppermute | solution.py:44
  (87 other events, 565.9 us)

commit v3 on v1

v3 whole, which is shorter than its diff:
```python
import functools

import jax
import jax.numpy as jnp
from jax import lax
from jax.experimental import pallas as pl
from jax.experimental.pallas import tpu as pltpu
from jax.sharding import PartitionSpec as P

HEADS = 12
HEAD_WIDTH = 64
GROUP = 4

ln_epsilon = 1e-05
stat_epsilon = 1e-06
beta_one = 0.5
beta_two = 0.6
rate_matrix = 0.04
rate_vector = 0.8
warmup_length = 20.0
decay_matrix = 0.05
adam_epsilon = 1e-08
score_scale = 0.125
masked_score = -1e30

f32 = jnp.float32
bf16 = jnp.bfloat16


def nn(a, b):
    return lax.dot_general(a, b, (((1,), (0,)), ((), ())), preferred_element_type=f32)


def nt(a, b):
    return lax.dot_general(a, b, (((1,), (1,)), ((), ())), preferred_element_type=f32)


def tn(a, b):
    return lax.dot_general(a, b, (((0,), (0,)), ((), ())), preferred_element_type=f32)


def flipped(block, axis, bit):
    size = lax.axis_size(axis)
    return lax.ppermute(block, axis, [(i, i ^ bit) for i in range(size)])


def moved(block, axis, distance):
    size = lax.axis_size(axis)
    route = [(i, i + distance) for i in range(size) if 0 <= i + distance < size]
    return lax.ppermute(block, axis, route)


def bits_of(axis):
    size = lax.axis_size(axis)
    return [1 << i for i in range(size.bit_length() - 1)]


class SmallSum:
    def __init__(self, block, paired=True):
        self.block, self.rounds = block, []
        for axis in ("dp", "blk"):
            bits = bits_of(axis)
            odd = len(bits) % 2 if paired else len(bits)
            if not paired:
                self.rounds += [(axis, [bit]) for bit in bits]
                continue
            parts = [bits[:odd]] * odd + [bits[i : i + 2] for i in range(odd, len(bits), 2)]
            self.rounds += [(axis, part) for part in parts]

    def left(self):
        return len(self.rounds)

    def send(self):
        axis, part = self.rounds.pop(0)
        ways = part if len(part) == 1 else [part[0], part[1], part[0] | part[1]]
        self.arrived = [flipped(self.block, axis, way) for way in ways]

    def take(self, tie=lambda *values: values):
        others = tie(*self.arrived)
        if len(others) == 1:
            self.block = self.block + others[0]
        else:
            self.block = (self.block + others[0]) + (others[1] + others[2])


def added(kept, arrived):
    return (kept.astype(f32) + arrived.astype(f32)).astype(bf16)


def summed(addends):
    total = addends[0].astype(f32)
    for addend in addends[1:]:
        total = total + addend.astype(f32)
    return total.astype(bf16)


class Scatter:
    def __init__(self, addends, order):
        self.addends, self.order = list(addends), list(order)

    def prepare(self):
        self.sent = summed([addend[1] for addend in self.addends])

    def send(self):
        self.arrived = flipped(self.sent, "dp", self.order.pop(0))

    def take(self):
        self.addends = [addend[0] for addend in self.addends] + [self.arrived]


class Line:
    def __init__(self, first, second, lows):
        self.bits, self.lows = bits_of("blk"), lows
        first, second = summed(first.addends), summed(second.addends)
        self.keep = jnp.where(lows[0], first, second)
        self.sent = jnp.where(lows[0], second, first)

    def scatter(self):
        self.arrived = flipped(self.sent, "blk", 1)

    def exchange(self):
        share = added(self.keep, self.arrived)
        for bit, low in zip(self.bits[1:-1], self.lows[1:]):
            middle = share.shape[0] // 2
            keep = jnp.where(low, share[:middle], share[middle:])
            sent = jnp.where(low, share[middle:], share[:middle])
            share = added(keep, flipped(sent, "blk", bit))
        self.keep = share
        self.arrived = flipped(share, "blk", self.bits[-1])

    def joined(self, low):
        mine, other = self.keep, self.arrived
        return jnp.concatenate(
            [jnp.where(low, mine, other), jnp.where(low, other, mine)], axis=0
        )

    def gather(self):
        share = added(self.keep, self.arrived)
        for bit, low in reversed(list(zip(self.bits[1:-1], self.lows[1:]))):
            self.keep, self.arrived = share, flipped(share, "blk", bit)
            share = self.joined(low)
        self.keep = share
        self.arrived = flipped(share, "blk", 1)

    def result(self):
        return self.joined(self.lows[0])


def together(*values):
    return lax.optimization_barrier(values)


def whole(shape):
    return pl.BlockSpec(shape, lambda *a: (0,) * len(shape))


def call(kernel, name, table, operands, outs, scratch=(), mib=8):
    scalar = pl.BlockSpec(memory_space=pltpu.SMEM)
    return pl.pallas_call(
        kernel,
        grid_spec=pltpu.PrefetchScalarGridSpec(
            num_scalar_prefetch=1,
            grid=(1,),
            in_specs=[
                spec if isinstance(spec, pl.BlockSpec) else whole(spec.shape)
                for spec in (o[0] if isinstance(o, tuple) else o for o in operands)
            ],
            out_specs=[scalar if o.shape == (2,) else whole(o.shape) for o in outs],
            scratch_shapes=list(scratch),
        ),
        out_shape=outs,
        cost_estimate=pl.CostEstimate(flops=1 << 20, bytes_accessed=1 << 16, transcendentals=0),
        compiler_params=pltpu.CompilerParams(vmem_limit_bytes=mib << 20),
        name=name,
    )(table, *[o[1] if isinstance(o, tuple) else o for o in operands])


def struct(shape, dtype):
    return jax.ShapeDtypeStruct(shape, dtype)


def unit_rows(rows):
    centred = rows - jnp.mean(rows, axis=-1, keepdims=True)
    scale = lax.rsqrt(jnp.mean(centred * centred, axis=-1, keepdims=True) + ln_epsilon)
    return centred * scale, scale


def norm_back(grad, unit, scale, gain):
    inner = grad * gain
    return scale * (
        inner
        - jnp.mean(inner, axis=-1, keepdims=True)
        - unit * jnp.mean(inner * unit, axis=-1, keepdims=True)
    )


def column_sum(rows):
    return jnp.sum(rows, axis=0, keepdims=True)


def totals_kernel(table, raw_ref, out_ref):
    raw = raw_ref[...]
    out_ref[0:1, :] = column_sum(raw)
    out_ref[1:2, :] = column_sum(raw * raw)


def enter_kernel(total_tokens, table, raw_ref, sum_ref, vec_ref, id_ref, x_ref, mean_ref, std_ref):
    width = raw_ref.shape[0]
    mean = sum_ref[0:1, :] / total_tokens
    variance = sum_ref[1:2, :] / total_tokens - mean * mean
    inverse = lax.rsqrt(variance + stat_epsilon)
    mean_ref[...] = mean
    std_ref[...] = inverse
    unit, _ = unit_rows((raw_ref[...] - mean) * inverse)
    x_ref[0:width, :] = (unit * vec_ref[0:1, :] + vec_ref[1:2, :]).astype(bf16)
    x_ref[width:, :] = jnp.zeros((x_ref.shape[0] - width, x_ref.shape[1]), bf16)
    ids = jnp.broadcast_to(id_ref[...], (16, width)).astype(f32).astype(bf16)
    x_ref[width:, 0:width] = ids


def id_columns(x_ref, width):
    rows = jnp.broadcast_to(x_ref[width : width + 8, 0:width].astype(f32)[0:1], (128, width))
    return rows.T


def project_own_kernel(table, x_ref, w_ref, vec_ref, q_ref, kv_ref, id_ref):
    width = q_ref.shape[0]
    features = q_ref.shape[1]
    slot = kv_ref.shape[0] // 2
    x = x_ref[0:width, :]
    q_ref[...] = ((nn(x, w_ref[:, :features]) + vec_ref[4:5, :]) * score_scale).astype(bf16)
    kv_ref[slot, :, :features] = nn(x, w_ref[:, features : 2 * features]).astype(bf16)
    kv_ref[slot, :, features:] = (nn(x, w_ref[:, 2 * features :]) + vec_ref[5:6, :]).astype(bf16)
    id_ref[slot] = id_columns(x_ref, width)


def project_pair_kernel(d, inside_at, table, xa_ref, xb_ref, x_ref, w_ref, vec_ref, kv_in, id_in, kv_ref, id_ref):
    width = kv_ref.shape[1]
    features = kv_ref.shape[2] // 2
    reach = kv_ref.shape[0] // 2
    done = slice(reach - d + 1, reach + d)
    kv_ref[done] = kv_in[done]
    id_ref[done] = id_in[done]
    own = x_ref[width : width + 8, 0:width].astype(f32)[0:1]
    low, high = jnp.min(own), jnp.max(own)
    for slot, inside, ref in ((reach - d, 0, xa_ref), (reach + d, 1, xb_ref)):
        ids = ref[width : width + 8, 0:width].astype(f32)[0:1]
        near = (table[inside_at + inside] > 0) & (jnp.max(ids) >= low) & (jnp.min(ids) <= high)
        id_ref[slot] = jnp.full((width, 128), -1.0, f32)

        @pl.when(near)
        def _(ref=ref, slot=slot):
            x = ref[0:width, :]
            kv_ref[slot, :, :features] = nn(x, w_ref[:, features : 2 * features]).astype(bf16)
            kv_ref[slot, :, features:] = (
                nn(x, w_ref[:, 2 * features :]) + vec_ref[5:6, :]
            ).astype(bf16)
            id_ref[slot] = id_columns(ref, width)


def lane_half(rows, which):
    lanes = lax.broadcasted_iota(jnp.int32, (rows, 128), 1)
    return (lanes >= 64) if which else (lanes < 64)


def mask_rows(own_row, width):
    ids = lax.broadcasted_iota(jnp.int32, (64, width), 0).astype(f32)
    return jnp.where(ids == own_row, 0.0, masked_score).astype(bf16)


def key_marks(column, width):
    lane_ids = (lax.broadcasted_iota(jnp.int32, (width, 128), 1) % 64).astype(f32)
    return (column == lane_ids).astype(f32).astype(bf16)


def lane_group(g):
    return pl.ds(pl.multiple_of(g * GROUP * HEAD_WIDTH, 128), GROUP * HEAD_WIDTH)


def attend_kernel(reach, table, q_ref, kv_ref, qid_ref, kid_ref, o_ref, lse_ref, bound_ref, acc, top, qm, sc):
    width, features = q_ref.shape
    slots = kv_ref.shape[0]
    steps = features // (GROUP * HEAD_WIDTH)
    low = kid_ref[reach, 0:1, :]
    high = kid_ref[reach, width - 1 : width, :]
    start = jnp.full_like(low, float(reach))
    end = jnp.full_like(low, float(reach))
    for s in range(slots):
        active = (kid_ref[s, width - 1 : width, :] >= low) & (kid_ref[s, 0:1, :] <= high)
        start = jnp.where(active, jnp.minimum(start, float(s)), start)
        end = jnp.where(active, jnp.maximum(end, float(s)), end)
    bound_ref[0] = jnp.min(start).astype(jnp.int32)
    bound_ref[1] = jnp.max(end).astype(jnp.int32) + 1
    barred = mask_rows(qid_ref[...].astype(f32), width)
    upper = lane_half(width, 1)
    one_rows = (lax.broadcasted_iota(jnp.int32, (16, width), 0) == 0).astype(f32).astype(bf16)

    def group(g, carry):
        lanes_g = lane_group(g)
        lanes_v = pl.ds(pl.multiple_of(features + g * GROUP * HEAD_WIDTH, 128), GROUP * HEAD_WIDTH)
        top[...] = jnp.full_like(top, masked_score)
        acc[...] = jnp.zeros_like(acc)
        q_t = q_ref[:, lanes_g].T
        for h in range(GROUP):
            head = q_t[64 * h : 64 * h + 64, :]
            qm[h, 0:64, :] = barred if h % 2 else head
            qm[h, 64:128, :] = head if h % 2 else barred

        def step(s, carry):
            keys = kv_ref[s, :, lanes_g]
            values_t = kv_ref[s, :, lanes_v].T
            marks = key_marks(kid_ref[s], width)
            for h in range(GROUP):
                lanes = slice(128 * (h // 2), 128 * (h // 2) + 128)
                pair = keys[:, lanes]
                marked = jnp.where(upper, pair, marks) if h % 2 else jnp.where(upper, marks, pair)
                sc[h] = nn(marked, qm[h])
            for h in range(GROUP):
                score = sc[h]
                old = top[h : h + 1, :]
                new = jnp.maximum(old, jnp.max(score, axis=0, keepdims=True))
                fade = jnp.exp(old - new)
                weight = jnp.exp(score - new).astype(bf16)
                top[h : h + 1, :] = new
                rows = slice(80 * h, 80 * h + 80)
                left = jnp.concatenate([values_t[64 * h : 64 * h + 64, :], one_rows], axis=0)
                acc[rows, :] = acc[rows, :] * fade + nn(left, weight)
            return carry

        lax.fori_loop(bound_ref[0], bound_ref[1], step, 0)
        outs, lses = [], []
        for h in range(GROUP):
            total = acc[80 * h + 64 : 80 * h + 65, :]
            outs.append(acc[80 * h : 80 * h + 64, :] / total)
            lses.append(top[h : h + 1, :] + jnp.log(total))
        o_ref[:, lanes_g] = jnp.concatenate(outs, axis=0).T.astype(bf16)
        lse_ref[g] = jnp.concatenate(lses, axis=0)
        return carry

    lax.fori_loop(0, steps, group, 0)


def spread_rows(table, plain, target, lanes, half):
    part = plain.shape[0] // (4 * half)
    for side in range(2):
        for h in range(2):
            for p in range(half):
                owner = table[half * (1 + 2 * h + side) + p]
                place = pl.multiple_of((2 * owner + h) * part, 8)
                to = ((side * 2 + h) * half + p) * part
                target[to : to + part, lanes] = plain[pl.ds(place, part), :].astype(bf16)


def ffn_kernel(
    half,
    table,
    o_ref,
    wo_ref,
    raw_ref,
    mean_ref,
    std_ref,
    vec_ref,
    cot_ref,
    w1_ref,
    w2_ref,
    out_ref,
    gm_ref,
    ga_ref,
    sk_ref,
    ss_ref,
    ek_ref,
    es_ref,
    row_ref,
    middle_s,
    gsec,
    s2,
    s2t,
    ot,
    plain,
    rows_s,
    acc,
):
    features = gm_ref.shape[1]
    inner = w1_ref.shape[1]
    chunk = inner // half
    wide = chunk // 2
    normed = (raw_ref[...] - mean_ref[...]) * std_ref[...]
    middle = normed + nn(o_ref[...], wo_ref[...]) + vec_ref[6:7, :]
    middle_s[...] = middle
    unit, _ = unit_rows(middle)
    second = unit * vec_ref[2:3, :] + vec_ref[3:4, :]
    s2[...] = second.astype(bf16)
    plain[...] = second.T
    spread_rows(table, plain, s2t, slice(None), half)
    plain[...] = o_ref[...].T.astype(f32)
    spread_rows(table, plain, ot, slice(None), half)
    acc[...] = jnp.zeros_like(acc)
    gsec[...] = jnp.zeros_like(gsec)
    own = table[half] % 2

    def step(i, carry):
        place = table[i] * chunk
        lanes = pl.ds(pl.multiple_of(place, 128), chunk)
        row = pl.ds(8 + place // features, 1)
        row_lanes = pl.ds(pl.multiple_of(place % features, 128), chunk)
        w1 = w1_ref[:, lanes]
        w2 = w2_ref[lanes, :]
        pre = nn(s2[...], w1) + vec_ref[row, row_lanes]
        back = nt(cot_ref[...], w2)
        area = 0.5 * (1.0 + lax.erf(pre * (0.5**0.5)))
        bell = jnp.exp(-0.5 * pre * pre) * (1.0 / (2.0 * jnp.pi) ** 0.5)
        hidden = (pre * area).astype(bf16)
        grad = ((area + pre * bell) * back).astype(bf16)
        acc[...] += nn(hidden, w2)
        gsec[...] += nt(grad, w1)
        row_ref[row, row_lanes] = column_sum(grad.astype(f32))
        rows_s[...] = nn(hidden.T, cot_ref[...]).astype(bf16)
        for side, ref in ((0, sk_ref), (1, ss_ref)):
            first = jnp.where(own == side, 0, wide)
            for h, at in ((0, i), (1, table[5 * half + i])):
                start = pl.multiple_of(first + h * (wide // 2), 16)
                ref[h, at] = rows_s[pl.ds(start, wide // 2), :]
        ek_ref[:, lanes] = nn(s2t[: features // 2, :], grad).astype(bf16)
        es_ref[:, lanes] = nn(s2t[features // 2 :, :], grad).astype(bf16)
        return carry

    lax.fori_loop(0, half, step, 0)
    out_ref[...] = (middle_s[...] + acc[...] + vec_ref[7:8, :]).astype(bf16)
    unit, scale = unit_rows(middle_s[...])
    grad = gsec[...]
    cot = cot_ref[...].astype(f32)
    row_ref[0:1, :] = column_sum(grad * unit)
    row_ref[1:2, :] = column_sum(grad)
    grad_middle = cot + norm_back(grad, unit, scale, vec_ref[2:3, :])
    gm_ref[...] = grad_middle
    branch = grad_middle.astype(bf16)
    row_ref[2:3, :] = column_sum(branch.astype(f32))
    row_ref[3:4, :] = column_sum(cot)
    ga_ref[...] = nt(branch, wo_ref[...]).astype(bf16)
    ek_ref[:, inner:] = nn(ot[: features // 2, :], branch).astype(bf16)
    es_ref[:, inner:] = nn(ot[features // 2 :, :], branch).astype(bf16)


def attend_back_kernel(
    g,
    bounds,
    q_ref,
    kv_ref,
    o_ref,
    g_ref,
    lse_ref,
    qid_ref,
    kid_ref,
    dq_ref,
    dk_ref,
    dv_ref,
    row_ref,
    acc,
    qm,
    gm,
    q_stack,
    g_stack,
    sc,
    dp,
    p_wide,
    g_wide,
    rows_s,
):
    width, features = q_ref.shape
    slots = kv_ref.shape[0]
    barred = mask_rows(qid_ref[...].astype(f32), width)
    nothing = jnp.zeros((64, width), bf16)
    upper = lane_half(width, 1)

    def blank(s, carry):
        dk_ref[s] = jnp.zeros(dk_ref.shape[1:], dk_ref.dtype)
        dv_ref[s] = jnp.zeros(dv_ref.shape[1:], dv_ref.dtype)
        return carry

    lax.fori_loop(0, bounds[0], blank, 0)
    lax.fori_loop(bounds[1], slots, blank, 0)

    base = g * GROUP * HEAD_WIDTH
    lanes_g = slice(base, base + GROUP * HEAD_WIDTH)
    lanes_v = slice(features + base, features + base + GROUP * HEAD_WIDTH)
    acc[...] = jnp.zeros_like(acc)
    q_all, g_all = q_ref[:, lanes_g], g_ref[:, lanes_g]
    product = (g_all.astype(f32) * o_ref[:, lanes_g].astype(f32)).T
    q_t, g_t = q_all.T, g_all.T
    for h in range(GROUP):
        lanes = slice(128 * (h // 2), 128 * (h // 2) + 128)
        rows = slice(64 * h, 64 * h + 64)
        odd = h % 2
        qm[h, 0:64, :] = barred if odd else q_t[rows, :]
        qm[h, 64:128, :] = q_t[rows, :] if odd else barred
        gm[h, 0:64, :] = nothing if odd else g_t[rows, :]
        gm[h, 64:128, :] = g_t[rows, :] if odd else nothing
        half = lane_half(width, odd)
        place = slice(width * odd, width * odd + width)
        pair = q_all[:, lanes]
        q_stack[h // 2, place, :] = jnp.where(half, pair, jnp.zeros_like(pair))
        pair = g_all[:, lanes]
        g_stack[h // 2, place, :] = jnp.where(half, pair, jnp.zeros_like(pair))
        rows_s[h : h + 1, :] = column_sum(product[rows, :])
    rows_s[8:9, :] = jnp.zeros((1, GROUP * HEAD_WIDTH), f32)

    def step(s, carry):
        keys = kv_ref[s, :, lanes_g]
        values = kv_ref[s, :, lanes_v]
        keys_t = keys.T
        marks = key_marks(kid_ref[s], width)
        for h in range(GROUP):
            lanes = slice(128 * (h // 2), 128 * (h // 2) + 128)
            pair = keys[:, lanes]
            marked = jnp.where(upper, pair, marks) if h % 2 else jnp.where(upper, marks, pair)
            sc[h] = nn(marked, qm[h])
            dp[h] = nn(values[:, lanes], gm[h])
        for h in range(GROUP):
            place = slice(width * (h % 2), width * (h % 2) + width)
            prob = jnp.exp(sc[h] - lse_ref[g, h : h + 1, :])
            p_wide[h // 2, :, place] = prob.astype(bf16)
            g_wide[h // 2, :, place] = (prob * (dp[h] - rows_s[h : h + 1, :])).astype(bf16)
        for h in range(GROUP):
            place = slice(width * (h % 2), width * (h % 2) + width)
            rows = slice(64 * h, 64 * h + 64)
            acc[rows, :] += nn(keys_t[rows, :], g_wide[h // 2, :, place])
        key_parts, value_parts = [], []
        for j in range(GROUP // 2):
            value_parts.append(nn(p_wide[j], g_stack[j]))
            key_parts.append(nn(g_wide[j], q_stack[j]))
        value_all = jnp.concatenate(value_parts, axis=1)
        dk_ref[s] = jnp.concatenate(key_parts, axis=1).astype(bf16)
        dv_ref[s] = value_all.astype(bf16)
        rows_s[8:9, :] += column_sum(value_all)
        return carry

    lax.fori_loop(bounds[0], bounds[1], step, 0)
    dq = (acc[...].T.astype(bf16).astype(f32) * score_scale).astype(bf16)
    dq_ref[...] = dq
    row_ref[0:1, :] = column_sum(dq.astype(f32))
    row_ref[1:2, :] = rows_s[8:9, :]


def parts_kernel(reach, bounds, *refs):
    groups = (len(refs) - 3) // 3
    dqs, dks, dvs = (refs[k * groups : (k + 1) * groups] for k in range(3))
    w_ref, p_ref, own_ref = refs[3 * groups :]
    features = p_ref.shape[2]
    size = features // groups

    def part(s):
        total = None
        for g in range(groups):
            for ref, base in ((dks[g], features), (dvs[g], 2 * features)):
                now = nt(ref[s], w_ref[:, base + g * size : base + (g + 1) * size])
                total = now if total is None else total + now
        return total

    def one(s, to):
        active = (s >= bounds[0]) & (s < bounds[1])

        @pl.when(active)
        def _():
            p_ref[to] = part(s).astype(bf16)

        @pl.when(jnp.logical_not(active))
        def _():
            p_ref[to] = jnp.zeros(p_ref.shape[1:], p_ref.dtype)

    def some(i, carry):
        one(jnp.where(i < reach, i, i + 1), i)
        return carry

    lax.fori_loop(0, 2 * reach, some, 0)
    total = part(reach)
    for g in range(groups):
        total = total + nt(dqs[g][...], w_ref[:, g * size : (g + 1) * size])
    own_ref[...] = total


def weight_kernel(reach, half, groups, table, *refs):
    slots = 2 * reach + 1
    xs, bounds = refs[:slots], refs[slots]
    refs = refs[slots + 1 :]
    dqs, dks, dvs = (refs[k * groups : (k + 1) * groups] for k in range(3))
    keep_ref, send_ref, xt, plain = refs[3 * groups :]
    width, size = dqs[0].shape
    features = size * groups
    few = min(3, slots)
    small = bounds[1] - bounds[0] <= few
    start = jnp.minimum(bounds[0], slots - few)

    for s in range(slots):

        @pl.when(jnp.logical_not(small) | ((s >= start) & (s < start + few)))
        def _(s=s):
            plain[...] = xs[s][0:width, :].T.astype(f32)
            spread_rows(table, plain, xt, slice(width * s, width * s + width), half)

    def put(tokens, right, base):
        lanes = slice(base, base + size)
        keep_ref[:, lanes] = nn(xt[: features // 2, tokens], right).astype(bf16)
        send_ref[:, lanes] = nn(xt[features // 2 :, tokens], right).astype(bf16)

    for g in range(groups):
        put(slice(width * reach, width * reach + width), dqs[g][...], g * size)

    def over(start, count):
        tokens = pl.ds(pl.multiple_of(start * width, 128), count * width)
        for base, group in ((features, dks), (2 * features, dvs)):
            for g in range(groups):
                rows = group[g][pl.ds(start, count)].reshape(count * width, size)
                put(tokens, rows, base + g * size)

    @pl.when(small)
    def _():
        over(start, few)

    @pl.when(jnp.logical_not(small))
    def _():
        over(0, slots)


def leave_kernel(
    table,
    raw_ref,
    mean_ref,
    std_ref,
    vec_ref,
    gm_ref,
    own_ref,
    left_ref,
    right_ref,
    ffn_rows,
    *refs,
):
    attend_rows, (gn_ref, row_ref) = refs[:-2], refs[-2:]
    features = raw_ref.shape[1]
    centred = raw_ref[...] - mean_ref[...]
    unit, scale = unit_rows(centred * std_ref[...])
    grad = own_ref[...] + left_ref[...].astype(f32) + right_ref[...].astype(f32)
    row_ref[0:1, :] = column_sum(grad * unit)
    row_ref[1:2, :] = column_sum(grad)
    row_ref[2:4, :] = ffn_rows[0:2, :]
    size = features // len(attend_rows)
    for g, ref in enumerate(attend_rows):
        row_ref[4:6, g * size : (g + 1) * size] = ref[...]
    row_ref[6:8, :] = ffn_rows[2:4, :]
    row_ref[8:12, :] = ffn_rows[8:12, :]
    whole_grad = gm_ref[...] + norm_back(grad, unit, scale, vec_ref[0:1, :])
    gn_ref[...] = whole_grad
    row_ref[12:13, :] = column_sum(whole_grad)
    row_ref[13:14, :] = column_sum(whole_grad * centred)
    row_ref[14:16, :] = jnp.zeros((2, features), f32)


def adam_rule(master, moment, square, gradient, step_value, step_rate, weight_decay):
    moment_new = beta_one * moment + (1.0 - beta_one) * gradient
    square_new = beta_two * square + (1.0 - beta_two) * gradient * gradient
    fix_first = 1.0 - jnp.power(beta_one, step_value)
    fix_second = 1.0 - jnp.power(beta_two, step_value)
    planned = step_rate * jnp.minimum(1.0, step_value / warmup_length)
    direction = moment_new / fix_first / (jnp.sqrt(square_new / fix_second) + adam_epsilon)
    weight_new = master - planned * (direction + weight_decay * master)
    return (weight_new, moment_new, square_new, weight_new.astype(bf16))


def per_device(
    raw_input,
    cotangent,
    segment_ids,
    step_count,
    inlet_copy,
    inlet_master,
    inlet_moment,
    inlet_square,
    outlet_copy,
    outlet_master,
    outlet_moment,
    outlet_square,
    expand_copy,
    expand_master,
    expand_moment,
    expand_square,
    shrink_copy,
    shrink_master,
    shrink_moment,
    shrink_square,
    vector_copy,
    vector_master,
    vector_moment,
    vector_square,
):
    sequences, block_length, features = raw_input.shape
    assert sequences == 1
    width = block_length
    group_size = lax.axis_size("blk")
    group_index = lax.axis_index("blk")
    owners = lax.axis_size("dp")
    owner = lax.axis_index("dp")
    half = owners // 2
    total_tokens = owners * group_size * block_length
    reach = group_size // 2
    slots = 2 * reach + 1
    inner = expand_copy.shape[1]
    chunk = inner // half
    vectors = vector_copy.astype(f32)
    raw = raw_input.reshape(width, features)
    cot = cotangent.reshape(width, features)
    own_ids = segment_ids
    count = owners.bit_length() - 1
    scalar = pl.BlockSpec(memory_space=pltpu.SMEM)
    vmem = pltpu.VMEM

    def reversed_bits(value):
        return int(format(value, f"0{count - 1}b")[::-1], 2) if count > 1 else 0

    straight = [reversed_bits(p) for p in range(half)]
    other_way = list(range(half))
    relative = jnp.array(
        [2 * v for v in straight]
        + [2 * v for v in straight]
        + [2 * v + 1 for v in straight]
        + [2 * v for v in other_way]
        + [2 * v + 1 for v in other_way],
        jnp.int32,
    ) ^ owner
    inside = [group_index >= d for d in range(1, reach + 1)]
    inside += [group_index + d < group_size for d in range(1, reach + 1)]
    table = jnp.concatenate(
        [
            relative[:half] // 2,
            relative[half:],
            jnp.array(straight, jnp.int32),
            jnp.stack([flag for pair in zip(inside[:reach], inside[reach:]) for flag in pair]).astype(jnp.int32),
        ]
    )
    lows = [(group_index // bit) % 2 == 0 for bit in bits_of("blk")]
    column_count = vector_master.shape[1]
    column_start = owner * column_count
    step_value = step_count[0].astype(f32)

    tokens, row = (width, features), (1, features)
    wkv = 3 * features
    lanes = GROUP * HEAD_WIDTH
    steps = features // lanes

    (totals,) = call(
        totals_kernel, "totals", jnp.zeros((1,), jnp.int32), [raw], [struct((2, features), f32)], mib=2
    )
    rounds = SmallSum(totals)
    rounds.send()
    tied = together(*rounds.arrived, table, column_start, vectors, *lows)
    ways = len(rounds.arrived)
    rounds.arrived = list(tied[:ways])
    table, column_start, vectors = tied[ways : ways + 3]
    lows = list(tied[ways + 3 :])
    rounds.take()
    while rounds.left():
        rounds.send()
        rounds.take()
    totals = rounds.block
    packed = width + 16
    x, mean_row, inverse_row = call(
        functools.partial(enter_kernel, total_tokens),
        "enter",
        table,
        [raw, totals, vectors, own_ids],
        [struct((packed, features), bf16), struct(row, f32), struct(row, f32)],
        mib=6,
    )

    xs = [None] * slots
    xs[reach] = x
    ahead, behind = moved(x, "blk", 1), moved(x, "blk", -1)
    queries, pairs, columns = call(
        project_own_kernel,
        "project_own",
        table,
        [x, inlet_copy, vectors],
        [
            struct(tokens, bf16),
            struct((slots, width, 2 * features), bf16),
            struct((slots, width, 128), f32),
        ],
        mib=6,
    )
    ahead, behind, queries = together(ahead, behind, queries)
    for d in range(1, reach + 1):
        if d > 1:
            ahead, behind = moved(ahead, "blk", 1), moved(behind, "blk", -1)
            ahead, behind, pairs = together(ahead, behind, pairs)
        xs[reach - d], xs[reach + d] = ahead, behind
        pairs, columns = call(
            functools.partial(project_pair_kernel, d, 6 * half + 2 * (d - 1)),
            "project_pair",
            table,
            [ahead, behind, x, inlet_copy, vectors, pairs, columns],
            [struct(pairs.shape, bf16), struct(columns.shape, f32)],
            mib=6,
        )

    attended, lse, bounds = call(
        functools.partial(attend_kernel, reach),
        "attend",
        table,
        [queries, pairs, own_ids, columns],
        [struct(tokens, bf16), struct((steps, GROUP, width), f32), struct((2,), jnp.int32)],
        [
            vmem((80 * GROUP, width), f32),
            vmem((8, width), f32),
            vmem((GROUP, 128, width), bf16),
            vmem((GROUP, width, width), f32),
        ],
        mib=6,
    )

    owned_wide, owned = inner // owners, features // owners
    kept_shrink = struct((2, half, owned_wide // 2, features), bf16)
    kept_expand = struct((features // 2, inner + features), bf16)
    layer_output, grad_middle, grad_attended, shrink_keep, shrink_send, expand_keep, expand_send, ffn_rows = call(
        functools.partial(ffn_kernel, half),
        "ffn",
        table,
        [attended, outlet_copy, raw, mean_row, inverse_row, vectors, cot, expand_copy, shrink_copy],
        [
            struct(tokens, bf16),
            struct(tokens, f32),
            struct(tokens, bf16),
            kept_shrink,
            kept_shrink,
            kept_expand,
            kept_expand,
            struct((12, features), f32),
        ],
        [
            vmem(tokens, f32),
            vmem(tokens, f32),
            vmem(tokens, bf16),
            vmem((features, width), bf16),
            vmem((features, width), bf16),
            vmem((features, width), f32),
            vmem((chunk, features), bf16),
            vmem(tokens, f32),
        ],
        mib=14,
    )
    bits = bits_of("dp")
    orders = (bits[1:], bits[:0:-1])

    def scatters(keep, arrived, rows):
        shape = (2,) + (2,) * (count - 1) + (rows // 2, keep.shape[-1])
        keep, arrived = keep.reshape(shape), arrived.reshape(shape)
        return [Scatter([keep[h], arrived[h]], orders[h]) for h in range(2)]

    token = [grad_attended]

    def after(*values):
        tied = together(*values, *token)[: len(values)]
        token[:] = tied
        return tied

    def launch(pair):
        for one in pair:
            one.prepare()
        token[:] = [one.sent for one in pair]
        for one in pair:
            one.send()

    def advance(pair):
        for one, value in zip(pair, after(*[one.arrived for one in pair])):
            one.arrived = value
            one.take()
        if pair[0].order:
            launch(pair)

    def follow(line, stage):
        (line.arrived,) = after(line.arrived)
        stage(line)
        token[:] = [line.keep]

    def begin(pair):
        line = Line(*pair, lows)
        token[:] = [line.sent]
        line.scatter()
        return line

    def next_round():
        rounds.take(after)
        token[:] = [rounds.block]
        if rounds.left():
            rounds.send()

    shrink_in = flipped(shrink_send, "dp", 1)
    expand_in = flipped(expand_send, "dp", 1)
    spread = struct((slots, width, lanes), bf16)
    back = []
    for g in range(steps):
        (grad_attended,) = after(grad_attended)
        back.append(
            call(
                functools.partial(attend_back_kernel, g),
                "attend_back",
                bounds,
                [queries, pairs, attended, grad_attended, lse, own_ids, columns],
                [struct((width, lanes), bf16), spread, spread, struct((2, lanes), f32)],
                [
                    vmem((lanes, width), f32),
                    vmem((GROUP, 128, width), bf16),
                    vmem((GROUP, 128, width), bf16),
                    vmem((GROUP // 2, 2 * width, 128), bf16),
                    vmem((GROUP // 2, 2 * width, 128), bf16),
                    vmem((GROUP, width, width), f32),
                    vmem((GROUP, width, width), f32),
                    vmem((GROUP // 2, width, 2 * width), bf16),
                    vmem((GROUP // 2, width, 2 * width), bf16),
                    vmem((16, width), f32),
                ],
                mib=8,
            )
        )
        token[:] = [back[-1][0]]
        if g == 0:
            (shrink_in,) = after(shrink_in)
            first = scatters(shrink_keep, shrink_in, owned_wide)
            launch(first)
    query_low, key_low, value_low, attend_rows = zip(*back)
    grads = [*query_low, *key_low, *value_low]
    advance(first)

    grads = after(*grads)
    parts, own_part = call(
        functools.partial(parts_kernel, reach),
        "parts",
        bounds,
        [*grads, inlet_copy],
        [struct((2 * reach, width, features), bf16), struct(tokens, f32)],
        mib=6,
    )
    to_left, to_right = parts[0], parts[2 * reach - 1]
    token[:] = [to_left, to_right]
    from_right, from_left = moved(to_left, "blk", -1), moved(to_right, "blk", 1)

    kept_inlet = struct((features // 2, wkv), bf16)
    grads = after(*grads)
    inlet_keep, inlet_send = call(
        functools.partial(weight_kernel, reach, half, steps),
        "weights",
        table,
        xs + [(scalar, bounds), *grads],
        [kept_inlet, kept_inlet],
        [vmem((features, slots * width), bf16), vmem((features, width), f32)],
        mib=8,
    )
    token[:] = [inlet_keep]
    inlet_in = flipped(inlet_send, "dp", 1)
    while first[0].order:
        advance(first)
    advance(first)
    (expand_in,) = after(expand_in)
    second = scatters(expand_keep, expand_in, owned)
    launch(second)
    for d in range(reach - 1, 0, -1):
        from_right, from_left = after(from_right, from_left)
        to_left = added(parts[reach - d], from_right)
        to_right = added(parts[reach + d - 1], from_left)
        token[:] = [to_left, to_right]
        from_right, from_left = moved(to_left, "blk", -1), moved(to_right, "blk", 1)
    line_one = begin(first)
    from_right, from_left = after(from_right, from_left)
    grad_normed, small = call(
        leave_kernel,
        "leave",
        table,
        [
            raw,
            mean_row,
            inverse_row,
            vectors,
            grad_middle,
            own_part,
            from_left,
            from_right,
            ffn_rows,
            *attend_rows,
        ],
        [struct(tokens, f32), struct((16, features), f32)],
        mib=8,
    )
    token[:] = [small]
    rounds = SmallSum(small, paired=False)
    rounds.send()
    advance(second)
    (inlet_in,) = after(inlet_in)
    third = scatters(inlet_keep, inlet_in, owned)
    launch(third)
    next_round()
    follow(line_one, Line.exchange)
    while second[0].order:
        advance(second)
    advance(second)
    line_two = begin(second)
    next_round()
    advance(third)
    follow(line_two, Line.exchange)
    follow(line_one, Line.gather)
    next_round()
    while third[0].order:
        advance(third)
    advance(third)
    line_three = begin(third)
    while rounds.left():
        next_round()
    follow(line_three, Line.exchange)
    (line_one.arrived,) = after(line_one.arrived)
    shrink_share = line_one.result()
    token[:] = [shrink_share]
    follow(line_two, Line.gather)
    next_round()
    small = rounds.block
    follow(line_three, Line.gather)
    (line_two.arrived,) = after(line_two.arrived)
    expand_share = line_two.result()
    token[:] = [expand_share]
    inlet_share = line_three.result()

    band_mean = totals[0] / total_tokens
    band_variance = totals[1] / total_tokens - band_mean * band_mean
    inverse = lax.rsqrt(band_variance + stat_epsilon)
    back_totals = small[12:14]
    grad_variance = -0.5 * back_totals[1] * inverse * inverse * inverse
    grad_centre = -inverse * back_totals[0] - 2.0 * band_mean * grad_variance
    input_gradient = (
        grad_normed * inverse
        + grad_centre / total_tokens
        + 2.0 * grad_variance * raw / total_tokens
    ).reshape(sequences, block_length, features)
    vector_share = lax.dynamic_slice_in_dim(small[:12], column_start, column_count, 1)

    updates = []
    for master, moment, square, share in (
        (inlet_master, inlet_moment, inlet_square, inlet_share),
        (outlet_master, outlet_moment, outlet_square, expand_share[:, inner:]),
        (expand_master, expand_moment, expand_square, expand_share[:, :inner]),
        (shrink_master, shrink_moment, shrink_square, shrink_share),
    ):
        updates.extend(
            adam_rule(
                master, moment, square, share.astype(f32), step_value, rate_matrix, decay_matrix
            )
        )
    updates.extend(
        adam_rule(
            vector_master, vector_moment, vector_square, vector_share, step_value, rate_vector, 0.0
        )
    )
    layer_output = layer_output.reshape(sequences, block_length, features)
    return (layer_output, input_gradient, band_mean, band_variance, *updates)


def solution(mesh):
    tokens = P("dp", "blk", None)
    rows = P("dp", None)
    columns = P(None, "dp")
    matrix = (P(), rows, rows, rows)
    return jax.shard_map(
        per_device,
        mesh=mesh,
        in_specs=(tokens, tokens, P("dp", "blk"), P())
        + matrix * 4
        + (P(), columns, columns, columns),
        out_specs=(tokens, tokens, P(), P()) + (rows,) * 16 + (columns,) * 4,
        check_vma=False,
    )
```

time: 335 us -> 217 us (0.65)
  matrix products: 52.6 us -> 0 us
  starting transfers between devices: 117 us -> 66.2 us
  local copies, waits for them, and re-layouts: 29.5 us -> 6.97 us
  Pallas kernels: 24.7 us -> 42.6 us
  other arithmetic: 36.1 us -> 26.2 us
    dot_general x17 -> x0, matrix products: 52.6 us -> none  [the longest x6 20.1 us: nt(): lax.dot_general(a, b, (((1,), (1,)), ((), ())), preferred_element_type=f32)]
    ppermute x40 -> x36, starting transfers between devices: 78 us -> 41.2 us  [flipped(): return lax.ppermute(block, axis, [(i, i ^ bit) for i in range(size)])]
    pallas_call x2 -> x13, Pallas kernels: 24.7 us -> 42.6 us  [call(): pl.pallas_call(kernel, grid_spec=pltpu.PrefetchScalarGridSpec(num_scalar_...]
    ppermute x12 -> x8, starting transfers between devices: 39 us -> 25.1 us  [moved(): return lax.ppermute(block, axis, route)]
    slice x6 -> x1, local copies, waits for them, and re-layouts: 9.93 us -> 0.07 us  [per_device(): relative[half:]]
    squeeze x20 -> x1, local copies, waits for them, and re-layouts: 7.94 us -> 0.05 us  [per_device(): to_left, to_right = (parts[0], parts[2 * reach - 1])]
    reduce_sum x10 -> x0, other arithmetic: 6.66 us -> none  [the longest x1 1.35 us: per_device(): jnp.sum(raw * raw, axis=0)]
    another operation x17 -> x0, local copies, waits for them, and re-layouts: 5.92 us -> none  [the longest x15 5.91 us: per_device(): jnp.stack([gain_one, shift_one, gain_two, shift_two, query_grad, value_gr...]
  transfers between devices with their start and end apart: 52 -> 44, of which waited for: 26 -> 20; matrix products, arithmetic and copies ran while one was open for 18% -> 11% of each run, Pallas kernels for 0% -> 10%
where the time goes in v3:
time: 217 us
  waiting for transfers between devices  72.5 us (33%)
  starting transfers between devices  66.2 us (31%)
  Pallas kernels  42.6 us (20%)
  other arithmetic  26.2 us (12%)
  local copies, waits for them, and re-layouts  6.97 us (3%)
    ppermute x36, waiting for transfers between devices, flipped(): return lax.ppermute(block, axis, [(i, i ^ bit) for i in range(size)])  58.9 us
    pallas_call x13, Pallas kernels, call(): pl.pallas_call(kernel, grid_spec=pltpu.PrefetchScalarGridSpec(num_scalar_...  42.6 us
    ppermute x36, starting transfers between devices, flipped(): return lax.ppermute(block, axis, [(i, i ^ bit) for i in range(size)])  41.2 us
    ppermute x8, starting transfers between devices, moved(): return lax.ppermute(block, axis, route)  25.1 us
    ppermute x8, waiting for transfers between devices, moved(): return lax.ppermute(block, axis, route)  13.6 us
    convert_element_type x5, other arithmetic, adam_rule(): return (weight_new, moment_new, square_new, weight_new.astype(bf16))  8.97 us
    unnamed x84, local copies, waits for them, and re-layouts  6.85 us
    convert_element_type x6, other arithmetic, summed(): return total.astype(bf16)  6.66 us
  transfers between devices with their start and end apart: 44, of which 20 were waited for; matrix products, arithmetic and copies ran while one was open for 11% of the time, Pallas kernels for 10%

profile of v3, /device:TPU:0, one launch (start us, length us, event | category | flops | bytes accessed | tf_op | source)
XLA Modules:
  0.0 216.7 jit_solution(4365302446382124879)
XLA Ops:
  4.7 2.6 %collective-permute-start.1 = (f32[2,768]{1,0:T(2,128)S(1)}, f32[2,768]{1,0:T(2,128)S(1)}, u32[]{:S(2)}, u32[]{:S(2)}) collective-permute-start(f32[2,768]{1,0:T(2,128)S(1)} %add.308), channel_id=1, source_target_pairs={{0,8},{4,12},{8,0},{12,4},{16,24},{20,28},{24,16},{28,20},{1,9},{5... | collective-permute-start | bytes 18440 | tf_op jit(solution)/shard_map/ppermute | solution.py:44
  11.0 2.4 %collective-permute-done.3 = f32[2,768]{1,0:T(2,128)S(1)} collective-permute-done((f32[2,768]{1,0:T(2,128)S(1)}, f32[2,768]{1,0:T(2,128)S(1)}, u32[]{:S(2)}, u32[]{:S(2)}) %collective-permute-start.3) | collective-permute-done | bytes 6176 | tf_op jit(solution)/shard_map/ppermute | solution.py:44
  15.1 2.6 %collective-permute-start.5 = (f32[2,768]{1,0:T(2,128)S(1)}, f32[2,768]{1,0:T(2,128)S(1)}, u32[]{:S(2)}, u32[]{:S(2)}) collective-permute-start(f32[2,768]{1,0:T(2,128)S(1)} %add_add_fusion.1), channel_id=1, source_target_pairs={{0,2},{1,3},{2,0},{3,1},{4,6},{5,7},{6,4},{7,5},{8,10},{9,11},{10,... | collective-permute-start | bytes 18440 | tf_op jit(solution)/shard_map/ppermute | solution.py:44
  19.6 3.5 %collective-permute-done.6 = f32[2,768]{1,0:T(2,128)S(1)} collective-permute-done((f32[2,768]{1,0:T(2,128)S(1)}, f32[2,768]{1,0:T(2,128)S(1)}, u32[]{:S(2)}, u32[]{:S(2)}) %collective-permute-start.6) | collective-permute-done | bytes 6176 | tf_op jit(solution)/shard_map/ppermute | solution.py:44
  32.3 4.1 %collective-permute-done.8.xb_ref.refs_3_ = bf16[272,768]{1,0:T(8,128)(2,1)S(1)} collective-permute-done((bf16[272,768]{1,0:T(8,128)(2,1)S(1)}, bf16[272,768]{1,0:T(8,128)(2,1)S(1)}, u32[]{:S(2)}, u32[]{:S(2)}) %collective-permute-start.8) | collective-permute-done | bytes 417824 | tf_op jit(solution)/shard_map/ppermute | solution.py:50
  37.7 4.6 %collective-permute-start.9 = (bf16[272,768]{1,0:T(8,128)(2,1)S(1)}, bf16[272,768]{1,0:T(8,128)(2,1)S(1)}, u32[]{:S(2)}, u32[]{:S(2)}) collective-permute-start(bf16[272,768]{1,0:T(8,128)(2,1)S(1)} %collective-permute-done.7.xa_ref.refs_1_), channel_id=1, source_target_pairs={{0,1},{1,2},{2,3},{4,5},{5,6},{6,7},{8,9},{9,10},{10,11},{12,13},{... | collective-permute-start | bytes 1253384 | tf_op jit(solution)/shard_map/ppermute | solution.py:50
  43.9 2.4 %collective-permute-done.10.xb_ref.refs_4_ = bf16[272,768]{1,0:T(8,128)(2,1)S(1)} collective-permute-done((bf16[272,768]{1,0:T(8,128)(2,1)S(1)}, bf16[272,768]{1,0:T(8,128)(2,1)S(1)}, u32[]{:S(2)}, u32[]{:S(2)}) %collective-permute-start.10) | collective-permute-done | bytes 417824 | tf_op jit(solution)/shard_map/ppermute | solution.py:50
  48.7 5.3 %attend.1 = (bf16[256,768]{1,0:T(8,128)(2,1)S(1)}, f32[3,4,256]{2,1,0:T(4,128)S(1)}, s32[2]{0:T(128)S(1)}) custom-call(s32[28]{0:T(128)S(1)} %pad_add_fusion.table, bf16[256,768]{1,0:T(8,128)(2,1)S(1)} %get-tuple-element.131.q_ref, bf16[5,256,1536]{2,1,0:T(8,128)(2,1)S(1)} %get-tuple-element.141.kv_ref, s32[1,256]{1,0:T(1,128)S(1)} %copy-done.14, ...), custom_call_target="tpu_custom_call" | custom-call | flops 1048576 | bytes 65536 | tf_op jit(solution)/shard_map/attend/pallas_call | solution.py:159
  54.1 13.3 %ffn.1 = (bf16[256,768]{1,0:T(8,128)(2,1)}, f32[256,768]{1,0:T(8,128)S(1)}, bf16[256,768]{1,0:T(8,128)(2,1)S(1)}, bf16[2,4,192,768]{3,2,1,0:T(8,128)(2,1)S(1)}, ...) custom-call(s32[28]{0:T(128)S(1)} %pad_add_fusion.table, ...), custom_call_target="tpu_custom_call" | custom-call | flops 1048576 | bytes 65536 | tf_op jit(solution)/shard_map/ffn/pallas_call | solution.py:159
  67.9 2.8 %attend_back.3 = (bf16[256,256]{1,0:T(8,128)(2,1)S(1)}, bf16[5,256,256]{2,1,0:T(8,128)(2,1)S(1)}, bf16[5,256,256]{2,1,0:T(8,128)(2,1)S(1)}, f32[2,256]{1,0:T(2,128)S(1)}) custom-call(s32[2]{0:T(128)S(1)} %get-tuple-element.148.bounds.refs_5_, bf16[256,768]{1,0:T(8,128)(2,1)S(1)} %get-tuple-element.131.q_ref, ...), custom_call_target="tpu_custom_call" | custom-call | flops 1048576 | bytes 65536 | tf_op jit(solution)/shard_map/attend_back/pallas_call | solution.py:159
  72.3 3.1 %collective-permute-start.12 = (bf16[2,192,768]{2,1,0:T(8,128)(2,1)S(1)}, bf16[2,192,768]{2,1,0:T(8,128)(2,1)S(1)}, u32[]{:S(2)}, u32[]{:S(2)}) collective-permute-start(bf16[2,192,768]{2,1,0:T(8,128)(2,1)S(1)} %get-tuple-element.271), channel_id=1, source_target_pairs={{0,8},{4,12},{8,0},{12,4},{16,24},{20,28},{24,16},{28,20},{1,9},{5... | collective-permute-start | bytes 1769480 | tf_op jit(solution)/shard_map/ppermute | solution.py:44
  75.4 2.7 %attend_back.4 = (bf16[256,256]{1,0:T(8,128)(2,1)S(1)}, bf16[5,256,256]{2,1,0:T(8,128)(2,1)S(1)}, bf16[5,256,256]{2,1,0:T(8,128)(2,1)S(1)}, f32[2,256]{1,0:T(2,128)S(1)}) custom-call(s32[2]{0:T(128)S(1)} %get-tuple-element.148.bounds.refs_5_, bf16[256,768]{1,0:T(8,128)(2,1)S(1)} %get-tuple-element.131.q_ref, ...), custom_call_target="tpu_custom_call" | custom-call | flops 1048576 | bytes 65536 | tf_op jit(solution)/shard_map/attend_back/pallas_call | solution.py:159
  78.1 2.7 %attend_back.5 = (bf16[256,256]{1,0:T(8,128)(2,1)S(1)}, bf16[5,256,256]{2,1,0:T(8,128)(2,1)S(1)}, bf16[5,256,256]{2,1,0:T(8,128)(2,1)S(1)}, f32[2,256]{1,0:T(2,128)S(1)}) custom-call(s32[2]{0:T(128)S(1)} %get-tuple-element.148.bounds.refs_5_, bf16[256,768]{1,0:T(8,128)(2,1)S(1)} %get-tuple-element.131.q_ref, ...), custom_call_target="tpu_custom_call" | custom-call | flops 1048576 | bytes 65536 | tf_op jit(solution)/shard_map/attend_back/pallas_call | solution.py:159
  80.8 8.3 %collective-permute-done.12 = bf16[2,192,768]{2,1,0:T(8,128)(2,1)S(1)} collective-permute-done((bf16[2,192,768]{2,1,0:T(8,128)(2,1)S(1)}, bf16[2,192,768]{2,1,0:T(8,128)(2,1)S(1)}, u32[]{:S(2)}, u32[]{:S(2)}) %collective-permute-start.12) | collective-permute-done | bytes 589856 | tf_op jit(solution)/shard_map/ppermute | solution.py:44
  92.0 2.6 %parts.1 = (bf16[4,256,768]{2,1,0:T(8,128)(2,1)S(1)}, f32[256,768]{1,0:T(8,128)S(1)}) custom-call(s32[2]{0:T(128)S(1)} %get-tuple-element.148.bounds.refs_5_, bf16[256,256]{1,0:T(8,128)(2,1)S(1)} %get-tuple-element.180.refs_0_.refs_6_, bf16[256,256]{1,0:T(8,128)(2,1)S(1)} %get-tuple-element.181.refs_1_.refs_7_, ...), custom_call_target="tpu_custom_call" | custom-call | flops 1048576 | bytes 65536 | tf_op jit(solution)/shard_map/parts/pallas_call | solution.py:159
  95.9 7.1 %collective-permute-start.15 = (bf16[256,768]{1,0:T(8,128)(2,1)S(1)}, bf16[256,768]{1,0:T(8,128)(2,1)S(1)}, u32[]{:S(2)}, u32[]{:S(2)}) collective-permute-start(bf16[256,768]{1,0:T(8,128)(2,1)S(1)} %get-tuple-element.278), channel_id=1, source_target_pairs={{0,1},{1,2},{2,3},{4,5},{5,6},{6,7},{8,9},{9,10},{10,11},{12,13},{... | collective-permute-start | bytes 1179656 | tf_op jit(solution)/shard_map/ppermute | solution.py:50
  103.1 5.5 %weights.1 = (bf16[384,2304]{1,0:T(8,128)(2,1)S(1)}, bf16[384,2304]{1,0:T(8,128)(2,1)}) custom-call(s32[28]{0:T(128)S(1)} %pad_add_fusion.table, bf16[272,768]{1,0:T(8,128)(2,1)S(1)} %collective-permute-done.9.xa_ref.refs_0_, bf16[272,768]{1,0:T(8,128)(2,1)S(1)} %collective-permute-done.7.xa_ref.refs_1_, ...), custom_call_target="tpu_custom_call" | custom-call | flops 1048576 | bytes 65536 | tf_op jit(solution)/shard_map/weights/pallas_call | solution.py:159
  112.6 2.3 %collective-permute-start.23 = (bf16[2,48,3840]{2,1,0:T(8,128)(2,1)}, bf16[2,48,3840]{2,1,0:T(8,128)(2,1)}, u32[]{:S(2)}, u32[]{:S(2)}) collective-permute-start(bf16[2,48,3840]{2,1,0:T(8,128)(2,1)} %bitcast.16), channel_id=1, source_target_pairs={{0,8},{4,12},{8,0},{12,4},{16,24},{20,28},{24,16},{28,20},{1,9},{5... | collective-permute-start | bytes 2211848 | tf_op jit(solution)/shard_map/ppermute | solution.py:44
  118.4 6.9 %collective-permute-start.20 = (bf16[256,768]{1,0:T(8,128)(2,1)}, bf16[256,768]{1,0:T(8,128)(2,1)}, u32[]{:S(2)}, u32[]{:S(2)}) collective-permute-start(bf16[256,768]{1,0:T(8,128)(2,1)} %get-tuple-element.276), channel_id=1, source_target_pairs={{0,1},{1,2},{2,3},{4,5},{5,6},{6,7},{8,9},{9,10},{10,11},{12,13},{... | collective-permute-start | bytes 1179656 | tf_op jit(solution)/shard_map/ppermute | solution.py:50
  127.9 4.1 %collective-permute-done.19.right_ref = bf16[256,768]{1,0:T(8,128)(2,1)} collective-permute-done((bf16[256,768]{1,0:T(8,128)(2,1)}, bf16[256,768]{1,0:T(8,128)(2,1)}, u32[]{:S(2)}, u32[]{:S(2)}) %collective-permute-start.19) | collective-permute-done | bytes 393248 | tf_op jit(solution)/shard_map/ppermute | solution.py:50
  133.8 2.8 %leave.1 = (f32[256,768]{1,0:T(8,128)S(1)}, f32[16,768]{1,0:T(8,128)S(1)}) custom-call(s32[28]{0:T(128)S(1)} %pad_add_fusion.table, f32[256,768]{1,0:T(8,128)S(1)} %bitcast.88, f32[1,768]{1,0:T(1,128)S(1)} %get-tuple-element.144.mean_ref, f32[1,768]{1,0:T(1,128)S(1)} %get-tuple-element.145.std_ref, f32[12,768]{1,0:T(8,128)S(1)} %convert_element_type.406.vec_ref, ...), custom_call_target="tpu_custom_call" | custom-call | flops 1048576 | bytes 65536 | tf_op jit(solution)/shard_map/leave/pallas_call | solution.py:159
  144.5 5.4 %collective-permute-done.26 = bf16[48,3840]{1,0:T(8,128)(2,1)S(1)} collective-permute-done((bf16[48,3840]{1,0:T(8,128)(2,1)S(1)}, bf16[48,3840]{1,0:T(8,128)(2,1)S(1)}, u32[]{:S(2)}, u32[]{:S(2)}) %collective-permute-start.26) | collective-permute-done | bytes 368672 | tf_op jit(solution)/shard_map/ppermute | solution.py:44
  149.9 3.1 %collective-permute-start.30 = (bf16[192,768]{1,0:T(8,128)(2,1)S(1)}, bf16[192,768]{1,0:T(8,128)(2,1)S(1)}, u32[]{:S(2)}, u32[]{:S(2)}) collective-permute-start(bf16[192,768]{1,0:T(8,128)(2,1)S(1)} %add_convert_fusion.9), channel_id=1, source_target_pairs={{0,2},{1,3},{2,0},{3,1},{4,6},{5,7},{6,4},{7,5},{8,10},{9,11},{10,... | collective-permute-start | bytes 884744 | tf_op jit(solution)/shard_map/ppermute | solution.py:44
  156.8 3.2 %collective-permute-done.25 = f32[16,768]{1,0:T(8,128)S(1)} collective-permute-done((f32[16,768]{1,0:T(8,128)S(1)}, f32[16,768]{1,0:T(8,128)S(1)}, u32[]{:S(2)}, u32[]{:S(2)}) %collective-permute-start.25) | collective-permute-done | bytes 49184 | tf_op jit(solution)/shard_map/ppermute | solution.py:44
  163.6 5.4 %collective-permute-done.31 = bf16[48,3840]{1,0:T(8,128)(2,1)S(1)} collective-permute-done((bf16[48,3840]{1,0:T(8,128)(2,1)S(1)}, bf16[48,3840]{1,0:T(8,128)(2,1)S(1)}, u32[]{:S(2)}, u32[]{:S(2)}) %collective-permute-start.31) | collective-permute-done | bytes 368672 | tf_op jit(solution)/shard_map/ppermute | solution.py:44
  169.2 2.4 %collective-permute-start.38 = (bf16[48,3840]{1,0:T(8,128)(2,1)S(1)}, bf16[48,3840]{1,0:T(8,128)(2,1)S(1)}, u32[]{:S(2)}, u32[]{:S(2)}) collective-permute-start(bf16[48,3840]{1,0:T(8,128)(2,1)S(1)} %add_convert_fusion.7), channel_id=1, source_target_pairs={{0,2},{1,3},{2,0},{3,1},{4,6},{5,7},{6,4},{7,5},{8,10},{9,11},{10,... | collective-permute-start | bytes 1105928 | tf_op jit(solution)/shard_map/ppermute | solution.py:44
  171.7 2.5 %collective-permute-start.39 = (bf16[192,768]{1,0:T(8,128)(2,1)S(1)}, bf16[192,768]{1,0:T(8,128)(2,1)S(1)}, u32[]{:S(2)}, u32[]{:S(2)}) collective-permute-start(bf16[192,768]{1,0:T(8,128)(2,1)S(1)} %add_convert_fusion.8), channel_id=1, source_target_pairs={{0,1},{1,0},{2,3},{3,2},{4,5},{5,4},{6,7},{7,6},{8,9},{9,8},{10,11... | collective-permute-start | bytes 884744 | tf_op jit(solution)/shard_map/ppermute | solution.py:44
  177.7 12.8 %collective-permute-done.34 = f32[16,768]{1,0:T(8,128)S(1)} collective-permute-done((f32[16,768]{1,0:T(8,128)S(1)}, f32[16,768]{1,0:T(8,128)S(1)}, u32[]{:S(2)}, u32[]{:S(2)}) %collective-permute-start.34) | collective-permute-done | bytes 49184 | tf_op jit(solution)/shard_map/ppermute | solution.py:44
  193.2 3.4 %collective-permute-done.37 = f32[16,768]{1,0:T(8,128)S(1)} collective-permute-done((f32[16,768]{1,0:T(8,128)S(1)}, f32[16,768]{1,0:T(8,128)S(1)}, u32[]{:S(2)}, u32[]{:S(2)}) %collective-permute-start.37) | collective-permute-done | bytes 49184 | tf_op jit(solution)/shard_map/ppermute | solution.py:44
  199.9 2.5 %fusion.36 = (bf16[384,768]{1,0:T(8,128)(2,1)}, f32[384,768]{1,0:T(8,128)}, f32[384,768]{1,0:T(8,128)}, f32[384,768]{1,0:T(8,128)}) fusion(f32[384,768]{1,0:T(8,128)S(1)} %copy-done.18, f32[]{:T(128)} %bitcast.36, f32[]{:T(128)} %bitcast.35, f32[]{:T(128)} %bitcast.34, bf16[192,768]{1,0:T(8,128)(2,1)S(1)} %get-tuple-element.283, ...), kind=kLoop, calls=%fused_computation.110 | loop fusion | flops 5603328 | bytes 8257548 | tf_op jit(solution)/shard_map/convert_element_type | solution.py:665
  202.5 6.0 %collective-permute-done.41 = bf16[48,2304]{1,0:T(8,128)(2,1)S(1)} collective-permute-done((bf16[48,2304]{1,0:T(8,128)(2,1)S(1)}, bf16[48,2304]{1,0:T(8,128)(2,1)S(1)}, u32[]{:S(2)}, u32[]{:S(2)}) %collective-permute-start.41) | collective-permute-done | bytes 221216 | tf_op jit(solution)/shard_map/ppermute | solution.py:44
  208.8 2.6 %fusion.39 = (bf16[96,3072]{1,0:T(8,128)(2,1)}, f32[96,3072]{1,0:T(8,128)}, f32[96,3072]{1,0:T(8,128)}, f32[96,3072]{1,0:T(8,128)}) fusion(f32[96,3072]{1,0:T(8,128)S(1)} %copy-done.21, f32[]{:T(128)} %bitcast.36, f32[]{:T(128)} %bitcast.35, f32[]{:T(128)} %bitcast.34, bf16[48,3840]{1,0:T(8,128)(2,1)S(1)} %get-tuple-element.281, ...), kind=kLoop, calls=%fused_computation.111 | loop fusion | flops 5603328 | bytes 8405004 | tf_op jit(solution)/shard_map/convert_element_type | solution.py:665
  (197 shorter events, 73.5 us)
Async XLA Ops:
  26.0 10.5 %collective-permute-start.8 = (bf16[272,768]{1,0:T(8,128)(2,1)S(1)}, bf16[272,768]{1,0:T(8,128)(2,1)S(1)}, u32[]{:S(2)}, u32[]{:S(2)}) collective-permute-start(bf16[272,768]{1,0:T(8,128)(2,1)S(1)} %get-tuple-element.129.x_ref.refs_2_), channel_id=1, source_target_pairs={{1,0},{2,1},{3,2},{5,4},{6,5},{7,6},{9,8},{10,9},{11,10},{13,12},{... | collective-permute-start | bytes 1253384 | tf_op jit(solution)/shard_map/ppermute | solution.py:50
  36.4 9.9 %collective-permute-start.10 = (bf16[272,768]{1,0:T(8,128)(2,1)S(1)}, bf16[272,768]{1,0:T(8,128)(2,1)S(1)}, u32[]{:S(2)}, u32[]{:S(2)}) collective-permute-start(bf16[272,768]{1,0:T(8,128)(2,1)S(1)} %collective-permute-done.8.xb_ref.refs_3_), channel_id=1, source_target_pairs={{1,0},{2,1},{3,2},{5,4},{6,5},{7,6},{9,8},{10,9},{11,10},{13,12},{... | collective-permute-start | bytes 1253384 | tf_op jit(solution)/shard_map/ppermute | solution.py:50
  37.7 10.1 %collective-permute-start.9 = (bf16[272,768]{1,0:T(8,128)(2,1)S(1)}, bf16[272,768]{1,0:T(8,128)(2,1)S(1)}, u32[]{:S(2)}, u32[]{:S(2)}) collective-permute-start(bf16[272,768]{1,0:T(8,128)(2,1)S(1)} %collective-permute-done.7.xa_ref.refs_1_), channel_id=1, source_target_pairs={{0,1},{1,2},{2,3},{4,5},{5,6},{6,7},{8,9},{9,10},{10,11},{12,13},{... | collective-permute-start | bytes 1253384 | tf_op jit(solution)/shard_map/ppermute | solution.py:50
  67.4 42.4 %collective-permute-start.16 = (bf16[384,3840]{1,0:T(8,128)(2,1)S(1)}, bf16[384,3840]{1,0:T(8,128)(2,1)S(1)}, u32[]{:S(2)}, u32[]{:S(2)}) collective-permute-start(bf16[384,3840]{1,0:T(8,128)(2,1)S(1)} %get-tuple-element.179), channel_id=1, source_target_pairs={{0,4},{4,0},{8,12},{12,8},{16,20},{20,16},{24,28},{28,24},{1,5},{5... | collective-permute-start | bytes 8847368 | tf_op jit(solution)/shard_map/ppermute | solution.py:44
  72.3 16.8 %collective-permute-start.12 = (bf16[2,192,768]{2,1,0:T(8,128)(2,1)S(1)}, bf16[2,192,768]{2,1,0:T(8,128)(2,1)S(1)}, u32[]{:S(2)}, u32[]{:S(2)}) collective-permute-start(bf16[2,192,768]{2,1,0:T(8,128)(2,1)S(1)} %get-tuple-element.271), channel_id=1, source_target_pairs={{0,8},{4,12},{8,0},{12,4},{16,24},{20,28},{24,16},{28,20},{1,9},{5... | collective-permute-start | bytes 1769480 | tf_op jit(solution)/shard_map/ppermute | solution.py:44
  75.4 15.1 %collective-permute-start.13 = (bf16[2,192,768]{2,1,0:T(8,128)(2,1)S(1)}, bf16[2,192,768]{2,1,0:T(8,128)(2,1)S(1)}, u32[]{:S(2)}, u32[]{:S(2)}) collective-permute-start(bf16[2,192,768]{2,1,0:T(8,128)(2,1)S(1)} %get-tuple-element.270), channel_id=1, source_target_pairs={{0,16},{4,20},{8,24},{12,28},{16,0},{20,4},{24,8},{28,12},{1,17},{... | collective-permute-start | bytes 1769480 | tf_op jit(solution)/shard_map/ppermute | solution.py:44
  91.3 18.4 %collective-permute-start.17 = (bf16[192,768]{1,0:T(8,128)(2,1)S(1)}, bf16[192,768]{1,0:T(8,128)(2,1)S(1)}, u32[]{:S(2)}, u32[]{:S(2)}) collective-permute-start(bf16[192,768]{1,0:T(8,128)(2,1)S(1)} %get-tuple-element.269), channel_id=1, source_target_pairs={{0,16},{4,20},{8,24},{12,28},{16,0},{20,4},{24,8},{28,12},{1,17},{... | collective-permute-start | bytes 884744 | tf_op jit(solution)/shard_map/ppermute | solution.py:44
  91.6 18.1 %collective-permute-start.18 = (bf16[192,768]{1,0:T(8,128)(2,1)S(1)}, bf16[192,768]{1,0:T(8,128)(2,1)S(1)}, u32[]{:S(2)}, u32[]{:S(2)}) collective-permute-start(bf16[192,768]{1,0:T(8,128)(2,1)S(1)} %get-tuple-element.268), channel_id=1, source_target_pairs={{0,8},{4,12},{8,0},{12,4},{16,24},{20,28},{24,16},{28,20},{1,9},{5... | collective-permute-start | bytes 884744 | tf_op jit(solution)/shard_map/ppermute | solution.py:44
  94.6 21.4 %collective-permute-start.14 = (bf16[256,768]{1,0:T(8,128)(2,1)S(1)}, bf16[256,768]{1,0:T(8,128)(2,1)S(1)}, u32[]{:S(2)}, u32[]{:S(2)}) collective-permute-start(bf16[256,768]{1,0:T(8,128)(2,1)S(1)} %get-tuple-element.279), channel_id=1, source_target_pairs={{1,0},{2,1},{3,2},{5,4},{6,5},{7,6},{9,8},{10,9},{11,10},{13,12},{... | collective-permute-start | bytes 1179656 | tf_op jit(solution)/shard_map/ppermute | solution.py:50
  95.9 20.1 %collective-permute-start.15 = (bf16[256,768]{1,0:T(8,128)(2,1)S(1)}, bf16[256,768]{1,0:T(8,128)(2,1)S(1)}, u32[]{:S(2)}, u32[]{:S(2)}) collective-permute-start(bf16[256,768]{1,0:T(8,128)(2,1)S(1)} %get-tuple-element.278), channel_id=1, source_target_pairs={{0,1},{1,2},{2,3},{4,5},{5,6},{6,7},{8,9},{9,10},{10,11},{12,13},{... | collective-permute-start | bytes 1179656 | tf_op jit(solution)/shard_map/ppermute | solution.py:50
  109.7 29.4 %collective-permute-start.22 = (bf16[384,2304]{1,0:T(8,128)(2,1)}, bf16[384,2304]{1,0:T(8,128)(2,1)}, u32[]{:S(2)}, u32[]{:S(2)}) collective-permute-start(bf16[384,2304]{1,0:T(8,128)(2,1)} %get-tuple-element.204), channel_id=1, source_target_pairs={{0,4},{4,0},{8,12},{12,8},{16,20},{20,16},{24,28},{28,24},{1,5},{5... | collective-permute-start | bytes 5308424 | tf_op jit(solution)/shard_map/ppermute | solution.py:44
  112.6 24.1 %collective-permute-start.23 = (bf16[2,48,3840]{2,1,0:T(8,128)(2,1)}, bf16[2,48,3840]{2,1,0:T(8,128)(2,1)}, u32[]{:S(2)}, u32[]{:S(2)}) collective-permute-start(bf16[2,48,3840]{2,1,0:T(8,128)(2,1)} %bitcast.16), channel_id=1, source_target_pairs={{0,8},{4,12},{8,0},{12,4},{16,24},{20,28},{24,16},{28,20},{1,9},{5... | collective-permute-start | bytes 2211848 | tf_op jit(solution)/shard_map/ppermute | solution.py:44
  115.0 21.7 %collective-permute-start.24 = (bf16[2,48,3840]{2,1,0:T(8,128)(2,1)}, bf16[2,48,3840]{2,1,0:T(8,128)(2,1)}, u32[]{:S(2)}, u32[]{:S(2)}) collective-permute-start(bf16[2,48,3840]{2,1,0:T(8,128)(2,1)} %bitcast.17), channel_id=1, source_target_pairs={{0,16},{4,20},{8,24},{12,28},{16,0},{20,4},{24,8},{28,12},{1,17},{... | collective-permute-start | bytes 2211848 | tf_op jit(solution)/shard_map/ppermute | solution.py:44
  117.1 15.0 %collective-permute-start.19 = (bf16[256,768]{1,0:T(8,128)(2,1)}, bf16[256,768]{1,0:T(8,128)(2,1)}, u32[]{:S(2)}, u32[]{:S(2)}) collective-permute-start(bf16[256,768]{1,0:T(8,128)(2,1)} %get-tuple-element.277), channel_id=1, source_target_pairs={{1,0},{2,1},{3,2},{5,4},{6,5},{7,6},{9,8},{10,9},{11,10},{13,12},{... | collective-permute-start | bytes 1179656 | tf_op jit(solution)/shard_map/ppermute | solution.py:50
  118.4 15.4 %collective-permute-start.20 = (bf16[256,768]{1,0:T(8,128)(2,1)}, bf16[256,768]{1,0:T(8,128)(2,1)}, u32[]{:S(2)}, u32[]{:S(2)}) collective-permute-start(bf16[256,768]{1,0:T(8,128)(2,1)} %get-tuple-element.276), channel_id=1, source_target_pairs={{0,1},{1,2},{2,3},{4,5},{5,6},{6,7},{8,9},{9,10},{10,11},{12,13},{... | collective-permute-start | bytes 1179656 | tf_op jit(solution)/shard_map/ppermute | solution.py:50
  132.1 12.0 %collective-permute-start.28 = (bf16[192,768]{1,0:T(8,128)(2,1)S(1)}, bf16[192,768]{1,0:T(8,128)(2,1)S(1)}, u32[]{:S(2)}, u32[]{:S(2)}) collective-permute-start(bf16[192,768]{1,0:T(8,128)(2,1)S(1)} %get-tuple-element.261), channel_id=1, source_target_pairs={{0,1},{1,0},{2,3},{3,2},{4,5},{5,4},{6,7},{7,6},{8,9},{9,8},{10,11... | collective-permute-start | bytes 884744 | tf_op jit(solution)/shard_map/ppermute | solution.py:44
  138.4 11.5 %collective-permute-start.26 = (bf16[48,3840]{1,0:T(8,128)(2,1)S(1)}, bf16[48,3840]{1,0:T(8,128)(2,1)S(1)}, u32[]{:S(2)}, u32[]{:S(2)}) collective-permute-start(bf16[48,3840]{1,0:T(8,128)(2,1)S(1)} %get-tuple-element.265), channel_id=1, source_target_pairs={{0,16},{4,20},{8,24},{12,28},{16,0},{20,4},{24,8},{28,12},{1,17},{... | collective-permute-start | bytes 1105928 | tf_op jit(solution)/shard_map/ppermute | solution.py:44
  138.8 14.2 %collective-permute-start.27 = (bf16[48,3840]{1,0:T(8,128)(2,1)S(1)}, bf16[48,3840]{1,0:T(8,128)(2,1)S(1)}, u32[]{:S(2)}, u32[]{:S(2)}) collective-permute-start(bf16[48,3840]{1,0:T(8,128)(2,1)S(1)} %get-tuple-element.264), channel_id=1, source_target_pairs={{0,8},{4,12},{8,0},{12,4},{16,24},{20,28},{24,16},{28,20},{1,9},{5... | collective-permute-start | bytes 1105928 | tf_op jit(solution)/shard_map/ppermute | solution.py:44
  140.5 21.2 %collective-permute-start.32 = (bf16[2,48,2304]{2,1,0:T(8,128)(2,1)S(1)}, bf16[2,48,2304]{2,1,0:T(8,128)(2,1)S(1)}, u32[]{:S(2)}, u32[]{:S(2)}) collective-permute-start(bf16[2,48,2304]{2,1,0:T(8,128)(2,1)S(1)} %bitcast.95), channel_id=1, source_target_pairs={{0,8},{4,12},{8,0},{12,4},{16,24},{20,28},{24,16},{28,20},{1,9},{5... | collective-permute-start | bytes 1327112 | tf_op jit(solution)/shard_map/ppermute | solution.py:44
  142.3 19.4 %collective-permute-start.33 = (bf16[2,48,2304]{2,1,0:T(8,128)(2,1)S(1)}, bf16[2,48,2304]{2,1,0:T(8,128)(2,1)S(1)}, u32[]{:S(2)}, u32[]{:S(2)}) collective-permute-start(bf16[2,48,2304]{2,1,0:T(8,128)(2,1)S(1)} %bitcast.94), channel_id=1, source_target_pairs={{0,16},{4,20},{8,24},{12,28},{16,0},{20,4},{24,8},{28,12},{1,17},{... | collective-permute-start | bytes 1327112 | tf_op jit(solution)/shard_map/ppermute | solution.py:44
  144.1 15.9 %collective-permute-start.25 = (f32[16,768]{1,0:T(8,128)S(1)}, f32[16,768]{1,0:T(8,128)S(1)}, u32[]{:S(2)}, u32[]{:S(2)}) collective-permute-start(f32[16,768]{1,0:T(8,128)S(1)} %add.343), channel_id=1, source_target_pairs={{0,8},{4,12},{8,0},{12,4},{16,24},{20,28},{24,16},{28,20},{1,9},{5... | collective-permute-start | bytes 147464 | tf_op jit(solution)/shard_map/ppermute | solution.py:44
  149.9 21.7 %collective-permute-start.30 = (bf16[192,768]{1,0:T(8,128)(2,1)S(1)}, bf16[192,768]{1,0:T(8,128)(2,1)S(1)}, u32[]{:S(2)}, u32[]{:S(2)}) collective-permute-start(bf16[192,768]{1,0:T(8,128)(2,1)S(1)} %add_convert_fusion.9), channel_id=1, source_target_pairs={{0,2},{1,3},{2,0},{3,1},{4,6},{5,7},{6,4},{7,5},{8,10},{9,11},{10,... | collective-permute-start | bytes 884744 | tf_op jit(solution)/shard_map/ppermute | solution.py:44
  154.7 14.3 %collective-permute-start.31 = (bf16[48,3840]{1,0:T(8,128)(2,1)S(1)}, bf16[48,3840]{1,0:T(8,128)(2,1)S(1)}, u32[]{:S(2)}, u32[]{:S(2)}) collective-permute-start(bf16[48,3840]{1,0:T(8,128)(2,1)S(1)} %get-tuple-element.258), channel_id=1, source_target_pairs={{0,1},{1,0},{2,3},{3,2},{4,5},{5,4},{6,7},{7,6},{8,9},{9,8},{10,11... | collective-permute-start | bytes 1105928 | tf_op jit(solution)/shard_map/ppermute | solution.py:44
  160.0 14.2 %collective-permute-start.29 = (f32[16,768]{1,0:T(8,128)S(1)}, f32[16,768]{1,0:T(8,128)S(1)}, u32[]{:S(2)}, u32[]{:S(2)}) collective-permute-start(f32[16,768]{1,0:T(8,128)S(1)} %add.351), channel_id=1, source_target_pairs={{0,16},{4,20},{8,24},{12,28},{16,0},{20,4},{24,8},{28,12},{1,17},{... | collective-permute-start | bytes 147464 | tf_op jit(solution)/shard_map/ppermute | solution.py:44
  162.9 11.4 %collective-permute-start.35 = (bf16[48,2304]{1,0:T(8,128)(2,1)S(1)}, bf16[48,2304]{1,0:T(8,128)(2,1)S(1)}, u32[]{:S(2)}, u32[]{:S(2)}) collective-permute-start(bf16[48,2304]{1,0:T(8,128)(2,1)S(1)} %get-tuple-element.273), channel_id=1, source_target_pairs={{0,16},{4,20},{8,24},{12,28},{16,0},{20,4},{24,8},{28,12},{1,17},{... | collective-permute-start | bytes 663560 | tf_op jit(solution)/shard_map/ppermute | solution.py:44
  163.4 11.0 %collective-permute-start.36 = (bf16[48,2304]{1,0:T(8,128)(2,1)S(1)}, bf16[48,2304]{1,0:T(8,128)(2,1)S(1)}, u32[]{:S(2)}, u32[]{:S(2)}) collective-permute-start(bf16[48,2304]{1,0:T(8,128)(2,1)S(1)} %get-tuple-element.272), channel_id=1, source_target_pairs={{0,8},{4,12},{8,0},{12,4},{16,24},{20,28},{24,16},{28,20},{1,9},{5... | collective-permute-start | bytes 663560 | tf_op jit(solution)/shard_map/ppermute | solution.py:44
  169.2 21.8 %collective-permute-start.38 = (bf16[48,3840]{1,0:T(8,128)(2,1)S(1)}, bf16[48,3840]{1,0:T(8,128)(2,1)S(1)}, u32[]{:S(2)}, u32[]{:S(2)}) collective-permute-start(bf16[48,3840]{1,0:T(8,128)(2,1)S(1)} %add_convert_fusion.7), channel_id=1, source_target_pairs={{0,2},{1,3},{2,0},{3,1},{4,6},{5,7},{6,4},{7,5},{8,10},{9,11},{10,... | collective-permute-start | bytes 1105928 | tf_op jit(solution)/shard_map/ppermute | solution.py:44
  171.7 28.1 %collective-permute-start.39 = (bf16[192,768]{1,0:T(8,128)(2,1)S(1)}, bf16[192,768]{1,0:T(8,128)(2,1)S(1)}, u32[]{:S(2)}, u32[]{:S(2)}) collective-permute-start(bf16[192,768]{1,0:T(8,128)(2,1)S(1)} %add_convert_fusion.8), channel_id=1, source_target_pairs={{0,1},{1,0},{2,3},{3,2},{4,5},{5,4},{6,7},{7,6},{8,9},{9,8},{10,11... | collective-permute-start | bytes 884744 | tf_op jit(solution)/shard_map/ppermute | solution.py:44
  174.2 16.3 %collective-permute-start.34 = (f32[16,768]{1,0:T(8,128)S(1)}, f32[16,768]{1,0:T(8,128)S(1)}, u32[]{:S(2)}, u32[]{:S(2)}) collective-permute-start(f32[16,768]{1,0:T(8,128)S(1)} %add.358), channel_id=1, source_target_pairs={{0,1},{1,0},{2,3},{3,2},{4,5},{5,4},{6,7},{7,6},{8,9},{9,8},{10,11... | collective-permute-start | bytes 147464 | tf_op jit(solution)/shard_map/ppermute | solution.py:44
  175.6 23.4 %collective-permute-start.40 = (bf16[48,2304]{1,0:T(8,128)(2,1)S(1)}, bf16[48,2304]{1,0:T(8,128)(2,1)S(1)}, u32[]{:S(2)}, u32[]{:S(2)}) collective-permute-start(bf16[48,2304]{1,0:T(8,128)(2,1)S(1)} %get-tuple-element.255), channel_id=1, source_target_pairs={{0,1},{1,0},{2,3},{3,2},{4,5},{5,4},{6,7},{7,6},{8,9},{9,8},{10,11... | collective-permute-start | bytes 663560 | tf_op jit(solution)/shard_map/ppermute | solution.py:44
  191.1 17.5 %collective-permute-start.43 = (bf16[48,3840]{1,0:T(8,128)(2,1)S(1)}, bf16[48,3840]{1,0:T(8,128)(2,1)S(1)}, u32[]{:S(2)}, u32[]{:S(2)}) collective-permute-start(bf16[48,3840]{1,0:T(8,128)(2,1)S(1)} %add_convert_fusion.6), channel_id=1, source_target_pairs={{0,1},{1,0},{2,3},{3,2},{4,5},{5,4},{6,7},{7,6},{8,9},{9,8},{10,11... | collective-permute-start | bytes 1105928 | tf_op jit(solution)/shard_map/ppermute | solution.py:44
  199.1 9.4 %collective-permute-start.41 = (bf16[48,2304]{1,0:T(8,128)(2,1)S(1)}, bf16[48,2304]{1,0:T(8,128)(2,1)S(1)}, u32[]{:S(2)}, u32[]{:S(2)}) collective-permute-start(bf16[48,2304]{1,0:T(8,128)(2,1)S(1)} %add_convert_fusion.11), channel_id=1, source_target_pairs={{0,2},{1,3},{2,0},{3,1},{4,6},{5,7},{6,4},{7,5},{8,10},{9,11},{10,... | collective-permute-start | bytes 663560 | tf_op jit(solution)/shard_map/ppermute | solution.py:44
  (54 other events, 326.7 us)

commit v4 on v3

--- a/solution.py
+++ b/solution.py
@@ -58,12 +58,12 @@
 class SmallSum:
     def __init__(self, block, paired=True):
         self.block, self.rounds = block, []
+        if not paired:
+            self.rounds = [(axis, [bit]) for axis in ("blk", "dp") for bit in bits_of(axis)]
+            return
         for axis in ("dp", "blk"):
             bits = bits_of(axis)
-            odd = len(bits) % 2 if paired else len(bits)
-            if not paired:
-                self.rounds += [(axis, [bit]) for bit in bits]
-                continue
+            odd = len(bits) % 2
             parts = [bits[:odd]] * odd + [bits[i : i + 2] for i in range(odd, len(bits), 2)]
             self.rounds += [(axis, part) for part in parts]
 
@@ -750,6 +750,8 @@
     )
     rounds = SmallSum(totals)
     rounds.send()
+    rounds.take()
+    rounds.send()
     tied = together(*rounds.arrived, table, column_start, vectors, *lows)
     ways = len(rounds.arrived)
     rounds.arrived = list(tied[:ways])
@@ -926,7 +928,7 @@
             launch(first)
     query_low, key_low, value_low, attend_rows = zip(*back)
     grads = [*query_low, *key_low, *value_low]
-    advance(first)
+    (expand_in,) = after(expand_in)
 
     grads = after(*grads)
     parts, own_part = call(
@@ -940,6 +942,7 @@
     to_left, to_right = parts[0], parts[2 * reach - 1]
     token[:] = [to_left, to_right]
     from_right, from_left = moved(to_left, "blk", -1), moved(to_right, "blk", 1)
+    advance(first)
 
     kept_inlet = struct((features // 2, wkv), bf16)
     grads = after(*grads)
@@ -1035,7 +1038,9 @@
         + grad_centre / total_tokens
         + 2.0 * grad_variance * raw / total_tokens
     ).reshape(sequences, block_length, features)
-    vector_share = lax.dynamic_slice_in_dim(small[:12], column_start, column_count, 1)
+    vector_share = lax.dynamic_slice(
+        small[:12], (0, column_start), (12, column_count), allow_negative_indices=False
+    )
 
     updates = []
     for master, moment, square, share in (

time: 217 us -> 194 us (0.89)
  other arithmetic: 26.2 us -> 16.5 us
  waiting for transfers between devices: 72.5 us -> 64.8 us
  local copies, waits for them, and re-layouts: 6.97 us -> 4.07 us
  Pallas kernels: 42.6 us -> 39.7 us
    ppermute x36, waiting for transfers between devices: 58.9 us -> 46.5 us  [flipped(): return lax.ppermute(block, axis, [(i, i ^ bit) for i in range(size)])]
    convert_element_type x6, other arithmetic: 6.66 us -> 1.62 us  [summed(): return total.astype(bf16)]
    ppermute x8, waiting for transfers between devices: 13.6 us -> 18.3 us  [moved(): return lax.ppermute(block, axis, route)]
    select_n x3, other arithmetic: 4.9 us -> 1.03 us  [__init__(): self.sent = jnp.where(lows[0], second, first)]
    pallas_call x13, Pallas kernels: 42.6 us -> 39.7 us  [call(): pl.pallas_call(kernel, grid_spec=pltpu.PrefetchScalarGridSpec(num_scalar_...]
    unnamed x84 -> x56, local copies, waits for them, and re-layouts: 6.85 us -> 3.94 us
  transfers between devices with their start and end apart: 44 -> 44, of which waited for: 20 -> 21; matrix products, arithmetic and copies ran while one was open for 11% -> 7% of each run, Pallas kernels for 10% -> 10%
where the time goes in v4:
time: 194 us; the launch traced here: 193 us
  starting transfers between devices  66.1 us (34%)
  waiting for transfers between devices  64.8 us (33%)
  Pallas kernels  39.7 us (20%)
  other arithmetic  16.5 us (9%)
  local copies, waits for them, and re-layouts  4.07 us (2%)
  between operations  2.04 us (1%)
    ppermute x36, waiting for transfers between devices, flipped(): return lax.ppermute(block, axis, [(i, i ^ bit) for i in range(size)])  46.5 us
    ppermute x36, starting transfers between devices, flipped(): return lax.ppermute(block, axis, [(i, i ^ bit) for i in range(size)])  43.1 us
    pallas_call x13, Pallas kernels, call(): pl.pallas_call(kernel, grid_spec=pltpu.PrefetchScalarGridSpec(num_scalar_...  39.7 us
    ppermute x8, starting transfers between devices, moved(): return lax.ppermute(block, axis, route)  23 us
    ppermute x8, waiting for transfers between devices, moved(): return lax.ppermute(block, axis, route)  18.3 us
    convert_element_type x5, other arithmetic, adam_rule(): return (weight_new, moment_new, square_new, weight_new.astype(bf16))  8.97 us
    unnamed x56, local copies, waits for them, and re-layouts  3.94 us
  transfers between devices with their start and end apart: 44, of which 21 were waited for; matrix products, arithmetic and copies ran while one was open for 7% of the time, Pallas kernels for 10%

profile of v4, /device:TPU:0, one launch (start us, length us, event | category | flops | bytes accessed | tf_op | source)
XLA Modules:
  0.0 193.3 jit_solution(3476779485793326051)
XLA Ops:
  3.3 2.8 %collective-permute-start.1 = (f32[2,768]{1,0:T(2,128)S(1)}, f32[2,768]{1,0:T(2,128)S(1)}, u32[]{:S(2)}, u32[]{:S(2)}) collective-permute-start(f32[2,768]{1,0:T(2,128)S(1)} %add.302), channel_id=1, source_target_pairs={{0,8},{4,12},{8,0},{12,4},{16,24},{20,28},{24,16},{28,20},{1,9},{5... | collective-permute-start | bytes 18440 | tf_op jit(solution)/shard_map/ppermute | solution.py:44
  9.7 2.4 %collective-permute-done.3 = f32[2,768]{1,0:T(2,128)S(1)} collective-permute-done((f32[2,768]{1,0:T(2,128)S(1)}, f32[2,768]{1,0:T(2,128)S(1)}, u32[]{:S(2)}, u32[]{:S(2)}) %collective-permute-start.3) | collective-permute-done | bytes 6176 | tf_op jit(solution)/shard_map/ppermute | solution.py:44
  12.2 2.7 %collective-permute-start.5 = (f32[2,768]{1,0:T(2,128)S(1)}, f32[2,768]{1,0:T(2,128)S(1)}, u32[]{:S(2)}, u32[]{:S(2)}) collective-permute-start(f32[2,768]{1,0:T(2,128)S(1)} %add_add_fusion.1), channel_id=1, source_target_pairs={{0,2},{1,3},{2,0},{3,1},{4,6},{5,7},{6,4},{7,5},{8,10},{9,11},{10,... | collective-permute-start | bytes 18440 | tf_op jit(solution)/shard_map/ppermute | solution.py:44
  16.8 3.4 %collective-permute-done.6 = f32[2,768]{1,0:T(2,128)S(1)} collective-permute-done((f32[2,768]{1,0:T(2,128)S(1)}, f32[2,768]{1,0:T(2,128)S(1)}, u32[]{:S(2)}, u32[]{:S(2)}) %collective-permute-start.6) | collective-permute-done | bytes 6176 | tf_op jit(solution)/shard_map/ppermute | solution.py:44
  29.7 4.1 %collective-permute-done.8.xb_ref.refs_3_ = bf16[272,768]{1,0:T(8,128)(2,1)S(1)} collective-permute-done((bf16[272,768]{1,0:T(8,128)(2,1)S(1)}, bf16[272,768]{1,0:T(8,128)(2,1)S(1)}, u32[]{:S(2)}, u32[]{:S(2)}) %collective-permute-start.8) | collective-permute-done | bytes 417824 | tf_op jit(solution)/shard_map/ppermute | solution.py:50
  33.8 3.6 %collective-permute-start.9 = (bf16[272,768]{1,0:T(8,128)(2,1)S(1)}, bf16[272,768]{1,0:T(8,128)(2,1)S(1)}, u32[]{:S(2)}, u32[]{:S(2)}) collective-permute-start(bf16[272,768]{1,0:T(8,128)(2,1)S(1)} %collective-permute-done.7.xa_ref.refs_1_), channel_id=1, source_target_pairs={{0,1},{1,2},{2,3},{4,5},{5,6},{6,7},{8,9},{9,10},{10,11},{12,13},{... | collective-permute-start | bytes 1253384 | tf_op jit(solution)/shard_map/ppermute | solution.py:50
  40.3 2.6 %collective-permute-done.9.xa_ref.refs_0_ = bf16[272,768]{1,0:T(8,128)(2,1)S(1)} collective-permute-done((bf16[272,768]{1,0:T(8,128)(2,1)S(1)}, bf16[272,768]{1,0:T(8,128)(2,1)S(1)}, u32[]{:S(2)}, u32[]{:S(2)}) %collective-permute-start.9) | collective-permute-done | bytes 417824 | tf_op jit(solution)/shard_map/ppermute | solution.py:50
  42.9 4.4 %collective-permute-done.10.xb_ref.refs_4_ = bf16[272,768]{1,0:T(8,128)(2,1)S(1)} collective-permute-done((bf16[272,768]{1,0:T(8,128)(2,1)S(1)}, bf16[272,768]{1,0:T(8,128)(2,1)S(1)}, u32[]{:S(2)}, u32[]{:S(2)}) %collective-permute-start.10) | collective-permute-done | bytes 417824 | tf_op jit(solution)/shard_map/ppermute | solution.py:50
  48.2 5.3 %attend.1 = (bf16[256,768]{1,0:T(8,128)(2,1)S(1)}, f32[3,4,256]{2,1,0:T(4,128)S(1)}, s32[2]{0:T(128)S(1)}) custom-call(s32[28]{0:T(128)S(1)} %pad_add_fusion.table, bf16[256,768]{1,0:T(8,128)(2,1)S(1)} %get-tuple-element.136.q_ref, bf16[5,256,1536]{2,1,0:T(8,128)(2,1)S(1)} %get-tuple-element.146.kv_ref, s32[1,256]{1,0:T(1,128)S(1)} %copy-done.6, ...), custom_call_target="tpu_custom_call" | custom-call | flops 1048576 | bytes 65536 | tf_op jit(solution)/shard_map/attend/pallas_call | solution.py:159
  53.6 13.1 %ffn.1 = (bf16[256,768]{1,0:T(8,128)(2,1)}, f32[256,768]{1,0:T(8,128)S(1)}, bf16[256,768]{1,0:T(8,128)(2,1)S(1)}, bf16[2,4,192,768]{3,2,1,0:T(8,128)(2,1)S(1)}, ...) custom-call(s32[28]{0:T(128)S(1)} %pad_add_fusion.table, ...), custom_call_target="tpu_custom_call" | custom-call | flops 1048576 | bytes 65536 | tf_op jit(solution)/shard_map/ffn/pallas_call | solution.py:159
  67.2 2.8 %attend_back.3 = (bf16[256,256]{1,0:T(8,128)(2,1)S(1)}, bf16[5,256,256]{2,1,0:T(8,128)(2,1)S(1)}, bf16[5,256,256]{2,1,0:T(8,128)(2,1)S(1)}, f32[2,256]{1,0:T(2,128)S(1)}) custom-call(s32[2]{0:T(128)S(1)} %get-tuple-element.153.bounds.refs_5_, bf16[256,768]{1,0:T(8,128)(2,1)S(1)} %get-tuple-element.136.q_ref, ...), custom_call_target="tpu_custom_call" | custom-call | flops 1048576 | bytes 65536 | tf_op jit(solution)/shard_map/attend_back/pallas_call | solution.py:159
  71.6 3.1 %collective-permute-start.15 = (bf16[2,192,768]{2,1,0:T(8,128)(2,1)S(1)}, bf16[2,192,768]{2,1,0:T(8,128)(2,1)S(1)}, u32[]{:S(2)}, u32[]{:S(2)}) collective-permute-start(bf16[2,192,768]{2,1,0:T(8,128)(2,1)S(1)} %get-tuple-element.277), channel_id=1, source_target_pairs={{0,8},{4,12},{8,0},{12,4},{16,24},{20,28},{24,16},{28,20},{1,9},{5... | collective-permute-start | bytes 1769480 | tf_op jit(solution)/shard_map/ppermute | solution.py:44
  74.7 2.7 %attend_back.4 = (bf16[256,256]{1,0:T(8,128)(2,1)S(1)}, bf16[5,256,256]{2,1,0:T(8,128)(2,1)S(1)}, bf16[5,256,256]{2,1,0:T(8,128)(2,1)S(1)}, f32[2,256]{1,0:T(2,128)S(1)}) custom-call(s32[2]{0:T(128)S(1)} %get-tuple-element.153.bounds.refs_5_, bf16[256,768]{1,0:T(8,128)(2,1)S(1)} %get-tuple-element.136.q_ref, ...), custom_call_target="tpu_custom_call" | custom-call | flops 1048576 | bytes 65536 | tf_op jit(solution)/shard_map/attend_back/pallas_call | solution.py:159
  77.4 2.7 %attend_back.5 = (bf16[256,256]{1,0:T(8,128)(2,1)S(1)}, bf16[5,256,256]{2,1,0:T(8,128)(2,1)S(1)}, bf16[5,256,256]{2,1,0:T(8,128)(2,1)S(1)}, f32[2,256]{1,0:T(2,128)S(1)}) custom-call(s32[2]{0:T(128)S(1)} %get-tuple-element.153.bounds.refs_5_, bf16[256,768]{1,0:T(8,128)(2,1)S(1)} %get-tuple-element.136.q_ref, ...), custom_call_target="tpu_custom_call" | custom-call | flops 1048576 | bytes 65536 | tf_op jit(solution)/shard_map/attend_back/pallas_call | solution.py:159
  80.1 2.6 %parts.1 = (bf16[4,256,768]{2,1,0:T(8,128)(2,1)S(1)}, f32[256,768]{1,0:T(8,128)S(1)}) custom-call(s32[2]{0:T(128)S(1)} %get-tuple-element.153.bounds.refs_5_, bf16[256,256]{1,0:T(8,128)(2,1)S(1)} %get-tuple-element.186.refs_0_.refs_6_, bf16[256,256]{1,0:T(8,128)(2,1)S(1)} %get-tuple-element.187.refs_1_.refs_7_, ...), custom_call_target="tpu_custom_call" | custom-call | flops 1048576 | bytes 65536 | tf_op jit(solution)/shard_map/parts/pallas_call | solution.py:159
  82.8 5.6 %collective-permute-done.15 = bf16[2,192,768]{2,1,0:T(8,128)(2,1)S(1)} collective-permute-done((bf16[2,192,768]{2,1,0:T(8,128)(2,1)S(1)}, bf16[2,192,768]{2,1,0:T(8,128)(2,1)S(1)}, u32[]{:S(2)}, u32[]{:S(2)}) %collective-permute-start.15) | collective-permute-done | bytes 589856 | tf_op jit(solution)/shard_map/ppermute | solution.py:44
  92.0 6.1 %collective-permute-start.14 = (bf16[256,768]{1,0:T(8,128)(2,1)S(1)}, bf16[256,768]{1,0:T(8,128)(2,1)S(1)}, u32[]{:S(2)}, u32[]{:S(2)}) collective-permute-start(bf16[256,768]{1,0:T(8,128)(2,1)S(1)} %get-tuple-element.284), channel_id=1, source_target_pairs={{0,1},{1,2},{2,3},{4,5},{5,6},{6,7},{8,9},{9,10},{10,11},{12,13},{... | collective-permute-start | bytes 1179656 | tf_op jit(solution)/shard_map/ppermute | solution.py:50
  98.2 4.2 %weights.1 = (bf16[384,2304]{1,0:T(8,128)(2,1)S(1)}, bf16[384,2304]{1,0:T(8,128)(2,1)S(1)}) custom-call(s32[28]{0:T(128)S(1)} %pad_add_fusion.table, bf16[272,768]{1,0:T(8,128)(2,1)S(1)} %collective-permute-done.9.xa_ref.refs_0_, bf16[272,768]{1,0:T(8,128)(2,1)S(1)} %collective-permute-done.7.xa_ref.refs_1_, ...), custom_call_target="tpu_custom_call" | custom-call | flops 1048576 | bytes 65536 | tf_op jit(solution)/shard_map/weights/pallas_call | solution.py:159
  106.4 6.4 %collective-permute-start.20 = (bf16[256,768]{1,0:T(8,128)(2,1)S(1)}, bf16[256,768]{1,0:T(8,128)(2,1)S(1)}, u32[]{:S(2)}, u32[]{:S(2)}) collective-permute-start(bf16[256,768]{1,0:T(8,128)(2,1)S(1)} %get-tuple-element.282), channel_id=1, source_target_pairs={{0,1},{1,2},{2,3},{4,5},{5,6},{6,7},{8,9},{9,10},{10,11},{12,13},{... | collective-permute-start | bytes 1179656 | tf_op jit(solution)/shard_map/ppermute | solution.py:50
  113.9 5.9 %collective-permute-done.19.right_ref = bf16[256,768]{1,0:T(8,128)(2,1)S(1)} collective-permute-done((bf16[256,768]{1,0:T(8,128)(2,1)S(1)}, bf16[256,768]{1,0:T(8,128)(2,1)S(1)}, u32[]{:S(2)}, u32[]{:S(2)}) %collective-permute-start.19) | collective-permute-done | bytes 393248 | tf_op jit(solution)/shard_map/ppermute | solution.py:50
  129.8 3.0 %collective-permute-start.25 = (f32[16,768]{1,0:T(8,128)S(1)}, f32[16,768]{1,0:T(8,128)S(1)}, u32[]{:S(2)}, u32[]{:S(2)}) collective-permute-start(f32[16,768]{1,0:T(8,128)S(1)} %add.340), channel_id=1, source_target_pairs={{0,2},{1,3},{2,0},{3,1},{4,6},{5,7},{6,4},{7,5},{8,10},{9,11},{10,... | collective-permute-start | bytes 147464 | tf_op jit(solution)/shard_map/ppermute | solution.py:44
  132.9 4.0 %collective-permute-done.26 = bf16[48,3840]{1,0:T(8,128)(2,1)S(1)} collective-permute-done((bf16[48,3840]{1,0:T(8,128)(2,1)S(1)}, bf16[48,3840]{1,0:T(8,128)(2,1)S(1)}, u32[]{:S(2)}, u32[]{:S(2)}) %collective-permute-start.26) | collective-permute-done | bytes 368672 | tf_op jit(solution)/shard_map/ppermute | solution.py:44
  137.0 2.9 %collective-permute-start.30 = (bf16[192,768]{1,0:T(8,128)(2,1)S(1)}, bf16[192,768]{1,0:T(8,128)(2,1)S(1)}, u32[]{:S(2)}, u32[]{:S(2)}) collective-permute-start(bf16[192,768]{1,0:T(8,128)(2,1)S(1)} %add_convert_fusion.9), channel_id=1, source_target_pairs={{0,2},{1,3},{2,0},{3,1},{4,6},{5,7},{6,4},{7,5},{8,10},{9,11},{10,... | collective-permute-start | bytes 884744 | tf_op jit(solution)/shard_map/ppermute | solution.py:44
  140.6 3.6 %collective-permute-done.32 = bf16[2,48,2304]{2,1,0:T(8,128)(2,1)S(1)} collective-permute-done((bf16[2,48,2304]{2,1,0:T(8,128)(2,1)S(1)}, bf16[2,48,2304]{2,1,0:T(8,128)(2,1)S(1)}, u32[]{:S(2)}, u32[]{:S(2)}) %collective-permute-start.32) | collective-permute-done | bytes 442400 | tf_op jit(solution)/shard_map/ppermute | solution.py:44
  146.5 4.0 %collective-permute-done.31 = bf16[48,3840]{1,0:T(8,128)(2,1)S(1)} collective-permute-done((bf16[48,3840]{1,0:T(8,128)(2,1)S(1)}, bf16[48,3840]{1,0:T(8,128)(2,1)S(1)}, u32[]{:S(2)}, u32[]{:S(2)}) %collective-permute-start.31) | collective-permute-done | bytes 368672 | tf_op jit(solution)/shard_map/ppermute | solution.py:44
  152.6 2.5 %collective-permute-start.39 = (bf16[192,768]{1,0:T(8,128)(2,1)S(1)}, bf16[192,768]{1,0:T(8,128)(2,1)S(1)}, u32[]{:S(2)}, u32[]{:S(2)}) collective-permute-start(bf16[192,768]{1,0:T(8,128)(2,1)S(1)} %add_convert_fusion.8), channel_id=1, source_target_pairs={{0,1},{1,0},{2,3},{3,2},{4,5},{5,4},{6,7},{7,6},{8,9},{9,8},{10,11... | collective-permute-start | bytes 884744 | tf_op jit(solution)/shard_map/ppermute | solution.py:44
  156.2 3.1 %collective-permute-done.34 = f32[16,768]{1,0:T(8,128)S(1)} collective-permute-done((f32[16,768]{1,0:T(8,128)S(1)}, f32[16,768]{1,0:T(8,128)S(1)}, u32[]{:S(2)}, u32[]{:S(2)}) %collective-permute-start.34) | collective-permute-done | bytes 49184 | tf_op jit(solution)/shard_map/ppermute | solution.py:44
  160.7 6.8 %collective-permute-done.38 = bf16[48,3840]{1,0:T(8,128)(2,1)S(1)} collective-permute-done((bf16[48,3840]{1,0:T(8,128)(2,1)S(1)}, bf16[48,3840]{1,0:T(8,128)(2,1)S(1)}, u32[]{:S(2)}, u32[]{:S(2)}) %collective-permute-start.38) | collective-permute-done | bytes 368672 | tf_op jit(solution)/shard_map/ppermute | solution.py:44
  174.6 2.5 %fusion.36 = (bf16[384,768]{1,0:T(8,128)(2,1)}, f32[384,768]{1,0:T(8,128)}, f32[384,768]{1,0:T(8,128)}, f32[384,768]{1,0:T(8,128)}) fusion(f32[384,768]{1,0:T(8,128)S(1)} %copy-done.8, f32[]{:T(128)} %bitcast.36, f32[]{:T(128)} %bitcast.35, f32[]{:T(128)} %bitcast.34, bf16[192,768]{1,0:T(8,128)(2,1)S(1)} %get-tuple-element.289, ...), kind=kLoop, calls=%fused_computation.110 | loop fusion | flops 5603328 | bytes 8257548 | tf_op jit(solution)/shard_map/convert_element_type | solution.py:665
  177.1 5.4 %collective-permute-done.41 = bf16[48,2304]{1,0:T(8,128)(2,1)S(1)} collective-permute-done((bf16[48,2304]{1,0:T(8,128)(2,1)S(1)}, bf16[48,2304]{1,0:T(8,128)(2,1)S(1)}, u32[]{:S(2)}, u32[]{:S(2)}) %collective-permute-start.41) | collective-permute-done | bytes 221216 | tf_op jit(solution)/shard_map/ppermute | solution.py:44
  182.6 3.3 %collective-permute-start.42 = (bf16[48,2304]{1,0:T(8,128)(2,1)S(1)}, bf16[48,2304]{1,0:T(8,128)(2,1)S(1)}, u32[]{:S(2)}, u32[]{:S(2)}) collective-permute-start(bf16[48,2304]{1,0:T(8,128)(2,1)S(1)} %add_convert_fusion.10), channel_id=1, source_target_pairs={{0,1},{1,0},{2,3},{3,2},{4,5},{5,4},{6,7},{7,6},{8,9},{9,8},{10,11... | collective-permute-start | bytes 663560 | tf_op jit(solution)/shard_map/ppermute | solution.py:44
  186.1 2.6 %fusion.39 = (bf16[96,3072]{1,0:T(8,128)(2,1)}, f32[96,3072]{1,0:T(8,128)}, f32[96,3072]{1,0:T(8,128)}, f32[96,3072]{1,0:T(8,128)}) fusion(f32[96,3072]{1,0:T(8,128)S(1)} %copy-done.11, f32[]{:T(128)} %bitcast.36, f32[]{:T(128)} %bitcast.35, f32[]{:T(128)} %bitcast.34, bf16[48,3840]{1,0:T(8,128)(2,1)S(1)} %get-tuple-element.287, ...), kind=kLoop, calls=%fused_computation.111 | loop fusion | flops 5603328 | bytes 8405004 | tf_op jit(solution)/shard_map/convert_element_type | solution.py:665
  (169 shorter events, 60.8 us)
Async XLA Ops:
  23.5 10.3 %collective-permute-start.8 = (bf16[272,768]{1,0:T(8,128)(2,1)S(1)}, bf16[272,768]{1,0:T(8,128)(2,1)S(1)}, u32[]{:S(2)}, u32[]{:S(2)}) collective-permute-start(bf16[272,768]{1,0:T(8,128)(2,1)S(1)} %get-tuple-element.134.x_ref.refs_2_), channel_id=1, source_target_pairs={{1,0},{2,1},{3,2},{5,4},{6,5},{7,6},{9,8},{10,9},{11,10},{13,12},{... | collective-permute-start | bytes 1253384 | tf_op jit(solution)/shard_map/ppermute | solution.py:50
  33.8 9.1 %collective-permute-start.9 = (bf16[272,768]{1,0:T(8,128)(2,1)S(1)}, bf16[272,768]{1,0:T(8,128)(2,1)S(1)}, u32[]{:S(2)}, u32[]{:S(2)}) collective-permute-start(bf16[272,768]{1,0:T(8,128)(2,1)S(1)} %collective-permute-done.7.xa_ref.refs_1_), channel_id=1, source_target_pairs={{0,1},{1,2},{2,3},{4,5},{5,6},{6,7},{8,9},{9,10},{10,11},{12,13},{... | collective-permute-start | bytes 1253384 | tf_op jit(solution)/shard_map/ppermute | solution.py:50
  37.4 9.9 %collective-permute-start.10 = (bf16[272,768]{1,0:T(8,128)(2,1)S(1)}, bf16[272,768]{1,0:T(8,128)(2,1)S(1)}, u32[]{:S(2)}, u32[]{:S(2)}) collective-permute-start(bf16[272,768]{1,0:T(8,128)(2,1)S(1)} %collective-permute-done.8.xb_ref.refs_3_), channel_id=1, source_target_pairs={{1,0},{2,1},{3,2},{5,4},{6,5},{7,6},{9,8},{10,9},{11,10},{13,12},{... | collective-permute-start | bytes 1253384 | tf_op jit(solution)/shard_map/ppermute | solution.py:50
  66.7 13.4 %collective-permute-start.12 = (bf16[384,3840]{1,0:T(8,128)(2,1)S(1)}, bf16[384,3840]{1,0:T(8,128)(2,1)S(1)}, u32[]{:S(2)}, u32[]{:S(2)}) collective-permute-start(bf16[384,3840]{1,0:T(8,128)(2,1)S(1)} %get-tuple-element.170), channel_id=1, source_target_pairs={{0,4},{4,0},{8,12},{12,8},{16,20},{20,16},{24,28},{28,24},{1,5},{5... | collective-permute-start | bytes 8847368 | tf_op jit(solution)/shard_map/ppermute | solution.py:44
  71.6 16.8 %collective-permute-start.15 = (bf16[2,192,768]{2,1,0:T(8,128)(2,1)S(1)}, bf16[2,192,768]{2,1,0:T(8,128)(2,1)S(1)}, u32[]{:S(2)}, u32[]{:S(2)}) collective-permute-start(bf16[2,192,768]{2,1,0:T(8,128)(2,1)S(1)} %get-tuple-element.277), channel_id=1, source_target_pairs={{0,8},{4,12},{8,0},{12,4},{16,24},{20,28},{24,16},{28,20},{1,9},{5... | collective-permute-start | bytes 1769480 | tf_op jit(solution)/shard_map/ppermute | solution.py:44
  74.7 15.1 %collective-permute-start.16 = (bf16[2,192,768]{2,1,0:T(8,128)(2,1)S(1)}, bf16[2,192,768]{2,1,0:T(8,128)(2,1)S(1)}, u32[]{:S(2)}, u32[]{:S(2)}) collective-permute-start(bf16[2,192,768]{2,1,0:T(8,128)(2,1)S(1)} %get-tuple-element.276), channel_id=1, source_target_pairs={{0,16},{4,20},{8,24},{12,28},{16,0},{20,4},{24,8},{28,12},{1,17},{... | collective-permute-start | bytes 1769480 | tf_op jit(solution)/shard_map/ppermute | solution.py:44
  90.0 12.4 %collective-permute-start.17 = (bf16[192,768]{1,0:T(8,128)(2,1)S(1)}, bf16[192,768]{1,0:T(8,128)(2,1)S(1)}, u32[]{:S(2)}, u32[]{:S(2)}) collective-permute-start(bf16[192,768]{1,0:T(8,128)(2,1)S(1)} %get-tuple-element.275), channel_id=1, source_target_pairs={{0,16},{4,20},{8,24},{12,28},{16,0},{20,4},{24,8},{28,12},{1,17},{... | collective-permute-start | bytes 884744 | tf_op jit(solution)/shard_map/ppermute | solution.py:44
  90.4 12.1 %collective-permute-start.18 = (bf16[192,768]{1,0:T(8,128)(2,1)S(1)}, bf16[192,768]{1,0:T(8,128)(2,1)S(1)}, u32[]{:S(2)}, u32[]{:S(2)}) collective-permute-start(bf16[192,768]{1,0:T(8,128)(2,1)S(1)} %get-tuple-element.274), channel_id=1, source_target_pairs={{0,8},{4,12},{8,0},{12,4},{16,24},{20,28},{24,16},{28,20},{1,9},{5... | collective-permute-start | bytes 884744 | tf_op jit(solution)/shard_map/ppermute | solution.py:44
  90.7 14.1 %collective-permute-start.13 = (bf16[256,768]{1,0:T(8,128)(2,1)S(1)}, bf16[256,768]{1,0:T(8,128)(2,1)S(1)}, u32[]{:S(2)}, u32[]{:S(2)}) collective-permute-start(bf16[256,768]{1,0:T(8,128)(2,1)S(1)} %get-tuple-element.285), channel_id=1, source_target_pairs={{1,0},{2,1},{3,2},{5,4},{6,5},{7,6},{9,8},{10,9},{11,10},{13,12},{... | collective-permute-start | bytes 1179656 | tf_op jit(solution)/shard_map/ppermute | solution.py:50
  92.0 12.8 %collective-permute-start.14 = (bf16[256,768]{1,0:T(8,128)(2,1)S(1)}, bf16[256,768]{1,0:T(8,128)(2,1)S(1)}, u32[]{:S(2)}, u32[]{:S(2)}) collective-permute-start(bf16[256,768]{1,0:T(8,128)(2,1)S(1)} %get-tuple-element.284), channel_id=1, source_target_pairs={{0,1},{1,2},{2,3},{4,5},{5,6},{6,7},{8,9},{9,10},{10,11},{12,13},{... | collective-permute-start | bytes 1179656 | tf_op jit(solution)/shard_map/ppermute | solution.py:50
  102.3 23.9 %collective-permute-start.22 = (bf16[384,2304]{1,0:T(8,128)(2,1)S(1)}, bf16[384,2304]{1,0:T(8,128)(2,1)S(1)}, u32[]{:S(2)}, u32[]{:S(2)}) collective-permute-start(bf16[384,2304]{1,0:T(8,128)(2,1)S(1)} %get-tuple-element.210), channel_id=1, source_target_pairs={{0,4},{4,0},{8,12},{12,8},{16,20},{20,16},{24,28},{28,24},{1,5},{5... | collective-permute-start | bytes 5308424 | tf_op jit(solution)/shard_map/ppermute | solution.py:44
  102.8 22.3 %collective-permute-start.23 = (bf16[2,48,3840]{2,1,0:T(8,128)(2,1)S(1)}, bf16[2,48,3840]{2,1,0:T(8,128)(2,1)S(1)}, u32[]{:S(2)}, u32[]{:S(2)}) collective-permute-start(bf16[2,48,3840]{2,1,0:T(8,128)(2,1)S(1)} %bitcast.95), channel_id=1, source_target_pairs={{0,8},{4,12},{8,0},{12,4},{16,24},{20,28},{24,16},{28,20},{1,9},{5... | collective-permute-start | bytes 2211848 | tf_op jit(solution)/shard_map/ppermute | solution.py:44
  104.6 20.5 %collective-permute-start.24 = (bf16[2,48,3840]{2,1,0:T(8,128)(2,1)S(1)}, bf16[2,48,3840]{2,1,0:T(8,128)(2,1)S(1)}, u32[]{:S(2)}, u32[]{:S(2)}) collective-permute-start(bf16[2,48,3840]{2,1,0:T(8,128)(2,1)S(1)} %bitcast.94), channel_id=1, source_target_pairs={{0,16},{4,20},{8,24},{12,28},{16,0},{20,4},{24,8},{28,12},{1,17},{... | collective-permute-start | bytes 2211848 | tf_op jit(solution)/shard_map/ppermute | solution.py:44
  105.1 14.7 %collective-permute-start.19 = (bf16[256,768]{1,0:T(8,128)(2,1)S(1)}, bf16[256,768]{1,0:T(8,128)(2,1)S(1)}, u32[]{:S(2)}, u32[]{:S(2)}) collective-permute-start(bf16[256,768]{1,0:T(8,128)(2,1)S(1)} %get-tuple-element.283), channel_id=1, source_target_pairs={{1,0},{2,1},{3,2},{5,4},{6,5},{7,6},{9,8},{10,9},{11,10},{13,12},{... | collective-permute-start | bytes 1179656 | tf_op jit(solution)/shard_map/ppermute | solution.py:50
  106.4 15.2 %collective-permute-start.20 = (bf16[256,768]{1,0:T(8,128)(2,1)S(1)}, bf16[256,768]{1,0:T(8,128)(2,1)S(1)}, u32[]{:S(2)}, u32[]{:S(2)}) collective-permute-start(bf16[256,768]{1,0:T(8,128)(2,1)S(1)} %get-tuple-element.282), channel_id=1, source_target_pairs={{0,1},{1,2},{2,3},{4,5},{5,6},{6,7},{8,9},{9,10},{10,11},{12,13},{... | collective-permute-start | bytes 1179656 | tf_op jit(solution)/shard_map/ppermute | solution.py:50
  119.8 10.0 %collective-permute-start.28 = (bf16[192,768]{1,0:T(8,128)(2,1)S(1)}, bf16[192,768]{1,0:T(8,128)(2,1)S(1)}, u32[]{:S(2)}, u32[]{:S(2)}) collective-permute-start(bf16[192,768]{1,0:T(8,128)(2,1)S(1)} %get-tuple-element.267), channel_id=1, source_target_pairs={{0,1},{1,0},{2,3},{3,2},{4,5},{5,4},{6,7},{7,6},{8,9},{9,8},{10,11... | collective-permute-start | bytes 884744 | tf_op jit(solution)/shard_map/ppermute | solution.py:44
  125.4 11.6 %collective-permute-start.26 = (bf16[48,3840]{1,0:T(8,128)(2,1)S(1)}, bf16[48,3840]{1,0:T(8,128)(2,1)S(1)}, u32[]{:S(2)}, u32[]{:S(2)}) collective-permute-start(bf16[48,3840]{1,0:T(8,128)(2,1)S(1)} %get-tuple-element.271), channel_id=1, source_target_pairs={{0,16},{4,20},{8,24},{12,28},{16,0},{20,4},{24,8},{28,12},{1,17},{... | collective-permute-start | bytes 1105928 | tf_op jit(solution)/shard_map/ppermute | solution.py:44
  125.5 14.4 %collective-permute-start.27 = (bf16[48,3840]{1,0:T(8,128)(2,1)S(1)}, bf16[48,3840]{1,0:T(8,128)(2,1)S(1)}, u32[]{:S(2)}, u32[]{:S(2)}) collective-permute-start(bf16[48,3840]{1,0:T(8,128)(2,1)S(1)} %get-tuple-element.270), channel_id=1, source_target_pairs={{0,8},{4,12},{8,0},{12,4},{16,24},{20,28},{24,16},{28,20},{1,9},{5... | collective-permute-start | bytes 1105928 | tf_op jit(solution)/shard_map/ppermute | solution.py:44
  126.5 17.7 %collective-permute-start.32 = (bf16[2,48,2304]{2,1,0:T(8,128)(2,1)S(1)}, bf16[2,48,2304]{2,1,0:T(8,128)(2,1)S(1)}, u32[]{:S(2)}, u32[]{:S(2)}) collective-permute-start(bf16[2,48,2304]{2,1,0:T(8,128)(2,1)S(1)} %bitcast.97), channel_id=1, source_target_pairs={{0,8},{4,12},{8,0},{12,4},{16,24},{20,28},{24,16},{28,20},{1,9},{5... | collective-permute-start | bytes 1327112 | tf_op jit(solution)/shard_map/ppermute | solution.py:44
  129.1 15.0 %collective-permute-start.33 = (bf16[2,48,2304]{2,1,0:T(8,128)(2,1)S(1)}, bf16[2,48,2304]{2,1,0:T(8,128)(2,1)S(1)}, u32[]{:S(2)}, u32[]{:S(2)}) collective-permute-start(bf16[2,48,2304]{2,1,0:T(8,128)(2,1)S(1)} %bitcast.96), channel_id=1, source_target_pairs={{0,16},{4,20},{8,24},{12,28},{16,0},{20,4},{24,8},{28,12},{1,17},{... | collective-permute-start | bytes 1327112 | tf_op jit(solution)/shard_map/ppermute | solution.py:44
  129.8 10.7 %collective-permute-start.25 = (f32[16,768]{1,0:T(8,128)S(1)}, f32[16,768]{1,0:T(8,128)S(1)}, u32[]{:S(2)}, u32[]{:S(2)}) collective-permute-start(f32[16,768]{1,0:T(8,128)S(1)} %add.340), channel_id=1, source_target_pairs={{0,2},{1,3},{2,0},{3,1},{4,6},{5,7},{6,4},{7,5},{8,10},{9,11},{10,... | collective-permute-start | bytes 147464 | tf_op jit(solution)/shard_map/ppermute | solution.py:44
  137.0 15.5 %collective-permute-start.30 = (bf16[192,768]{1,0:T(8,128)(2,1)S(1)}, bf16[192,768]{1,0:T(8,128)(2,1)S(1)}, u32[]{:S(2)}, u32[]{:S(2)}) collective-permute-start(bf16[192,768]{1,0:T(8,128)(2,1)S(1)} %add_convert_fusion.9), channel_id=1, source_target_pairs={{0,2},{1,3},{2,0},{3,1},{4,6},{5,7},{6,4},{7,5},{8,10},{9,11},{10,... | collective-permute-start | bytes 884744 | tf_op jit(solution)/shard_map/ppermute | solution.py:44
  140.4 10.1 %collective-permute-start.31 = (bf16[48,3840]{1,0:T(8,128)(2,1)S(1)}, bf16[48,3840]{1,0:T(8,128)(2,1)S(1)}, u32[]{:S(2)}, u32[]{:S(2)}) collective-permute-start(bf16[48,3840]{1,0:T(8,128)(2,1)S(1)} %get-tuple-element.264), channel_id=1, source_target_pairs={{0,1},{1,0},{2,3},{3,2},{4,5},{5,4},{6,7},{7,6},{8,9},{9,8},{10,11... | collective-permute-start | bytes 1105928 | tf_op jit(solution)/shard_map/ppermute | solution.py:44
  140.5 14.7 %collective-permute-start.29 = (f32[16,768]{1,0:T(8,128)S(1)}, f32[16,768]{1,0:T(8,128)S(1)}, u32[]{:S(2)}, u32[]{:S(2)}) collective-permute-start(f32[16,768]{1,0:T(8,128)S(1)} %add.348), channel_id=1, source_target_pairs={{0,4},{4,0},{8,12},{12,8},{16,20},{20,16},{24,28},{28,24},{1,5},{5... | collective-permute-start | bytes 147464 | tf_op jit(solution)/shard_map/ppermute | solution.py:44
  144.3 11.5 %collective-permute-start.35 = (bf16[48,2304]{1,0:T(8,128)(2,1)S(1)}, bf16[48,2304]{1,0:T(8,128)(2,1)S(1)}, u32[]{:S(2)}, u32[]{:S(2)}) collective-permute-start(bf16[48,2304]{1,0:T(8,128)(2,1)S(1)} %get-tuple-element.279), channel_id=1, source_target_pairs={{0,16},{4,20},{8,24},{12,28},{16,0},{20,4},{24,8},{28,12},{1,17},{... | collective-permute-start | bytes 663560 | tf_op jit(solution)/shard_map/ppermute | solution.py:44
  146.0 9.9 %collective-permute-start.36 = (bf16[48,2304]{1,0:T(8,128)(2,1)S(1)}, bf16[48,2304]{1,0:T(8,128)(2,1)S(1)}, u32[]{:S(2)}, u32[]{:S(2)}) collective-permute-start(bf16[48,2304]{1,0:T(8,128)(2,1)S(1)} %get-tuple-element.278), channel_id=1, source_target_pairs={{0,8},{4,12},{8,0},{12,4},{16,24},{20,28},{24,16},{28,20},{1,9},{5... | collective-permute-start | bytes 663560 | tf_op jit(solution)/shard_map/ppermute | solution.py:44
  150.7 16.9 %collective-permute-start.38 = (bf16[48,3840]{1,0:T(8,128)(2,1)S(1)}, bf16[48,3840]{1,0:T(8,128)(2,1)S(1)}, u32[]{:S(2)}, u32[]{:S(2)}) collective-permute-start(bf16[48,3840]{1,0:T(8,128)(2,1)S(1)} %add_convert_fusion.7), channel_id=1, source_target_pairs={{0,2},{1,3},{2,0},{3,1},{4,6},{5,7},{6,4},{7,5},{8,10},{9,11},{10,... | collective-permute-start | bytes 1105928 | tf_op jit(solution)/shard_map/ppermute | solution.py:44
  152.6 21.9 %collective-permute-start.39 = (bf16[192,768]{1,0:T(8,128)(2,1)S(1)}, bf16[192,768]{1,0:T(8,128)(2,1)S(1)}, u32[]{:S(2)}, u32[]{:S(2)}) collective-permute-start(bf16[192,768]{1,0:T(8,128)(2,1)S(1)} %add_convert_fusion.8), channel_id=1, source_target_pairs={{0,1},{1,0},{2,3},{3,2},{4,5},{5,4},{6,7},{7,6},{8,9},{9,8},{10,11... | collective-permute-start | bytes 884744 | tf_op jit(solution)/shard_map/ppermute | solution.py:44
  156.1 16.4 %collective-permute-start.40 = (bf16[48,2304]{1,0:T(8,128)(2,1)S(1)}, bf16[48,2304]{1,0:T(8,128)(2,1)S(1)}, u32[]{:S(2)}, u32[]{:S(2)}) collective-permute-start(bf16[48,2304]{1,0:T(8,128)(2,1)S(1)} %get-tuple-element.261), channel_id=1, source_target_pairs={{0,1},{1,0},{2,3},{3,2},{4,5},{5,4},{6,7},{7,6},{8,9},{9,8},{10,11... | collective-permute-start | bytes 663560 | tf_op jit(solution)/shard_map/ppermute | solution.py:44
  159.3 9.1 %collective-permute-start.37 = (f32[16,768]{1,0:T(8,128)S(1)}, f32[16,768]{1,0:T(8,128)S(1)}, u32[]{:S(2)}, u32[]{:S(2)}) collective-permute-start(f32[16,768]{1,0:T(8,128)S(1)} %add.362), channel_id=1, source_target_pairs={{0,16},{4,20},{8,24},{12,28},{16,0},{20,4},{24,8},{28,12},{1,17},{... | collective-permute-start | bytes 147464 | tf_op jit(solution)/shard_map/ppermute | solution.py:44
  167.6 18.3 %collective-permute-start.43 = (bf16[48,3840]{1,0:T(8,128)(2,1)S(1)}, bf16[48,3840]{1,0:T(8,128)(2,1)S(1)}, u32[]{:S(2)}, u32[]{:S(2)}) collective-permute-start(bf16[48,3840]{1,0:T(8,128)(2,1)S(1)} %add_convert_fusion.6), channel_id=1, source_target_pairs={{0,1},{1,0},{2,3},{3,2},{4,5},{5,4},{6,7},{7,6},{8,9},{9,8},{10,11... | collective-permute-start | bytes 1105928 | tf_op jit(solution)/shard_map/ppermute | solution.py:44
  172.6 9.9 %collective-permute-start.41 = (bf16[48,2304]{1,0:T(8,128)(2,1)S(1)}, bf16[48,2304]{1,0:T(8,128)(2,1)S(1)}, u32[]{:S(2)}, u32[]{:S(2)}) collective-permute-start(bf16[48,2304]{1,0:T(8,128)(2,1)S(1)} %add_convert_fusion.11), channel_id=1, source_target_pairs={{0,2},{1,3},{2,0},{3,1},{4,6},{5,7},{6,4},{7,5},{8,10},{9,11},{10,... | collective-permute-start | bytes 663560 | tf_op jit(solution)/shard_map/ppermute | solution.py:44
  (40 other events, 222.5 us)

commit v5 on v4

--- a/solution.py
+++ b/solution.py
@@ -218,9 +218,12 @@
     x_ref[width:, 0:width] = ids
 
 
-def id_columns(x_ref, width):
-    rows = jnp.broadcast_to(x_ref[width : width + 8, 0:width].astype(f32)[0:1], (128, width))
-    return rows.T
+def id_columns(ids, width):
+    return jnp.broadcast_to(ids, (128, width)).T
+
+
+def id_row(rows):
+    return rows.astype(f32)[0:1]
 
 
 def project_own_kernel(table, x_ref, w_ref, vec_ref, q_ref, kv_ref, id_ref):
@@ -231,31 +234,40 @@
     q_ref[...] = ((nn(x, w_ref[:, :features]) + vec_ref[4:5, :]) * score_scale).astype(bf16)
     kv_ref[slot, :, :features] = nn(x, w_ref[:, features : 2 * features]).astype(bf16)
     kv_ref[slot, :, features:] = (nn(x, w_ref[:, 2 * features :]) + vec_ref[5:6, :]).astype(bf16)
-    id_ref[slot] = id_columns(x_ref, width)
-
-
-def project_pair_kernel(d, inside_at, table, xa_ref, xb_ref, x_ref, w_ref, vec_ref, kv_in, id_in, kv_ref, id_ref):
+    id_ref[slot] = id_columns(id_row(x_ref[width : width + 8, 0:width]), width)
+
+
+def project_pair_kernel(
+    d, inside_at, table, xa_ref, xb_ref, x_ref, w_ref, vec_ref, kv_in, id_in, kv_ref, id_ref, both
+):
     width = kv_ref.shape[1]
     features = kv_ref.shape[2] // 2
     reach = kv_ref.shape[0] // 2
     done = slice(reach - d + 1, reach + d)
     kv_ref[done] = kv_in[done]
     id_ref[done] = id_in[done]
-    own = x_ref[width : width + 8, 0:width].astype(f32)[0:1]
+    both[0], both[1] = xa_ref[...], xb_ref[...]
+    own = id_row(x_ref[width : width + 8, 0:width])
     low, high = jnp.min(own), jnp.max(own)
-    for slot, inside, ref in ((reach - d, 0, xa_ref), (reach + d, 1, xb_ref)):
-        ids = ref[width : width + 8, 0:width].astype(f32)[0:1]
-        near = (table[inside_at + inside] > 0) & (jnp.max(ids) >= low) & (jnp.min(ids) <= high)
+
+    def one(i, carry):
+        slot = reach - d + 2 * d * i
+        ids = id_row(both[i, width : width + 8, 0:width])
+        near = (table[inside_at + i] > 0) & (jnp.max(ids) >= low) & (jnp.min(ids) <= high)
         id_ref[slot] = jnp.full((width, 128), -1.0, f32)
 
         @pl.when(near)
-        def _(ref=ref, slot=slot):
-            x = ref[0:width, :]
+        def _():
+            x = both[i, 0:width, :]
             kv_ref[slot, :, :features] = nn(x, w_ref[:, features : 2 * features]).astype(bf16)
             kv_ref[slot, :, features:] = (
                 nn(x, w_ref[:, 2 * features :]) + vec_ref[5:6, :]
             ).astype(bf16)
-            id_ref[slot] = id_columns(ref, width)
+            id_ref[slot] = id_columns(ids, width)
+
+        return carry
+
+    lax.fori_loop(0, 2, one, 0)
 
 
 def lane_half(rows, which):
@@ -424,7 +436,7 @@
         es_ref[:, lanes] = nn(s2t[features // 2 :, :], grad).astype(bf16)
         return carry
 
-    lax.fori_loop(0, half, step, 0)
+    lax.fori_loop(0, half, step, 0, unroll=True)
     out_ref[...] = (middle_s[...] + acc[...] + vec_ref[7:8, :]).astype(bf16)
     unit, scale = unit_rows(middle_s[...])
     grad = gsec[...]
@@ -799,6 +811,7 @@
             table,
             [ahead, behind, x, inlet_copy, vectors, pairs, columns],
             [struct(pairs.shape, bf16), struct(columns.shape, f32)],
+            [vmem((2, packed, features), bf16)],
             mib=6,
         )
 
@@ -1014,17 +1027,16 @@
     line_three = begin(third)
     while rounds.left():
         next_round()
-    follow(line_three, Line.exchange)
-    (line_one.arrived,) = after(line_one.arrived)
+    (line_two.arrived, line_three.arrived) = after(line_two.arrived, line_three.arrived)
+    line_three.exchange()
+    line_two.gather()
+    *rounds.arrived, line_three.keep = together(*rounds.arrived, line_three.keep)
+    rounds.take()
+    small = rounds.block
+    line_one.arrived, line_three.keep = together(line_one.arrived, line_three.keep)
     shrink_share = line_one.result()
-    token[:] = [shrink_share]
-    follow(line_two, Line.gather)
-    next_round()
-    small = rounds.block
-    follow(line_three, Line.gather)
-    (line_two.arrived,) = after(line_two.arrived)
+    line_three.gather()
     expand_share = line_two.result()
-    token[:] = [expand_share]
     inlet_share = line_three.result()
 
     band_mean = totals[0] / total_tokens

time: 194 us -> 193 us (level); the launches traced: 193 us -> 194 us
  local copies, waits for them, and re-layouts: 4.07 us -> 6.11 us
    ppermute x36, starting transfers between devices: 43.1 us -> 45.8 us  [flipped(): return lax.ppermute(block, axis, [(i, i ^ bit) for i in range(size)])]
    unnamed x56, local copies, waits for them, and re-layouts: 3.94 us -> 5.99 us
  transfers between devices with their start and end apart: 44 -> 44, of which waited for: 21 -> 19; matrix products, arithmetic and copies ran while one was open for 7% -> 7% of each run, Pallas kernels for 10% -> 10%
where the time goes in v5:
time: 193 us; the launch traced here: 194 us
  starting transfers between devices  67.8 us (35%)
  waiting for transfers between devices  64.1 us (33%)
  Pallas kernels  37.8 us (20%)
  other arithmetic  16.6 us (9%)
  local copies, waits for them, and re-layouts  6.11 us (3%)
  between operations  2.07 us (1%)
    ppermute x36, starting transfers between devices, flipped(): return lax.ppermute(block, axis, [(i, i ^ bit) for i in range(size)])  45.8 us
    ppermute x36, waiting for transfers between devices, flipped(): return lax.ppermute(block, axis, [(i, i ^ bit) for i in range(size)])  45.5 us
    pallas_call x13, Pallas kernels, call(): pl.pallas_call(kernel, grid_spec=pltpu.PrefetchScalarGridSpec(num_scalar_...  37.8 us
    ppermute x8, starting transfers between devices, moved(): return lax.ppermute(block, axis, route)  21.9 us
    ppermute x8, waiting for transfers between devices, moved(): return lax.ppermute(block, axis, route)  18.6 us
    convert_element_type x5, other arithmetic, adam_rule(): return (weight_new, moment_new, square_new, weight_new.astype(bf16))  8.96 us
    unnamed x56, local copies, waits for them, and re-layouts  5.99 us
  transfers between devices with their start and end apart: 44, of which 19 were waited for; matrix products, arithmetic and copies ran while one was open for 7% of the time, Pallas kernels for 10%

profile of v5, /device:TPU:0, one launch (start us, length us, event | category | flops | bytes accessed | tf_op | source)
XLA Modules:
  0.0 194.4 jit_solution(18141774591943353212)
XLA Ops:
  3.3 2.8 %collective-permute-start.1 = (f32[2,768]{1,0:T(2,128)S(1)}, f32[2,768]{1,0:T(2,128)S(1)}, u32[]{:S(2)}, u32[]{:S(2)}) collective-permute-start(f32[2,768]{1,0:T(2,128)S(1)} %add.302), channel_id=1, source_target_pairs={{0,8},{4,12},{8,0},{12,4},{16,24},{20,28},{24,16},{28,20},{1,9},{5... | collective-permute-start | bytes 18440 | tf_op jit(solution)/shard_map/ppermute | solution.py:44
  9.7 2.4 %collective-permute-done.3 = f32[2,768]{1,0:T(2,128)S(1)} collective-permute-done((f32[2,768]{1,0:T(2,128)S(1)}, f32[2,768]{1,0:T(2,128)S(1)}, u32[]{:S(2)}, u32[]{:S(2)}) %collective-permute-start.3) | collective-permute-done | bytes 6176 | tf_op jit(solution)/shard_map/ppermute | solution.py:44
  12.2 2.7 %collective-permute-start.5 = (f32[2,768]{1,0:T(2,128)S(1)}, f32[2,768]{1,0:T(2,128)S(1)}, u32[]{:S(2)}, u32[]{:S(2)}) collective-permute-start(f32[2,768]{1,0:T(2,128)S(1)} %add_add_fusion.1), channel_id=1, source_target_pairs={{0,2},{1,3},{2,0},{3,1},{4,6},{5,7},{6,4},{7,5},{8,10},{9,11},{10,... | collective-permute-start | bytes 18440 | tf_op jit(solution)/shard_map/ppermute | solution.py:44
  16.8 3.4 %collective-permute-done.6 = f32[2,768]{1,0:T(2,128)S(1)} collective-permute-done((f32[2,768]{1,0:T(2,128)S(1)}, f32[2,768]{1,0:T(2,128)S(1)}, u32[]{:S(2)}, u32[]{:S(2)}) %collective-permute-start.6) | collective-permute-done | bytes 6176 | tf_op jit(solution)/shard_map/ppermute | solution.py:44
  29.7 4.1 %collective-permute-done.8.xb_ref.refs_3_ = bf16[272,768]{1,0:T(8,128)(2,1)S(1)} collective-permute-done((bf16[272,768]{1,0:T(8,128)(2,1)S(1)}, bf16[272,768]{1,0:T(8,128)(2,1)S(1)}, u32[]{:S(2)}, u32[]{:S(2)}) %collective-permute-start.8) | collective-permute-done | bytes 417824 | tf_op jit(solution)/shard_map/ppermute | solution.py:50
  33.8 3.6 %collective-permute-start.9 = (bf16[272,768]{1,0:T(8,128)(2,1)S(1)}, bf16[272,768]{1,0:T(8,128)(2,1)S(1)}, u32[]{:S(2)}, u32[]{:S(2)}) collective-permute-start(bf16[272,768]{1,0:T(8,128)(2,1)S(1)} %collective-permute-done.7.xa_ref.refs_1_), channel_id=1, source_target_pairs={{0,1},{1,2},{2,3},{4,5},{5,6},{6,7},{8,9},{9,10},{10,11},{12,13},{... | collective-permute-start | bytes 1253384 | tf_op jit(solution)/shard_map/ppermute | solution.py:50
  42.9 4.4 %collective-permute-done.10.xb_ref.refs_4_ = bf16[272,768]{1,0:T(8,128)(2,1)S(1)} collective-permute-done((bf16[272,768]{1,0:T(8,128)(2,1)S(1)}, bf16[272,768]{1,0:T(8,128)(2,1)S(1)}, u32[]{:S(2)}, u32[]{:S(2)}) %collective-permute-start.10) | collective-permute-done | bytes 417824 | tf_op jit(solution)/shard_map/ppermute | solution.py:50
  48.4 5.3 %attend.1 = (bf16[256,768]{1,0:T(8,128)(2,1)S(1)}, f32[3,4,256]{2,1,0:T(4,128)S(1)}, s32[2]{0:T(128)S(1)}) custom-call(s32[28]{0:T(128)S(1)} %pad_add_fusion.table, bf16[256,768]{1,0:T(8,128)(2,1)S(1)} %get-tuple-element.136.q_ref, bf16[5,256,1536]{2,1,0:T(8,128)(2,1)S(1)} %get-tuple-element.146.kv_ref, s32[1,256]{1,0:T(1,128)S(1)} %copy-done.6, ...), custom_call_target="tpu_custom_call" | custom-call | flops 1048576 | bytes 65536 | tf_op jit(solution)/shard_map/attend/pallas_call | solution.py:159
  53.8 10.8 %ffn.1 = (bf16[256,768]{1,0:T(8,128)(2,1)}, f32[256,768]{1,0:T(8,128)S(1)}, bf16[256,768]{1,0:T(8,128)(2,1)S(1)}, bf16[2,4,192,768]{3,2,1,0:T(8,128)(2,1)S(1)}, ...) custom-call(s32[28]{0:T(128)S(1)} %pad_add_fusion.table, ...), custom_call_target="tpu_custom_call" | custom-call | flops 1048576 | bytes 65536 | tf_op jit(solution)/shard_map/ffn/pallas_call | solution.py:159
  65.1 2.9 %attend_back.3 = (bf16[256,256]{1,0:T(8,128)(2,1)S(1)}, bf16[5,256,256]{2,1,0:T(8,128)(2,1)S(1)}, bf16[5,256,256]{2,1,0:T(8,128)(2,1)S(1)}, f32[2,256]{1,0:T(2,128)S(1)}) custom-call(s32[2]{0:T(128)S(1)} %get-tuple-element.153.bounds.refs_5_, bf16[256,768]{1,0:T(8,128)(2,1)S(1)} %get-tuple-element.136.q_ref, ...), custom_call_target="tpu_custom_call" | custom-call | flops 1048576 | bytes 65536 | tf_op jit(solution)/shard_map/attend_back/pallas_call | solution.py:159
  70.0 3.4 %collective-permute-start.16 = (bf16[2,192,768]{2,1,0:T(8,128)(2,1)S(1)}, bf16[2,192,768]{2,1,0:T(8,128)(2,1)S(1)}, u32[]{:S(2)}, u32[]{:S(2)}) collective-permute-start(bf16[2,192,768]{2,1,0:T(8,128)(2,1)S(1)} %get-tuple-element.276), channel_id=1, source_target_pairs={{0,16},{4,20},{8,24},{12,28},{16,0},{20,4},{24,8},{28,12},{1,17},{... | collective-permute-start | bytes 1769480 | tf_op jit(solution)/shard_map/ppermute | solution.py:44
  73.4 2.7 %attend_back.4 = (bf16[256,256]{1,0:T(8,128)(2,1)S(1)}, bf16[5,256,256]{2,1,0:T(8,128)(2,1)S(1)}, bf16[5,256,256]{2,1,0:T(8,128)(2,1)S(1)}, f32[2,256]{1,0:T(2,128)S(1)}) custom-call(s32[2]{0:T(128)S(1)} %get-tuple-element.153.bounds.refs_5_, bf16[256,768]{1,0:T(8,128)(2,1)S(1)} %get-tuple-element.136.q_ref, ...), custom_call_target="tpu_custom_call" | custom-call | flops 1048576 | bytes 65536 | tf_op jit(solution)/shard_map/attend_back/pallas_call | solution.py:159
  76.1 2.7 %attend_back.5 = (bf16[256,256]{1,0:T(8,128)(2,1)S(1)}, bf16[5,256,256]{2,1,0:T(8,128)(2,1)S(1)}, bf16[5,256,256]{2,1,0:T(8,128)(2,1)S(1)}, f32[2,256]{1,0:T(2,128)S(1)}) custom-call(s32[2]{0:T(128)S(1)} %get-tuple-element.153.bounds.refs_5_, bf16[256,768]{1,0:T(8,128)(2,1)S(1)} %get-tuple-element.136.q_ref, ...), custom_call_target="tpu_custom_call" | custom-call | flops 1048576 | bytes 65536 | tf_op jit(solution)/shard_map/attend_back/pallas_call | solution.py:159
  78.8 2.6 %parts.1 = (bf16[4,256,768]{2,1,0:T(8,128)(2,1)S(1)}, f32[256,768]{1,0:T(8,128)S(1)}) custom-call(s32[2]{0:T(128)S(1)} %get-tuple-element.153.bounds.refs_5_, bf16[256,256]{1,0:T(8,128)(2,1)S(1)} %get-tuple-element.186.refs_0_.refs_6_, bf16[256,256]{1,0:T(8,128)(2,1)S(1)} %get-tuple-element.187.refs_1_.refs_7_, ...), custom_call_target="tpu_custom_call" | custom-call | flops 1048576 | bytes 65536 | tf_op jit(solution)/shard_map/parts/pallas_call | solution.py:159
  81.5 3.4 %collective-permute-done.15 = bf16[2,192,768]{2,1,0:T(8,128)(2,1)S(1)} collective-permute-done((bf16[2,192,768]{2,1,0:T(8,128)(2,1)S(1)}, bf16[2,192,768]{2,1,0:T(8,128)(2,1)S(1)}, u32[]{:S(2)}, u32[]{:S(2)}) %collective-permute-start.15) | collective-permute-done | bytes 589856 | tf_op jit(solution)/shard_map/ppermute | solution.py:44
  90.4 6.2 %collective-permute-start.14 = (bf16[256,768]{1,0:T(8,128)(2,1)S(1)}, bf16[256,768]{1,0:T(8,128)(2,1)S(1)}, u32[]{:S(2)}, u32[]{:S(2)}) collective-permute-start(bf16[256,768]{1,0:T(8,128)(2,1)S(1)} %get-tuple-element.284), channel_id=1, source_target_pairs={{0,1},{1,2},{2,3},{4,5},{5,6},{6,7},{8,9},{9,10},{10,11},{12,13},{... | collective-permute-start | bytes 1179656 | tf_op jit(solution)/shard_map/ppermute | solution.py:50
  96.7 4.2 %weights.1 = (bf16[384,2304]{1,0:T(8,128)(2,1)S(1)}, bf16[384,2304]{1,0:T(8,128)(2,1)S(1)}) custom-call(s32[28]{0:T(128)S(1)} %pad_add_fusion.table, bf16[272,768]{1,0:T(8,128)(2,1)S(1)} %collective-permute-done.9.xa_ref.refs_0_, bf16[272,768]{1,0:T(8,128)(2,1)S(1)} %collective-permute-done.7.xa_ref.refs_1_, ...), custom_call_target="tpu_custom_call" | custom-call | flops 1048576 | bytes 65536 | tf_op jit(solution)/shard_map/weights/pallas_call | solution.py:159
  105.0 5.1 %collective-permute-start.20 = (bf16[256,768]{1,0:T(8,128)(2,1)S(1)}, bf16[256,768]{1,0:T(8,128)(2,1)S(1)}, u32[]{:S(2)}, u32[]{:S(2)}) collective-permute-start(bf16[256,768]{1,0:T(8,128)(2,1)S(1)} %get-tuple-element.282), channel_id=1, source_target_pairs={{0,1},{1,2},{2,3},{4,5},{5,6},{6,7},{8,9},{9,10},{10,11},{12,13},{... | collective-permute-start | bytes 1179656 | tf_op jit(solution)/shard_map/ppermute | solution.py:50
  110.4 6.5 %collective-permute-done.19.right_ref = bf16[256,768]{1,0:T(8,128)(2,1)S(1)} collective-permute-done((bf16[256,768]{1,0:T(8,128)(2,1)S(1)}, bf16[256,768]{1,0:T(8,128)(2,1)S(1)}, u32[]{:S(2)}, u32[]{:S(2)}) %collective-permute-start.19) | collective-permute-done | bytes 393248 | tf_op jit(solution)/shard_map/ppermute | solution.py:50
  120.1 2.3 %collective-permute-start.21 = (f32[16,768]{1,0:T(8,128)S(1)}, f32[16,768]{1,0:T(8,128)S(1)}, u32[]{:S(2)}, u32[]{:S(2)}) collective-permute-start(f32[16,768]{1,0:T(8,128)S(1)} %get-tuple-element.209), channel_id=1, source_target_pairs={{0,1},{1,0},{2,3},{3,2},{4,5},{5,4},{6,7},{7,6},{8,9},{9,8},{10,11... | collective-permute-start | bytes 147464 | tf_op jit(solution)/shard_map/ppermute | solution.py:44
  128.3 3.0 %collective-permute-start.25 = (f32[16,768]{1,0:T(8,128)S(1)}, f32[16,768]{1,0:T(8,128)S(1)}, u32[]{:S(2)}, u32[]{:S(2)}) collective-permute-start(f32[16,768]{1,0:T(8,128)S(1)} %add.340), channel_id=1, source_target_pairs={{0,2},{1,3},{2,0},{3,1},{4,6},{5,7},{6,4},{7,5},{8,10},{9,11},{10,... | collective-permute-start | bytes 147464 | tf_op jit(solution)/shard_map/ppermute | solution.py:44
  131.4 2.9 %collective-permute-done.26 = bf16[48,3840]{1,0:T(8,128)(2,1)S(1)} collective-permute-done((bf16[48,3840]{1,0:T(8,128)(2,1)S(1)}, bf16[48,3840]{1,0:T(8,128)(2,1)S(1)}, u32[]{:S(2)}, u32[]{:S(2)}) %collective-permute-start.26) | collective-permute-done | bytes 368672 | tf_op jit(solution)/shard_map/ppermute | solution.py:44
  134.3 4.1 %collective-permute-start.30 = (bf16[192,768]{1,0:T(8,128)(2,1)S(1)}, bf16[192,768]{1,0:T(8,128)(2,1)S(1)}, u32[]{:S(2)}, u32[]{:S(2)}) collective-permute-start(bf16[192,768]{1,0:T(8,128)(2,1)S(1)} %add_convert_fusion.9), channel_id=1, source_target_pairs={{0,2},{1,3},{2,0},{3,1},{4,6},{5,7},{6,4},{7,5},{8,10},{9,11},{10,... | collective-permute-start | bytes 884744 | tf_op jit(solution)/shard_map/ppermute | solution.py:44
  139.0 3.9 %collective-permute-done.32 = bf16[2,48,2304]{2,1,0:T(8,128)(2,1)S(1)} collective-permute-done((bf16[2,48,2304]{2,1,0:T(8,128)(2,1)S(1)}, bf16[2,48,2304]{2,1,0:T(8,128)(2,1)S(1)}, u32[]{:S(2)}, u32[]{:S(2)}) %collective-permute-start.32) | collective-permute-done | bytes 442400 | tf_op jit(solution)/shard_map/ppermute | solution.py:44
  145.0 3.6 %collective-permute-done.31 = bf16[48,3840]{1,0:T(8,128)(2,1)S(1)} collective-permute-done((bf16[48,3840]{1,0:T(8,128)(2,1)S(1)}, bf16[48,3840]{1,0:T(8,128)(2,1)S(1)}, u32[]{:S(2)}, u32[]{:S(2)}) %collective-permute-start.31) | collective-permute-done | bytes 368672 | tf_op jit(solution)/shard_map/ppermute | solution.py:44
  148.8 2.5 %collective-permute-start.38 = (bf16[48,3840]{1,0:T(8,128)(2,1)S(1)}, bf16[48,3840]{1,0:T(8,128)(2,1)S(1)}, u32[]{:S(2)}, u32[]{:S(2)}) collective-permute-start(bf16[48,3840]{1,0:T(8,128)(2,1)S(1)} %add_convert_fusion.7), channel_id=1, source_target_pairs={{0,2},{1,3},{2,0},{3,1},{4,6},{5,7},{6,4},{7,5},{8,10},{9,11},{10,... | collective-permute-start | bytes 1105928 | tf_op jit(solution)/shard_map/ppermute | solution.py:44
  151.7 2.4 %collective-permute-start.39 = (bf16[48,2304]{1,0:T(8,128)(2,1)S(1)}, bf16[48,2304]{1,0:T(8,128)(2,1)S(1)}, u32[]{:S(2)}, u32[]{:S(2)}) collective-permute-start(bf16[48,2304]{1,0:T(8,128)(2,1)S(1)} %get-tuple-element.261), channel_id=1, source_target_pairs={{0,1},{1,0},{2,3},{3,2},{4,5},{5,4},{6,7},{7,6},{8,9},{9,8},{10,11... | collective-permute-start | bytes 663560 | tf_op jit(solution)/shard_map/ppermute | solution.py:44
  158.8 9.0 %collective-permute-done.38 = bf16[48,3840]{1,0:T(8,128)(2,1)S(1)} collective-permute-done((bf16[48,3840]{1,0:T(8,128)(2,1)S(1)}, bf16[48,3840]{1,0:T(8,128)(2,1)S(1)}, u32[]{:S(2)}, u32[]{:S(2)}) %collective-permute-start.38) | collective-permute-done | bytes 368672 | tf_op jit(solution)/shard_map/ppermute | solution.py:44
  168.1 6.2 %collective-permute-done.40 = bf16[192,768]{1,0:T(8,128)(2,1)S(1)} collective-permute-done((bf16[192,768]{1,0:T(8,128)(2,1)S(1)}, bf16[192,768]{1,0:T(8,128)(2,1)S(1)}, u32[]{:S(2)}, u32[]{:S(2)}) %collective-permute-start.40) | collective-permute-done | bytes 294944 | tf_op jit(solution)/shard_map/ppermute | solution.py:44
  176.8 2.6 %fusion.36 = (bf16[384,768]{1,0:T(8,128)(2,1)}, f32[384,768]{1,0:T(8,128)}, f32[384,768]{1,0:T(8,128)}, f32[384,768]{1,0:T(8,128)}) fusion(f32[384,768]{1,0:T(8,128)S(1)} %copy-done.8, f32[]{:T(128)} %bitcast.36, f32[]{:T(128)} %bitcast.35, f32[]{:T(128)} %bitcast.34, bf16[192,768]{1,0:T(8,128)(2,1)S(1)} %get-tuple-element.289, ...), kind=kLoop, calls=%fused_computation.110 | loop fusion | flops 5603328 | bytes 8257548 | tf_op jit(solution)/shard_map/convert_element_type | solution.py:677
  182.8 4.7 %collective-permute-done.43 = bf16[48,3840]{1,0:T(8,128)(2,1)S(1)} collective-permute-done((bf16[48,3840]{1,0:T(8,128)(2,1)S(1)}, bf16[48,3840]{1,0:T(8,128)(2,1)S(1)}, u32[]{:S(2)}, u32[]{:S(2)}) %collective-permute-start.43) | collective-permute-done | bytes 368672 | tf_op jit(solution)/shard_map/ppermute | solution.py:44
  187.7 2.6 %fusion.39 = (bf16[96,3072]{1,0:T(8,128)(2,1)}, f32[96,3072]{1,0:T(8,128)}, f32[96,3072]{1,0:T(8,128)}, f32[96,3072]{1,0:T(8,128)}) fusion(f32[96,3072]{1,0:T(8,128)S(1)} %copy-done.11, f32[]{:T(128)} %bitcast.36, f32[]{:T(128)} %bitcast.35, f32[]{:T(128)} %bitcast.34, bf16[48,3840]{1,0:T(8,128)(2,1)S(1)} %get-tuple-element.287, ...), kind=kLoop, calls=%fused_computation.111 | loop fusion | flops 5603328 | bytes 8405004 | tf_op jit(solution)/shard_map/convert_element_type | solution.py:677
  (169 shorter events, 63.6 us)
Async XLA Ops:
  23.5 10.3 %collective-permute-start.8 = (bf16[272,768]{1,0:T(8,128)(2,1)S(1)}, bf16[272,768]{1,0:T(8,128)(2,1)S(1)}, u32[]{:S(2)}, u32[]{:S(2)}) collective-permute-start(bf16[272,768]{1,0:T(8,128)(2,1)S(1)} %get-tuple-element.134.x_ref.refs_2_), channel_id=1, source_target_pairs={{1,0},{2,1},{3,2},{5,4},{6,5},{7,6},{9,8},{10,9},{11,10},{13,12},{... | collective-permute-start | bytes 1253384 | tf_op jit(solution)/shard_map/ppermute | solution.py:50
  33.8 9.1 %collective-permute-start.9 = (bf16[272,768]{1,0:T(8,128)(2,1)S(1)}, bf16[272,768]{1,0:T(8,128)(2,1)S(1)}, u32[]{:S(2)}, u32[]{:S(2)}) collective-permute-start(bf16[272,768]{1,0:T(8,128)(2,1)S(1)} %collective-permute-done.7.xa_ref.refs_1_), channel_id=1, source_target_pairs={{0,1},{1,2},{2,3},{4,5},{5,6},{6,7},{8,9},{9,10},{10,11},{12,13},{... | collective-permute-start | bytes 1253384 | tf_op jit(solution)/shard_map/ppermute | solution.py:50
  37.4 9.9 %collective-permute-start.10 = (bf16[272,768]{1,0:T(8,128)(2,1)S(1)}, bf16[272,768]{1,0:T(8,128)(2,1)S(1)}, u32[]{:S(2)}, u32[]{:S(2)}) collective-permute-start(bf16[272,768]{1,0:T(8,128)(2,1)S(1)} %collective-permute-done.8.xb_ref.refs_3_), channel_id=1, source_target_pairs={{1,0},{2,1},{3,2},{5,4},{6,5},{7,6},{9,8},{10,9},{11,10},{13,12},{... | collective-permute-start | bytes 1253384 | tf_op jit(solution)/shard_map/ppermute | solution.py:50
  64.6 14.2 %collective-permute-start.12 = (bf16[384,3840]{1,0:T(8,128)(2,1)S(1)}, bf16[384,3840]{1,0:T(8,128)(2,1)S(1)}, u32[]{:S(2)}, u32[]{:S(2)}) collective-permute-start(bf16[384,3840]{1,0:T(8,128)(2,1)S(1)} %get-tuple-element.170), channel_id=1, source_target_pairs={{0,4},{4,0},{8,12},{12,8},{16,20},{20,16},{24,28},{28,24},{1,5},{5... | collective-permute-start | bytes 8847368 | tf_op jit(solution)/shard_map/ppermute | solution.py:44
  69.4 15.4 %collective-permute-start.15 = (bf16[2,192,768]{2,1,0:T(8,128)(2,1)S(1)}, bf16[2,192,768]{2,1,0:T(8,128)(2,1)S(1)}, u32[]{:S(2)}, u32[]{:S(2)}) collective-permute-start(bf16[2,192,768]{2,1,0:T(8,128)(2,1)S(1)} %get-tuple-element.277), channel_id=1, source_target_pairs={{0,8},{4,12},{8,0},{12,4},{16,24},{20,28},{24,16},{28,20},{1,9},{5... | collective-permute-start | bytes 1769480 | tf_op jit(solution)/shard_map/ppermute | solution.py:44
  70.0 16.7 %collective-permute-start.16 = (bf16[2,192,768]{2,1,0:T(8,128)(2,1)S(1)}, bf16[2,192,768]{2,1,0:T(8,128)(2,1)S(1)}, u32[]{:S(2)}, u32[]{:S(2)}) collective-permute-start(bf16[2,192,768]{2,1,0:T(8,128)(2,1)S(1)} %get-tuple-element.276), channel_id=1, source_target_pairs={{0,16},{4,20},{8,24},{12,28},{16,0},{20,4},{24,8},{28,12},{1,17},{... | collective-permute-start | bytes 1769480 | tf_op jit(solution)/shard_map/ppermute | solution.py:44
  87.0 13.9 %collective-permute-start.17 = (bf16[192,768]{1,0:T(8,128)(2,1)S(1)}, bf16[192,768]{1,0:T(8,128)(2,1)S(1)}, u32[]{:S(2)}, u32[]{:S(2)}) collective-permute-start(bf16[192,768]{1,0:T(8,128)(2,1)S(1)} %get-tuple-element.275), channel_id=1, source_target_pairs={{0,16},{4,20},{8,24},{12,28},{16,0},{20,4},{24,8},{28,12},{1,17},{... | collective-permute-start | bytes 884744 | tf_op jit(solution)/shard_map/ppermute | solution.py:44
  88.8 12.1 %collective-permute-start.18 = (bf16[192,768]{1,0:T(8,128)(2,1)S(1)}, bf16[192,768]{1,0:T(8,128)(2,1)S(1)}, u32[]{:S(2)}, u32[]{:S(2)}) collective-permute-start(bf16[192,768]{1,0:T(8,128)(2,1)S(1)} %get-tuple-element.274), channel_id=1, source_target_pairs={{0,8},{4,12},{8,0},{12,4},{16,24},{20,28},{24,16},{28,20},{1,9},{5... | collective-permute-start | bytes 884744 | tf_op jit(solution)/shard_map/ppermute | solution.py:44
  89.2 14.4 %collective-permute-start.13 = (bf16[256,768]{1,0:T(8,128)(2,1)S(1)}, bf16[256,768]{1,0:T(8,128)(2,1)S(1)}, u32[]{:S(2)}, u32[]{:S(2)}) collective-permute-start(bf16[256,768]{1,0:T(8,128)(2,1)S(1)} %get-tuple-element.285), channel_id=1, source_target_pairs={{1,0},{2,1},{3,2},{5,4},{6,5},{7,6},{9,8},{10,9},{11,10},{13,12},{... | collective-permute-start | bytes 1179656 | tf_op jit(solution)/shard_map/ppermute | solution.py:50
  90.4 13.1 %collective-permute-start.14 = (bf16[256,768]{1,0:T(8,128)(2,1)S(1)}, bf16[256,768]{1,0:T(8,128)(2,1)S(1)}, u32[]{:S(2)}, u32[]{:S(2)}) collective-permute-start(bf16[256,768]{1,0:T(8,128)(2,1)S(1)} %get-tuple-element.284), channel_id=1, source_target_pairs={{0,1},{1,2},{2,3},{4,5},{5,6},{6,7},{8,9},{9,10},{10,11},{12,13},{... | collective-permute-start | bytes 1179656 | tf_op jit(solution)/shard_map/ppermute | solution.py:50
  100.8 25.2 %collective-permute-start.22 = (bf16[384,2304]{1,0:T(8,128)(2,1)S(1)}, bf16[384,2304]{1,0:T(8,128)(2,1)S(1)}, u32[]{:S(2)}, u32[]{:S(2)}) collective-permute-start(bf16[384,2304]{1,0:T(8,128)(2,1)S(1)} %get-tuple-element.210), channel_id=1, source_target_pairs={{0,4},{4,0},{8,12},{12,8},{16,20},{20,16},{24,28},{28,24},{1,5},{5... | collective-permute-start | bytes 5308424 | tf_op jit(solution)/shard_map/ppermute | solution.py:44
  101.3 21.0 %collective-permute-start.23 = (bf16[2,48,3840]{2,1,0:T(8,128)(2,1)S(1)}, bf16[2,48,3840]{2,1,0:T(8,128)(2,1)S(1)}, u32[]{:S(2)}, u32[]{:S(2)}) collective-permute-start(bf16[2,48,3840]{2,1,0:T(8,128)(2,1)S(1)} %bitcast.95), channel_id=1, source_target_pairs={{0,8},{4,12},{8,0},{12,4},{16,24},{20,28},{24,16},{28,20},{1,9},{5... | collective-permute-start | bytes 2211848 | tf_op jit(solution)/shard_map/ppermute | solution.py:44
  101.8 20.6 %collective-permute-start.24 = (bf16[2,48,3840]{2,1,0:T(8,128)(2,1)S(1)}, bf16[2,48,3840]{2,1,0:T(8,128)(2,1)S(1)}, u32[]{:S(2)}, u32[]{:S(2)}) collective-permute-start(bf16[2,48,3840]{2,1,0:T(8,128)(2,1)S(1)} %bitcast.94), channel_id=1, source_target_pairs={{0,16},{4,20},{8,24},{12,28},{16,0},{20,4},{24,8},{28,12},{1,17},{... | collective-permute-start | bytes 2211848 | tf_op jit(solution)/shard_map/ppermute | solution.py:44
  103.7 13.3 %collective-permute-start.19 = (bf16[256,768]{1,0:T(8,128)(2,1)S(1)}, bf16[256,768]{1,0:T(8,128)(2,1)S(1)}, u32[]{:S(2)}, u32[]{:S(2)}) collective-permute-start(bf16[256,768]{1,0:T(8,128)(2,1)S(1)} %get-tuple-element.283), channel_id=1, source_target_pairs={{1,0},{2,1},{3,2},{5,4},{6,5},{7,6},{9,8},{10,9},{11,10},{13,12},{... | collective-permute-start | bytes 1179656 | tf_op jit(solution)/shard_map/ppermute | solution.py:50
  105.0 13.7 %collective-permute-start.20 = (bf16[256,768]{1,0:T(8,128)(2,1)S(1)}, bf16[256,768]{1,0:T(8,128)(2,1)S(1)}, u32[]{:S(2)}, u32[]{:S(2)}) collective-permute-start(bf16[256,768]{1,0:T(8,128)(2,1)S(1)} %get-tuple-element.282), channel_id=1, source_target_pairs={{0,1},{1,2},{2,3},{4,5},{5,6},{6,7},{8,9},{9,10},{10,11},{12,13},{... | collective-permute-start | bytes 1179656 | tf_op jit(solution)/shard_map/ppermute | solution.py:50
  117.0 11.3 %collective-permute-start.28 = (bf16[192,768]{1,0:T(8,128)(2,1)S(1)}, bf16[192,768]{1,0:T(8,128)(2,1)S(1)}, u32[]{:S(2)}, u32[]{:S(2)}) collective-permute-start(bf16[192,768]{1,0:T(8,128)(2,1)S(1)} %get-tuple-element.267), channel_id=1, source_target_pairs={{0,1},{1,0},{2,3},{3,2},{4,5},{5,4},{6,7},{7,6},{8,9},{9,8},{10,11... | collective-permute-start | bytes 884744 | tf_op jit(solution)/shard_map/ppermute | solution.py:44
  122.7 11.6 %collective-permute-start.26 = (bf16[48,3840]{1,0:T(8,128)(2,1)S(1)}, bf16[48,3840]{1,0:T(8,128)(2,1)S(1)}, u32[]{:S(2)}, u32[]{:S(2)}) collective-permute-start(bf16[48,3840]{1,0:T(8,128)(2,1)S(1)} %get-tuple-element.271), channel_id=1, source_target_pairs={{0,16},{4,20},{8,24},{12,28},{16,0},{20,4},{24,8},{28,12},{1,17},{... | collective-permute-start | bytes 1105928 | tf_op jit(solution)/shard_map/ppermute | solution.py:44
  124.2 14.2 %collective-permute-start.27 = (bf16[48,3840]{1,0:T(8,128)(2,1)S(1)}, bf16[48,3840]{1,0:T(8,128)(2,1)S(1)}, u32[]{:S(2)}, u32[]{:S(2)}) collective-permute-start(bf16[48,3840]{1,0:T(8,128)(2,1)S(1)} %get-tuple-element.270), channel_id=1, source_target_pairs={{0,8},{4,12},{8,0},{12,4},{16,24},{20,28},{24,16},{28,20},{1,9},{5... | collective-permute-start | bytes 1105928 | tf_op jit(solution)/shard_map/ppermute | solution.py:44
  126.2 16.6 %collective-permute-start.32 = (bf16[2,48,2304]{2,1,0:T(8,128)(2,1)S(1)}, bf16[2,48,2304]{2,1,0:T(8,128)(2,1)S(1)}, u32[]{:S(2)}, u32[]{:S(2)}) collective-permute-start(bf16[2,48,2304]{2,1,0:T(8,128)(2,1)S(1)} %bitcast.97), channel_id=1, source_target_pairs={{0,8},{4,12},{8,0},{12,4},{16,24},{20,28},{24,16},{28,20},{1,9},{5... | collective-permute-start | bytes 1327112 | tf_op jit(solution)/shard_map/ppermute | solution.py:44
  126.5 16.4 %collective-permute-start.33 = (bf16[2,48,2304]{2,1,0:T(8,128)(2,1)S(1)}, bf16[2,48,2304]{2,1,0:T(8,128)(2,1)S(1)}, u32[]{:S(2)}, u32[]{:S(2)}) collective-permute-start(bf16[2,48,2304]{2,1,0:T(8,128)(2,1)S(1)} %bitcast.96), channel_id=1, source_target_pairs={{0,16},{4,20},{8,24},{12,28},{16,0},{20,4},{24,8},{28,12},{1,17},{... | collective-permute-start | bytes 1327112 | tf_op jit(solution)/shard_map/ppermute | solution.py:44
  128.3 10.6 %collective-permute-start.25 = (f32[16,768]{1,0:T(8,128)S(1)}, f32[16,768]{1,0:T(8,128)S(1)}, u32[]{:S(2)}, u32[]{:S(2)}) collective-permute-start(f32[16,768]{1,0:T(8,128)S(1)} %add.340), channel_id=1, source_target_pairs={{0,2},{1,3},{2,0},{3,1},{4,6},{5,7},{6,4},{7,5},{8,10},{9,11},{10,... | collective-permute-start | bytes 147464 | tf_op jit(solution)/shard_map/ppermute | solution.py:44
  134.3 17.0 %collective-permute-start.30 = (bf16[192,768]{1,0:T(8,128)(2,1)S(1)}, bf16[192,768]{1,0:T(8,128)(2,1)S(1)}, u32[]{:S(2)}, u32[]{:S(2)}) collective-permute-start(bf16[192,768]{1,0:T(8,128)(2,1)S(1)} %add_convert_fusion.9), channel_id=1, source_target_pairs={{0,2},{1,3},{2,0},{3,1},{4,6},{5,7},{6,4},{7,5},{8,10},{9,11},{10,... | collective-permute-start | bytes 884744 | tf_op jit(solution)/shard_map/ppermute | solution.py:44
  138.8 9.8 %collective-permute-start.31 = (bf16[48,3840]{1,0:T(8,128)(2,1)S(1)}, bf16[48,3840]{1,0:T(8,128)(2,1)S(1)}, u32[]{:S(2)}, u32[]{:S(2)}) collective-permute-start(bf16[48,3840]{1,0:T(8,128)(2,1)S(1)} %get-tuple-element.264), channel_id=1, source_target_pairs={{0,1},{1,0},{2,3},{3,2},{4,5},{5,4},{6,7},{7,6},{8,9},{9,8},{10,11... | collective-permute-start | bytes 1105928 | tf_op jit(solution)/shard_map/ppermute | solution.py:44
  138.9 12.5 %collective-permute-start.29 = (f32[16,768]{1,0:T(8,128)S(1)}, f32[16,768]{1,0:T(8,128)S(1)}, u32[]{:S(2)}, u32[]{:S(2)}) collective-permute-start(f32[16,768]{1,0:T(8,128)S(1)} %add.348), channel_id=1, source_target_pairs={{0,4},{4,0},{8,12},{12,8},{16,20},{20,16},{24,28},{28,24},{1,5},{5... | collective-permute-start | bytes 147464 | tf_op jit(solution)/shard_map/ppermute | solution.py:44
  143.0 8.4 %collective-permute-start.35 = (bf16[48,2304]{1,0:T(8,128)(2,1)S(1)}, bf16[48,2304]{1,0:T(8,128)(2,1)S(1)}, u32[]{:S(2)}, u32[]{:S(2)}) collective-permute-start(bf16[48,2304]{1,0:T(8,128)(2,1)S(1)} %get-tuple-element.279), channel_id=1, source_target_pairs={{0,16},{4,20},{8,24},{12,28},{16,0},{20,4},{24,8},{28,12},{1,17},{... | collective-permute-start | bytes 663560 | tf_op jit(solution)/shard_map/ppermute | solution.py:44
  148.8 19.0 %collective-permute-start.38 = (bf16[48,3840]{1,0:T(8,128)(2,1)S(1)}, bf16[48,3840]{1,0:T(8,128)(2,1)S(1)}, u32[]{:S(2)}, u32[]{:S(2)}) collective-permute-start(bf16[48,3840]{1,0:T(8,128)(2,1)S(1)} %add_convert_fusion.7), channel_id=1, source_target_pairs={{0,2},{1,3},{2,0},{3,1},{4,6},{5,7},{6,4},{7,5},{8,10},{9,11},{10,... | collective-permute-start | bytes 1105928 | tf_op jit(solution)/shard_map/ppermute | solution.py:44
  151.7 16.1 %collective-permute-start.39 = (bf16[48,2304]{1,0:T(8,128)(2,1)S(1)}, bf16[48,2304]{1,0:T(8,128)(2,1)S(1)}, u32[]{:S(2)}, u32[]{:S(2)}) collective-permute-start(bf16[48,2304]{1,0:T(8,128)(2,1)S(1)} %get-tuple-element.261), channel_id=1, source_target_pairs={{0,1},{1,0},{2,3},{3,2},{4,5},{5,4},{6,7},{7,6},{8,9},{9,8},{10,11... | collective-permute-start | bytes 663560 | tf_op jit(solution)/shard_map/ppermute | solution.py:44
  156.1 18.2 %collective-permute-start.40 = (bf16[192,768]{1,0:T(8,128)(2,1)S(1)}, bf16[192,768]{1,0:T(8,128)(2,1)S(1)}, u32[]{:S(2)}, u32[]{:S(2)}) collective-permute-start(bf16[192,768]{1,0:T(8,128)(2,1)S(1)} %add_convert_fusion.8), channel_id=1, source_target_pairs={{0,1},{1,0},{2,3},{3,2},{4,5},{5,4},{6,7},{7,6},{8,9},{9,8},{10,11... | collective-permute-start | bytes 884744 | tf_op jit(solution)/shard_map/ppermute | solution.py:44
  158.1 9.9 %collective-permute-start.37 = (f32[16,768]{1,0:T(8,128)S(1)}, f32[16,768]{1,0:T(8,128)S(1)}, u32[]{:S(2)}, u32[]{:S(2)}) collective-permute-start(f32[16,768]{1,0:T(8,128)S(1)} %add.362), channel_id=1, source_target_pairs={{0,16},{4,20},{8,24},{12,28},{16,0},{20,4},{24,8},{28,12},{1,17},{... | collective-permute-start | bytes 147464 | tf_op jit(solution)/shard_map/ppermute | solution.py:44
  167.9 12.8 %collective-permute-start.41 = (bf16[48,2304]{1,0:T(8,128)(2,1)S(1)}, bf16[48,2304]{1,0:T(8,128)(2,1)S(1)}, u32[]{:S(2)}, u32[]{:S(2)}) collective-permute-start(bf16[48,2304]{1,0:T(8,128)(2,1)S(1)} %add_convert_fusion.11), channel_id=1, source_target_pairs={{0,2},{1,3},{2,0},{3,1},{4,6},{5,7},{6,4},{7,5},{8,10},{9,11},{10,... | collective-permute-start | bytes 663560 | tf_op jit(solution)/shard_map/ppermute | solution.py:44
  174.4 13.1 %collective-permute-start.43 = (bf16[48,3840]{1,0:T(8,128)(2,1)S(1)}, bf16[48,3840]{1,0:T(8,128)(2,1)S(1)}, u32[]{:S(2)}, u32[]{:S(2)}) collective-permute-start(bf16[48,3840]{1,0:T(8,128)(2,1)S(1)} %add_convert_fusion.6), channel_id=1, source_target_pairs={{0,1},{1,0},{2,3},{3,2},{4,5},{5,4},{6,7},{7,6},{8,9},{9,8},{10,11... | collective-permute-start | bytes 1105928 | tf_op jit(solution)/shard_map/ppermute | solution.py:44
  180.8 10.6 %collective-permute-start.42 = (bf16[48,2304]{1,0:T(8,128)(2,1)S(1)}, bf16[48,2304]{1,0:T(8,128)(2,1)S(1)}, u32[]{:S(2)}, u32[]{:S(2)}) collective-permute-start(bf16[48,2304]{1,0:T(8,128)(2,1)S(1)} %add_convert_fusion.10), channel_id=1, source_target_pairs={{0,1},{1,0},{2,3},{3,2},{4,5},{5,4},{6,7},{7,6},{8,9},{9,8},{10,11... | collective-permute-start | bytes 663560 | tf_op jit(solution)/shard_map/ppermute | solution.py:44
  (40 other events, 218.2 us)

commit v6 on v5

--- a/solution.py
+++ b/solution.py
@@ -974,6 +974,7 @@
         advance(first)
     advance(first)
     (expand_in,) = after(expand_in)
+    from_right, from_left, expand_in = together(from_right, from_left, expand_in)
     second = scatters(expand_keep, expand_in, owned)
     launch(second)
     for d in range(reach - 1, 0, -1):
@@ -982,7 +983,7 @@
         to_right = added(parts[reach + d - 1], from_left)
         token[:] = [to_left, to_right]
         from_right, from_left = moved(to_left, "blk", -1), moved(to_right, "blk", 1)
-    line_one = begin(first)
+    advance(second)
     from_right, from_left = after(from_right, from_left)
     grad_normed, small = call(
         leave_kernel,
@@ -1005,22 +1006,21 @@
     )
     token[:] = [small]
     rounds = SmallSum(small, paired=False)
-    rounds.send()
-    advance(second)
     (inlet_in,) = after(inlet_in)
     third = scatters(inlet_keep, inlet_in, owned)
     launch(third)
-    next_round()
-    follow(line_one, Line.exchange)
+    line_one = begin(first)
+    rounds.send()
     while second[0].order:
         advance(second)
     advance(second)
     line_two = begin(second)
     next_round()
+    follow(line_one, Line.exchange)
     advance(third)
     follow(line_two, Line.exchange)
+    next_round()
     follow(line_one, Line.gather)
-    next_round()
     while third[0].order:
         advance(third)
     advance(third)

time: 193 us -> 198 us (1.026); the launches traced: 194 us -> 195 us
  waiting for transfers between devices: 64.1 us -> 66.2 us
    ppermute x36, waiting for transfers between devices: 45.5 us -> 54.2 us  [flipped(): return lax.ppermute(block, axis, [(i, i ^ bit) for i in range(size)])]
    ppermute x8, waiting for transfers between devices: 18.6 us -> 12.1 us  [moved(): return lax.ppermute(block, axis, route)]
    ppermute x36, starting transfers between devices: 45.8 us -> 43 us  [flipped(): return lax.ppermute(block, axis, [(i, i ^ bit) for i in range(size)])]
  transfers between devices with their start and end apart: 44 -> 44, of which waited for: 19 -> 23; matrix products, arithmetic and copies ran while one was open for 7% -> 7% of each run, Pallas kernels for 10% -> 10%
where the time goes in v6:
time: 198 us; the launch traced here: 195 us
  starting transfers between devices  66.4 us (34%)
  waiting for transfers between devices  66.2 us (33%)
  Pallas kernels  37.8 us (19%)
  other arithmetic  16.6 us (8%)
  local copies, waits for them, and re-layouts  6.11 us (3%)
  between operations  2.04 us (1%)
    ppermute x36, waiting for transfers between devices, flipped(): return lax.ppermute(block, axis, [(i, i ^ bit) for i in range(size)])  54.2 us
    ppermute x36, starting transfers between devices, flipped(): return lax.ppermute(block, axis, [(i, i ^ bit) for i in range(size)])  43 us
    pallas_call x13, Pallas kernels, call(): pl.pallas_call(kernel, grid_spec=pltpu.PrefetchScalarGridSpec(num_scalar_...  37.8 us
    ppermute x8, starting transfers between devices, moved(): return lax.ppermute(block, axis, route)  23.4 us
    ppermute x8, waiting for transfers between devices, moved(): return lax.ppermute(block, axis, route)  12.1 us
    convert_element_type x5, other arithmetic, adam_rule(): return (weight_new, moment_new, square_new, weight_new.astype(bf16))  8.96 us
    unnamed x56, local copies, waits for them, and re-layouts  5.99 us
  transfers between devices with their start and end apart: 44, of which 23 were waited for; matrix products, arithmetic and copies ran while one was open for 7% of the time, Pallas kernels for 10%

profile of v6, /device:TPU:0, one launch (start us, length us, event | category | flops | bytes accessed | tf_op | source)
XLA Modules:
  0.0 195.1 jit_solution(6558742394196061680)
XLA Ops:
  3.3 2.8 %collective-permute-start.1 = (f32[2,768]{1,0:T(2,128)S(1)}, f32[2,768]{1,0:T(2,128)S(1)}, u32[]{:S(2)}, u32[]{:S(2)}) collective-permute-start(f32[2,768]{1,0:T(2,128)S(1)} %add.302), channel_id=1, source_target_pairs={{0,8},{4,12},{8,0},{12,4},{16,24},{20,28},{24,16},{28,20},{1,9},{5... | collective-permute-start | bytes 18440 | tf_op jit(solution)/shard_map/ppermute | solution.py:44
  9.7 2.4 %collective-permute-done.3 = f32[2,768]{1,0:T(2,128)S(1)} collective-permute-done((f32[2,768]{1,0:T(2,128)S(1)}, f32[2,768]{1,0:T(2,128)S(1)}, u32[]{:S(2)}, u32[]{:S(2)}) %collective-permute-start.3) | collective-permute-done | bytes 6176 | tf_op jit(solution)/shard_map/ppermute | solution.py:44
  12.2 2.7 %collective-permute-start.5 = (f32[2,768]{1,0:T(2,128)S(1)}, f32[2,768]{1,0:T(2,128)S(1)}, u32[]{:S(2)}, u32[]{:S(2)}) collective-permute-start(f32[2,768]{1,0:T(2,128)S(1)} %add_add_fusion.1), channel_id=1, source_target_pairs={{0,2},{1,3},{2,0},{3,1},{4,6},{5,7},{6,4},{7,5},{8,10},{9,11},{10,... | collective-permute-start | bytes 18440 | tf_op jit(solution)/shard_map/ppermute | solution.py:44
  16.8 3.4 %collective-permute-done.6 = f32[2,768]{1,0:T(2,128)S(1)} collective-permute-done((f32[2,768]{1,0:T(2,128)S(1)}, f32[2,768]{1,0:T(2,128)S(1)}, u32[]{:S(2)}, u32[]{:S(2)}) %collective-permute-start.6) | collective-permute-done | bytes 6176 | tf_op jit(solution)/shard_map/ppermute | solution.py:44
  29.7 4.1 %collective-permute-done.8.xb_ref.refs_3_ = bf16[272,768]{1,0:T(8,128)(2,1)S(1)} collective-permute-done((bf16[272,768]{1,0:T(8,128)(2,1)S(1)}, bf16[272,768]{1,0:T(8,128)(2,1)S(1)}, u32[]{:S(2)}, u32[]{:S(2)}) %collective-permute-start.8) | collective-permute-done | bytes 417824 | tf_op jit(solution)/shard_map/ppermute | solution.py:50
  33.8 3.6 %collective-permute-start.9 = (bf16[272,768]{1,0:T(8,128)(2,1)S(1)}, bf16[272,768]{1,0:T(8,128)(2,1)S(1)}, u32[]{:S(2)}, u32[]{:S(2)}) collective-permute-start(bf16[272,768]{1,0:T(8,128)(2,1)S(1)} %collective-permute-done.7.xa_ref.refs_1_), channel_id=1, source_target_pairs={{0,1},{1,2},{2,3},{4,5},{5,6},{6,7},{8,9},{9,10},{10,11},{12,13},{... | collective-permute-start | bytes 1253384 | tf_op jit(solution)/shard_map/ppermute | solution.py:50
  40.7 2.3 %collective-permute-done.9.xa_ref.refs_0_ = bf16[272,768]{1,0:T(8,128)(2,1)S(1)} collective-permute-done((bf16[272,768]{1,0:T(8,128)(2,1)S(1)}, bf16[272,768]{1,0:T(8,128)(2,1)S(1)}, u32[]{:S(2)}, u32[]{:S(2)}) %collective-permute-start.9) | collective-permute-done | bytes 417824 | tf_op jit(solution)/shard_map/ppermute | solution.py:50
  42.9 4.4 %collective-permute-done.10.xb_ref.refs_4_ = bf16[272,768]{1,0:T(8,128)(2,1)S(1)} collective-permute-done((bf16[272,768]{1,0:T(8,128)(2,1)S(1)}, bf16[272,768]{1,0:T(8,128)(2,1)S(1)}, u32[]{:S(2)}, u32[]{:S(2)}) %collective-permute-start.10) | collective-permute-done | bytes 417824 | tf_op jit(solution)/shard_map/ppermute | solution.py:50
  48.4 5.3 %attend.1 = (bf16[256,768]{1,0:T(8,128)(2,1)S(1)}, f32[3,4,256]{2,1,0:T(4,128)S(1)}, s32[2]{0:T(128)S(1)}) custom-call(s32[28]{0:T(128)S(1)} %pad_add_fusion.table, bf16[256,768]{1,0:T(8,128)(2,1)S(1)} %get-tuple-element.139.q_ref, bf16[5,256,1536]{2,1,0:T(8,128)(2,1)S(1)} %get-tuple-element.149.kv_ref, s32[1,256]{1,0:T(1,128)S(1)} %copy-done.6, ...), custom_call_target="tpu_custom_call" | custom-call | flops 1048576 | bytes 65536 | tf_op jit(solution)/shard_map/attend/pallas_call | solution.py:159
  53.8 10.8 %ffn.1 = (bf16[256,768]{1,0:T(8,128)(2,1)}, f32[256,768]{1,0:T(8,128)S(1)}, bf16[256,768]{1,0:T(8,128)(2,1)S(1)}, bf16[2,4,192,768]{3,2,1,0:T(8,128)(2,1)S(1)}, ...) custom-call(s32[28]{0:T(128)S(1)} %pad_add_fusion.table, ...), custom_call_target="tpu_custom_call" | custom-call | flops 1048576 | bytes 65536 | tf_op jit(solution)/shard_map/ffn/pallas_call | solution.py:159
  65.1 2.9 %attend_back.3 = (bf16[256,256]{1,0:T(8,128)(2,1)S(1)}, bf16[5,256,256]{2,1,0:T(8,128)(2,1)S(1)}, bf16[5,256,256]{2,1,0:T(8,128)(2,1)S(1)}, f32[2,256]{1,0:T(2,128)S(1)}) custom-call(s32[2]{0:T(128)S(1)} %get-tuple-element.156.bounds.refs_5_, bf16[256,768]{1,0:T(8,128)(2,1)S(1)} %get-tuple-element.139.q_ref, ...), custom_call_target="tpu_custom_call" | custom-call | flops 1048576 | bytes 65536 | tf_op jit(solution)/shard_map/attend_back/pallas_call | solution.py:159
  70.9 2.7 %attend_back.4 = (bf16[256,256]{1,0:T(8,128)(2,1)S(1)}, bf16[5,256,256]{2,1,0:T(8,128)(2,1)S(1)}, bf16[5,256,256]{2,1,0:T(8,128)(2,1)S(1)}, f32[2,256]{1,0:T(2,128)S(1)}) custom-call(s32[2]{0:T(128)S(1)} %get-tuple-element.156.bounds.refs_5_, bf16[256,768]{1,0:T(8,128)(2,1)S(1)} %get-tuple-element.139.q_ref, ...), custom_call_target="tpu_custom_call" | custom-call | flops 1048576 | bytes 65536 | tf_op jit(solution)/shard_map/attend_back/pallas_call | solution.py:159
  73.5 2.7 %attend_back.5 = (bf16[256,256]{1,0:T(8,128)(2,1)S(1)}, bf16[5,256,256]{2,1,0:T(8,128)(2,1)S(1)}, bf16[5,256,256]{2,1,0:T(8,128)(2,1)S(1)}, f32[2,256]{1,0:T(2,128)S(1)}) custom-call(s32[2]{0:T(128)S(1)} %get-tuple-element.156.bounds.refs_5_, bf16[256,768]{1,0:T(8,128)(2,1)S(1)} %get-tuple-element.139.q_ref, ...), custom_call_target="tpu_custom_call" | custom-call | flops 1048576 | bytes 65536 | tf_op jit(solution)/shard_map/attend_back/pallas_call | solution.py:159
  76.3 2.6 %parts.1 = (bf16[4,256,768]{2,1,0:T(8,128)(2,1)S(1)}, f32[256,768]{1,0:T(8,128)S(1)}) custom-call(s32[2]{0:T(128)S(1)} %get-tuple-element.156.bounds.refs_5_, bf16[256,256]{1,0:T(8,128)(2,1)S(1)} %get-tuple-element.188.refs_0_.refs_6_, bf16[256,256]{1,0:T(8,128)(2,1)S(1)} %get-tuple-element.189.refs_1_.refs_7_, ...), custom_call_target="tpu_custom_call" | custom-call | flops 1048576 | bytes 65536 | tf_op jit(solution)/shard_map/parts/pallas_call | solution.py:159
  80.2 8.0 %collective-permute-start.14 = (bf16[256,768]{1,0:T(8,128)(2,1)S(1)}, bf16[256,768]{1,0:T(8,128)(2,1)S(1)}, u32[]{:S(2)}, u32[]{:S(2)}) collective-permute-start(bf16[256,768]{1,0:T(8,128)(2,1)S(1)} %get-tuple-element.290), channel_id=1, source_target_pairs={{0,1},{1,2},{2,3},{4,5},{5,6},{6,7},{8,9},{9,10},{10,11},{12,13},{... | collective-permute-start | bytes 1179656 | tf_op jit(solution)/shard_map/ppermute | solution.py:50
  88.4 6.9 %collective-permute-start.17 = (bf16[192,768]{1,0:T(8,128)(2,1)S(1)}, bf16[192,768]{1,0:T(8,128)(2,1)S(1)}, u32[]{:S(2)}, u32[]{:S(2)}) collective-permute-start(bf16[192,768]{1,0:T(8,128)(2,1)S(1)} %get-tuple-element.281), channel_id=1, source_target_pairs={{0,16},{4,20},{8,24},{12,28},{16,0},{20,4},{24,8},{28,12},{1,17},{... | collective-permute-start | bytes 884744 | tf_op jit(solution)/shard_map/ppermute | solution.py:44
  95.4 4.1 %weights.1 = (bf16[384,2304]{1,0:T(8,128)(2,1)S(1)}, bf16[384,2304]{1,0:T(8,128)(2,1)S(1)}) custom-call(s32[28]{0:T(128)S(1)} %pad_add_fusion.table, bf16[272,768]{1,0:T(8,128)(2,1)S(1)} %collective-permute-done.9.xa_ref.refs_0_, bf16[272,768]{1,0:T(8,128)(2,1)S(1)} %collective-permute-done.7.xa_ref.refs_1_, ...), custom_call_target="tpu_custom_call" | custom-call | flops 1048576 | bytes 65536 | tf_op jit(solution)/shard_map/weights/pallas_call | solution.py:159
  106.1 4.8 %collective-permute-start.20 = (bf16[256,768]{1,0:T(8,128)(2,1)S(1)}, bf16[256,768]{1,0:T(8,128)(2,1)S(1)}, u32[]{:S(2)}, u32[]{:S(2)}) collective-permute-start(bf16[256,768]{1,0:T(8,128)(2,1)S(1)} %get-tuple-element.288), channel_id=1, source_target_pairs={{0,1},{1,2},{2,3},{4,5},{5,6},{6,7},{8,9},{9,10},{10,11},{12,13},{... | collective-permute-start | bytes 1179656 | tf_op jit(solution)/shard_map/ppermute | solution.py:50
  110.9 7.2 %collective-permute-done.21 = bf16[2,48,3840]{2,1,0:T(8,128)(2,1)S(1)} collective-permute-done((bf16[2,48,3840]{2,1,0:T(8,128)(2,1)S(1)}, bf16[2,48,3840]{2,1,0:T(8,128)(2,1)S(1)}, u32[]{:S(2)}, u32[]{:S(2)}) %collective-permute-start.21) | collective-permute-done | bytes 737312 | tf_op jit(solution)/shard_map/ppermute | solution.py:44
  121.7 2.1 %collective-permute-start.31 = (bf16[192,768]{1,0:T(8,128)(2,1)S(1)}, bf16[192,768]{1,0:T(8,128)(2,1)S(1)}, u32[]{:S(2)}, u32[]{:S(2)}) collective-permute-start(bf16[192,768]{1,0:T(8,128)(2,1)S(1)} %get-tuple-element.273), channel_id=1, source_target_pairs={{0,1},{1,0},{2,3},{3,2},{4,5},{5,4},{6,7},{7,6},{8,9},{9,8},{10,11... | collective-permute-start | bytes 884744 | tf_op jit(solution)/shard_map/ppermute | solution.py:44
  125.3 3.5 %collective-permute-done.24 = bf16[48,3840]{1,0:T(8,128)(2,1)S(1)} collective-permute-done((bf16[48,3840]{1,0:T(8,128)(2,1)S(1)}, bf16[48,3840]{1,0:T(8,128)(2,1)S(1)}, u32[]{:S(2)}, u32[]{:S(2)}) %collective-permute-start.24) | collective-permute-done | bytes 368672 | tf_op jit(solution)/shard_map/ppermute | solution.py:44
  128.8 2.5 %collective-permute-done.25 = bf16[48,3840]{1,0:T(8,128)(2,1)S(1)} collective-permute-done((bf16[48,3840]{1,0:T(8,128)(2,1)S(1)}, bf16[48,3840]{1,0:T(8,128)(2,1)S(1)}, u32[]{:S(2)}, u32[]{:S(2)}) %collective-permute-start.25) | collective-permute-done | bytes 368672 | tf_op jit(solution)/shard_map/ppermute | solution.py:44
  132.5 3.8 %collective-permute-start.27 = (bf16[48,3840]{1,0:T(8,128)(2,1)S(1)}, bf16[48,3840]{1,0:T(8,128)(2,1)S(1)}, u32[]{:S(2)}, u32[]{:S(2)}) collective-permute-start(bf16[48,3840]{1,0:T(8,128)(2,1)S(1)} %get-tuple-element.270), channel_id=1, source_target_pairs={{0,1},{1,0},{2,3},{3,2},{4,5},{5,4},{6,7},{7,6},{8,9},{9,8},{10,11... | collective-permute-start | bytes 1105928 | tf_op jit(solution)/shard_map/ppermute | solution.py:44
  136.6 3.0 %collective-permute-start.35 = (bf16[192,768]{1,0:T(8,128)(2,1)S(1)}, bf16[192,768]{1,0:T(8,128)(2,1)S(1)}, u32[]{:S(2)}, u32[]{:S(2)}) collective-permute-start(bf16[192,768]{1,0:T(8,128)(2,1)S(1)} %add_convert_fusion.9), channel_id=1, source_target_pairs={{0,2},{1,3},{2,0},{3,1},{4,6},{5,7},{6,4},{7,5},{8,10},{9,11},{10,... | collective-permute-start | bytes 884744 | tf_op jit(solution)/shard_map/ppermute | solution.py:44
  139.5 2.7 %collective-permute-done.29 = bf16[2,48,2304]{2,1,0:T(8,128)(2,1)S(1)} collective-permute-done((bf16[2,48,2304]{2,1,0:T(8,128)(2,1)S(1)}, bf16[2,48,2304]{2,1,0:T(8,128)(2,1)S(1)}, u32[]{:S(2)}, u32[]{:S(2)}) %collective-permute-start.29) | collective-permute-done | bytes 442400 | tf_op jit(solution)/shard_map/ppermute | solution.py:44
  146.4 12.5 %collective-permute-done.35 = bf16[192,768]{1,0:T(8,128)(2,1)S(1)} collective-permute-done((bf16[192,768]{1,0:T(8,128)(2,1)S(1)}, bf16[192,768]{1,0:T(8,128)(2,1)S(1)}, u32[]{:S(2)}, u32[]{:S(2)}) %collective-permute-start.35) | collective-permute-done | bytes 294944 | tf_op jit(solution)/shard_map/ppermute | solution.py:44
  160.6 2.3 %collective-permute-start.36 = (f32[16,768]{1,0:T(8,128)S(1)}, f32[16,768]{1,0:T(8,128)S(1)}, u32[]{:S(2)}, u32[]{:S(2)}) collective-permute-start(f32[16,768]{1,0:T(8,128)S(1)} %add.361), channel_id=1, source_target_pairs={{0,8},{4,12},{8,0},{12,4},{16,24},{20,28},{24,16},{28,20},{1,9},{5... | collective-permute-start | bytes 147464 | tf_op jit(solution)/shard_map/ppermute | solution.py:44
  169.8 7.0 %collective-permute-done.40 = bf16[192,768]{1,0:T(8,128)(2,1)S(1)} collective-permute-done((bf16[192,768]{1,0:T(8,128)(2,1)S(1)}, bf16[192,768]{1,0:T(8,128)(2,1)S(1)}, u32[]{:S(2)}, u32[]{:S(2)}) %collective-permute-start.40) | collective-permute-done | bytes 294944 | tf_op jit(solution)/shard_map/ppermute | solution.py:44
  179.3 2.6 %fusion.36 = (bf16[384,768]{1,0:T(8,128)(2,1)}, f32[384,768]{1,0:T(8,128)}, f32[384,768]{1,0:T(8,128)}, f32[384,768]{1,0:T(8,128)}) fusion(f32[384,768]{1,0:T(8,128)S(1)} %copy-done.8, f32[]{:T(128)} %bitcast.36, f32[]{:T(128)} %bitcast.35, f32[]{:T(128)} %bitcast.34, bf16[192,768]{1,0:T(8,128)(2,1)S(1)} %get-tuple-element.295, ...), kind=kLoop, calls=%fused_computation.110 | loop fusion | flops 5603328 | bytes 8257548 | tf_op jit(solution)/shard_map/convert_element_type | solution.py:677
  183.2 2.1 %collective-permute-start.42 = (bf16[48,2304]{1,0:T(8,128)(2,1)S(1)}, bf16[48,2304]{1,0:T(8,128)(2,1)S(1)}, u32[]{:S(2)}, u32[]{:S(2)}) collective-permute-start(bf16[48,2304]{1,0:T(8,128)(2,1)S(1)} %add_convert_fusion.10), channel_id=1, source_target_pairs={{0,1},{1,0},{2,3},{3,2},{4,5},{5,4},{6,7},{7,6},{8,9},{9,8},{10,11... | collective-permute-start | bytes 663560 | tf_op jit(solution)/shard_map/ppermute | solution.py:44
  185.3 3.0 %collective-permute-done.43 = bf16[48,3840]{1,0:T(8,128)(2,1)S(1)} collective-permute-done((bf16[48,3840]{1,0:T(8,128)(2,1)S(1)}, bf16[48,3840]{1,0:T(8,128)(2,1)S(1)}, u32[]{:S(2)}, u32[]{:S(2)}) %collective-permute-start.43) | collective-permute-done | bytes 368672 | tf_op jit(solution)/shard_map/ppermute | solution.py:44
  188.4 2.6 %fusion.39 = (bf16[96,3072]{1,0:T(8,128)(2,1)}, f32[96,3072]{1,0:T(8,128)}, f32[96,3072]{1,0:T(8,128)}, f32[96,3072]{1,0:T(8,128)}) fusion(f32[96,3072]{1,0:T(8,128)S(1)} %copy-done.11, f32[]{:T(128)} %bitcast.36, f32[]{:T(128)} %bitcast.35, f32[]{:T(128)} %bitcast.34, bf16[48,3840]{1,0:T(8,128)(2,1)S(1)} %get-tuple-element.293, ...), kind=kLoop, calls=%fused_computation.111 | loop fusion | flops 5603328 | bytes 8405004 | tf_op jit(solution)/shard_map/convert_element_type | solution.py:677
  (169 shorter events, 60.0 us)
Async XLA Ops:
  21.8 7.9 %collective-permute-start.7 = (bf16[272,768]{1,0:T(8,128)(2,1)S(1)}, bf16[272,768]{1,0:T(8,128)(2,1)S(1)}, u32[]{:S(2)}, u32[]{:S(2)}) collective-permute-start(bf16[272,768]{1,0:T(8,128)(2,1)S(1)} %get-tuple-element.137.x_ref.refs_2_), channel_id=1, source_target_pairs={{0,1},{1,2},{2,3},{4,5},{5,6},{6,7},{8,9},{9,10},{10,11},{12,13},{... | collective-permute-start | bytes 1253384 | tf_op jit(solution)/shard_map/ppermute | solution.py:50
  23.5 10.3 %collective-permute-start.8 = (bf16[272,768]{1,0:T(8,128)(2,1)S(1)}, bf16[272,768]{1,0:T(8,128)(2,1)S(1)}, u32[]{:S(2)}, u32[]{:S(2)}) collective-permute-start(bf16[272,768]{1,0:T(8,128)(2,1)S(1)} %get-tuple-element.137.x_ref.refs_2_), channel_id=1, source_target_pairs={{1,0},{2,1},{3,2},{5,4},{6,5},{7,6},{9,8},{10,9},{11,10},{13,12},{... | collective-permute-start | bytes 1253384 | tf_op jit(solution)/shard_map/ppermute | solution.py:50
  33.8 9.1 %collective-permute-start.9 = (bf16[272,768]{1,0:T(8,128)(2,1)S(1)}, bf16[272,768]{1,0:T(8,128)(2,1)S(1)}, u32[]{:S(2)}, u32[]{:S(2)}) collective-permute-start(bf16[272,768]{1,0:T(8,128)(2,1)S(1)} %collective-permute-done.7.xa_ref.refs_1_), channel_id=1, source_target_pairs={{0,1},{1,2},{2,3},{4,5},{5,6},{6,7},{8,9},{9,10},{10,11},{12,13},{... | collective-permute-start | bytes 1253384 | tf_op jit(solution)/shard_map/ppermute | solution.py:50
  37.4 9.9 %collective-permute-start.10 = (bf16[272,768]{1,0:T(8,128)(2,1)S(1)}, bf16[272,768]{1,0:T(8,128)(2,1)S(1)}, u32[]{:S(2)}, u32[]{:S(2)}) collective-permute-start(bf16[272,768]{1,0:T(8,128)(2,1)S(1)} %collective-permute-done.8.xb_ref.refs_3_), channel_id=1, source_target_pairs={{1,0},{2,1},{3,2},{5,4},{6,5},{7,6},{9,8},{10,9},{11,10},{13,12},{... | collective-permute-start | bytes 1253384 | tf_op jit(solution)/shard_map/ppermute | solution.py:50
  64.6 11.7 %collective-permute-start.12 = (bf16[384,3840]{1,0:T(8,128)(2,1)S(1)}, bf16[384,3840]{1,0:T(8,128)(2,1)S(1)}, u32[]{:S(2)}, u32[]{:S(2)}) collective-permute-start(bf16[384,3840]{1,0:T(8,128)(2,1)S(1)} %get-tuple-element.173), channel_id=1, source_target_pairs={{0,4},{4,0},{8,12},{12,8},{16,20},{20,16},{24,28},{28,24},{1,5},{5... | collective-permute-start | bytes 8847368 | tf_op jit(solution)/shard_map/ppermute | solution.py:44
  69.4 18.8 %collective-permute-start.15 = (bf16[2,192,768]{2,1,0:T(8,128)(2,1)S(1)}, bf16[2,192,768]{2,1,0:T(8,128)(2,1)S(1)}, u32[]{:S(2)}, u32[]{:S(2)}) collective-permute-start(bf16[2,192,768]{2,1,0:T(8,128)(2,1)S(1)} %get-tuple-element.283), channel_id=1, source_target_pairs={{0,8},{4,12},{8,0},{12,4},{16,24},{20,28},{24,16},{28,20},{1,9},{5... | collective-permute-start | bytes 1769480 | tf_op jit(solution)/shard_map/ppermute | solution.py:44
  70.0 18.2 %collective-permute-start.16 = (bf16[2,192,768]{2,1,0:T(8,128)(2,1)S(1)}, bf16[2,192,768]{2,1,0:T(8,128)(2,1)S(1)}, u32[]{:S(2)}, u32[]{:S(2)}) collective-permute-start(bf16[2,192,768]{2,1,0:T(8,128)(2,1)S(1)} %get-tuple-element.282), channel_id=1, source_target_pairs={{0,16},{4,20},{8,24},{12,28},{16,0},{20,4},{24,8},{28,12},{1,17},{... | collective-permute-start | bytes 1769480 | tf_op jit(solution)/shard_map/ppermute | solution.py:44
  78.9 23.2 %collective-permute-start.13 = (bf16[256,768]{1,0:T(8,128)(2,1)S(1)}, bf16[256,768]{1,0:T(8,128)(2,1)S(1)}, u32[]{:S(2)}, u32[]{:S(2)}) collective-permute-start(bf16[256,768]{1,0:T(8,128)(2,1)S(1)} %get-tuple-element.291), channel_id=1, source_target_pairs={{1,0},{2,1},{3,2},{5,4},{6,5},{7,6},{9,8},{10,9},{11,10},{13,12},{... | collective-permute-start | bytes 1179656 | tf_op jit(solution)/shard_map/ppermute | solution.py:50
  80.2 21.9 %collective-permute-start.14 = (bf16[256,768]{1,0:T(8,128)(2,1)S(1)}, bf16[256,768]{1,0:T(8,128)(2,1)S(1)}, u32[]{:S(2)}, u32[]{:S(2)}) collective-permute-start(bf16[256,768]{1,0:T(8,128)(2,1)S(1)} %get-tuple-element.290), channel_id=1, source_target_pairs={{0,1},{1,2},{2,3},{4,5},{5,6},{6,7},{8,9},{9,10},{10,11},{12,13},{... | collective-permute-start | bytes 1179656 | tf_op jit(solution)/shard_map/ppermute | solution.py:50
  88.4 11.6 %collective-permute-start.17 = (bf16[192,768]{1,0:T(8,128)(2,1)S(1)}, bf16[192,768]{1,0:T(8,128)(2,1)S(1)}, u32[]{:S(2)}, u32[]{:S(2)}) collective-permute-start(bf16[192,768]{1,0:T(8,128)(2,1)S(1)} %get-tuple-element.281), channel_id=1, source_target_pairs={{0,16},{4,20},{8,24},{12,28},{16,0},{20,4},{24,8},{28,12},{1,17},{... | collective-permute-start | bytes 884744 | tf_op jit(solution)/shard_map/ppermute | solution.py:44
  102.5 15.6 %collective-permute-start.21 = (bf16[2,48,3840]{2,1,0:T(8,128)(2,1)S(1)}, bf16[2,48,3840]{2,1,0:T(8,128)(2,1)S(1)}, u32[]{:S(2)}, u32[]{:S(2)}) collective-permute-start(bf16[2,48,3840]{2,1,0:T(8,128)(2,1)S(1)} %bitcast.95), channel_id=1, source_target_pairs={{0,8},{4,12},{8,0},{12,4},{16,24},{20,28},{24,16},{28,20},{1,9},{5... | collective-permute-start | bytes 2211848 | tf_op jit(solution)/shard_map/ppermute | solution.py:44
  103.6 16.3 %collective-permute-start.22 = (bf16[2,48,3840]{2,1,0:T(8,128)(2,1)S(1)}, bf16[2,48,3840]{2,1,0:T(8,128)(2,1)S(1)}, u32[]{:S(2)}, u32[]{:S(2)}) collective-permute-start(bf16[2,48,3840]{2,1,0:T(8,128)(2,1)S(1)} %bitcast.94), channel_id=1, source_target_pairs={{0,16},{4,20},{8,24},{12,28},{16,0},{20,4},{24,8},{28,12},{1,17},{... | collective-permute-start | bytes 2211848 | tf_op jit(solution)/shard_map/ppermute | solution.py:44
  104.6 26.7 %collective-permute-start.28 = (bf16[384,2304]{1,0:T(8,128)(2,1)S(1)}, bf16[384,2304]{1,0:T(8,128)(2,1)S(1)}, u32[]{:S(2)}, u32[]{:S(2)}) collective-permute-start(bf16[384,2304]{1,0:T(8,128)(2,1)S(1)} %get-tuple-element.221), channel_id=1, source_target_pairs={{0,4},{4,0},{8,12},{12,8},{16,20},{20,16},{24,28},{28,24},{1,5},{5... | collective-permute-start | bytes 5308424 | tf_op jit(solution)/shard_map/ppermute | solution.py:44
  104.8 16.9 %collective-permute-start.19 = (bf16[256,768]{1,0:T(8,128)(2,1)S(1)}, bf16[256,768]{1,0:T(8,128)(2,1)S(1)}, u32[]{:S(2)}, u32[]{:S(2)}) collective-permute-start(bf16[256,768]{1,0:T(8,128)(2,1)S(1)} %get-tuple-element.289), channel_id=1, source_target_pairs={{1,0},{2,1},{3,2},{5,4},{6,5},{7,6},{9,8},{10,9},{11,10},{13,12},{... | collective-permute-start | bytes 1179656 | tf_op jit(solution)/shard_map/ppermute | solution.py:50
  106.1 17.7 %collective-permute-start.20 = (bf16[256,768]{1,0:T(8,128)(2,1)S(1)}, bf16[256,768]{1,0:T(8,128)(2,1)S(1)}, u32[]{:S(2)}, u32[]{:S(2)}) collective-permute-start(bf16[256,768]{1,0:T(8,128)(2,1)S(1)} %get-tuple-element.288), channel_id=1, source_target_pairs={{0,1},{1,2},{2,3},{4,5},{5,6},{6,7},{8,9},{9,10},{10,11},{12,13},{... | collective-permute-start | bytes 1179656 | tf_op jit(solution)/shard_map/ppermute | solution.py:50
  120.2 8.6 %collective-permute-start.24 = (bf16[48,3840]{1,0:T(8,128)(2,1)S(1)}, bf16[48,3840]{1,0:T(8,128)(2,1)S(1)}, u32[]{:S(2)}, u32[]{:S(2)}) collective-permute-start(bf16[48,3840]{1,0:T(8,128)(2,1)S(1)} %get-tuple-element.277), channel_id=1, source_target_pairs={{0,16},{4,20},{8,24},{12,28},{16,0},{20,4},{24,8},{28,12},{1,17},{... | collective-permute-start | bytes 1105928 | tf_op jit(solution)/shard_map/ppermute | solution.py:44
  121.2 10.0 %collective-permute-start.25 = (bf16[48,3840]{1,0:T(8,128)(2,1)S(1)}, bf16[48,3840]{1,0:T(8,128)(2,1)S(1)}, u32[]{:S(2)}, u32[]{:S(2)}) collective-permute-start(bf16[48,3840]{1,0:T(8,128)(2,1)S(1)} %get-tuple-element.276), channel_id=1, source_target_pairs={{0,8},{4,12},{8,0},{12,4},{16,24},{20,28},{24,16},{28,20},{1,9},{5... | collective-permute-start | bytes 1105928 | tf_op jit(solution)/shard_map/ppermute | solution.py:44
  121.7 14.7 %collective-permute-start.31 = (bf16[192,768]{1,0:T(8,128)(2,1)S(1)}, bf16[192,768]{1,0:T(8,128)(2,1)S(1)}, u32[]{:S(2)}, u32[]{:S(2)}) collective-permute-start(bf16[192,768]{1,0:T(8,128)(2,1)S(1)} %get-tuple-element.273), channel_id=1, source_target_pairs={{0,1},{1,0},{2,3},{3,2},{4,5},{5,4},{6,7},{7,6},{8,9},{9,8},{10,11... | collective-permute-start | bytes 884744 | tf_op jit(solution)/shard_map/ppermute | solution.py:44
  125.2 11.1 %collective-permute-start.23 = (f32[16,768]{1,0:T(8,128)S(1)}, f32[16,768]{1,0:T(8,128)S(1)}, u32[]{:S(2)}, u32[]{:S(2)}) collective-permute-start(f32[16,768]{1,0:T(8,128)S(1)} %get-tuple-element.216), channel_id=1, source_target_pairs={{0,1},{1,0},{2,3},{3,2},{4,5},{5,4},{6,7},{7,6},{8,9},{9,8},{10,11... | collective-permute-start | bytes 147464 | tf_op jit(solution)/shard_map/ppermute | solution.py:44
  131.5 10.7 %collective-permute-start.29 = (bf16[2,48,2304]{2,1,0:T(8,128)(2,1)S(1)}, bf16[2,48,2304]{2,1,0:T(8,128)(2,1)S(1)}, u32[]{:S(2)}, u32[]{:S(2)}) collective-permute-start(bf16[2,48,2304]{2,1,0:T(8,128)(2,1)S(1)} %bitcast.97), channel_id=1, source_target_pairs={{0,8},{4,12},{8,0},{12,4},{16,24},{20,28},{24,16},{28,20},{1,9},{5... | collective-permute-start | bytes 1327112 | tf_op jit(solution)/shard_map/ppermute | solution.py:44
  131.5 10.7 %collective-permute-start.30 = (bf16[2,48,2304]{2,1,0:T(8,128)(2,1)S(1)}, bf16[2,48,2304]{2,1,0:T(8,128)(2,1)S(1)}, u32[]{:S(2)}, u32[]{:S(2)}) collective-permute-start(bf16[2,48,2304]{2,1,0:T(8,128)(2,1)S(1)} %bitcast.96), channel_id=1, source_target_pairs={{0,16},{4,20},{8,24},{12,28},{16,0},{20,4},{24,8},{28,12},{1,17},{... | collective-permute-start | bytes 1327112 | tf_op jit(solution)/shard_map/ppermute | solution.py:44
  132.5 12.5 %collective-permute-start.27 = (bf16[48,3840]{1,0:T(8,128)(2,1)S(1)}, bf16[48,3840]{1,0:T(8,128)(2,1)S(1)}, u32[]{:S(2)}, u32[]{:S(2)}) collective-permute-start(bf16[48,3840]{1,0:T(8,128)(2,1)S(1)} %get-tuple-element.270), channel_id=1, source_target_pairs={{0,1},{1,0},{2,3},{3,2},{4,5},{5,4},{6,7},{7,6},{8,9},{9,8},{10,11... | collective-permute-start | bytes 1105928 | tf_op jit(solution)/shard_map/ppermute | solution.py:44
  136.3 10.0 %collective-permute-start.26 = (f32[16,768]{1,0:T(8,128)S(1)}, f32[16,768]{1,0:T(8,128)S(1)}, u32[]{:S(2)}, u32[]{:S(2)}) collective-permute-start(f32[16,768]{1,0:T(8,128)S(1)} %add.344), channel_id=1, source_target_pairs={{0,2},{1,3},{2,0},{3,1},{4,6},{5,7},{6,4},{7,5},{8,10},{9,11},{10,... | collective-permute-start | bytes 147464 | tf_op jit(solution)/shard_map/ppermute | solution.py:44
  136.6 22.3 %collective-permute-start.35 = (bf16[192,768]{1,0:T(8,128)(2,1)S(1)}, bf16[192,768]{1,0:T(8,128)(2,1)S(1)}, u32[]{:S(2)}, u32[]{:S(2)}) collective-permute-start(bf16[192,768]{1,0:T(8,128)(2,1)S(1)} %add_convert_fusion.9), channel_id=1, source_target_pairs={{0,2},{1,3},{2,0},{3,1},{4,6},{5,7},{6,4},{7,5},{8,10},{9,11},{10,... | collective-permute-start | bytes 884744 | tf_op jit(solution)/shard_map/ppermute | solution.py:44
  142.4 16.4 %collective-permute-start.33 = (bf16[48,2304]{1,0:T(8,128)(2,1)S(1)}, bf16[48,2304]{1,0:T(8,128)(2,1)S(1)}, u32[]{:S(2)}, u32[]{:S(2)}) collective-permute-start(bf16[48,2304]{1,0:T(8,128)(2,1)S(1)} %get-tuple-element.285), channel_id=1, source_target_pairs={{0,16},{4,20},{8,24},{12,28},{16,0},{20,4},{24,8},{28,12},{1,17},{... | collective-permute-start | bytes 663560 | tf_op jit(solution)/shard_map/ppermute | solution.py:44
  142.9 16.0 %collective-permute-start.34 = (bf16[48,2304]{1,0:T(8,128)(2,1)S(1)}, bf16[48,2304]{1,0:T(8,128)(2,1)S(1)}, u32[]{:S(2)}, u32[]{:S(2)}) collective-permute-start(bf16[48,2304]{1,0:T(8,128)(2,1)S(1)} %get-tuple-element.284), channel_id=1, source_target_pairs={{0,8},{4,12},{8,0},{12,4},{16,24},{20,28},{24,16},{28,20},{1,9},{5... | collective-permute-start | bytes 663560 | tf_op jit(solution)/shard_map/ppermute | solution.py:44
  145.1 21.2 %collective-permute-start.38 = (bf16[48,3840]{1,0:T(8,128)(2,1)S(1)}, bf16[48,3840]{1,0:T(8,128)(2,1)S(1)}, u32[]{:S(2)}, u32[]{:S(2)}) collective-permute-start(bf16[48,3840]{1,0:T(8,128)(2,1)S(1)} %add_convert_fusion.7), channel_id=1, source_target_pairs={{0,2},{1,3},{2,0},{3,1},{4,6},{5,7},{6,4},{7,5},{8,10},{9,11},{10,... | collective-permute-start | bytes 1105928 | tf_op jit(solution)/shard_map/ppermute | solution.py:44
  159.2 7.2 %collective-permute-start.39 = (bf16[48,2304]{1,0:T(8,128)(2,1)S(1)}, bf16[48,2304]{1,0:T(8,128)(2,1)S(1)}, u32[]{:S(2)}, u32[]{:S(2)}) collective-permute-start(bf16[48,2304]{1,0:T(8,128)(2,1)S(1)} %get-tuple-element.267), channel_id=1, source_target_pairs={{0,1},{1,0},{2,3},{3,2},{4,5},{5,4},{6,7},{7,6},{8,9},{9,8},{10,11... | collective-permute-start | bytes 663560 | tf_op jit(solution)/shard_map/ppermute | solution.py:44
  163.5 13.2 %collective-permute-start.40 = (bf16[192,768]{1,0:T(8,128)(2,1)S(1)}, bf16[192,768]{1,0:T(8,128)(2,1)S(1)}, u32[]{:S(2)}, u32[]{:S(2)}) collective-permute-start(bf16[192,768]{1,0:T(8,128)(2,1)S(1)} %add_convert_fusion.8), channel_id=1, source_target_pairs={{0,1},{1,0},{2,3},{3,2},{4,5},{5,4},{6,7},{7,6},{8,9},{9,8},{10,11... | collective-permute-start | bytes 884744 | tf_op jit(solution)/shard_map/ppermute | solution.py:44
  166.4 16.7 %collective-permute-start.41 = (bf16[48,2304]{1,0:T(8,128)(2,1)S(1)}, bf16[48,2304]{1,0:T(8,128)(2,1)S(1)}, u32[]{:S(2)}, u32[]{:S(2)}) collective-permute-start(bf16[48,2304]{1,0:T(8,128)(2,1)S(1)} %add_convert_fusion.11), channel_id=1, source_target_pairs={{0,2},{1,3},{2,0},{3,1},{4,6},{5,7},{6,4},{7,5},{8,10},{9,11},{10,... | collective-permute-start | bytes 663560 | tf_op jit(solution)/shard_map/ppermute | solution.py:44
  176.9 11.4 %collective-permute-start.43 = (bf16[48,3840]{1,0:T(8,128)(2,1)S(1)}, bf16[48,3840]{1,0:T(8,128)(2,1)S(1)}, u32[]{:S(2)}, u32[]{:S(2)}) collective-permute-start(bf16[48,3840]{1,0:T(8,128)(2,1)S(1)} %add_convert_fusion.6), channel_id=1, source_target_pairs={{0,1},{1,0},{2,3},{3,2},{4,5},{5,4},{6,7},{7,6},{8,9},{9,8},{10,11... | collective-permute-start | bytes 1105928 | tf_op jit(solution)/shard_map/ppermute | solution.py:44
  183.2 8.9 %collective-permute-start.42 = (bf16[48,2304]{1,0:T(8,128)(2,1)S(1)}, bf16[48,2304]{1,0:T(8,128)(2,1)S(1)}, u32[]{:S(2)}, u32[]{:S(2)}) collective-permute-start(bf16[48,2304]{1,0:T(8,128)(2,1)S(1)} %add_convert_fusion.10), channel_id=1, source_target_pairs={{0,1},{1,0},{2,3},{3,2},{4,5},{5,4},{6,7},{7,6},{8,9},{9,8},{10,11... | collective-permute-start | bytes 663560 | tf_op jit(solution)/shard_map/ppermute | solution.py:44
  (40 other events, 204.7 us)

commit v7 on v6

--- a/solution.py
+++ b/solution.py
@@ -595,7 +595,7 @@
     xs, bounds = refs[:slots], refs[slots]
     refs = refs[slots + 1 :]
     dqs, dks, dvs = (refs[k * groups : (k + 1) * groups] for k in range(3))
-    keep_ref, send_ref, xt, plain = refs[3 * groups :]
+    keep_ref, send_ref, xt, plain = refs[-4:]
     width, size = dqs[0].shape
     features = size * groups
     few = min(3, slots)
@@ -953,37 +953,78 @@
         mib=6,
     )
     to_left, to_right = parts[0], parts[2 * reach - 1]
-    token[:] = [to_left, to_right]
-    from_right, from_left = moved(to_left, "blk", -1), moved(to_right, "blk", 1)
-    advance(first)
+    back_one = together(*[one.arrived for one in first], expand_in, to_left)
+    for one, value in zip(first, back_one):
+        one.arrived = value
+        one.take()
+    expand_in, to_left = back_one[-2:]
+    second = scatters(expand_keep, expand_in, owned)
+    for one in first + second:
+        if one.order:
+            one.prepare()
 
     kept_inlet = struct((features // 2, wkv), bf16)
-    grads = after(*grads)
     inlet_keep, inlet_send = call(
         functools.partial(weight_kernel, reach, half, steps),
         "weights",
         table,
-        xs + [(scalar, bounds), *grads],
+        xs
+        + [(scalar, bounds), *grads]
+        + [(pl.BlockSpec(memory_space=pl.ANY), one.sent) for one in first + second if one.order],
         [kept_inlet, kept_inlet],
         [vmem((features, slots * width), bf16), vmem((features, width), f32)],
         mib=8,
     )
+    for one in first + second:
+        if one.order:
+            one.send()
+    inlet_in = flipped(inlet_send, "dp", 1)
+    tied = together(*[one.arrived for one in second], inlet_keep)
+    for one, value in zip(second, tied):
+        one.arrived = value
+        one.take()
+    inlet_keep = tied[-1]
+    if second[0].order:
+        launch(second)
+    while True:
+        tied = together(
+            *[one.arrived for one in first],
+            to_left,
+            to_right,
+            *[one.addends[-1] for one in second],
+        )
+        for one, value in zip(first, tied):
+            one.arrived = value
+            one.take()
+        to_left, to_right = tied[2:4]
+        for one, value in zip(second, tied[4:]):
+            one.addends[-1] = value
+        if not first[0].order:
+            break
+        for one in first:
+            one.prepare()
+            one.send()
+    from_right, from_left = moved(to_left, "blk", -1), moved(to_right, "blk", 1)
     token[:] = [inlet_keep]
-    inlet_in = flipped(inlet_send, "dp", 1)
-    while first[0].order:
-        advance(first)
-    advance(first)
-    (expand_in,) = after(expand_in)
-    from_right, from_left, expand_in = together(from_right, from_left, expand_in)
-    second = scatters(expand_keep, expand_in, owned)
-    launch(second)
+    line_one = begin(first)
+    while second[0].order:
+        advance(second)
+    from_right, from_left, inlet_in, *arrived = together(
+        from_right, from_left, inlet_in, *[one.arrived for one in second]
+    )
+    for one, value in zip(second, arrived):
+        one.arrived = value
+        one.take()
+    third = scatters(inlet_keep, inlet_in, owned)
+    launch(third)
     for d in range(reach - 1, 0, -1):
         from_right, from_left = after(from_right, from_left)
         to_left = added(parts[reach - d], from_right)
         to_right = added(parts[reach + d - 1], from_left)
         token[:] = [to_left, to_right]
         from_right, from_left = moved(to_left, "blk", -1), moved(to_right, "blk", 1)
-    advance(second)
+    line_two = begin(second)
+    follow(line_one, Line.exchange)
     from_right, from_left = after(from_right, from_left)
     grad_normed, small = call(
         leave_kernel,
@@ -1006,25 +1047,15 @@
     )
     token[:] = [small]
     rounds = SmallSum(small, paired=False)
-    (inlet_in,) = after(inlet_in)
-    third = scatters(inlet_keep, inlet_in, owned)
-    launch(third)
-    line_one = begin(first)
     rounds.send()
-    while second[0].order:
-        advance(second)
-    advance(second)
-    line_two = begin(second)
-    next_round()
-    follow(line_one, Line.exchange)
     advance(third)
     follow(line_two, Line.exchange)
     next_round()
-    follow(line_one, Line.gather)
     while third[0].order:
         advance(third)
     advance(third)
     line_three = begin(third)
+    follow(line_one, Line.gather)
     while rounds.left():
         next_round()
     (line_two.arrived, line_three.arrived) = after(line_two.arrived, line_three.arrived)

time: 198 us -> 210 us (1.061); the launches traced: 195 us -> 210 us
  waiting for transfers between devices: 66.2 us -> 92.2 us
  starting transfers between devices: 66.4 us -> 56.4 us
    ppermute x36, waiting for transfers between devices: 54.2 us -> 74.4 us  [flipped(): return lax.ppermute(block, axis, [(i, i ^ bit) for i in range(size)])]
    ppermute x36, starting transfers between devices: 43 us -> 33.2 us  [flipped(): return lax.ppermute(block, axis, [(i, i ^ bit) for i in range(size)])]
    ppermute x8, waiting for transfers between devices: 12.1 us -> 17.8 us  [moved(): return lax.ppermute(block, axis, route)]
  transfers between devices with their start and end apart: 44 -> 44, of which waited for: 23 -> 25; matrix products, arithmetic and copies ran while one was open for 7% -> 7% of each run, Pallas kernels for 10% -> 9%
where the time goes in v7:
time: 210 us
  waiting for transfers between devices  92.2 us (44%)
  starting transfers between devices  56.4 us (27%)
  Pallas kernels  37.8 us (18%)
  other arithmetic  16.4 us (8%)
  local copies, waits for them, and re-layouts  4.97 us (2%)
    ppermute x36, waiting for transfers between devices, flipped(): return lax.ppermute(block, axis, [(i, i ^ bit) for i in range(size)])  74.4 us
    pallas_call x13, Pallas kernels, call(): pl.pallas_call(kernel, grid_spec=pltpu.PrefetchScalarGridSpec(num_scalar_...  37.8 us
    ppermute x36, starting transfers between devices, flipped(): return lax.ppermute(block, axis, [(i, i ^ bit) for i in range(size)])  33.2 us
    ppermute x8, starting transfers between devices, moved(): return lax.ppermute(block, axis, route)  23.2 us
    ppermute x8, waiting for transfers between devices, moved(): return lax.ppermute(block, axis, route)  17.8 us
    convert_element_type x5, other arithmetic, adam_rule(): return (weight_new, moment_new, square_new, weight_new.astype(bf16))  8.91 us
    unnamed x56, local copies, waits for them, and re-layouts  4.85 us
  transfers between devices with their start and end apart: 44, of which 25 were waited for; matrix products, arithmetic and copies ran while one was open for 7% of the time, Pallas kernels for 9%

profile of v7, /device:TPU:0, one launch (start us, length us, event | category | flops | bytes accessed | tf_op | source)
XLA Modules:
  0.0 209.8 jit_solution(2808196918551640373)
XLA Ops:
  3.3 2.8 %collective-permute-start.1 = (f32[2,768]{1,0:T(2,128)S(1)}, f32[2,768]{1,0:T(2,128)S(1)}, u32[]{:S(2)}, u32[]{:S(2)}) collective-permute-start(f32[2,768]{1,0:T(2,128)S(1)} %add.302), channel_id=1, source_target_pairs={{0,8},{4,12},{8,0},{12,4},{16,24},{20,28},{24,16},{28,20},{1,9},{5... | collective-permute-start | bytes 18440 | tf_op jit(solution)/shard_map/ppermute | solution.py:44
  9.7 2.4 %collective-permute-done.3 = f32[2,768]{1,0:T(2,128)S(1)} collective-permute-done((f32[2,768]{1,0:T(2,128)S(1)}, f32[2,768]{1,0:T(2,128)S(1)}, u32[]{:S(2)}, u32[]{:S(2)}) %collective-permute-start.3) | collective-permute-done | bytes 6176 | tf_op jit(solution)/shard_map/ppermute | solution.py:44
  13.8 2.6 %collective-permute-start.5 = (f32[2,768]{1,0:T(2,128)S(1)}, f32[2,768]{1,0:T(2,128)S(1)}, u32[]{:S(2)}, u32[]{:S(2)}) collective-permute-start(f32[2,768]{1,0:T(2,128)S(1)} %add_add_fusion.1), channel_id=1, source_target_pairs={{0,2},{1,3},{2,0},{3,1},{4,6},{5,7},{6,4},{7,5},{8,10},{9,11},{10,... | collective-permute-start | bytes 18440 | tf_op jit(solution)/shard_map/ppermute | solution.py:44
  18.3 3.5 %collective-permute-done.6 = f32[2,768]{1,0:T(2,128)S(1)} collective-permute-done((f32[2,768]{1,0:T(2,128)S(1)}, f32[2,768]{1,0:T(2,128)S(1)}, u32[]{:S(2)}, u32[]{:S(2)}) %collective-permute-start.6) | collective-permute-done | bytes 6176 | tf_op jit(solution)/shard_map/ppermute | solution.py:44
  30.8 4.1 %collective-permute-done.8.xb_ref.refs_3_ = bf16[272,768]{1,0:T(8,128)(2,1)S(1)} collective-permute-done((bf16[272,768]{1,0:T(8,128)(2,1)S(1)}, bf16[272,768]{1,0:T(8,128)(2,1)S(1)}, u32[]{:S(2)}, u32[]{:S(2)}) %collective-permute-start.8) | collective-permute-done | bytes 417824 | tf_op jit(solution)/shard_map/ppermute | solution.py:50
  36.2 4.8 %collective-permute-start.9 = (bf16[272,768]{1,0:T(8,128)(2,1)S(1)}, bf16[272,768]{1,0:T(8,128)(2,1)S(1)}, u32[]{:S(2)}, u32[]{:S(2)}) collective-permute-start(bf16[272,768]{1,0:T(8,128)(2,1)S(1)} %collective-permute-done.7.xa_ref.refs_1_), channel_id=1, source_target_pairs={{0,1},{1,2},{2,3},{4,5},{5,6},{6,7},{8,9},{9,10},{10,11},{12,13},{... | collective-permute-start | bytes 1253384 | tf_op jit(solution)/shard_map/ppermute | solution.py:50
  42.8 2.1 %collective-permute-done.10.xb_ref.refs_4_ = bf16[272,768]{1,0:T(8,128)(2,1)S(1)} collective-permute-done((bf16[272,768]{1,0:T(8,128)(2,1)S(1)}, bf16[272,768]{1,0:T(8,128)(2,1)S(1)}, u32[]{:S(2)}, u32[]{:S(2)}) %collective-permute-start.10) | collective-permute-done | bytes 417824 | tf_op jit(solution)/shard_map/ppermute | solution.py:50
  47.4 5.3 %attend.1 = (bf16[256,768]{1,0:T(8,128)(2,1)S(1)}, f32[3,4,256]{2,1,0:T(4,128)S(1)}, s32[2]{0:T(128)S(1)}) custom-call(s32[28]{0:T(128)S(1)} %pad_add_fusion.table, bf16[256,768]{1,0:T(8,128)(2,1)S(1)} %get-tuple-element.135.q_ref, bf16[5,256,1536]{2,1,0:T(8,128)(2,1)S(1)} %get-tuple-element.145.kv_ref, s32[1,256]{1,0:T(1,128)S(1)} %copy-done.7, ...), custom_call_target="tpu_custom_call" | custom-call | flops 1048576 | bytes 65536 | tf_op jit(solution)/shard_map/attend/pallas_call | solution.py:159
  52.8 10.8 %ffn.1 = (bf16[256,768]{1,0:T(8,128)(2,1)}, f32[256,768]{1,0:T(8,128)S(1)}, bf16[256,768]{1,0:T(8,128)(2,1)S(1)}, bf16[2,4,192,768]{3,2,1,0:T(8,128)(2,1)S(1)}, ...) custom-call(s32[28]{0:T(128)S(1)} %pad_add_fusion.table, ...), custom_call_target="tpu_custom_call" | custom-call | flops 1048576 | bytes 65536 | tf_op jit(solution)/shard_map/ffn/pallas_call | solution.py:159
  64.1 2.9 %attend_back.3 = (bf16[256,256]{1,0:T(8,128)(2,1)S(1)}, bf16[5,256,256]{2,1,0:T(8,128)(2,1)S(1)}, bf16[5,256,256]{2,1,0:T(8,128)(2,1)S(1)}, f32[2,256]{1,0:T(2,128)S(1)}) custom-call(s32[2]{0:T(128)S(1)} %get-tuple-element.152.bounds.refs_5_, bf16[256,768]{1,0:T(8,128)(2,1)S(1)} %get-tuple-element.135.q_ref, ...), custom_call_target="tpu_custom_call" | custom-call | flops 1048576 | bytes 65536 | tf_op jit(solution)/shard_map/attend_back/pallas_call | solution.py:159
  69.8 2.7 %attend_back.4 = (bf16[256,256]{1,0:T(8,128)(2,1)S(1)}, bf16[5,256,256]{2,1,0:T(8,128)(2,1)S(1)}, bf16[5,256,256]{2,1,0:T(8,128)(2,1)S(1)}, f32[2,256]{1,0:T(2,128)S(1)}) custom-call(s32[2]{0:T(128)S(1)} %get-tuple-element.152.bounds.refs_5_, bf16[256,768]{1,0:T(8,128)(2,1)S(1)} %get-tuple-element.135.q_ref, ...), custom_call_target="tpu_custom_call" | custom-call | flops 1048576 | bytes 65536 | tf_op jit(solution)/shard_map/attend_back/pallas_call | solution.py:159
  72.5 2.7 %attend_back.5 = (bf16[256,256]{1,0:T(8,128)(2,1)S(1)}, bf16[5,256,256]{2,1,0:T(8,128)(2,1)S(1)}, bf16[5,256,256]{2,1,0:T(8,128)(2,1)S(1)}, f32[2,256]{1,0:T(2,128)S(1)}) custom-call(s32[2]{0:T(128)S(1)} %get-tuple-element.152.bounds.refs_5_, bf16[256,768]{1,0:T(8,128)(2,1)S(1)} %get-tuple-element.135.q_ref, ...), custom_call_target="tpu_custom_call" | custom-call | flops 1048576 | bytes 65536 | tf_op jit(solution)/shard_map/attend_back/pallas_call | solution.py:159
  75.2 2.6 %parts.1 = (bf16[4,256,768]{2,1,0:T(8,128)(2,1)S(1)}, f32[256,768]{1,0:T(8,128)S(1)}) custom-call(s32[2]{0:T(128)S(1)} %get-tuple-element.152.bounds.refs_5_, bf16[256,256]{1,0:T(8,128)(2,1)S(1)} %get-tuple-element.171.refs_0_.refs_6_, bf16[256,256]{1,0:T(8,128)(2,1)S(1)} %get-tuple-element.172.refs_1_.refs_7_, ...), custom_call_target="tpu_custom_call" | custom-call | flops 1048576 | bytes 65536 | tf_op jit(solution)/shard_map/parts/pallas_call | solution.py:159
  77.9 6.0 %collective-permute-done.13 = bf16[2,192,768]{2,1,0:T(8,128)(2,1)S(1)} collective-permute-done((bf16[2,192,768]{2,1,0:T(8,128)(2,1)S(1)}, bf16[2,192,768]{2,1,0:T(8,128)(2,1)S(1)}, u32[]{:S(2)}, u32[]{:S(2)}) %collective-permute-start.13) | collective-permute-done | bytes 589856 | tf_op jit(solution)/shard_map/ppermute | solution.py:44
  86.8 4.2 %weights.1 = (bf16[384,2304]{1,0:T(8,128)(2,1)S(1)}, bf16[384,2304]{1,0:T(8,128)(2,1)S(1)}) custom-call(s32[28]{0:T(128)S(1)} %pad_add_fusion.table, bf16[272,768]{1,0:T(8,128)(2,1)S(1)} %collective-permute-done.9.xa_ref.refs_0_, bf16[272,768]{1,0:T(8,128)(2,1)S(1)} %collective-permute-done.7.xa_ref.refs_1_, ...), custom_call_target="tpu_custom_call" | custom-call | flops 1048576 | bytes 65536 | tf_op jit(solution)/shard_map/weights/pallas_call | solution.py:159
  93.2 10.8 %collective-permute-done.17 = bf16[2,48,3840]{2,1,0:T(8,128)(2,1)S(1)} collective-permute-done((bf16[2,48,3840]{2,1,0:T(8,128)(2,1)S(1)}, bf16[2,48,3840]{2,1,0:T(8,128)(2,1)S(1)}, u32[]{:S(2)}, u32[]{:S(2)}) %collective-permute-start.17) | collective-permute-done | bytes 737312 | tf_op jit(solution)/shard_map/ppermute | solution.py:44
  105.5 4.0 %collective-permute-done.15 = bf16[192,768]{1,0:T(8,128)(2,1)S(1)} collective-permute-done((bf16[192,768]{1,0:T(8,128)(2,1)S(1)}, bf16[192,768]{1,0:T(8,128)(2,1)S(1)}, u32[]{:S(2)}, u32[]{:S(2)}) %collective-permute-start.15) | collective-permute-done | bytes 294944 | tf_op jit(solution)/shard_map/ppermute | solution.py:44
  110.8 7.3 %collective-permute-start.20 = (bf16[256,768]{1,0:T(8,128)(2,1)S(1)}, bf16[256,768]{1,0:T(8,128)(2,1)S(1)}, u32[]{:S(2)}, u32[]{:S(2)}) collective-permute-start(bf16[256,768]{1,0:T(8,128)(2,1)S(1)} %get-tuple-element.191), channel_id=1, source_target_pairs={{0,1},{1,2},{2,3},{4,5},{5,6},{6,7},{8,9},{9,10},{10,11},{12,13},{... | collective-permute-start | bytes 1179656 | tf_op jit(solution)/shard_map/ppermute | solution.py:50
  121.6 4.9 %collective-permute-done.22 = bf16[48,3840]{1,0:T(8,128)(2,1)S(1)} collective-permute-done((bf16[48,3840]{1,0:T(8,128)(2,1)S(1)}, bf16[48,3840]{1,0:T(8,128)(2,1)S(1)}, u32[]{:S(2)}, u32[]{:S(2)}) %collective-permute-start.22) | collective-permute-done | bytes 368672 | tf_op jit(solution)/shard_map/ppermute | solution.py:44
  132.8 4.4 %collective-permute-start.25 = (bf16[256,768]{1,0:T(8,128)(2,1)S(1)}, bf16[256,768]{1,0:T(8,128)(2,1)S(1)}, u32[]{:S(2)}, u32[]{:S(2)}) collective-permute-start(bf16[256,768]{1,0:T(8,128)(2,1)S(1)} %get-tuple-element.280), channel_id=1, source_target_pairs={{0,1},{1,2},{2,3},{4,5},{5,6},{6,7},{8,9},{9,10},{10,11},{12,13},{... | collective-permute-start | bytes 1179656 | tf_op jit(solution)/shard_map/ppermute | solution.py:50
  139.6 8.9 %collective-permute-done.24.right_ref = bf16[256,768]{1,0:T(8,128)(2,1)S(1)} collective-permute-done((bf16[256,768]{1,0:T(8,128)(2,1)S(1)}, bf16[256,768]{1,0:T(8,128)(2,1)S(1)}, u32[]{:S(2)}, u32[]{:S(2)}) %collective-permute-start.24) | collective-permute-done | bytes 393248 | tf_op jit(solution)/shard_map/ppermute | solution.py:50
  156.0 6.1 %collective-permute-done.27 = f32[16,768]{1,0:T(8,128)S(1)} collective-permute-done((f32[16,768]{1,0:T(8,128)S(1)}, f32[16,768]{1,0:T(8,128)S(1)}, u32[]{:S(2)}, u32[]{:S(2)}) %collective-permute-start.27) | collective-permute-done | bytes 49184 | tf_op jit(solution)/shard_map/ppermute | solution.py:44
  162.4 2.6 %collective-permute-start.39 = (bf16[48,2304]{1,0:T(8,128)(2,1)S(1)}, bf16[48,2304]{1,0:T(8,128)(2,1)S(1)}, u32[]{:S(2)}, u32[]{:S(2)}) collective-permute-start(bf16[48,2304]{1,0:T(8,128)(2,1)S(1)} %get-tuple-element.259), channel_id=1, source_target_pairs={{0,1},{1,0},{2,3},{3,2},{4,5},{5,4},{6,7},{7,6},{8,9},{9,8},{10,11... | collective-permute-start | bytes 663560 | tf_op jit(solution)/shard_map/ppermute | solution.py:44
  165.0 6.6 %collective-permute-done.32 = bf16[192,768]{1,0:T(8,128)(2,1)S(1)} collective-permute-done((bf16[192,768]{1,0:T(8,128)(2,1)S(1)}, bf16[192,768]{1,0:T(8,128)(2,1)S(1)}, u32[]{:S(2)}, u32[]{:S(2)}) %collective-permute-start.32) | collective-permute-done | bytes 294944 | tf_op jit(solution)/shard_map/ppermute | solution.py:44
  171.6 5.7 %collective-permute-done.31 = f32[16,768]{1,0:T(8,128)S(1)} collective-permute-done((f32[16,768]{1,0:T(8,128)S(1)}, f32[16,768]{1,0:T(8,128)S(1)}, u32[]{:S(2)}, u32[]{:S(2)}) %collective-permute-start.31) | collective-permute-done | bytes 49184 | tf_op jit(solution)/shard_map/ppermute | solution.py:44
  180.5 2.3 %collective-permute-done.36 = f32[16,768]{1,0:T(8,128)S(1)} collective-permute-done((f32[16,768]{1,0:T(8,128)S(1)}, f32[16,768]{1,0:T(8,128)S(1)}, u32[]{:S(2)}, u32[]{:S(2)}) %collective-permute-start.36) | collective-permute-done | bytes 49184 | tf_op jit(solution)/shard_map/ppermute | solution.py:44
  183.6 3.4 %collective-permute-done.37 = f32[16,768]{1,0:T(8,128)S(1)} collective-permute-done((f32[16,768]{1,0:T(8,128)S(1)}, f32[16,768]{1,0:T(8,128)S(1)}, u32[]{:S(2)}, u32[]{:S(2)}) %collective-permute-start.37) | collective-permute-done | bytes 49184 | tf_op jit(solution)/shard_map/ppermute | solution.py:44
  189.6 4.0 %collective-permute-done.40 = bf16[192,768]{1,0:T(8,128)(2,1)S(1)} collective-permute-done((bf16[192,768]{1,0:T(8,128)(2,1)S(1)}, bf16[192,768]{1,0:T(8,128)(2,1)S(1)}, u32[]{:S(2)}, u32[]{:S(2)}) %collective-permute-start.40) | collective-permute-done | bytes 294944 | tf_op jit(solution)/shard_map/ppermute | solution.py:44
  193.7 2.5 %fusion.36 = (bf16[384,768]{1,0:T(8,128)(2,1)}, f32[384,768]{1,0:T(8,128)}, f32[384,768]{1,0:T(8,128)}, f32[384,768]{1,0:T(8,128)}) fusion(f32[384,768]{1,0:T(8,128)S(1)} %copy-done.8, f32[]{:T(128)} %bitcast.36, f32[]{:T(128)} %bitcast.35, f32[]{:T(128)} %bitcast.34, bf16[192,768]{1,0:T(8,128)(2,1)S(1)} %get-tuple-element.287, ...), kind=kLoop, calls=%fused_computation.110 | loop fusion | flops 5603328 | bytes 8257548 | tf_op jit(solution)/shard_map/convert_element_type | solution.py:677
  196.3 6.6 %collective-permute-done.43 = bf16[48,3840]{1,0:T(8,128)(2,1)S(1)} collective-permute-done((bf16[48,3840]{1,0:T(8,128)(2,1)S(1)}, bf16[48,3840]{1,0:T(8,128)(2,1)S(1)}, u32[]{:S(2)}, u32[]{:S(2)}) %collective-permute-start.43) | collective-permute-done | bytes 368672 | tf_op jit(solution)/shard_map/ppermute | solution.py:44
  203.1 2.6 %fusion.39 = (bf16[96,3072]{1,0:T(8,128)(2,1)}, f32[96,3072]{1,0:T(8,128)}, f32[96,3072]{1,0:T(8,128)}, f32[96,3072]{1,0:T(8,128)}) fusion(f32[96,3072]{1,0:T(8,128)S(1)} %copy-done.11, f32[]{:T(128)} %bitcast.36, f32[]{:T(128)} %bitcast.35, f32[]{:T(128)} %bitcast.34, bf16[48,3840]{1,0:T(8,128)(2,1)S(1)} %get-tuple-element.285, ...), kind=kLoop, calls=%fused_computation.111 | loop fusion | flops 5603328 | bytes 8405004 | tf_op jit(solution)/shard_map/convert_element_type | solution.py:677
  207.7 2.1 fusion.45
  (169 shorter events, 63.7 us)
Async XLA Ops:
  24.7 10.3 %collective-permute-start.8 = (bf16[272,768]{1,0:T(8,128)(2,1)S(1)}, bf16[272,768]{1,0:T(8,128)(2,1)S(1)}, u32[]{:S(2)}, u32[]{:S(2)}) collective-permute-start(bf16[272,768]{1,0:T(8,128)(2,1)S(1)} %get-tuple-element.133.x_ref.refs_2_), channel_id=1, source_target_pairs={{1,0},{2,1},{3,2},{5,4},{6,5},{7,6},{9,8},{10,9},{11,10},{13,12},{... | collective-permute-start | bytes 1253384 | tf_op jit(solution)/shard_map/ppermute | solution.py:50
  35.0 9.9 %collective-permute-start.10 = (bf16[272,768]{1,0:T(8,128)(2,1)S(1)}, bf16[272,768]{1,0:T(8,128)(2,1)S(1)}, u32[]{:S(2)}, u32[]{:S(2)}) collective-permute-start(bf16[272,768]{1,0:T(8,128)(2,1)S(1)} %collective-permute-done.8.xb_ref.refs_3_), channel_id=1, source_target_pairs={{1,0},{2,1},{3,2},{5,4},{6,5},{7,6},{9,8},{10,9},{11,10},{13,12},{... | collective-permute-start | bytes 1253384 | tf_op jit(solution)/shard_map/ppermute | solution.py:50
  36.2 10.1 %collective-permute-start.9 = (bf16[272,768]{1,0:T(8,128)(2,1)S(1)}, bf16[272,768]{1,0:T(8,128)(2,1)S(1)}, u32[]{:S(2)}, u32[]{:S(2)}) collective-permute-start(bf16[272,768]{1,0:T(8,128)(2,1)S(1)} %collective-permute-done.7.xa_ref.refs_1_), channel_id=1, source_target_pairs={{0,1},{1,2},{2,3},{4,5},{5,6},{6,7},{8,9},{9,10},{10,11},{12,13},{... | collective-permute-start | bytes 1253384 | tf_op jit(solution)/shard_map/ppermute | solution.py:50
  63.5 11.7 %collective-permute-start.12 = (bf16[384,3840]{1,0:T(8,128)(2,1)S(1)}, bf16[384,3840]{1,0:T(8,128)(2,1)S(1)}, u32[]{:S(2)}, u32[]{:S(2)}) collective-permute-start(bf16[384,3840]{1,0:T(8,128)(2,1)S(1)} %get-tuple-element.169), channel_id=1, source_target_pairs={{0,4},{4,0},{8,12},{12,8},{16,20},{20,16},{24,28},{28,24},{1,5},{5... | collective-permute-start | bytes 8847368 | tf_op jit(solution)/shard_map/ppermute | solution.py:44
  68.4 15.4 %collective-permute-start.13 = (bf16[2,192,768]{2,1,0:T(8,128)(2,1)S(1)}, bf16[2,192,768]{2,1,0:T(8,128)(2,1)S(1)}, u32[]{:S(2)}, u32[]{:S(2)}) collective-permute-start(bf16[2,192,768]{2,1,0:T(8,128)(2,1)S(1)} %get-tuple-element.275), channel_id=1, source_target_pairs={{0,8},{4,12},{8,0},{12,4},{16,24},{20,28},{24,16},{28,20},{1,9},{5... | collective-permute-start | bytes 1769480 | tf_op jit(solution)/shard_map/ppermute | solution.py:44
  69.0 15.1 %collective-permute-start.14 = (bf16[2,192,768]{2,1,0:T(8,128)(2,1)S(1)}, bf16[2,192,768]{2,1,0:T(8,128)(2,1)S(1)}, u32[]{:S(2)}, u32[]{:S(2)}) collective-permute-start(bf16[2,192,768]{2,1,0:T(8,128)(2,1)S(1)} %get-tuple-element.274), channel_id=1, source_target_pairs={{0,16},{4,20},{8,24},{12,28},{16,0},{20,4},{24,8},{28,12},{1,17},{... | collective-permute-start | bytes 1769480 | tf_op jit(solution)/shard_map/ppermute | solution.py:44
  84.5 19.5 %collective-permute-start.17 = (bf16[2,48,3840]{2,1,0:T(8,128)(2,1)S(1)}, bf16[2,48,3840]{2,1,0:T(8,128)(2,1)S(1)}, u32[]{:S(2)}, u32[]{:S(2)}) collective-permute-start(bf16[2,48,3840]{2,1,0:T(8,128)(2,1)S(1)} %bitcast.95), channel_id=1, source_target_pairs={{0,8},{4,12},{8,0},{12,4},{16,24},{20,28},{24,16},{28,20},{1,9},{5... | collective-permute-start | bytes 2211848 | tf_op jit(solution)/shard_map/ppermute | solution.py:44
  86.1 19.4 %collective-permute-start.18 = (bf16[2,48,3840]{2,1,0:T(8,128)(2,1)S(1)}, bf16[2,48,3840]{2,1,0:T(8,128)(2,1)S(1)}, u32[]{:S(2)}, u32[]{:S(2)}) collective-permute-start(bf16[2,48,3840]{2,1,0:T(8,128)(2,1)S(1)} %bitcast.93), channel_id=1, source_target_pairs={{0,16},{4,20},{8,24},{12,28},{16,0},{20,4},{24,8},{28,12},{1,17},{... | collective-permute-start | bytes 2211848 | tf_op jit(solution)/shard_map/ppermute | solution.py:44
  91.0 37.2 %collective-permute-start.21 = (bf16[384,2304]{1,0:T(8,128)(2,1)S(1)}, bf16[384,2304]{1,0:T(8,128)(2,1)S(1)}, u32[]{:S(2)}, u32[]{:S(2)}) collective-permute-start(bf16[384,2304]{1,0:T(8,128)(2,1)S(1)} %get-tuple-element.192), channel_id=1, source_target_pairs={{0,4},{4,0},{8,12},{12,8},{16,20},{20,16},{24,28},{28,24},{1,5},{5... | collective-permute-start | bytes 5308424 | tf_op jit(solution)/shard_map/ppermute | solution.py:44
  91.1 18.4 %collective-permute-start.15 = (bf16[192,768]{1,0:T(8,128)(2,1)S(1)}, bf16[192,768]{1,0:T(8,128)(2,1)S(1)}, u32[]{:S(2)}, u32[]{:S(2)}) collective-permute-start(bf16[192,768]{1,0:T(8,128)(2,1)S(1)} %get-tuple-element.273.refs_15_), channel_id=1, source_target_pairs={{0,16},{4,20},{8,24},{12,28},{16,0},{20,4},{24,8},{28,12},{1,17},{... | collective-permute-start | bytes 884744 | tf_op jit(solution)/shard_map/ppermute | solution.py:44
  92.6 16.9 %collective-permute-start.16 = (bf16[192,768]{1,0:T(8,128)(2,1)S(1)}, bf16[192,768]{1,0:T(8,128)(2,1)S(1)}, u32[]{:S(2)}, u32[]{:S(2)}) collective-permute-start(bf16[192,768]{1,0:T(8,128)(2,1)S(1)} %get-tuple-element.272.refs_16_), channel_id=1, source_target_pairs={{0,8},{4,12},{8,0},{12,4},{16,24},{20,28},{24,16},{28,20},{1,9},{5... | collective-permute-start | bytes 884744 | tf_op jit(solution)/shard_map/ppermute | solution.py:44
  109.5 18.7 %collective-permute-start.19 = (bf16[256,768]{1,0:T(8,128)(2,1)S(1)}, bf16[256,768]{1,0:T(8,128)(2,1)S(1)}, u32[]{:S(2)}, u32[]{:S(2)}) collective-permute-start(bf16[256,768]{1,0:T(8,128)(2,1)S(1)} %get-tuple-element.190), channel_id=1, source_target_pairs={{1,0},{2,1},{3,2},{5,4},{6,5},{7,6},{9,8},{10,9},{11,10},{13,12},{... | collective-permute-start | bytes 1179656 | tf_op jit(solution)/shard_map/ppermute | solution.py:50
  110.8 17.4 %collective-permute-start.20 = (bf16[256,768]{1,0:T(8,128)(2,1)S(1)}, bf16[256,768]{1,0:T(8,128)(2,1)S(1)}, u32[]{:S(2)}, u32[]{:S(2)}) collective-permute-start(bf16[256,768]{1,0:T(8,128)(2,1)S(1)} %get-tuple-element.191), channel_id=1, source_target_pairs={{0,1},{1,2},{2,3},{4,5},{5,6},{6,7},{8,9},{9,10},{10,11},{12,13},{... | collective-permute-start | bytes 1179656 | tf_op jit(solution)/shard_map/ppermute | solution.py:50
  118.4 8.1 %collective-permute-start.22 = (bf16[48,3840]{1,0:T(8,128)(2,1)S(1)}, bf16[48,3840]{1,0:T(8,128)(2,1)S(1)}, u32[]{:S(2)}, u32[]{:S(2)}) collective-permute-start(bf16[48,3840]{1,0:T(8,128)(2,1)S(1)} %get-tuple-element.269), channel_id=1, source_target_pairs={{0,16},{4,20},{8,24},{12,28},{16,0},{20,4},{24,8},{28,12},{1,17},{... | collective-permute-start | bytes 1105928 | tf_op jit(solution)/shard_map/ppermute | solution.py:44
  119.9 8.3 %collective-permute-start.23 = (bf16[48,3840]{1,0:T(8,128)(2,1)S(1)}, bf16[48,3840]{1,0:T(8,128)(2,1)S(1)}, u32[]{:S(2)}, u32[]{:S(2)}) collective-permute-start(bf16[48,3840]{1,0:T(8,128)(2,1)S(1)} %get-tuple-element.268), channel_id=1, source_target_pairs={{0,8},{4,12},{8,0},{12,4},{16,24},{20,28},{24,16},{28,20},{1,9},{5... | collective-permute-start | bytes 1105928 | tf_op jit(solution)/shard_map/ppermute | solution.py:44
  126.4 11.2 %collective-permute-start.26 = (bf16[192,768]{1,0:T(8,128)(2,1)S(1)}, bf16[192,768]{1,0:T(8,128)(2,1)S(1)}, u32[]{:S(2)}, u32[]{:S(2)}) collective-permute-start(bf16[192,768]{1,0:T(8,128)(2,1)S(1)} %get-tuple-element.265), channel_id=1, source_target_pairs={{0,1},{1,0},{2,3},{3,2},{4,5},{5,4},{6,7},{7,6},{8,9},{9,8},{10,11... | collective-permute-start | bytes 884744 | tf_op jit(solution)/shard_map/ppermute | solution.py:44
  128.4 22.3 %collective-permute-start.29 = (bf16[2,48,2304]{2,1,0:T(8,128)(2,1)S(1)}, bf16[2,48,2304]{2,1,0:T(8,128)(2,1)S(1)}, u32[]{:S(2)}, u32[]{:S(2)}) collective-permute-start(bf16[2,48,2304]{2,1,0:T(8,128)(2,1)S(1)} %bitcast.99), channel_id=1, source_target_pairs={{0,8},{4,12},{8,0},{12,4},{16,24},{20,28},{24,16},{28,20},{1,9},{5... | collective-permute-start | bytes 1327112 | tf_op jit(solution)/shard_map/ppermute | solution.py:44
  129.7 20.9 %collective-permute-start.30 = (bf16[2,48,2304]{2,1,0:T(8,128)(2,1)S(1)}, bf16[2,48,2304]{2,1,0:T(8,128)(2,1)S(1)}, u32[]{:S(2)}, u32[]{:S(2)}) collective-permute-start(bf16[2,48,2304]{2,1,0:T(8,128)(2,1)S(1)} %bitcast.98), channel_id=1, source_target_pairs={{0,16},{4,20},{8,24},{12,28},{16,0},{20,4},{24,8},{28,12},{1,17},{... | collective-permute-start | bytes 1327112 | tf_op jit(solution)/shard_map/ppermute | solution.py:44
  131.2 17.2 %collective-permute-start.24 = (bf16[256,768]{1,0:T(8,128)(2,1)S(1)}, bf16[256,768]{1,0:T(8,128)(2,1)S(1)}, u32[]{:S(2)}, u32[]{:S(2)}) collective-permute-start(bf16[256,768]{1,0:T(8,128)(2,1)S(1)} %get-tuple-element.281), channel_id=1, source_target_pairs={{1,0},{2,1},{3,2},{5,4},{6,5},{7,6},{9,8},{10,9},{11,10},{13,12},{... | collective-permute-start | bytes 1179656 | tf_op jit(solution)/shard_map/ppermute | solution.py:50
  132.8 15.6 %collective-permute-start.25 = (bf16[256,768]{1,0:T(8,128)(2,1)S(1)}, bf16[256,768]{1,0:T(8,128)(2,1)S(1)}, u32[]{:S(2)}, u32[]{:S(2)}) collective-permute-start(bf16[256,768]{1,0:T(8,128)(2,1)S(1)} %get-tuple-element.280), channel_id=1, source_target_pairs={{0,1},{1,2},{2,3},{4,5},{5,6},{6,7},{8,9},{9,10},{10,11},{12,13},{... | collective-permute-start | bytes 1179656 | tf_op jit(solution)/shard_map/ppermute | solution.py:50
  137.7 17.0 %collective-permute-start.28 = (bf16[48,3840]{1,0:T(8,128)(2,1)S(1)}, bf16[48,3840]{1,0:T(8,128)(2,1)S(1)}, u32[]{:S(2)}, u32[]{:S(2)}) collective-permute-start(bf16[48,3840]{1,0:T(8,128)(2,1)S(1)} %get-tuple-element.262), channel_id=1, source_target_pairs={{0,1},{1,0},{2,3},{3,2},{4,5},{5,4},{6,7},{7,6},{8,9},{9,8},{10,11... | collective-permute-start | bytes 1105928 | tf_op jit(solution)/shard_map/ppermute | solution.py:44
  148.4 23.1 %collective-permute-start.32 = (bf16[192,768]{1,0:T(8,128)(2,1)S(1)}, bf16[192,768]{1,0:T(8,128)(2,1)S(1)}, u32[]{:S(2)}, u32[]{:S(2)}) collective-permute-start(bf16[192,768]{1,0:T(8,128)(2,1)S(1)} %add_convert_fusion.9), channel_id=1, source_target_pairs={{0,2},{1,3},{2,0},{3,1},{4,6},{5,7},{6,4},{7,5},{8,10},{9,11},{10,... | collective-permute-start | bytes 884744 | tf_op jit(solution)/shard_map/ppermute | solution.py:44
  149.8 12.2 %collective-permute-start.27 = (f32[16,768]{1,0:T(8,128)S(1)}, f32[16,768]{1,0:T(8,128)S(1)}, u32[]{:S(2)}, u32[]{:S(2)}) collective-permute-start(f32[16,768]{1,0:T(8,128)S(1)} %get-tuple-element.214), channel_id=1, source_target_pairs={{0,1},{1,0},{2,3},{3,2},{4,5},{5,4},{6,7},{7,6},{8,9},{9,8},{10,11... | collective-permute-start | bytes 147464 | tf_op jit(solution)/shard_map/ppermute | solution.py:44
  150.8 11.2 %collective-permute-start.33 = (bf16[48,2304]{1,0:T(8,128)(2,1)S(1)}, bf16[48,2304]{1,0:T(8,128)(2,1)S(1)}, u32[]{:S(2)}, u32[]{:S(2)}) collective-permute-start(bf16[48,2304]{1,0:T(8,128)(2,1)S(1)} %get-tuple-element.277), channel_id=1, source_target_pairs={{0,16},{4,20},{8,24},{12,28},{16,0},{20,4},{24,8},{28,12},{1,17},{... | collective-permute-start | bytes 663560 | tf_op jit(solution)/shard_map/ppermute | solution.py:44
  152.6 9.4 %collective-permute-start.34 = (bf16[48,2304]{1,0:T(8,128)(2,1)S(1)}, bf16[48,2304]{1,0:T(8,128)(2,1)S(1)}, u32[]{:S(2)}, u32[]{:S(2)}) collective-permute-start(bf16[48,2304]{1,0:T(8,128)(2,1)S(1)} %get-tuple-element.276), channel_id=1, source_target_pairs={{0,8},{4,12},{8,0},{12,4},{16,24},{20,28},{24,16},{28,20},{1,9},{5... | collective-permute-start | bytes 663560 | tf_op jit(solution)/shard_map/ppermute | solution.py:44
  154.8 28.6 %collective-permute-start.38 = (bf16[48,3840]{1,0:T(8,128)(2,1)S(1)}, bf16[48,3840]{1,0:T(8,128)(2,1)S(1)}, u32[]{:S(2)}, u32[]{:S(2)}) collective-permute-start(bf16[48,3840]{1,0:T(8,128)(2,1)S(1)} %add_convert_fusion.7), channel_id=1, source_target_pairs={{0,2},{1,3},{2,0},{3,1},{4,6},{5,7},{6,4},{7,5},{8,10},{9,11},{10,... | collective-permute-start | bytes 1105928 | tf_op jit(solution)/shard_map/ppermute | solution.py:44
  162.1 15.3 %collective-permute-start.31 = (f32[16,768]{1,0:T(8,128)S(1)}, f32[16,768]{1,0:T(8,128)S(1)}, u32[]{:S(2)}, u32[]{:S(2)}) collective-permute-start(f32[16,768]{1,0:T(8,128)S(1)} %add.352), channel_id=1, source_target_pairs={{0,2},{1,3},{2,0},{3,1},{4,6},{5,7},{6,4},{7,5},{8,10},{9,11},{10,... | collective-permute-start | bytes 147464 | tf_op jit(solution)/shard_map/ppermute | solution.py:44
  162.4 21.0 %collective-permute-start.39 = (bf16[48,2304]{1,0:T(8,128)(2,1)S(1)}, bf16[48,2304]{1,0:T(8,128)(2,1)S(1)}, u32[]{:S(2)}, u32[]{:S(2)}) collective-permute-start(bf16[48,2304]{1,0:T(8,128)(2,1)S(1)} %get-tuple-element.259), channel_id=1, source_target_pairs={{0,1},{1,0},{2,3},{3,2},{4,5},{5,4},{6,7},{7,6},{8,9},{9,8},{10,11... | collective-permute-start | bytes 663560 | tf_op jit(solution)/shard_map/ppermute | solution.py:44
  180.4 13.2 %collective-permute-start.40 = (bf16[192,768]{1,0:T(8,128)(2,1)S(1)}, bf16[192,768]{1,0:T(8,128)(2,1)S(1)}, u32[]{:S(2)}, u32[]{:S(2)}) collective-permute-start(bf16[192,768]{1,0:T(8,128)(2,1)S(1)} %add_convert_fusion.8), channel_id=1, source_target_pairs={{0,1},{1,0},{2,3},{3,2},{4,5},{5,4},{6,7},{7,6},{8,9},{9,8},{10,11... | collective-permute-start | bytes 884744 | tf_op jit(solution)/shard_map/ppermute | solution.py:44
  183.5 12.7 %collective-permute-start.41 = (bf16[48,2304]{1,0:T(8,128)(2,1)S(1)}, bf16[48,2304]{1,0:T(8,128)(2,1)S(1)}, u32[]{:S(2)}, u32[]{:S(2)}) collective-permute-start(bf16[48,2304]{1,0:T(8,128)(2,1)S(1)} %add_convert_fusion.11), channel_id=1, source_target_pairs={{0,2},{1,3},{2,0},{3,1},{4,6},{5,7},{6,4},{7,5},{8,10},{9,11},{10,... | collective-permute-start | bytes 663560 | tf_op jit(solution)/shard_map/ppermute | solution.py:44
  187.1 15.9 %collective-permute-start.43 = (bf16[48,3840]{1,0:T(8,128)(2,1)S(1)}, bf16[48,3840]{1,0:T(8,128)(2,1)S(1)}, u32[]{:S(2)}, u32[]{:S(2)}) collective-permute-start(bf16[48,3840]{1,0:T(8,128)(2,1)S(1)} %add_convert_fusion.6), channel_id=1, source_target_pairs={{0,1},{1,0},{2,3},{3,2},{4,5},{5,4},{6,7},{7,6},{8,9},{9,8},{10,11... | collective-permute-start | bytes 1105928 | tf_op jit(solution)/shard_map/ppermute | solution.py:44
  196.3 10.5 %collective-permute-start.42 = (bf16[48,2304]{1,0:T(8,128)(2,1)S(1)}, bf16[48,2304]{1,0:T(8,128)(2,1)S(1)}, u32[]{:S(2)}, u32[]{:S(2)}) collective-permute-start(bf16[48,2304]{1,0:T(8,128)(2,1)S(1)} %add_convert_fusion.10), channel_id=1, source_target_pairs={{0,1},{1,0},{2,3},{3,2},{4,5},{5,4},{6,7},{7,6},{8,9},{9,8},{10,11... | collective-permute-start | bytes 663560 | tf_op jit(solution)/shard_map/ppermute | solution.py:44
  (40 other events, 207.0 us)

commit v8 on v6

--- a/solution.py
+++ b/solution.py
@@ -59,7 +59,7 @@
     def __init__(self, block, paired=True):
         self.block, self.rounds = block, []
         if not paired:
-            self.rounds = [(axis, [bit]) for axis in ("blk", "dp") for bit in bits_of(axis)]
+            self.rounds = [(axis, [bit]) for axis in ("dp", "blk") for bit in bits_of(axis)]
             return
         for axis in ("dp", "blk"):
             bits = bits_of(axis)
@@ -953,12 +953,7 @@
         mib=6,
     )
     to_left, to_right = parts[0], parts[2 * reach - 1]
-    token[:] = [to_left, to_right]
-    from_right, from_left = moved(to_left, "blk", -1), moved(to_right, "blk", 1)
-    advance(first)
-
     kept_inlet = struct((features // 2, wkv), bf16)
-    grads = after(*grads)
     inlet_keep, inlet_send = call(
         functools.partial(weight_kernel, reach, half, steps),
         "weights",
@@ -968,23 +963,59 @@
         [vmem((features, slots * width), bf16), vmem((features, width), f32)],
         mib=8,
     )
-    token[:] = [inlet_keep]
     inlet_in = flipped(inlet_send, "dp", 1)
-    while first[0].order:
-        advance(first)
-    advance(first)
-    (expand_in,) = after(expand_in)
-    from_right, from_left, expand_in = together(from_right, from_left, expand_in)
+
+    def taken(pair, arrived):
+        for one, value in zip(pair, arrived):
+            one.arrived = value
+            one.take()
+
+    *arrived, expand_in, inlet_keep = together(
+        *[one.arrived for one in first], expand_in, inlet_keep
+    )
+    taken(first, arrived)
+    for one in first:
+        one.prepare()
+    expand_in, first[0].sent, first[1].sent = together(expand_in, first[0].sent, first[1].sent)
+    for one in first:
+        one.send()
     second = scatters(expand_keep, expand_in, owned)
-    launch(second)
+    for one in second:
+        one.prepare()
+        one.send()
+    while True:
+        *arrived, to_left, to_right, inlet_in = together(
+            *[one.arrived for one in first], to_left, to_right, inlet_in
+        )
+        taken(first, arrived)
+        if not first[0].order:
+            break
+        for one in first:
+            one.prepare()
+            one.send()
+    from_right, from_left = moved(to_left, "blk", -1), moved(to_right, "blk", 1)
+    line_one = Line(*first, lows)
+    line_one.scatter()
     for d in range(reach - 1, 0, -1):
-        from_right, from_left = after(from_right, from_left)
+        from_right, from_left, line_one.keep = together(from_right, from_left, line_one.keep)
         to_left = added(parts[reach - d], from_right)
         to_right = added(parts[reach + d - 1], from_left)
-        token[:] = [to_left, to_right]
         from_right, from_left = moved(to_left, "blk", -1), moved(to_right, "blk", 1)
-    advance(second)
-    from_right, from_left = after(from_right, from_left)
+    *arrived, line_one.arrived, line_one.keep = together(
+        *[one.arrived for one in second], line_one.arrived, line_one.keep
+    )
+    taken(second, arrived)
+    for one in second:
+        one.prepare()
+        one.send()
+    line_one.exchange()
+    from_right, from_left, inlet_in, line_one.keep = together(
+        from_right, from_left, inlet_in, line_one.keep
+    )
+    third = scatters(inlet_keep, inlet_in, owned)
+    for one in third:
+        one.prepare()
+        one.send()
     grad_normed, small = call(
         leave_kernel,
         "leave",
@@ -1004,38 +1035,72 @@
         [struct(tokens, f32), struct((16, features), f32)],
         mib=8,
     )
-    token[:] = [small]
     rounds = SmallSum(small, paired=False)
-    (inlet_in,) = after(inlet_in)
-    third = scatters(inlet_keep, inlet_in, owned)
-    launch(third)
-    line_one = begin(first)
+    while True:
+        *arrived, rounds.block, line_one.keep = together(
+            *[one.arrived for one in second], rounds.block, line_one.keep
+        )
+        taken(second, arrived)
+        if not second[0].order:
+            break
+        for one in second:
+            one.prepare()
+            one.send()
+    line_two = Line(*second, lows)
+    line_two.scatter()
+
+    def round_beside(line):
+        *rounds.arrived, line.keep = together(*rounds.arrived, line.keep)
+        rounds.take()
+
     rounds.send()
-    while second[0].order:
-        advance(second)
-    advance(second)
-    line_two = begin(second)
-    next_round()
-    follow(line_one, Line.exchange)
-    advance(third)
-    follow(line_two, Line.exchange)
-    next_round()
-    follow(line_one, Line.gather)
-    while third[0].order:
-        advance(third)
-    advance(third)
-    line_three = begin(third)
-    while rounds.left():
-        next_round()
-    (line_two.arrived, line_three.arrived) = after(line_two.arrived, line_three.arrived)
+    round_beside(line_two)
+    rounds.send()
+    while True:
+        *arrived, line_two.keep = together(*[one.arrived for one in third], line_two.keep)
+        taken(third, arrived)
+        for one in third:
+            one.prepare()
+            one.send()
+        if not third[0].order:
+            break
+    line_two.arrived, line_one.keep = together(line_two.arrived, line_one.keep)
+    line_two.exchange()
+    for _ in bits_of("dp")[1:-1]:
+        round_beside(line_two)
+        rounds.send()
+    *arrived, line_two.keep = together(*[one.arrived for one in third], line_two.keep)
+    taken(third, arrived)
+    line_three = Line(*third, lows)
+    line_three.scatter()
+    line_one.arrived, line_three.keep = together(line_one.arrived, line_three.keep)
+    line_one.gather()
+    round_beside(line_three)
+    rounds.send()
+    line_two.arrived, line_three.arrived, *rounds.arrived = together(
+        line_two.arrived, line_three.arrived, *rounds.arrived
+    )
+    rounds.take()
     line_three.exchange()
     line_two.gather()
-    *rounds.arrived, line_three.keep = together(*rounds.arrived, line_three.keep)
-    rounds.take()
+    line_one.arrived, line_three.keep = together(line_one.arrived, line_three.keep)
+    shrink_new = adam_rule(
+        shrink_master,
+        shrink_moment,
+        shrink_square,
+        line_one.result().astype(f32),
+        step_value,
+        rate_matrix,
+        decay_matrix,
+    )
+    line_three.arrived, rounds.block, *shrink_new = together(
+        line_three.arrived, rounds.block, *shrink_new
+    )
+    line_three.gather()
+    while rounds.left():
+        rounds.send()
+        round_beside(line_three)
     small = rounds.block
-    line_one.arrived, line_three.keep = together(line_one.arrived, line_three.keep)
-    shrink_share = line_one.result()
-    line_three.gather()
     expand_share = line_two.result()
     inlet_share = line_three.result()
 
@@ -1059,13 +1124,13 @@
         (inlet_master, inlet_moment, inlet_square, inlet_share),
         (outlet_master, outlet_moment, outlet_square, expand_share[:, inner:]),
         (expand_master, expand_moment, expand_square, expand_share[:, :inner]),
-        (shrink_master, shrink_moment, shrink_square, shrink_share),
     ):
         updates.extend(
             adam_rule(
                 master, moment, square, share.astype(f32), step_value, rate_matrix, decay_matrix
             )
         )
+    updates.extend(shrink_new)
     updates.extend(
         adam_rule(
             vector_master, vector_moment, vector_square, vector_share, step_value, rate_vector, 0.0

time: 198 us -> 208 us (1.051); the launches traced: 195 us -> 208 us
  starting transfers between devices: 66.4 us -> 75.8 us
  waiting for transfers between devices: 66.2 us -> 69.2 us
    ppermute x8, waiting for transfers between devices: 12.1 us -> 22.1 us  [moved(): return lax.ppermute(block, axis, route)]
    ppermute x36, starting transfers between devices: 43 us -> 52.3 us  [flipped(): return lax.ppermute(block, axis, [(i, i ^ bit) for i in range(size)])]
    ppermute x36, waiting for transfers between devices: 54.2 us -> 47.1 us  [flipped(): return lax.ppermute(block, axis, [(i, i ^ bit) for i in range(size)])]
  transfers between devices with their start and end apart: 44 -> 44, of which waited for: 23 -> 24; matrix products, arithmetic and copies ran while one was open for 7% -> 7% of each run, Pallas kernels for 10% -> 10%
where the time goes in v8:
time: 208 us
  starting transfers between devices  75.8 us (36%)
  waiting for transfers between devices  69.2 us (33%)
  Pallas kernels  37.8 us (18%)
  other arithmetic  16.4 us (8%)
  local copies, waits for them, and re-layouts  6.34 us (3%)
    ppermute x36, starting transfers between devices, flipped(): return lax.ppermute(block, axis, [(i, i ^ bit) for i in range(size)])  52.3 us
    ppermute x36, waiting for transfers between devices, flipped(): return lax.ppermute(block, axis, [(i, i ^ bit) for i in range(size)])  47.1 us
    pallas_call x13, Pallas kernels, call(): pl.pallas_call(kernel, grid_spec=pltpu.PrefetchScalarGridSpec(num_scalar_...  37.8 us
    ppermute x8, starting transfers between devices, moved(): return lax.ppermute(block, axis, route)  23.6 us
    ppermute x8, waiting for transfers between devices, moved(): return lax.ppermute(block, axis, route)  22.1 us
    convert_element_type x5, other arithmetic, adam_rule(): return (weight_new, moment_new, square_new, weight_new.astype(bf16))  8.96 us
    unnamed x56, local copies, waits for them, and re-layouts  6.22 us
  transfers between devices with their start and end apart: 44, of which 24 were waited for; matrix products, arithmetic and copies ran while one was open for 7% of the time, Pallas kernels for 10%

profile of v8, /device:TPU:0, one launch (start us, length us, event | category | flops | bytes accessed | tf_op | source)
XLA Modules:
  0.0 207.5 jit_solution(4793336515946786834)
XLA Ops:
  3.3 3.8 %collective-permute-start.3 = (f32[2,768]{1,0:T(2,128)S(1)}, f32[2,768]{1,0:T(2,128)S(1)}, u32[]{:S(2)}, u32[]{:S(2)}) collective-permute-start(f32[2,768]{1,0:T(2,128)S(1)} %add.302), channel_id=1, source_target_pairs={{0,24},{4,28},{8,16},{12,20},{16,8},{20,12},{24,0},{28,4},{1,25},{... | collective-permute-start | bytes 18440 | tf_op jit(solution)/shard_map/ppermute | solution.py:44
  11.2 3.7 %collective-permute-start.6 = (f32[2,768]{1,0:T(2,128)S(1)}, f32[2,768]{1,0:T(2,128)S(1)}, u32[]{:S(2)}, u32[]{:S(2)}) collective-permute-start(f32[2,768]{1,0:T(2,128)S(1)} %add_add_fusion.1), channel_id=1, source_target_pairs={{0,3},{1,2},{2,1},{3,0},{4,7},{5,6},{6,5},{7,4},{8,11},{9,10},{10,... | collective-permute-start | bytes 18440 | tf_op jit(solution)/shard_map/ppermute | solution.py:44
  16.7 2.7 %collective-permute-done.5 = f32[2,768]{1,0:T(2,128)S(1)} collective-permute-done((f32[2,768]{1,0:T(2,128)S(1)}, f32[2,768]{1,0:T(2,128)S(1)}, u32[]{:S(2)}, u32[]{:S(2)}) %collective-permute-start.5) | collective-permute-done | bytes 6176 | tf_op jit(solution)/shard_map/ppermute | solution.py:44
  22.3 4.6 %collective-permute-start.7 = (bf16[272,768]{1,0:T(8,128)(2,1)S(1)}, bf16[272,768]{1,0:T(8,128)(2,1)S(1)}, u32[]{:S(2)}, u32[]{:S(2)}) collective-permute-start(bf16[272,768]{1,0:T(8,128)(2,1)S(1)} %get-tuple-element.150.x_ref.refs_2_), channel_id=1, source_target_pairs={{0,1},{1,2},{2,3},{4,5},{5,6},{6,7},{8,9},{9,10},{10,11},{12,13},{... | collective-permute-start | bytes 1253384 | tf_op jit(solution)/shard_map/ppermute | solution.py:50
  33.0 4.4 %collective-permute-start.9 = (bf16[272,768]{1,0:T(8,128)(2,1)S(1)}, bf16[272,768]{1,0:T(8,128)(2,1)S(1)}, u32[]{:S(2)}, u32[]{:S(2)}) collective-permute-start(bf16[272,768]{1,0:T(8,128)(2,1)S(1)} %collective-permute-done.7.xa_ref.refs_1_), channel_id=1, source_target_pairs={{0,1},{1,2},{2,3},{4,5},{5,6},{6,7},{8,9},{9,10},{10,11},{12,13},{... | collective-permute-start | bytes 1253384 | tf_op jit(solution)/shard_map/ppermute | solution.py:50
  42.9 4.4 %collective-permute-done.10.xb_ref.refs_4_ = bf16[272,768]{1,0:T(8,128)(2,1)S(1)} collective-permute-done((bf16[272,768]{1,0:T(8,128)(2,1)S(1)}, bf16[272,768]{1,0:T(8,128)(2,1)S(1)}, u32[]{:S(2)}, u32[]{:S(2)}) %collective-permute-start.10) | collective-permute-done | bytes 417824 | tf_op jit(solution)/shard_map/ppermute | solution.py:50
  48.4 5.3 %attend.1 = (bf16[256,768]{1,0:T(8,128)(2,1)S(1)}, f32[3,4,256]{2,1,0:T(4,128)S(1)}, s32[2]{0:T(128)S(1)}) custom-call(s32[28]{0:T(128)S(1)} %pad_add_fusion.table, bf16[256,768]{1,0:T(8,128)(2,1)S(1)} %get-tuple-element.152.q_ref, bf16[5,256,1536]{2,1,0:T(8,128)(2,1)S(1)} %get-tuple-element.162.kv_ref, s32[1,256]{1,0:T(1,128)S(1)} %copy-done.7, ...), custom_call_target="tpu_custom_call" | custom-call | flops 1048576 | bytes 65536 | tf_op jit(solution)/shard_map/attend/pallas_call | solution.py:159
  53.8 10.8 %ffn.1 = (bf16[256,768]{1,0:T(8,128)(2,1)}, f32[256,768]{1,0:T(8,128)S(1)}, bf16[256,768]{1,0:T(8,128)(2,1)S(1)}, bf16[2,4,192,768]{3,2,1,0:T(8,128)(2,1)S(1)}, ...) custom-call(s32[28]{0:T(128)S(1)} %pad_add_fusion.table, ...), custom_call_target="tpu_custom_call" | custom-call | flops 1048576 | bytes 65536 | tf_op jit(solution)/shard_map/ffn/pallas_call | solution.py:159
  65.0 2.9 %attend_back.3 = (bf16[256,256]{1,0:T(8,128)(2,1)S(1)}, bf16[5,256,256]{2,1,0:T(8,128)(2,1)S(1)}, bf16[5,256,256]{2,1,0:T(8,128)(2,1)S(1)}, f32[2,256]{1,0:T(2,128)S(1)}) custom-call(s32[2]{0:T(128)S(1)} %get-tuple-element.169.bounds.refs_5_, bf16[256,768]{1,0:T(8,128)(2,1)S(1)} %get-tuple-element.152.q_ref, ...), custom_call_target="tpu_custom_call" | custom-call | flops 1048576 | bytes 65536 | tf_op jit(solution)/shard_map/attend_back/pallas_call | solution.py:159
  69.4 4.2 %collective-permute-start.14 = (bf16[2,192,768]{2,1,0:T(8,128)(2,1)S(1)}, bf16[2,192,768]{2,1,0:T(8,128)(2,1)S(1)}, u32[]{:S(2)}, u32[]{:S(2)}) collective-permute-start(bf16[2,192,768]{2,1,0:T(8,128)(2,1)S(1)} %get-tuple-element.308), channel_id=1, source_target_pairs={{0,16},{4,20},{8,24},{12,28},{16,0},{20,4},{24,8},{28,12},{1,17},{... | collective-permute-start | bytes 1769480 | tf_op jit(solution)/shard_map/ppermute | solution.py:44
  74.1 2.7 %attend_back.4 = (bf16[256,256]{1,0:T(8,128)(2,1)S(1)}, bf16[5,256,256]{2,1,0:T(8,128)(2,1)S(1)}, bf16[5,256,256]{2,1,0:T(8,128)(2,1)S(1)}, f32[2,256]{1,0:T(2,128)S(1)}) custom-call(s32[2]{0:T(128)S(1)} %get-tuple-element.169.bounds.refs_5_, bf16[256,768]{1,0:T(8,128)(2,1)S(1)} %get-tuple-element.152.q_ref, ...), custom_call_target="tpu_custom_call" | custom-call | flops 1048576 | bytes 65536 | tf_op jit(solution)/shard_map/attend_back/pallas_call | solution.py:159
  76.8 2.7 %attend_back.5 = (bf16[256,256]{1,0:T(8,128)(2,1)S(1)}, bf16[5,256,256]{2,1,0:T(8,128)(2,1)S(1)}, bf16[5,256,256]{2,1,0:T(8,128)(2,1)S(1)}, f32[2,256]{1,0:T(2,128)S(1)}) custom-call(s32[2]{0:T(128)S(1)} %get-tuple-element.169.bounds.refs_5_, bf16[256,768]{1,0:T(8,128)(2,1)S(1)} %get-tuple-element.152.q_ref, ...), custom_call_target="tpu_custom_call" | custom-call | flops 1048576 | bytes 65536 | tf_op jit(solution)/shard_map/attend_back/pallas_call | solution.py:159
  79.5 4.1 %weights.1 = (bf16[384,2304]{1,0:T(8,128)(2,1)S(1)}, bf16[384,2304]{1,0:T(8,128)(2,1)S(1)}) custom-call(s32[28]{0:T(128)S(1)} %pad_add_fusion.table, bf16[272,768]{1,0:T(8,128)(2,1)S(1)} %collective-permute-done.9.xa_ref.refs_0_, bf16[272,768]{1,0:T(8,128)(2,1)S(1)} %collective-permute-done.7.xa_ref.refs_1_, ...), custom_call_target="tpu_custom_call" | custom-call | flops 1048576 | bytes 65536 | tf_op jit(solution)/shard_map/weights/pallas_call | solution.py:159
  93.5 2.6 %parts.1 = (bf16[4,256,768]{2,1,0:T(8,128)(2,1)S(1)}, f32[256,768]{1,0:T(8,128)S(1)}) custom-call(s32[2]{0:T(128)S(1)} %get-tuple-element.169.bounds.refs_5_, bf16[256,256]{1,0:T(8,128)(2,1)S(1)} %get-tuple-element.188.refs_0_.refs_6_, bf16[256,256]{1,0:T(8,128)(2,1)S(1)} %get-tuple-element.189.refs_1_.refs_7_, ...), custom_call_target="tpu_custom_call" | custom-call | flops 1048576 | bytes 65536 | tf_op jit(solution)/shard_map/parts/pallas_call | solution.py:159
  96.2 2.7 %collective-permute-done.15 = bf16[192,768]{1,0:T(8,128)(2,1)S(1)} collective-permute-done((bf16[192,768]{1,0:T(8,128)(2,1)S(1)}, bf16[192,768]{1,0:T(8,128)(2,1)S(1)}, u32[]{:S(2)}, u32[]{:S(2)}) %collective-permute-start.15) | collective-permute-done | bytes 294944 | tf_op jit(solution)/shard_map/ppermute | solution.py:44
  100.5 4.6 %collective-permute-start.19 = (bf16[256,768]{1,0:T(8,128)(2,1)S(1)}, bf16[256,768]{1,0:T(8,128)(2,1)S(1)}, u32[]{:S(2)}, u32[]{:S(2)}) collective-permute-start(bf16[256,768]{1,0:T(8,128)(2,1)S(1)} %get-tuple-element.207), channel_id=1, source_target_pairs={{0,1},{1,2},{2,3},{4,5},{5,6},{6,7},{8,9},{9,10},{10,11},{12,13},{... | collective-permute-start | bytes 1179656 | tf_op jit(solution)/shard_map/ppermute | solution.py:50
  107.8 3.1 %collective-permute-done.18 = bf16[256,768]{1,0:T(8,128)(2,1)S(1)} collective-permute-done((bf16[256,768]{1,0:T(8,128)(2,1)S(1)}, bf16[256,768]{1,0:T(8,128)(2,1)S(1)}, u32[]{:S(2)}, u32[]{:S(2)}) %collective-permute-start.18) | collective-permute-done | bytes 393248 | tf_op jit(solution)/shard_map/ppermute | solution.py:50
  110.8 2.7 %collective-permute-done.19 = bf16[256,768]{1,0:T(8,128)(2,1)S(1)} collective-permute-done((bf16[256,768]{1,0:T(8,128)(2,1)S(1)}, bf16[256,768]{1,0:T(8,128)(2,1)S(1)}, u32[]{:S(2)}, u32[]{:S(2)}) %collective-permute-start.19) | collective-permute-done | bytes 393248 | tf_op jit(solution)/shard_map/ppermute | solution.py:50
  113.5 3.2 %collective-permute-done.24 = bf16[192,768]{1,0:T(8,128)(2,1)S(1)} collective-permute-done((bf16[192,768]{1,0:T(8,128)(2,1)S(1)}, bf16[192,768]{1,0:T(8,128)(2,1)S(1)}, u32[]{:S(2)}, u32[]{:S(2)}) %collective-permute-start.24) | collective-permute-done | bytes 294944 | tf_op jit(solution)/shard_map/ppermute | solution.py:44
  116.9 4.4 %collective-permute-start.21 = (bf16[256,768]{1,0:T(8,128)(2,1)S(1)}, bf16[256,768]{1,0:T(8,128)(2,1)S(1)}, u32[]{:S(2)}, u32[]{:S(2)}) collective-permute-start(bf16[256,768]{1,0:T(8,128)(2,1)S(1)} %get-tuple-element.314), channel_id=1, source_target_pairs={{0,1},{1,2},{2,3},{4,5},{5,6},{6,7},{8,9},{9,10},{10,11},{12,13},{... | collective-permute-start | bytes 1179656 | tf_op jit(solution)/shard_map/ppermute | solution.py:50
  126.6 6.4 %collective-permute-done.20.right_ref = bf16[256,768]{1,0:T(8,128)(2,1)S(1)} collective-permute-done((bf16[256,768]{1,0:T(8,128)(2,1)S(1)}, bf16[256,768]{1,0:T(8,128)(2,1)S(1)}, u32[]{:S(2)}, u32[]{:S(2)}) %collective-permute-start.20) | collective-permute-done | bytes 393248 | tf_op jit(solution)/shard_map/ppermute | solution.py:50
  140.2 3.2 %collective-permute-start.33 = (bf16[192,768]{1,0:T(8,128)(2,1)S(1)}, bf16[192,768]{1,0:T(8,128)(2,1)S(1)}, u32[]{:S(2)}, u32[]{:S(2)}) collective-permute-start(bf16[192,768]{1,0:T(8,128)(2,1)S(1)} %add_convert_fusion.9), channel_id=1, source_target_pairs={{0,2},{1,3},{2,0},{3,1},{4,6},{5,7},{6,4},{7,5},{8,10},{9,11},{10,... | collective-permute-start | bytes 884744 | tf_op jit(solution)/shard_map/ppermute | solution.py:44
  147.6 7.2 %collective-permute-start.36 = (bf16[48,3840]{1,0:T(8,128)(2,1)S(1)}, bf16[48,3840]{1,0:T(8,128)(2,1)S(1)}, u32[]{:S(2)}, u32[]{:S(2)}) collective-permute-start(bf16[48,3840]{1,0:T(8,128)(2,1)S(1)} %add_convert_fusion.7), channel_id=1, source_target_pairs={{0,2},{1,3},{2,0},{3,1},{4,6},{5,7},{6,4},{7,5},{8,10},{9,11},{10,... | collective-permute-start | bytes 1105928 | tf_op jit(solution)/shard_map/ppermute | solution.py:44
  156.1 9.1 %collective-permute-done.33 = bf16[192,768]{1,0:T(8,128)(2,1)S(1)} collective-permute-done((bf16[192,768]{1,0:T(8,128)(2,1)S(1)}, bf16[192,768]{1,0:T(8,128)(2,1)S(1)}, u32[]{:S(2)}, u32[]{:S(2)}) %collective-permute-start.33) | collective-permute-done | bytes 294944 | tf_op jit(solution)/shard_map/ppermute | solution.py:44
  167.5 6.6 %collective-permute-done.38 = f32[16,768]{1,0:T(8,128)S(1)} collective-permute-done((f32[16,768]{1,0:T(8,128)S(1)}, f32[16,768]{1,0:T(8,128)S(1)}, u32[]{:S(2)}, u32[]{:S(2)}) %collective-permute-start.38) | collective-permute-done | bytes 49184 | tf_op jit(solution)/shard_map/ppermute | solution.py:44
  174.1 4.7 %collective-permute-done.37 = bf16[48,2304]{1,0:T(8,128)(2,1)S(1)} collective-permute-done((bf16[48,2304]{1,0:T(8,128)(2,1)S(1)}, bf16[48,2304]{1,0:T(8,128)(2,1)S(1)}, u32[]{:S(2)}, u32[]{:S(2)}) %collective-permute-start.37) | collective-permute-done | bytes 221216 | tf_op jit(solution)/shard_map/ppermute | solution.py:44
  179.6 2.5 %collective-permute-start.43 = (bf16[48,3840]{1,0:T(8,128)(2,1)S(1)}, bf16[48,3840]{1,0:T(8,128)(2,1)S(1)}, u32[]{:S(2)}, u32[]{:S(2)}) collective-permute-start(bf16[48,3840]{1,0:T(8,128)(2,1)S(1)} %add_convert_fusion.6), channel_id=1, source_target_pairs={{0,1},{1,0},{2,3},{3,2},{4,5},{5,4},{6,7},{7,6},{8,9},{9,8},{10,11... | collective-permute-start | bytes 1105928 | tf_op jit(solution)/shard_map/ppermute | solution.py:44
  182.2 3.1 %collective-permute-done.40 = bf16[192,768]{1,0:T(8,128)(2,1)S(1)} collective-permute-done((bf16[192,768]{1,0:T(8,128)(2,1)S(1)}, bf16[192,768]{1,0:T(8,128)(2,1)S(1)}, u32[]{:S(2)}, u32[]{:S(2)}) %collective-permute-start.40) | collective-permute-done | bytes 294944 | tf_op jit(solution)/shard_map/ppermute | solution.py:44
  185.3 2.6 %fusion.45 = (bf16[384,768]{1,0:T(8,128)(2,1)}, f32[384,768]{1,0:T(8,128)}, f32[384,768]{1,0:T(8,128)}, f32[384,768]{1,0:T(8,128)}) fusion(f32[384,768]{1,0:T(8,128)S(1)} %copy-done.8, f32[]{:T(128)} %bitcast.35, f32[]{:T(128)} %bitcast.34, f32[]{:T(128)} %bitcast.33, bf16[192,768]{1,0:T(8,128)(2,1)S(1)} %get-tuple-element.321, ...), kind=kLoop, calls=%fused_computation.116 | loop fusion | flops 5603328 | bytes 8257548 | tf_op jit(solution)/shard_map/convert_element_type | solution.py:677
  187.9 3.9 %collective-permute-done.39 = bf16[48,2304]{1,0:T(8,128)(2,1)S(1)} collective-permute-done((bf16[48,2304]{1,0:T(8,128)(2,1)S(1)}, bf16[48,2304]{1,0:T(8,128)(2,1)S(1)}, u32[]{:S(2)}, u32[]{:S(2)}) %collective-permute-start.39) | collective-permute-done | bytes 221216 | tf_op jit(solution)/shard_map/ppermute | solution.py:44
  194.1 2.8 %collective-permute-done.41 = f32[16,768]{1,0:T(8,128)S(1)} collective-permute-done((f32[16,768]{1,0:T(8,128)S(1)}, f32[16,768]{1,0:T(8,128)S(1)}, u32[]{:S(2)}, u32[]{:S(2)}) %collective-permute-start.41) | collective-permute-done | bytes 49184 | tf_op jit(solution)/shard_map/ppermute | solution.py:44
  200.8 2.6 %fusion.36 = (bf16[96,3072]{1,0:T(8,128)(2,1)}, f32[96,3072]{1,0:T(8,128)}, f32[96,3072]{1,0:T(8,128)}, f32[96,3072]{1,0:T(8,128)}) fusion(f32[96,3072]{1,0:T(8,128)S(1)} %copy-done.11, f32[]{:T(128)} %bitcast.35, f32[]{:T(128)} %bitcast.34, f32[]{:T(128)} %bitcast.33, bf16[48,3840]{1,0:T(8,128)(2,1)S(1)} %get-tuple-element.319, ...), kind=kLoop, calls=%fused_computation.113 | loop fusion | flops 5603328 | bytes 8405004 | tf_op jit(solution)/shard_map/convert_element_type | solution.py:677
  (172 shorter events, 71.5 us)
Async XLA Ops:
  21.0 10.8 %collective-permute-start.8 = (bf16[272,768]{1,0:T(8,128)(2,1)S(1)}, bf16[272,768]{1,0:T(8,128)(2,1)S(1)}, u32[]{:S(2)}, u32[]{:S(2)}) collective-permute-start(bf16[272,768]{1,0:T(8,128)(2,1)S(1)} %get-tuple-element.150.x_ref.refs_2_), channel_id=1, source_target_pairs={{1,0},{2,1},{3,2},{5,4},{6,5},{7,6},{9,8},{10,9},{11,10},{13,12},{... | collective-permute-start | bytes 1253384 | tf_op jit(solution)/shard_map/ppermute | solution.py:50
  22.3 10.7 %collective-permute-start.7 = (bf16[272,768]{1,0:T(8,128)(2,1)S(1)}, bf16[272,768]{1,0:T(8,128)(2,1)S(1)}, u32[]{:S(2)}, u32[]{:S(2)}) collective-permute-start(bf16[272,768]{1,0:T(8,128)(2,1)S(1)} %get-tuple-element.150.x_ref.refs_2_), channel_id=1, source_target_pairs={{0,1},{1,2},{2,3},{4,5},{5,6},{6,7},{8,9},{9,10},{10,11},{12,13},{... | collective-permute-start | bytes 1253384 | tf_op jit(solution)/shard_map/ppermute | solution.py:50
  33.0 9.9 %collective-permute-start.9 = (bf16[272,768]{1,0:T(8,128)(2,1)S(1)}, bf16[272,768]{1,0:T(8,128)(2,1)S(1)}, u32[]{:S(2)}, u32[]{:S(2)}) collective-permute-start(bf16[272,768]{1,0:T(8,128)(2,1)S(1)} %collective-permute-done.7.xa_ref.refs_1_), channel_id=1, source_target_pairs={{0,1},{1,2},{2,3},{4,5},{5,6},{6,7},{8,9},{9,10},{10,11},{12,13},{... | collective-permute-start | bytes 1253384 | tf_op jit(solution)/shard_map/ppermute | solution.py:50
  37.4 9.9 %collective-permute-start.10 = (bf16[272,768]{1,0:T(8,128)(2,1)S(1)}, bf16[272,768]{1,0:T(8,128)(2,1)S(1)}, u32[]{:S(2)}, u32[]{:S(2)}) collective-permute-start(bf16[272,768]{1,0:T(8,128)(2,1)S(1)} %collective-permute-done.8.xb_ref.refs_3_), channel_id=1, source_target_pairs={{1,0},{2,1},{3,2},{5,4},{6,5},{7,6},{9,8},{10,9},{11,10},{13,12},{... | collective-permute-start | bytes 1253384 | tf_op jit(solution)/shard_map/ppermute | solution.py:50
  64.5 14.9 %collective-permute-start.12 = (bf16[384,3840]{1,0:T(8,128)(2,1)S(1)}, bf16[384,3840]{1,0:T(8,128)(2,1)S(1)}, u32[]{:S(2)}, u32[]{:S(2)}) collective-permute-start(bf16[384,3840]{1,0:T(8,128)(2,1)S(1)} %get-tuple-element.186), channel_id=1, source_target_pairs={{0,4},{4,0},{8,12},{12,8},{16,20},{20,16},{24,28},{28,24},{1,5},{5... | collective-permute-start | bytes 8847368 | tf_op jit(solution)/shard_map/ppermute | solution.py:44
  69.4 17.8 %collective-permute-start.14 = (bf16[2,192,768]{2,1,0:T(8,128)(2,1)S(1)}, bf16[2,192,768]{2,1,0:T(8,128)(2,1)S(1)}, u32[]{:S(2)}, u32[]{:S(2)}) collective-permute-start(bf16[2,192,768]{2,1,0:T(8,128)(2,1)S(1)} %get-tuple-element.308), channel_id=1, source_target_pairs={{0,16},{4,20},{8,24},{12,28},{16,0},{20,4},{24,8},{28,12},{1,17},{... | collective-permute-start | bytes 1769480 | tf_op jit(solution)/shard_map/ppermute | solution.py:44
  73.6 15.1 %collective-permute-start.13 = (bf16[2,192,768]{2,1,0:T(8,128)(2,1)S(1)}, bf16[2,192,768]{2,1,0:T(8,128)(2,1)S(1)}, u32[]{:S(2)}, u32[]{:S(2)}) collective-permute-start(bf16[2,192,768]{2,1,0:T(8,128)(2,1)S(1)} %get-tuple-element.309), channel_id=1, source_target_pairs={{0,8},{4,12},{8,0},{12,4},{16,24},{20,28},{24,16},{28,20},{1,9},{5... | collective-permute-start | bytes 1769480 | tf_op jit(solution)/shard_map/ppermute | solution.py:44
  83.6 15.6 %collective-permute-start.17 = (bf16[384,2304]{1,0:T(8,128)(2,1)S(1)}, bf16[384,2304]{1,0:T(8,128)(2,1)S(1)}, u32[]{:S(2)}, u32[]{:S(2)}) collective-permute-start(bf16[384,2304]{1,0:T(8,128)(2,1)S(1)} %get-tuple-element.205), channel_id=1, source_target_pairs={{0,4},{4,0},{8,12},{12,8},{16,20},{20,16},{24,28},{28,24},{1,5},{5... | collective-permute-start | bytes 5308424 | tf_op jit(solution)/shard_map/ppermute | solution.py:44
  88.9 10.0 %collective-permute-start.15 = (bf16[192,768]{1,0:T(8,128)(2,1)S(1)}, bf16[192,768]{1,0:T(8,128)(2,1)S(1)}, u32[]{:S(2)}, u32[]{:S(2)}) collective-permute-start(bf16[192,768]{1,0:T(8,128)(2,1)S(1)} %get-tuple-element.203), channel_id=1, source_target_pairs={{0,16},{4,20},{8,24},{12,28},{16,0},{20,4},{24,8},{28,12},{1,17},{... | collective-permute-start | bytes 884744 | tf_op jit(solution)/shard_map/ppermute | solution.py:44
  89.3 9.9 %collective-permute-start.16 = (bf16[192,768]{1,0:T(8,128)(2,1)S(1)}, bf16[192,768]{1,0:T(8,128)(2,1)S(1)}, u32[]{:S(2)}, u32[]{:S(2)}) collective-permute-start(bf16[192,768]{1,0:T(8,128)(2,1)S(1)} %get-tuple-element.204), channel_id=1, source_target_pairs={{0,8},{4,12},{8,0},{12,4},{16,24},{20,28},{24,16},{28,20},{1,9},{5... | collective-permute-start | bytes 884744 | tf_op jit(solution)/shard_map/ppermute | solution.py:44
  90.3 23.3 %collective-permute-start.22 = (bf16[2,48,3840]{2,1,0:T(8,128)(2,1)S(1)}, bf16[2,48,3840]{2,1,0:T(8,128)(2,1)S(1)}, u32[]{:S(2)}, u32[]{:S(2)}) collective-permute-start(bf16[2,48,3840]{2,1,0:T(8,128)(2,1)S(1)} %bitcast.95), channel_id=1, source_target_pairs={{0,8},{4,12},{8,0},{12,4},{16,24},{20,28},{24,16},{28,20},{1,9},{5... | collective-permute-start | bytes 2211848 | tf_op jit(solution)/shard_map/ppermute | solution.py:44
  91.8 21.7 %collective-permute-start.23 = (bf16[2,48,3840]{2,1,0:T(8,128)(2,1)S(1)}, bf16[2,48,3840]{2,1,0:T(8,128)(2,1)S(1)}, u32[]{:S(2)}, u32[]{:S(2)}) collective-permute-start(bf16[2,48,3840]{2,1,0:T(8,128)(2,1)S(1)} %bitcast.94), channel_id=1, source_target_pairs={{0,16},{4,20},{8,24},{12,28},{16,0},{20,4},{24,8},{28,12},{1,17},{... | collective-permute-start | bytes 2211848 | tf_op jit(solution)/shard_map/ppermute | solution.py:44
  99.3 11.6 %collective-permute-start.18 = (bf16[256,768]{1,0:T(8,128)(2,1)S(1)}, bf16[256,768]{1,0:T(8,128)(2,1)S(1)}, u32[]{:S(2)}, u32[]{:S(2)}) collective-permute-start(bf16[256,768]{1,0:T(8,128)(2,1)S(1)} %get-tuple-element.206), channel_id=1, source_target_pairs={{1,0},{2,1},{3,2},{5,4},{6,5},{7,6},{9,8},{10,9},{11,10},{13,12},{... | collective-permute-start | bytes 1179656 | tf_op jit(solution)/shard_map/ppermute | solution.py:50
  100.5 13.0 %collective-permute-start.19 = (bf16[256,768]{1,0:T(8,128)(2,1)S(1)}, bf16[256,768]{1,0:T(8,128)(2,1)S(1)}, u32[]{:S(2)}, u32[]{:S(2)}) collective-permute-start(bf16[256,768]{1,0:T(8,128)(2,1)S(1)} %get-tuple-element.207), channel_id=1, source_target_pairs={{0,1},{1,2},{2,3},{4,5},{5,6},{6,7},{8,9},{9,10},{10,11},{12,13},{... | collective-permute-start | bytes 1179656 | tf_op jit(solution)/shard_map/ppermute | solution.py:50
  105.5 11.2 %collective-permute-start.24 = (bf16[192,768]{1,0:T(8,128)(2,1)S(1)}, bf16[192,768]{1,0:T(8,128)(2,1)S(1)}, u32[]{:S(2)}, u32[]{:S(2)}) collective-permute-start(bf16[192,768]{1,0:T(8,128)(2,1)S(1)} %get-tuple-element.299), channel_id=1, source_target_pairs={{0,1},{1,0},{2,3},{3,2},{4,5},{5,4},{6,7},{7,6},{8,9},{9,8},{10,11... | collective-permute-start | bytes 884744 | tf_op jit(solution)/shard_map/ppermute | solution.py:44
  116.9 9.7 %collective-permute-start.21 = (bf16[256,768]{1,0:T(8,128)(2,1)S(1)}, bf16[256,768]{1,0:T(8,128)(2,1)S(1)}, u32[]{:S(2)}, u32[]{:S(2)}) collective-permute-start(bf16[256,768]{1,0:T(8,128)(2,1)S(1)} %get-tuple-element.314), channel_id=1, source_target_pairs={{0,1},{1,2},{2,3},{4,5},{5,6},{6,7},{8,9},{9,10},{10,11},{12,13},{... | collective-permute-start | bytes 1179656 | tf_op jit(solution)/shard_map/ppermute | solution.py:50
  121.3 11.7 %collective-permute-start.20 = (bf16[256,768]{1,0:T(8,128)(2,1)S(1)}, bf16[256,768]{1,0:T(8,128)(2,1)S(1)}, u32[]{:S(2)}, u32[]{:S(2)}) collective-permute-start(bf16[256,768]{1,0:T(8,128)(2,1)S(1)} %get-tuple-element.315), channel_id=1, source_target_pairs={{1,0},{2,1},{3,2},{5,4},{6,5},{7,6},{9,8},{10,9},{11,10},{13,12},{... | collective-permute-start | bytes 1179656 | tf_op jit(solution)/shard_map/ppermute | solution.py:50
  123.2 11.2 %collective-permute-start.26 = (bf16[48,3840]{1,0:T(8,128)(2,1)S(1)}, bf16[48,3840]{1,0:T(8,128)(2,1)S(1)}, u32[]{:S(2)}, u32[]{:S(2)}) collective-permute-start(bf16[48,3840]{1,0:T(8,128)(2,1)S(1)} %get-tuple-element.302), channel_id=1, source_target_pairs={{0,8},{4,12},{8,0},{12,4},{16,24},{20,28},{24,16},{28,20},{1,9},{5... | collective-permute-start | bytes 1105928 | tf_op jit(solution)/shard_map/ppermute | solution.py:44
  124.4 10.0 %collective-permute-start.25 = (bf16[48,3840]{1,0:T(8,128)(2,1)S(1)}, bf16[48,3840]{1,0:T(8,128)(2,1)S(1)}, u32[]{:S(2)}, u32[]{:S(2)}) collective-permute-start(bf16[48,3840]{1,0:T(8,128)(2,1)S(1)} %get-tuple-element.303), channel_id=1, source_target_pairs={{0,16},{4,20},{8,24},{12,28},{16,0},{20,4},{24,8},{28,12},{1,17},{... | collective-permute-start | bytes 1105928 | tf_op jit(solution)/shard_map/ppermute | solution.py:44
  134.6 10.8 %collective-permute-start.29 = (bf16[2,48,2304]{2,1,0:T(8,128)(2,1)S(1)}, bf16[2,48,2304]{2,1,0:T(8,128)(2,1)S(1)}, u32[]{:S(2)}, u32[]{:S(2)}) collective-permute-start(bf16[2,48,2304]{2,1,0:T(8,128)(2,1)S(1)} %bitcast.97), channel_id=1, source_target_pairs={{0,8},{4,12},{8,0},{12,4},{16,24},{20,28},{24,16},{28,20},{1,9},{5... | collective-permute-start | bytes 1327112 | tf_op jit(solution)/shard_map/ppermute | solution.py:44
  135.9 9.4 %collective-permute-start.30 = (bf16[2,48,2304]{2,1,0:T(8,128)(2,1)S(1)}, bf16[2,48,2304]{2,1,0:T(8,128)(2,1)S(1)}, u32[]{:S(2)}, u32[]{:S(2)}) collective-permute-start(bf16[2,48,2304]{2,1,0:T(8,128)(2,1)S(1)} %bitcast.96), channel_id=1, source_target_pairs={{0,16},{4,20},{8,24},{12,28},{16,0},{20,4},{24,8},{28,12},{1,17},{... | collective-permute-start | bytes 1327112 | tf_op jit(solution)/shard_map/ppermute | solution.py:44
  140.2 24.9 %collective-permute-start.33 = (bf16[192,768]{1,0:T(8,128)(2,1)S(1)}, bf16[192,768]{1,0:T(8,128)(2,1)S(1)}, u32[]{:S(2)}, u32[]{:S(2)}) collective-permute-start(bf16[192,768]{1,0:T(8,128)(2,1)S(1)} %add_convert_fusion.9), channel_id=1, source_target_pairs={{0,2},{1,3},{2,0},{3,1},{4,6},{5,7},{6,4},{7,5},{8,10},{9,11},{10,... | collective-permute-start | bytes 884744 | tf_op jit(solution)/shard_map/ppermute | solution.py:44
  143.4 11.4 %collective-permute-start.28 = (f32[16,768]{1,0:T(8,128)S(1)}, f32[16,768]{1,0:T(8,128)S(1)}, u32[]{:S(2)}, u32[]{:S(2)}) collective-permute-start(f32[16,768]{1,0:T(8,128)S(1)} %add.345), channel_id=1, source_target_pairs={{0,8},{4,12},{8,0},{12,4},{16,24},{20,28},{24,16},{28,20},{1,9},{5... | collective-permute-start | bytes 147464 | tf_op jit(solution)/shard_map/ppermute | solution.py:44
  145.6 10.2 %collective-permute-start.35 = (bf16[48,2304]{1,0:T(8,128)(2,1)S(1)}, bf16[48,2304]{1,0:T(8,128)(2,1)S(1)}, u32[]{:S(2)}, u32[]{:S(2)}) collective-permute-start(bf16[48,2304]{1,0:T(8,128)(2,1)S(1)} %get-tuple-element.310), channel_id=1, source_target_pairs={{0,8},{4,12},{8,0},{12,4},{16,24},{20,28},{24,16},{28,20},{1,9},{5... | collective-permute-start | bytes 663560 | tf_op jit(solution)/shard_map/ppermute | solution.py:44
  145.8 10.0 %collective-permute-start.34 = (bf16[48,2304]{1,0:T(8,128)(2,1)S(1)}, bf16[48,2304]{1,0:T(8,128)(2,1)S(1)}, u32[]{:S(2)}, u32[]{:S(2)}) collective-permute-start(bf16[48,2304]{1,0:T(8,128)(2,1)S(1)} %get-tuple-element.311), channel_id=1, source_target_pairs={{0,16},{4,20},{8,24},{12,28},{16,0},{20,4},{24,8},{28,12},{1,17},{... | collective-permute-start | bytes 663560 | tf_op jit(solution)/shard_map/ppermute | solution.py:44
  147.6 26.5 %collective-permute-start.36 = (bf16[48,3840]{1,0:T(8,128)(2,1)S(1)}, bf16[48,3840]{1,0:T(8,128)(2,1)S(1)}, u32[]{:S(2)}, u32[]{:S(2)}) collective-permute-start(bf16[48,3840]{1,0:T(8,128)(2,1)S(1)} %add_convert_fusion.7), channel_id=1, source_target_pairs={{0,2},{1,3},{2,0},{3,1},{4,6},{5,7},{6,4},{7,5},{8,10},{9,11},{10,... | collective-permute-start | bytes 1105928 | tf_op jit(solution)/shard_map/ppermute | solution.py:44
  154.8 10.3 %collective-permute-start.32 = (f32[16,768]{1,0:T(8,128)S(1)}, f32[16,768]{1,0:T(8,128)S(1)}, u32[]{:S(2)}, u32[]{:S(2)}) collective-permute-start(f32[16,768]{1,0:T(8,128)S(1)} %add.349), channel_id=1, source_target_pairs={{0,16},{4,20},{8,24},{12,28},{16,0},{20,4},{24,8},{28,12},{1,17},{... | collective-permute-start | bytes 147464 | tf_op jit(solution)/shard_map/ppermute | solution.py:44
  165.3 13.6 %collective-permute-start.37 = (bf16[48,2304]{1,0:T(8,128)(2,1)S(1)}, bf16[48,2304]{1,0:T(8,128)(2,1)S(1)}, u32[]{:S(2)}, u32[]{:S(2)}) collective-permute-start(bf16[48,2304]{1,0:T(8,128)(2,1)S(1)} %broadcast_select_fusion.10), channel_id=1, source_target_pairs={{0,1},{1,0},{2,3},{3,2},{4,5},{5,4},{6,7},{7,6},{8,9},{9,8},{10,11... | collective-permute-start | bytes 663560 | tf_op jit(solution)/shard_map/ppermute | solution.py:44
  167.4 17.8 %collective-permute-start.40 = (bf16[192,768]{1,0:T(8,128)(2,1)S(1)}, bf16[192,768]{1,0:T(8,128)(2,1)S(1)}, u32[]{:S(2)}, u32[]{:S(2)}) collective-permute-start(bf16[192,768]{1,0:T(8,128)(2,1)S(1)} %add_convert_fusion.8), channel_id=1, source_target_pairs={{0,1},{1,0},{2,3},{3,2},{4,5},{5,4},{6,7},{7,6},{8,9},{9,8},{10,11... | collective-permute-start | bytes 884744 | tf_op jit(solution)/shard_map/ppermute | solution.py:44
  178.9 12.9 %collective-permute-start.39 = (bf16[48,2304]{1,0:T(8,128)(2,1)S(1)}, bf16[48,2304]{1,0:T(8,128)(2,1)S(1)}, u32[]{:S(2)}, u32[]{:S(2)}) collective-permute-start(bf16[48,2304]{1,0:T(8,128)(2,1)S(1)} %add_convert_fusion.11), channel_id=1, source_target_pairs={{0,2},{1,3},{2,0},{3,1},{4,6},{5,7},{6,4},{7,5},{8,10},{9,11},{10,... | collective-permute-start | bytes 663560 | tf_op jit(solution)/shard_map/ppermute | solution.py:44
  179.6 19.8 %collective-permute-start.43 = (bf16[48,3840]{1,0:T(8,128)(2,1)S(1)}, bf16[48,3840]{1,0:T(8,128)(2,1)S(1)}, u32[]{:S(2)}, u32[]{:S(2)}) collective-permute-start(bf16[48,3840]{1,0:T(8,128)(2,1)S(1)} %add_convert_fusion.6), channel_id=1, source_target_pairs={{0,1},{1,0},{2,3},{3,2},{4,5},{5,4},{6,7},{7,6},{8,9},{9,8},{10,11... | collective-permute-start | bytes 1105928 | tf_op jit(solution)/shard_map/ppermute | solution.py:44
  191.9 12.7 %collective-permute-start.42 = (bf16[48,2304]{1,0:T(8,128)(2,1)S(1)}, bf16[48,2304]{1,0:T(8,128)(2,1)S(1)}, u32[]{:S(2)}, u32[]{:S(2)}) collective-permute-start(bf16[48,2304]{1,0:T(8,128)(2,1)S(1)} %add_convert_fusion.10), channel_id=1, source_target_pairs={{0,1},{1,0},{2,3},{3,2},{4,5},{5,4},{6,7},{7,6},{8,9},{9,8},{10,11... | collective-permute-start | bytes 663560 | tf_op jit(solution)/shard_map/ppermute | solution.py:44
  (40 other events, 227.8 us)

commit v9 on v5

--- a/solution.py
+++ b/solution.py
@@ -719,7 +719,7 @@
     vectors = vector_copy.astype(f32)
     raw = raw_input.reshape(width, features)
     cot = cotangent.reshape(width, features)
-    own_ids = segment_ids
+    own_ids = segment_ids.astype(f32)
     count = owners.bit_length() - 1
     scalar = pl.BlockSpec(memory_space=pltpu.SMEM)
     vmem = pltpu.VMEM
@@ -764,11 +764,11 @@
     rounds.send()
     rounds.take()
     rounds.send()
-    tied = together(*rounds.arrived, table, column_start, vectors, *lows)
+    tied = together(*rounds.arrived, table, column_start, vectors, own_ids, *lows)
     ways = len(rounds.arrived)
     rounds.arrived = list(tied[:ways])
-    table, column_start, vectors = tied[ways : ways + 3]
-    lows = list(tied[ways + 3 :])
+    table, column_start, vectors, own_ids = tied[ways : ways + 4]
+    lows = list(tied[ways + 4 :])
     rounds.take()
     while rounds.left():
         rounds.send()
@@ -1034,7 +1034,16 @@
     rounds.take()
     small = rounds.block
     line_one.arrived, line_three.keep = together(line_one.arrived, line_three.keep)
-    shrink_share = line_one.result()
+    shrink_new = adam_rule(
+        shrink_master,
+        shrink_moment,
+        shrink_square,
+        line_one.result().astype(f32),
+        step_value,
+        rate_matrix,
+        decay_matrix,
+    )
+    line_three.arrived, small, *shrink_new = together(line_three.arrived, small, *shrink_new)
     line_three.gather()
     expand_share = line_two.result()
     inlet_share = line_three.result()
@@ -1059,13 +1068,13 @@
         (inlet_master, inlet_moment, inlet_square, inlet_share),
         (outlet_master, outlet_moment, outlet_square, expand_share[:, inner:]),
         (expand_master, expand_moment, expand_square, expand_share[:, :inner]),
-        (shrink_master, shrink_moment, shrink_square, shrink_share),
     ):
         updates.extend(
             adam_rule(
                 master, moment, square, share.astype(f32), step_value, rate_matrix, decay_matrix
             )
         )
+    updates.extend(shrink_new)
     updates.extend(
         adam_rule(
             vector_master, vector_moment, vector_square, vector_share, step_value, rate_vector, 0.0

time: 193 us -> 192 us (level)
  starting transfers between devices: 67.8 us -> 65.6 us
  waiting for transfers between devices: 64.1 us -> 66.3 us
    ppermute x36, starting transfers between devices: 45.8 us -> 40.4 us  [flipped(): return lax.ppermute(block, axis, [(i, i ^ bit) for i in range(size)])]
    ppermute x8, starting transfers between devices: 21.9 us -> 25.3 us  [moved(): return lax.ppermute(block, axis, route)]
    ppermute x36, waiting for transfers between devices: 45.5 us -> 47.6 us  [flipped(): return lax.ppermute(block, axis, [(i, i ^ bit) for i in range(size)])]
    unnamed x56 -> x52, local copies, waits for them, and re-layouts: 5.99 us -> 4.17 us
  transfers between devices with their start and end apart: 44 -> 44, of which waited for: 19 -> 20; matrix products, arithmetic and copies ran while one was open for 7% -> 8% of each run, Pallas kernels for 10% -> 10%
where the time goes in v9:
time: 192 us; the launch traced here: 193 us
  waiting for transfers between devices  66.3 us (35%)
  starting transfers between devices  65.6 us (34%)
  Pallas kernels  37.8 us (20%)
  other arithmetic  17.2 us (9%)
  local copies, waits for them, and re-layouts  4.3 us (2%)
  between operations  2 us (1%)
    ppermute x36, waiting for transfers between devices, flipped(): return lax.ppermute(block, axis, [(i, i ^ bit) for i in range(size)])  47.6 us
    ppermute x36, starting transfers between devices, flipped(): return lax.ppermute(block, axis, [(i, i ^ bit) for i in range(size)])  40.4 us
    pallas_call x13, Pallas kernels, call(): pl.pallas_call(kernel, grid_spec=pltpu.PrefetchScalarGridSpec(num_scalar_...  37.8 us
    ppermute x8, starting transfers between devices, moved(): return lax.ppermute(block, axis, route)  25.3 us
    ppermute x8, waiting for transfers between devices, moved(): return lax.ppermute(block, axis, route)  18.7 us
    convert_element_type x5, other arithmetic, adam_rule(): return (weight_new, moment_new, square_new, weight_new.astype(bf16))  8.96 us
    unnamed x52, local copies, waits for them, and re-layouts  4.17 us
  transfers between devices with their start and end apart: 44, of which 20 were waited for; matrix products, arithmetic and copies ran while one was open for 8% of the time, Pallas kernels for 10%

profile of v9, /device:TPU:0, one launch (start us, length us, event | category | flops | bytes accessed | tf_op | source)
XLA Modules:
  0.0 193.2 jit_solution(12938836186004094053)
XLA Ops:
  3.3 2.8 %collective-permute-start.1 = (f32[2,768]{1,0:T(2,128)S(1)}, f32[2,768]{1,0:T(2,128)S(1)}, u32[]{:S(2)}, u32[]{:S(2)}) collective-permute-start(f32[2,768]{1,0:T(2,128)S(1)} %add.302), channel_id=1, source_target_pairs={{0,8},{4,12},{8,0},{12,4},{16,24},{20,28},{24,16},{28,20},{1,9},{5... | collective-permute-start | bytes 18440 | tf_op jit(solution)/shard_map/ppermute | solution.py:44
  9.8 2.4 %collective-permute-done.3 = f32[2,768]{1,0:T(2,128)S(1)} collective-permute-done((f32[2,768]{1,0:T(2,128)S(1)}, f32[2,768]{1,0:T(2,128)S(1)}, u32[]{:S(2)}, u32[]{:S(2)}) %collective-permute-start.3) | collective-permute-done | bytes 6176 | tf_op jit(solution)/shard_map/ppermute | solution.py:44
  12.2 2.7 %collective-permute-start.5 = (f32[2,768]{1,0:T(2,128)S(1)}, f32[2,768]{1,0:T(2,128)S(1)}, u32[]{:S(2)}, u32[]{:S(2)}) collective-permute-start(f32[2,768]{1,0:T(2,128)S(1)} %add_add_fusion.1), channel_id=1, source_target_pairs={{0,2},{1,3},{2,0},{3,1},{4,6},{5,7},{6,4},{7,5},{8,10},{9,11},{10,... | collective-permute-start | bytes 18440 | tf_op jit(solution)/shard_map/ppermute | solution.py:44
  16.8 3.4 %collective-permute-done.6 = f32[2,768]{1,0:T(2,128)S(1)} collective-permute-done((f32[2,768]{1,0:T(2,128)S(1)}, f32[2,768]{1,0:T(2,128)S(1)}, u32[]{:S(2)}, u32[]{:S(2)}) %collective-permute-start.6) | collective-permute-done | bytes 6176 | tf_op jit(solution)/shard_map/ppermute | solution.py:44
  29.0 4.1 %collective-permute-done.8.xb_ref.refs_3_ = bf16[272,768]{1,0:T(8,128)(2,1)S(1)} collective-permute-done((bf16[272,768]{1,0:T(8,128)(2,1)S(1)}, bf16[272,768]{1,0:T(8,128)(2,1)S(1)}, u32[]{:S(2)}, u32[]{:S(2)}) %collective-permute-start.8) | collective-permute-done | bytes 417824 | tf_op jit(solution)/shard_map/ppermute | solution.py:50
  33.1 3.6 %collective-permute-start.9 = (bf16[272,768]{1,0:T(8,128)(2,1)S(1)}, bf16[272,768]{1,0:T(8,128)(2,1)S(1)}, u32[]{:S(2)}, u32[]{:S(2)}) collective-permute-start(bf16[272,768]{1,0:T(8,128)(2,1)S(1)} %collective-permute-done.7.xa_ref.refs_1_), channel_id=1, source_target_pairs={{0,1},{1,2},{2,3},{4,5},{5,6},{6,7},{8,9},{9,10},{10,11},{12,13},{... | collective-permute-start | bytes 1253384 | tf_op jit(solution)/shard_map/ppermute | solution.py:50
  40.0 2.3 %collective-permute-done.9.xa_ref.refs_0_ = bf16[272,768]{1,0:T(8,128)(2,1)S(1)} collective-permute-done((bf16[272,768]{1,0:T(8,128)(2,1)S(1)}, bf16[272,768]{1,0:T(8,128)(2,1)S(1)}, u32[]{:S(2)}, u32[]{:S(2)}) %collective-permute-start.9) | collective-permute-done | bytes 417824 | tf_op jit(solution)/shard_map/ppermute | solution.py:50
  42.3 4.4 %collective-permute-done.10.xb_ref.refs_4_ = bf16[272,768]{1,0:T(8,128)(2,1)S(1)} collective-permute-done((bf16[272,768]{1,0:T(8,128)(2,1)S(1)}, bf16[272,768]{1,0:T(8,128)(2,1)S(1)}, u32[]{:S(2)}, u32[]{:S(2)}) %collective-permute-start.10) | collective-permute-done | bytes 417824 | tf_op jit(solution)/shard_map/ppermute | solution.py:50
  47.8 5.3 %attend.1 = (bf16[256,768]{1,0:T(8,128)(2,1)S(1)}, f32[3,4,256]{2,1,0:T(4,128)S(1)}, s32[2]{0:T(128)S(1)}) custom-call(s32[28]{0:T(128)S(1)} %pad_add_fusion.table, bf16[256,768]{1,0:T(8,128)(2,1)S(1)} %get-tuple-element.144.q_ref, bf16[5,256,1536]{2,1,0:T(8,128)(2,1)S(1)} %get-tuple-element.154.kv_ref, f32[1,256]{1,0:T(1,128)S(1)} %convert_element_type.410.id_ref.qid_ref, ...), custom_call_target="tpu_custom_call" | custom-call | flops 1048576 | bytes 65536 | tf_op jit(solution)/shard_map/attend/pallas_call | solution.py:159
  53.1 10.8 %ffn.1 = (bf16[256,768]{1,0:T(8,128)(2,1)}, f32[256,768]{1,0:T(8,128)S(1)}, bf16[256,768]{1,0:T(8,128)(2,1)S(1)}, bf16[2,4,192,768]{3,2,1,0:T(8,128)(2,1)S(1)}, ...) custom-call(s32[28]{0:T(128)S(1)} %pad_add_fusion.table, ...), custom_call_target="tpu_custom_call" | custom-call | flops 1048576 | bytes 65536 | tf_op jit(solution)/shard_map/ffn/pallas_call | solution.py:159
  64.4 2.9 %attend_back.3 = (bf16[256,256]{1,0:T(8,128)(2,1)S(1)}, bf16[5,256,256]{2,1,0:T(8,128)(2,1)S(1)}, bf16[5,256,256]{2,1,0:T(8,128)(2,1)S(1)}, f32[2,256]{1,0:T(2,128)S(1)}) custom-call(s32[2]{0:T(128)S(1)} %get-tuple-element.161.bounds.refs_5_, bf16[256,768]{1,0:T(8,128)(2,1)S(1)} %get-tuple-element.144.q_ref, ...), custom_call_target="tpu_custom_call" | custom-call | flops 1048576 | bytes 65536 | tf_op jit(solution)/shard_map/attend_back/pallas_call | solution.py:159
  71.1 2.7 %attend_back.4 = (bf16[256,256]{1,0:T(8,128)(2,1)S(1)}, bf16[5,256,256]{2,1,0:T(8,128)(2,1)S(1)}, bf16[5,256,256]{2,1,0:T(8,128)(2,1)S(1)}, f32[2,256]{1,0:T(2,128)S(1)}) custom-call(s32[2]{0:T(128)S(1)} %get-tuple-element.161.bounds.refs_5_, bf16[256,768]{1,0:T(8,128)(2,1)S(1)} %get-tuple-element.144.q_ref, ...), custom_call_target="tpu_custom_call" | custom-call | flops 1048576 | bytes 65536 | tf_op jit(solution)/shard_map/attend_back/pallas_call | solution.py:159
  73.8 2.7 %attend_back.5 = (bf16[256,256]{1,0:T(8,128)(2,1)S(1)}, bf16[5,256,256]{2,1,0:T(8,128)(2,1)S(1)}, bf16[5,256,256]{2,1,0:T(8,128)(2,1)S(1)}, f32[2,256]{1,0:T(2,128)S(1)}) custom-call(s32[2]{0:T(128)S(1)} %get-tuple-element.161.bounds.refs_5_, bf16[256,768]{1,0:T(8,128)(2,1)S(1)} %get-tuple-element.144.q_ref, ...), custom_call_target="tpu_custom_call" | custom-call | flops 1048576 | bytes 65536 | tf_op jit(solution)/shard_map/attend_back/pallas_call | solution.py:159
  76.5 2.6 %parts.1 = (bf16[4,256,768]{2,1,0:T(8,128)(2,1)S(1)}, f32[256,768]{1,0:T(8,128)S(1)}) custom-call(s32[2]{0:T(128)S(1)} %get-tuple-element.161.bounds.refs_5_, bf16[256,256]{1,0:T(8,128)(2,1)S(1)} %get-tuple-element.194.refs_0_.refs_6_, bf16[256,256]{1,0:T(8,128)(2,1)S(1)} %get-tuple-element.195.refs_1_.refs_7_, ...), custom_call_target="tpu_custom_call" | custom-call | flops 1048576 | bytes 65536 | tf_op jit(solution)/shard_map/parts/pallas_call | solution.py:159
  79.2 5.0 %collective-permute-done.15 = bf16[2,192,768]{2,1,0:T(8,128)(2,1)S(1)} collective-permute-done((bf16[2,192,768]{2,1,0:T(8,128)(2,1)S(1)}, bf16[2,192,768]{2,1,0:T(8,128)(2,1)S(1)}, u32[]{:S(2)}, u32[]{:S(2)}) %collective-permute-start.15) | collective-permute-done | bytes 589856 | tf_op jit(solution)/shard_map/ppermute | solution.py:44
  88.2 8.2 %collective-permute-start.14 = (bf16[256,768]{1,0:T(8,128)(2,1)S(1)}, bf16[256,768]{1,0:T(8,128)(2,1)S(1)}, u32[]{:S(2)}, u32[]{:S(2)}) collective-permute-start(bf16[256,768]{1,0:T(8,128)(2,1)S(1)} %get-tuple-element.298), channel_id=1, source_target_pairs={{0,1},{1,2},{2,3},{4,5},{5,6},{6,7},{8,9},{9,10},{10,11},{12,13},{... | collective-permute-start | bytes 1179656 | tf_op jit(solution)/shard_map/ppermute | solution.py:50
  96.4 4.1 %weights.1 = (bf16[384,2304]{1,0:T(8,128)(2,1)S(1)}, bf16[384,2304]{1,0:T(8,128)(2,1)S(1)}) custom-call(s32[28]{0:T(128)S(1)} %pad_add_fusion.table, bf16[272,768]{1,0:T(8,128)(2,1)S(1)} %collective-permute-done.9.xa_ref.refs_0_, bf16[272,768]{1,0:T(8,128)(2,1)S(1)} %collective-permute-done.7.xa_ref.refs_1_, ...), custom_call_target="tpu_custom_call" | custom-call | flops 1048576 | bytes 65536 | tf_op jit(solution)/shard_map/weights/pallas_call | solution.py:159
  104.7 6.4 %collective-permute-start.20 = (bf16[256,768]{1,0:T(8,128)(2,1)S(1)}, bf16[256,768]{1,0:T(8,128)(2,1)S(1)}, u32[]{:S(2)}, u32[]{:S(2)}) collective-permute-start(bf16[256,768]{1,0:T(8,128)(2,1)S(1)} %get-tuple-element.296), channel_id=1, source_target_pairs={{0,1},{1,2},{2,3},{4,5},{5,6},{6,7},{8,9},{9,10},{10,11},{12,13},{... | collective-permute-start | bytes 1179656 | tf_op jit(solution)/shard_map/ppermute | solution.py:50
  111.5 6.6 %collective-permute-done.19.right_ref = bf16[256,768]{1,0:T(8,128)(2,1)S(1)} collective-permute-done((bf16[256,768]{1,0:T(8,128)(2,1)S(1)}, bf16[256,768]{1,0:T(8,128)(2,1)S(1)}, u32[]{:S(2)}, u32[]{:S(2)}) %collective-permute-start.19) | collective-permute-done | bytes 393248 | tf_op jit(solution)/shard_map/ppermute | solution.py:50
  128.2 2.8 %collective-permute-start.27 = (f32[16,768]{1,0:T(8,128)S(1)}, f32[16,768]{1,0:T(8,128)S(1)}, u32[]{:S(2)}, u32[]{:S(2)}) collective-permute-start(f32[16,768]{1,0:T(8,128)S(1)} %add.341), channel_id=1, source_target_pairs={{0,2},{1,3},{2,0},{3,1},{4,6},{5,7},{6,4},{7,5},{8,10},{9,11},{10,... | collective-permute-start | bytes 147464 | tf_op jit(solution)/shard_map/ppermute | solution.py:44
  131.1 4.3 %collective-permute-done.28 = bf16[48,3840]{1,0:T(8,128)(2,1)S(1)} collective-permute-done((bf16[48,3840]{1,0:T(8,128)(2,1)S(1)}, bf16[48,3840]{1,0:T(8,128)(2,1)S(1)}, u32[]{:S(2)}, u32[]{:S(2)}) %collective-permute-start.28) | collective-permute-done | bytes 368672 | tf_op jit(solution)/shard_map/ppermute | solution.py:44
  135.4 2.7 %collective-permute-start.34 = (bf16[192,768]{1,0:T(8,128)(2,1)S(1)}, bf16[192,768]{1,0:T(8,128)(2,1)S(1)}, u32[]{:S(2)}, u32[]{:S(2)}) collective-permute-start(bf16[192,768]{1,0:T(8,128)(2,1)S(1)} %add_convert_fusion.9), channel_id=1, source_target_pairs={{0,2},{1,3},{2,0},{3,1},{4,6},{5,7},{6,4},{7,5},{8,10},{9,11},{10,... | collective-permute-start | bytes 884744 | tf_op jit(solution)/shard_map/ppermute | solution.py:44
  139.0 3.8 %collective-permute-done.24 = bf16[2,48,2304]{2,1,0:T(8,128)(2,1)S(1)} collective-permute-done((bf16[2,48,2304]{2,1,0:T(8,128)(2,1)S(1)}, bf16[2,48,2304]{2,1,0:T(8,128)(2,1)S(1)}, u32[]{:S(2)}, u32[]{:S(2)}) %collective-permute-start.24) | collective-permute-done | bytes 442400 | tf_op jit(solution)/shard_map/ppermute | solution.py:44
  145.0 3.7 %collective-permute-done.35 = bf16[48,3840]{1,0:T(8,128)(2,1)S(1)} collective-permute-done((bf16[48,3840]{1,0:T(8,128)(2,1)S(1)}, bf16[48,3840]{1,0:T(8,128)(2,1)S(1)}, u32[]{:S(2)}, u32[]{:S(2)}) %collective-permute-start.35) | collective-permute-done | bytes 368672 | tf_op jit(solution)/shard_map/ppermute | solution.py:44
  148.9 2.2 %collective-permute-start.36 = (bf16[48,3840]{1,0:T(8,128)(2,1)S(1)}, bf16[48,3840]{1,0:T(8,128)(2,1)S(1)}, u32[]{:S(2)}, u32[]{:S(2)}) collective-permute-start(bf16[48,3840]{1,0:T(8,128)(2,1)S(1)} %add_convert_fusion.7), channel_id=1, source_target_pairs={{0,2},{1,3},{2,0},{3,1},{4,6},{5,7},{6,4},{7,5},{8,10},{9,11},{10,... | collective-permute-start | bytes 1105928 | tf_op jit(solution)/shard_map/ppermute | solution.py:44
  151.5 2.5 %collective-permute-start.37 = (bf16[48,2304]{1,0:T(8,128)(2,1)S(1)}, bf16[48,2304]{1,0:T(8,128)(2,1)S(1)}, u32[]{:S(2)}, u32[]{:S(2)}) collective-permute-start(bf16[48,2304]{1,0:T(8,128)(2,1)S(1)} %get-tuple-element.275), channel_id=1, source_target_pairs={{0,1},{1,0},{2,3},{3,2},{4,5},{5,4},{6,7},{7,6},{8,9},{9,8},{10,11... | collective-permute-start | bytes 663560 | tf_op jit(solution)/shard_map/ppermute | solution.py:44
  159.4 7.7 %collective-permute-done.36 = bf16[48,3840]{1,0:T(8,128)(2,1)S(1)} collective-permute-done((bf16[48,3840]{1,0:T(8,128)(2,1)S(1)}, bf16[48,3840]{1,0:T(8,128)(2,1)S(1)}, u32[]{:S(2)}, u32[]{:S(2)}) %collective-permute-start.36) | collective-permute-done | bytes 368672 | tf_op jit(solution)/shard_map/ppermute | solution.py:44
  168.0 5.6 %collective-permute-done.41 = bf16[192,768]{1,0:T(8,128)(2,1)S(1)} collective-permute-done((bf16[192,768]{1,0:T(8,128)(2,1)S(1)}, bf16[192,768]{1,0:T(8,128)(2,1)S(1)}, u32[]{:S(2)}, u32[]{:S(2)}) %collective-permute-start.41) | collective-permute-done | bytes 294944 | tf_op jit(solution)/shard_map/ppermute | solution.py:44
  174.0 2.6 %fusion.44 = (bf16[384,768]{1,0:T(8,128)(2,1)}, f32[384,768]{1,0:T(8,128)}, f32[384,768]{1,0:T(8,128)}, f32[384,768]{1,0:T(8,128)}) fusion(f32[384,768]{1,0:T(8,128)S(1)} %copy-done.6, f32[]{:T(128)} %bitcast.35, f32[]{:T(128)} %bitcast.34, f32[]{:T(128)} %bitcast.33, bf16[192,768]{1,0:T(8,128)(2,1)S(1)} %get-tuple-element.303, ...), kind=kLoop, calls=%fused_computation.110 | loop fusion | flops 5603328 | bytes 8257548 | tf_op jit(solution)/shard_map/convert_element_type | solution.py:677
  176.6 2.3 %collective-permute-done.39 = bf16[48,2304]{1,0:T(8,128)(2,1)S(1)} collective-permute-done((bf16[48,2304]{1,0:T(8,128)(2,1)S(1)}, bf16[48,2304]{1,0:T(8,128)(2,1)S(1)}, u32[]{:S(2)}, u32[]{:S(2)}) %collective-permute-start.39) | collective-permute-done | bytes 221216 | tf_op jit(solution)/shard_map/ppermute | solution.py:44
  182.3 4.1 %collective-permute-done.43 = bf16[48,3840]{1,0:T(8,128)(2,1)S(1)} collective-permute-done((bf16[48,3840]{1,0:T(8,128)(2,1)S(1)}, bf16[48,3840]{1,0:T(8,128)(2,1)S(1)}, u32[]{:S(2)}, u32[]{:S(2)}) %collective-permute-start.43) | collective-permute-done | bytes 368672 | tf_op jit(solution)/shard_map/ppermute | solution.py:44
  186.5 2.6 %fusion.35 = (bf16[96,3072]{1,0:T(8,128)(2,1)}, f32[96,3072]{1,0:T(8,128)}, f32[96,3072]{1,0:T(8,128)}, f32[96,3072]{1,0:T(8,128)}) fusion(f32[96,3072]{1,0:T(8,128)S(1)} %copy-done.9, f32[]{:T(128)} %bitcast.35, f32[]{:T(128)} %bitcast.34, f32[]{:T(128)} %bitcast.33, bf16[48,3840]{1,0:T(8,128)(2,1)S(1)} %get-tuple-element.301, ...), kind=kLoop, calls=%fused_computation.107 | loop fusion | flops 5603328 | bytes 8405004 | tf_op jit(solution)/shard_map/convert_element_type | solution.py:677
  (166 shorter events, 61.5 us)
Async XLA Ops:
  22.8 10.3 %collective-permute-start.8 = (bf16[272,768]{1,0:T(8,128)(2,1)S(1)}, bf16[272,768]{1,0:T(8,128)(2,1)S(1)}, u32[]{:S(2)}, u32[]{:S(2)}) collective-permute-start(bf16[272,768]{1,0:T(8,128)(2,1)S(1)} %get-tuple-element.142.x_ref.refs_2_), channel_id=1, source_target_pairs={{1,0},{2,1},{3,2},{5,4},{6,5},{7,6},{9,8},{10,9},{11,10},{13,12},{... | collective-permute-start | bytes 1253384 | tf_op jit(solution)/shard_map/ppermute | solution.py:50
  33.1 9.1 %collective-permute-start.9 = (bf16[272,768]{1,0:T(8,128)(2,1)S(1)}, bf16[272,768]{1,0:T(8,128)(2,1)S(1)}, u32[]{:S(2)}, u32[]{:S(2)}) collective-permute-start(bf16[272,768]{1,0:T(8,128)(2,1)S(1)} %collective-permute-done.7.xa_ref.refs_1_), channel_id=1, source_target_pairs={{0,1},{1,2},{2,3},{4,5},{5,6},{6,7},{8,9},{9,10},{10,11},{12,13},{... | collective-permute-start | bytes 1253384 | tf_op jit(solution)/shard_map/ppermute | solution.py:50
  36.7 9.9 %collective-permute-start.10 = (bf16[272,768]{1,0:T(8,128)(2,1)S(1)}, bf16[272,768]{1,0:T(8,128)(2,1)S(1)}, u32[]{:S(2)}, u32[]{:S(2)}) collective-permute-start(bf16[272,768]{1,0:T(8,128)(2,1)S(1)} %collective-permute-done.8.xb_ref.refs_3_), channel_id=1, source_target_pairs={{1,0},{2,1},{3,2},{5,4},{6,5},{7,6},{9,8},{10,9},{11,10},{13,12},{... | collective-permute-start | bytes 1253384 | tf_op jit(solution)/shard_map/ppermute | solution.py:50
  63.9 12.6 %collective-permute-start.12 = (bf16[384,3840]{1,0:T(8,128)(2,1)S(1)}, bf16[384,3840]{1,0:T(8,128)(2,1)S(1)}, u32[]{:S(2)}, u32[]{:S(2)}) collective-permute-start(bf16[384,3840]{1,0:T(8,128)(2,1)S(1)} %get-tuple-element.178), channel_id=1, source_target_pairs={{0,4},{4,0},{8,12},{12,8},{16,20},{20,16},{24,28},{28,24},{1,5},{5... | collective-permute-start | bytes 8847368 | tf_op jit(solution)/shard_map/ppermute | solution.py:44
  68.7 15.4 %collective-permute-start.15 = (bf16[2,192,768]{2,1,0:T(8,128)(2,1)S(1)}, bf16[2,192,768]{2,1,0:T(8,128)(2,1)S(1)}, u32[]{:S(2)}, u32[]{:S(2)}) collective-permute-start(bf16[2,192,768]{2,1,0:T(8,128)(2,1)S(1)} %get-tuple-element.291), channel_id=1, source_target_pairs={{0,8},{4,12},{8,0},{12,4},{16,24},{20,28},{24,16},{28,20},{1,9},{5... | collective-permute-start | bytes 1769480 | tf_op jit(solution)/shard_map/ppermute | solution.py:44
  69.3 15.1 %collective-permute-start.16 = (bf16[2,192,768]{2,1,0:T(8,128)(2,1)S(1)}, bf16[2,192,768]{2,1,0:T(8,128)(2,1)S(1)}, u32[]{:S(2)}, u32[]{:S(2)}) collective-permute-start(bf16[2,192,768]{2,1,0:T(8,128)(2,1)S(1)} %get-tuple-element.290), channel_id=1, source_target_pairs={{0,16},{4,20},{8,24},{12,28},{16,0},{20,4},{24,8},{28,12},{1,17},{... | collective-permute-start | bytes 1769480 | tf_op jit(solution)/shard_map/ppermute | solution.py:44
  84.7 15.9 %collective-permute-start.17 = (bf16[192,768]{1,0:T(8,128)(2,1)S(1)}, bf16[192,768]{1,0:T(8,128)(2,1)S(1)}, u32[]{:S(2)}, u32[]{:S(2)}) collective-permute-start(bf16[192,768]{1,0:T(8,128)(2,1)S(1)} %get-tuple-element.289), channel_id=1, source_target_pairs={{0,16},{4,20},{8,24},{12,28},{16,0},{20,4},{24,8},{28,12},{1,17},{... | collective-permute-start | bytes 884744 | tf_op jit(solution)/shard_map/ppermute | solution.py:44
  86.5 14.1 %collective-permute-start.18 = (bf16[192,768]{1,0:T(8,128)(2,1)S(1)}, bf16[192,768]{1,0:T(8,128)(2,1)S(1)}, u32[]{:S(2)}, u32[]{:S(2)}) collective-permute-start(bf16[192,768]{1,0:T(8,128)(2,1)S(1)} %get-tuple-element.288), channel_id=1, source_target_pairs={{0,8},{4,12},{8,0},{12,4},{16,24},{20,28},{24,16},{28,20},{1,9},{5... | collective-permute-start | bytes 884744 | tf_op jit(solution)/shard_map/ppermute | solution.py:44
  86.9 16.4 %collective-permute-start.13 = (bf16[256,768]{1,0:T(8,128)(2,1)S(1)}, bf16[256,768]{1,0:T(8,128)(2,1)S(1)}, u32[]{:S(2)}, u32[]{:S(2)}) collective-permute-start(bf16[256,768]{1,0:T(8,128)(2,1)S(1)} %get-tuple-element.299), channel_id=1, source_target_pairs={{1,0},{2,1},{3,2},{5,4},{6,5},{7,6},{9,8},{10,9},{11,10},{13,12},{... | collective-permute-start | bytes 1179656 | tf_op jit(solution)/shard_map/ppermute | solution.py:50
  88.2 15.1 %collective-permute-start.14 = (bf16[256,768]{1,0:T(8,128)(2,1)S(1)}, bf16[256,768]{1,0:T(8,128)(2,1)S(1)}, u32[]{:S(2)}, u32[]{:S(2)}) collective-permute-start(bf16[256,768]{1,0:T(8,128)(2,1)S(1)} %get-tuple-element.298), channel_id=1, source_target_pairs={{0,1},{1,2},{2,3},{4,5},{5,6},{6,7},{8,9},{9,10},{10,11},{12,13},{... | collective-permute-start | bytes 1179656 | tf_op jit(solution)/shard_map/ppermute | solution.py:50
  100.5 25.2 %collective-permute-start.21 = (bf16[384,2304]{1,0:T(8,128)(2,1)S(1)}, bf16[384,2304]{1,0:T(8,128)(2,1)S(1)}, u32[]{:S(2)}, u32[]{:S(2)}) collective-permute-start(bf16[384,2304]{1,0:T(8,128)(2,1)S(1)} %get-tuple-element.217), channel_id=1, source_target_pairs={{0,4},{4,0},{8,12},{12,8},{16,20},{20,16},{24,28},{28,24},{1,5},{5... | collective-permute-start | bytes 5308424 | tf_op jit(solution)/shard_map/ppermute | solution.py:44
  101.0 22.4 %collective-permute-start.22 = (bf16[2,48,3840]{2,1,0:T(8,128)(2,1)S(1)}, bf16[2,48,3840]{2,1,0:T(8,128)(2,1)S(1)}, u32[]{:S(2)}, u32[]{:S(2)}) collective-permute-start(bf16[2,48,3840]{2,1,0:T(8,128)(2,1)S(1)} %bitcast.95), channel_id=1, source_target_pairs={{0,8},{4,12},{8,0},{12,4},{16,24},{20,28},{24,16},{28,20},{1,9},{5... | collective-permute-start | bytes 2211848 | tf_op jit(solution)/shard_map/ppermute | solution.py:44
  102.8 20.7 %collective-permute-start.23 = (bf16[2,48,3840]{2,1,0:T(8,128)(2,1)S(1)}, bf16[2,48,3840]{2,1,0:T(8,128)(2,1)S(1)}, u32[]{:S(2)}, u32[]{:S(2)}) collective-permute-start(bf16[2,48,3840]{2,1,0:T(8,128)(2,1)S(1)} %bitcast.94), channel_id=1, source_target_pairs={{0,16},{4,20},{8,24},{12,28},{16,0},{20,4},{24,8},{28,12},{1,17},{... | collective-permute-start | bytes 2211848 | tf_op jit(solution)/shard_map/ppermute | solution.py:44
  103.4 14.7 %collective-permute-start.19 = (bf16[256,768]{1,0:T(8,128)(2,1)S(1)}, bf16[256,768]{1,0:T(8,128)(2,1)S(1)}, u32[]{:S(2)}, u32[]{:S(2)}) collective-permute-start(bf16[256,768]{1,0:T(8,128)(2,1)S(1)} %get-tuple-element.297), channel_id=1, source_target_pairs={{1,0},{2,1},{3,2},{5,4},{6,5},{7,6},{9,8},{10,9},{11,10},{13,12},{... | collective-permute-start | bytes 1179656 | tf_op jit(solution)/shard_map/ppermute | solution.py:50
  104.7 15.2 %collective-permute-start.20 = (bf16[256,768]{1,0:T(8,128)(2,1)S(1)}, bf16[256,768]{1,0:T(8,128)(2,1)S(1)}, u32[]{:S(2)}, u32[]{:S(2)}) collective-permute-start(bf16[256,768]{1,0:T(8,128)(2,1)S(1)} %get-tuple-element.296), channel_id=1, source_target_pairs={{0,1},{1,2},{2,3},{4,5},{5,6},{6,7},{8,9},{9,10},{10,11},{12,13},{... | collective-permute-start | bytes 1179656 | tf_op jit(solution)/shard_map/ppermute | solution.py:50
  118.2 10.0 %collective-permute-start.30 = (bf16[192,768]{1,0:T(8,128)(2,1)S(1)}, bf16[192,768]{1,0:T(8,128)(2,1)S(1)}, u32[]{:S(2)}, u32[]{:S(2)}) collective-permute-start(bf16[192,768]{1,0:T(8,128)(2,1)S(1)} %get-tuple-element.281), channel_id=1, source_target_pairs={{0,1},{1,0},{2,3},{3,2},{4,5},{5,4},{6,7},{7,6},{8,9},{9,8},{10,11... | collective-permute-start | bytes 884744 | tf_op jit(solution)/shard_map/ppermute | solution.py:44
  123.8 11.6 %collective-permute-start.28 = (bf16[48,3840]{1,0:T(8,128)(2,1)S(1)}, bf16[48,3840]{1,0:T(8,128)(2,1)S(1)}, u32[]{:S(2)}, u32[]{:S(2)}) collective-permute-start(bf16[48,3840]{1,0:T(8,128)(2,1)S(1)} %get-tuple-element.285), channel_id=1, source_target_pairs={{0,16},{4,20},{8,24},{12,28},{16,0},{20,4},{24,8},{28,12},{1,17},{... | collective-permute-start | bytes 1105928 | tf_op jit(solution)/shard_map/ppermute | solution.py:44
  123.9 14.1 %collective-permute-start.29 = (bf16[48,3840]{1,0:T(8,128)(2,1)S(1)}, bf16[48,3840]{1,0:T(8,128)(2,1)S(1)}, u32[]{:S(2)}, u32[]{:S(2)}) collective-permute-start(bf16[48,3840]{1,0:T(8,128)(2,1)S(1)} %get-tuple-element.284), channel_id=1, source_target_pairs={{0,8},{4,12},{8,0},{12,4},{16,24},{20,28},{24,16},{28,20},{1,9},{5... | collective-permute-start | bytes 1105928 | tf_op jit(solution)/shard_map/ppermute | solution.py:44
  126.0 16.8 %collective-permute-start.24 = (bf16[2,48,2304]{2,1,0:T(8,128)(2,1)S(1)}, bf16[2,48,2304]{2,1,0:T(8,128)(2,1)S(1)}, u32[]{:S(2)}, u32[]{:S(2)}) collective-permute-start(bf16[2,48,2304]{2,1,0:T(8,128)(2,1)S(1)} %bitcast.97), channel_id=1, source_target_pairs={{0,8},{4,12},{8,0},{12,4},{16,24},{20,28},{24,16},{28,20},{1,9},{5... | collective-permute-start | bytes 1327112 | tf_op jit(solution)/shard_map/ppermute | solution.py:44
  127.5 15.2 %collective-permute-start.25 = (bf16[2,48,2304]{2,1,0:T(8,128)(2,1)S(1)}, bf16[2,48,2304]{2,1,0:T(8,128)(2,1)S(1)}, u32[]{:S(2)}, u32[]{:S(2)}) collective-permute-start(bf16[2,48,2304]{2,1,0:T(8,128)(2,1)S(1)} %bitcast.96), channel_id=1, source_target_pairs={{0,16},{4,20},{8,24},{12,28},{16,0},{20,4},{24,8},{28,12},{1,17},{... | collective-permute-start | bytes 1327112 | tf_op jit(solution)/shard_map/ppermute | solution.py:44
  128.2 10.7 %collective-permute-start.27 = (f32[16,768]{1,0:T(8,128)S(1)}, f32[16,768]{1,0:T(8,128)S(1)}, u32[]{:S(2)}, u32[]{:S(2)}) collective-permute-start(f32[16,768]{1,0:T(8,128)S(1)} %add.341), channel_id=1, source_target_pairs={{0,2},{1,3},{2,0},{3,1},{4,6},{5,7},{6,4},{7,5},{8,10},{9,11},{10,... | collective-permute-start | bytes 147464 | tf_op jit(solution)/shard_map/ppermute | solution.py:44
  135.4 15.8 %collective-permute-start.34 = (bf16[192,768]{1,0:T(8,128)(2,1)S(1)}, bf16[192,768]{1,0:T(8,128)(2,1)S(1)}, u32[]{:S(2)}, u32[]{:S(2)}) collective-permute-start(bf16[192,768]{1,0:T(8,128)(2,1)S(1)} %add_convert_fusion.9), channel_id=1, source_target_pairs={{0,2},{1,3},{2,0},{3,1},{4,6},{5,7},{6,4},{7,5},{8,10},{9,11},{10,... | collective-permute-start | bytes 884744 | tf_op jit(solution)/shard_map/ppermute | solution.py:44
  138.5 10.3 %collective-permute-start.35 = (bf16[48,3840]{1,0:T(8,128)(2,1)S(1)}, bf16[48,3840]{1,0:T(8,128)(2,1)S(1)}, u32[]{:S(2)}, u32[]{:S(2)}) collective-permute-start(bf16[48,3840]{1,0:T(8,128)(2,1)S(1)} %get-tuple-element.278), channel_id=1, source_target_pairs={{0,1},{1,0},{2,3},{3,2},{4,5},{5,4},{6,7},{7,6},{8,9},{9,8},{10,11... | collective-permute-start | bytes 1105928 | tf_op jit(solution)/shard_map/ppermute | solution.py:44
  138.9 12.3 %collective-permute-start.33 = (f32[16,768]{1,0:T(8,128)S(1)}, f32[16,768]{1,0:T(8,128)S(1)}, u32[]{:S(2)}, u32[]{:S(2)}) collective-permute-start(f32[16,768]{1,0:T(8,128)S(1)} %add.349), channel_id=1, source_target_pairs={{0,4},{4,0},{8,12},{12,8},{16,20},{20,16},{24,28},{28,24},{1,5},{5... | collective-permute-start | bytes 147464 | tf_op jit(solution)/shard_map/ppermute | solution.py:44
  142.9 8.4 %collective-permute-start.31 = (bf16[48,2304]{1,0:T(8,128)(2,1)S(1)}, bf16[48,2304]{1,0:T(8,128)(2,1)S(1)}, u32[]{:S(2)}, u32[]{:S(2)}) collective-permute-start(bf16[48,2304]{1,0:T(8,128)(2,1)S(1)} %get-tuple-element.293), channel_id=1, source_target_pairs={{0,16},{4,20},{8,24},{12,28},{16,0},{20,4},{24,8},{28,12},{1,17},{... | collective-permute-start | bytes 663560 | tf_op jit(solution)/shard_map/ppermute | solution.py:44
  148.9 18.2 %collective-permute-start.36 = (bf16[48,3840]{1,0:T(8,128)(2,1)S(1)}, bf16[48,3840]{1,0:T(8,128)(2,1)S(1)}, u32[]{:S(2)}, u32[]{:S(2)}) collective-permute-start(bf16[48,3840]{1,0:T(8,128)(2,1)S(1)} %add_convert_fusion.7), channel_id=1, source_target_pairs={{0,2},{1,3},{2,0},{3,1},{4,6},{5,7},{6,4},{7,5},{8,10},{9,11},{10,... | collective-permute-start | bytes 1105928 | tf_op jit(solution)/shard_map/ppermute | solution.py:44
  151.5 15.5 %collective-permute-start.37 = (bf16[48,2304]{1,0:T(8,128)(2,1)S(1)}, bf16[48,2304]{1,0:T(8,128)(2,1)S(1)}, u32[]{:S(2)}, u32[]{:S(2)}) collective-permute-start(bf16[48,2304]{1,0:T(8,128)(2,1)S(1)} %get-tuple-element.275), channel_id=1, source_target_pairs={{0,1},{1,0},{2,3},{3,2},{4,5},{5,4},{6,7},{7,6},{8,9},{9,8},{10,11... | collective-permute-start | bytes 663560 | tf_op jit(solution)/shard_map/ppermute | solution.py:44
  155.9 17.8 %collective-permute-start.41 = (bf16[192,768]{1,0:T(8,128)(2,1)S(1)}, bf16[192,768]{1,0:T(8,128)(2,1)S(1)}, u32[]{:S(2)}, u32[]{:S(2)}) collective-permute-start(bf16[192,768]{1,0:T(8,128)(2,1)S(1)} %add_convert_fusion.8), channel_id=1, source_target_pairs={{0,1},{1,0},{2,3},{3,2},{4,5},{5,4},{6,7},{7,6},{8,9},{9,8},{10,11... | collective-permute-start | bytes 884744 | tf_op jit(solution)/shard_map/ppermute | solution.py:44
  158.2 9.8 %collective-permute-start.40 = (f32[16,768]{1,0:T(8,128)S(1)}, f32[16,768]{1,0:T(8,128)S(1)}, u32[]{:S(2)}, u32[]{:S(2)}) collective-permute-start(f32[16,768]{1,0:T(8,128)S(1)} %add.362), channel_id=1, source_target_pairs={{0,16},{4,20},{8,24},{12,28},{16,0},{20,4},{24,8},{28,12},{1,17},{... | collective-permute-start | bytes 147464 | tf_op jit(solution)/shard_map/ppermute | solution.py:44
  167.2 11.7 %collective-permute-start.39 = (bf16[48,2304]{1,0:T(8,128)(2,1)S(1)}, bf16[48,2304]{1,0:T(8,128)(2,1)S(1)}, u32[]{:S(2)}, u32[]{:S(2)}) collective-permute-start(bf16[48,2304]{1,0:T(8,128)(2,1)S(1)} %add_convert_fusion.11), channel_id=1, source_target_pairs={{0,2},{1,3},{2,0},{3,1},{4,6},{5,7},{6,4},{7,5},{8,10},{9,11},{10,... | collective-permute-start | bytes 663560 | tf_op jit(solution)/shard_map/ppermute | solution.py:44
  173.8 12.5 %collective-permute-start.43 = (bf16[48,3840]{1,0:T(8,128)(2,1)S(1)}, bf16[48,3840]{1,0:T(8,128)(2,1)S(1)}, u32[]{:S(2)}, u32[]{:S(2)}) collective-permute-start(bf16[48,3840]{1,0:T(8,128)(2,1)S(1)} %add_convert_fusion.6), channel_id=1, source_target_pairs={{0,1},{1,0},{2,3},{3,2},{4,5},{5,4},{6,7},{7,6},{8,9},{9,8},{10,11... | collective-permute-start | bytes 1105928 | tf_op jit(solution)/shard_map/ppermute | solution.py:44
  179.0 11.1 %collective-permute-start.42 = (bf16[48,2304]{1,0:T(8,128)(2,1)S(1)}, bf16[48,2304]{1,0:T(8,128)(2,1)S(1)}, u32[]{:S(2)}, u32[]{:S(2)}) collective-permute-start(bf16[48,2304]{1,0:T(8,128)(2,1)S(1)} %add_convert_fusion.10), channel_id=1, source_target_pairs={{0,1},{1,0},{2,3},{3,2},{4,5},{5,4},{6,7},{7,6},{8,9},{9,8},{10,11... | collective-permute-start | bytes 663560 | tf_op jit(solution)/shard_map/ppermute | solution.py:44
  (38 other events, 222.6 us)
